TPU v7x, 32 devices: a whole 2x2x4 slice. The times are simulated.
32 devices in a mesh: ep: 8 (over z, y), tp: 4 (over x, core).
Axes of the slice: x: 2, y: 2, z: 4, core: 2. Of those that a mesh axis runs over, the one named last changes fastest.
Arguments:
- hidden_in: bfloat16 [4096, 1536], P(('ep', 'tp')), may hold values from -6 to 6
- gain_attn: bfloat16 [1536], replicated, may hold values from 0.5 to 1.5
- w_query: bfloat16 [1536, 1536], P('tp'), may hold values from -0.15625 to 0.15625
- key_projection_weight: bfloat16 [512, 1536], P('tp'), may hold values from -0.15625 to 0.15625
- value_projection_weight: bfloat16 [512, 1536], P('tp'), may hold values from -0.15625 to 0.15625
- w_out: bfloat16 [1536, 1536], P('tp'), may hold values from -0.625 to 0.625
- gain_ffn: bfloat16 [1536], replicated, may hold values from 0.5 to 1.5
- w_router: bfloat16 [16, 1536], replicated, may hold values from -0.078125 to 0.078125
- w_gate: bfloat16 [16, 1536, 512], P('ep', None, 'tp'), may hold values from -0.15625 to 0.15625
- w_up: bfloat16 [16, 1536, 512], P('ep', None, 'tp'), may hold values from -0.15625 to 0.15625
- w_down: bfloat16 [16, 512, 1536], P('ep', 'tp'), may hold values from -0.75 to 0.75
- expert_ids: int32 [4096, 8], P('ep'), may hold values from 0 to 15, all different within a row; in each aligned block of 512 rows (0 to 511, 512 to 1023, ...) at most 512 rows name the same one
- slot_order: int32 [4096, 8], P('ep'), may hold values from 0 to 4095, as said below
- segment: int32 [4096], P('ep'), may hold values from 0 to 12, as said below
- position: int32 [4096], P('ep'), may hold values from 0 to 303, as said below
- cotangent: bfloat16 [4096, 1536], P(('ep', 'tp')), may hold values from -6 to 6
Outputs:
- output: bfloat16 [4096, 1536], P(('ep', 'tp'))
- grad_input: float32 [4096, 1536], P(('ep', 'tp'))
- grad_gain_attn: float32 [1536], replicated
- grad_query: float32 [1536, 1536], P('tp')
- grad_key: float32 [512, 1536], P('tp')
- grad_value: float32 [512, 1536], P('tp')
- grad_out: float32 [1536, 1536], P('tp')
- grad_gain_ffn: float32 [1536], replicated
- grad_router: float32 [16, 1536], replicated
- grad_gate: float32 [16, 1536, 512], P('ep', None, 'tp')
- grad_up: float32 [16, 1536, 512], P('ep', None, 'tp')
- grad_down: float32 [16, 512, 1536], P('ep', 'tp')
Inputs may be any that keep to these rules, and one draw needn't show every extreme that they name: `expert_ids`: in the 512 rows of one index of ep no expert is named by more than 512 rows, a bound that some block reaches of them. `slot_order`: within the 512 rows of one index of ep every number from 0 to 4095 appears once. Each tree is 512 consecutive tokens: its first 256 tokens are segment 0; segments 1 to 4 (branches, parent 0) hold 32 tokens each and segments 5 to 12 (leaves, parent 1 + (s - 5) // 2) hold 16 tokens each, each segment contiguous, in an order drawn for every tree. A token's position is its depth on its path: trunk 0 to 255, a branch from 256, a leaf from 288, rising by one along its segment.
All inputs are finite; a program needn't handle non-finite values.
Results may differ from a plain program's by a relative error of at most 0.02.
Values may be sent and summed in bfloat16 or wider, within the bound.
A program may use at most 320 MiB of HBM per device.

v0:
```python
import jax
import jax.numpy as jnp
from jax import lax
from jax.sharding import PartitionSpec as P

HEAD_DIMENSION = 64
TOP = 8
TREE_TOKENS = 512
CAP = 2304


EPSILON = 1e-06
ROPE_BASE = 10000.0
EXACT_PRECISION = lax.Precision.HIGHEST


def carried_in(array, axis, combine, identity):
    length, mine = (lax.axis_size(axis), lax.axis_index(axis))
    everything = lax.all_gather(array, axis)
    start = jnp.broadcast_to(jnp.asarray(identity, array.dtype), array.shape)

    def turn(k, before):
        reached = k < mine
        new = combine(before, everything[k])
        return jnp.where(reached, new, before)

    return lax.fori_loop(0, length, turn, start)


def rope_tables(position, head_width):
    half_width = head_width // 2
    freqs = ROPE_BASE ** (-(jnp.arange(half_width, dtype=jnp.float32) * 2.0 / head_width))
    angle = position.astype(jnp.float32)[:, None] * freqs[None, :]
    return (jnp.cos(angle)[:, None, :], jnp.sin(angle)[:, None, :])


def apply_rotation(value_rows, cosine_lookup, sine_lookup):
    half_width = value_rows.shape[-1] // 2
    first = value_rows[..., :half_width]
    second = value_rows[..., half_width:]
    return jnp.concatenate(
        [
            first * cosine_lookup - second * sine_lookup,
            first * sine_lookup + second * cosine_lookup,
        ],
        axis=-1,
    )


def rotate_back(grads, cosine_lookup, sine_lookup):
    half_width = grads.shape[-1] // 2
    first = grads[..., :half_width]
    second = grads[..., half_width:]
    return jnp.concatenate(
        [
            first * cosine_lookup + second * sine_lookup,
            second * cosine_lookup - first * sine_lookup,
        ],
        axis=-1,
    )


def norm_scale(value_rows):
    return lax.rsqrt(jnp.mean(value_rows * value_rows, axis=-1, keepdims=True) + EPSILON)


def norm_back(value_rows, scale, gain, grad_normed):
    weighted = grad_normed * gain
    inner = jnp.mean(value_rows * weighted, axis=-1, keepdims=True)
    grad_values = scale * weighted - value_rows * (scale * scale * scale) * inner
    return (grad_values, jnp.sum(grad_normed * value_rows * scale, axis=0))


def group_rows(value_rows):
    return lax.all_gather(value_rows, "tp", axis=0, tiled=True)


def group_totals(value_rows):
    return lax.psum_scatter(value_rows, "tp", scatter_dimension=0, tiled=True)


def deal_rows(buffer):
    return lax.all_to_all(buffer, "ep", split_axis=0, concat_axis=0, tiled=True)


def return_rows(buffer):
    return lax.all_to_all(buffer, "ep", split_axis=0, concat_axis=0, tiled=True)


def visible_block(query_seg, query_pos, query_row, key_seg, key_pos, key_row):
    seg_q = query_seg[:, None]
    seg_k = key_seg[None, :]
    above = (
        (seg_k == seg_q)
        | (seg_k == 0)
        | (seg_k >= 1) & (seg_k <= 4) & (seg_q >= 5) & ((seg_q - 5) // 2 + 1 == seg_k)
    )
    same_tree = query_row[:, None] // TREE_TOKENS == key_row[None, :] // TREE_TOKENS
    return above & same_tree & (key_pos[None, :] <= query_pos[:, None])


def block_scores(query_part, key_rows, allowed, scale):
    scores = (
        jnp.einsum("qkgd,pkd->kgqp", query_part, key_rows, preferred_element_type=jnp.float32)
        * scale
    )
    return jnp.where(allowed[None, None], scores, -1e30)


def attend_forward(query_rows, key_rows, value_rows, segment, position):
    total_rows = query_rows.shape[0]
    scale = query_rows.shape[-1] ** (-0.5)
    row_ids = jnp.arange(total_rows, dtype=jnp.int32)
    allowed = visible_block(segment, position, row_ids, segment, position, row_ids)
    scores = block_scores(query_rows, key_rows, allowed, scale)
    top_score = jnp.max(scores, axis=-1, keepdims=True)
    weights = jnp.exp(scores - top_score)
    weight_sum = jnp.sum(weights, axis=-1, keepdims=True)
    probs = (weights / weight_sum).astype(jnp.bfloat16)
    outputs = jnp.einsum(
        "kgqp,pkd->qkgd", probs, value_rows, preferred_element_type=jnp.float32
    ).astype(jnp.bfloat16)
    log_sums = [top_score + jnp.log(weight_sum)]
    return (outputs, log_sums)


def attend_backward(
    query_rows, key_rows, value_rows, segment, position, log_sums, grad_heads, block_rows
):
    total_rows = query_rows.shape[0]
    scale = query_rows.shape[-1] ** (-0.5)
    row_ids = jnp.arange(total_rows, dtype=jnp.int32)
    grad_keys = jnp.zeros(key_rows.shape, jnp.float32)
    grad_values = jnp.zeros(value_rows.shape, jnp.float32)
    grad_query = []
    for number, first_row in enumerate(range(0, total_rows, block_rows)):
        allowed = visible_block(segment, position, row_ids, segment, position, row_ids)
        scores = block_scores(query_rows, key_rows, allowed, scale)
        probs = jnp.where(allowed[None, None], jnp.exp(scores - log_sums[number]), 0.0)
        grad_values = jnp.einsum(
            "kgqp,qkgd->pkd",
            probs.astype(jnp.bfloat16),
            grad_heads,
            preferred_element_type=jnp.float32,
        )
        grad_probs = jnp.einsum(
            "qkgd,pkd->kgqp", grad_heads, value_rows, preferred_element_type=jnp.float32
        )
        inner = jnp.sum(probs * grad_probs, axis=-1, keepdims=True)
        grad_scores = (probs * (grad_probs - inner)).astype(jnp.bfloat16)
        grad_query.append(
            jnp.einsum("kgqp,pkd->qkgd", grad_scores, key_rows, preferred_element_type=jnp.float32)
            * scale
        )
        grad_keys = (
            jnp.einsum(
                "kgqp,qkgd->pkd", grad_scores, query_rows, preferred_element_type=jnp.float32
            )
            * scale
        )
    return (grad_query[0], grad_keys, grad_values)


def local(
    hidden_in,
    gain_attn,
    w_query,
    key_projection_weight,
    value_projection_weight,
    w_out,
    gain_ffn,
    w_router,
    w_gate,
    w_up,
    w_down,
    expert_ids,
    slot_order,
    segment,
    position,
    cotangent,
):
    model_width = w_query.shape[1]
    head_width = HEAD_DIMENSION
    local_heads = w_query.shape[0] // head_width
    local_kv = key_projection_weight.shape[0] // head_width
    group_factor = local_heads // local_kv
    token_count = expert_ids.shape[0]
    share = hidden_in.shape[0]
    row_start = lax.axis_index("tp") * share
    expert_count = w_router.shape[0]
    owners = lax.axis_size("ep")
    per_owner = w_gate.shape[0]
    capacity = 2 * token_count * TOP // expert_count
    pair_count = token_count * TOP
    block_rows = 512
    inputs_own = hidden_in.astype(jnp.float32)
    gain_one = gain_attn.astype(jnp.float32)
    gain_two = gain_ffn.astype(jnp.float32)
    scale_one = norm_scale(inputs_own)
    first_normalized = group_rows((inputs_own * scale_one * gain_one).astype(jnp.bfloat16))
    cosine_lookup, sine_lookup = rope_tables(position, head_width)
    query_proj = jnp.einsum(
        "rd,fd->rf", first_normalized, w_query, preferred_element_type=jnp.float32
    ).reshape(token_count, local_heads, head_width)
    key_proj = jnp.einsum(
        "rd,fd->rf", first_normalized, key_projection_weight, preferred_element_type=jnp.float32
    ).reshape(token_count, local_kv, head_width)
    query_rows = (
        apply_rotation(query_proj, cosine_lookup, sine_lookup)
        .astype(jnp.bfloat16)
        .reshape(token_count, local_kv, group_factor, head_width)
    )
    key_rows = apply_rotation(key_proj, cosine_lookup, sine_lookup).astype(jnp.bfloat16)
    value_rows = (
        jnp.einsum(
            "rd,fd->rf",
            first_normalized,
            value_projection_weight,
            preferred_element_type=jnp.float32,
        )
        .astype(jnp.bfloat16)
        .reshape(token_count, local_kv, head_width)
    )
    head_outputs, log_sums = attend_forward(query_rows, key_rows, value_rows, segment, position)
    head_outputs = head_outputs.reshape(token_count, local_heads * head_width)
    middle_own = inputs_own + group_totals(
        jnp.dot(head_outputs, w_out, preferred_element_type=jnp.float32)
    )
    scale_two = norm_scale(middle_own)
    normed_own = (middle_own * scale_two * gain_two).astype(jnp.bfloat16)
    normed_two = group_rows(normed_own)
    logits = jnp.einsum("rd,ed->re", normed_two, w_router, preferred_element_type=jnp.float32)
    expert_line = jnp.arange(expert_count, dtype=jnp.int32)
    chosen = expert_ids[:, :, None] == expert_line[None, None, :]
    selected = jnp.sum(jnp.where(chosen, logits[:, None, :], 0.0), axis=2)
    gates = jax.nn.softmax(selected, axis=-1)
    ids_flat = expert_ids.reshape(-1)
    order_flat = slot_order.reshape(-1)
    sorted_ids = jnp.zeros((pair_count,), jnp.int32).at[order_flat].set(ids_flat)
    hits = (sorted_ids[:, None] == expert_line[None, :]).astype(jnp.int32)
    running = jnp.cumsum(hits, axis=0)
    rank_sorted = jnp.sum(running * hits, axis=1) - 1
    local_rank = rank_sorted[order_flat]
    counts = jnp.sum(hits, axis=0)
    offsets = carried_in(
        counts, "ep", lambda earlier, later: earlier + later, jnp.zeros_like(counts)
    )
    pair_hot = ids_flat[:, None] == expert_line[None, :]
    global_rank = local_rank + jnp.sum(jnp.where(pair_hot, offsets[None, :], 0), axis=1)
    kept = global_rank < CAP
    slot_index = jnp.where(kept, ids_flat * capacity + local_rank, expert_count * capacity)
    pair_of_slot = (
        jnp.full((expert_count * capacity + 1,), pair_count, jnp.int32)
        .at[slot_index]
        .set(jnp.arange(pair_count, dtype=jnp.int32))[: expert_count * capacity]
    )
    token_of_slot = pair_of_slot // TOP
    send_rows = jnp.take(normed_two, token_of_slot, axis=0, mode="fill", fill_value=0).reshape(
        owners, per_owner, capacity, model_width
    )
    arrived = deal_rows(send_rows)
    gate_act = jnp.einsum("secd,edf->secf", arrived, w_gate, preferred_element_type=jnp.float32)
    up_act = jnp.einsum("secd,edf->secf", arrived, w_up, preferred_element_type=jnp.float32)
    hidden = (jax.nn.silu(gate_act) * up_act).astype(jnp.bfloat16)
    partial_value = jnp.einsum(
        "secf,efd->secd", hidden, w_down, preferred_element_type=jnp.float32
    ).astype(jnp.bfloat16)
    cot_rows = group_rows(cotangent)
    back_rows = return_rows(partial_value).reshape(expert_count * capacity, model_width)
    picked = jnp.take(back_rows, slot_index, axis=0, mode="fill", fill_value=0).reshape(
        token_count, TOP, model_width
    )
    combined = jnp.einsum("rk,rkd->rd", gates, picked, preferred_element_type=jnp.float32)
    output_own = (middle_own + group_totals(combined)).astype(jnp.bfloat16)
    grad_gates_part = jnp.einsum("rd,rkd->rk", cot_rows, picked, preferred_element_type=jnp.float32)
    gate_slot = jnp.take(gates.reshape(-1), pair_of_slot, axis=0, mode="fill", fill_value=0.0)
    cot_slot = jnp.take(cot_rows, token_of_slot, axis=0, mode="fill", fill_value=0)
    grad_send = (
        (gate_slot[:, None] * cot_slot)
        .astype(jnp.bfloat16)
        .reshape(owners, per_owner, capacity, model_width)
    )
    grad_arrived = deal_rows(grad_send)
    sigma = jax.nn.sigmoid(gate_act)
    grad_hidden = jnp.einsum(
        "secd,efd->secf", grad_arrived, w_down, preferred_element_type=jnp.float32
    )
    grad_gate_act = (grad_hidden * up_act * sigma * (1.0 + gate_act * (1.0 - sigma))).astype(
        jnp.bfloat16
    )
    grad_up_act = (grad_hidden * gate_act * sigma).astype(jnp.bfloat16)
    grad_slot_rows = (
        jnp.einsum("secf,edf->secd", grad_gate_act, w_gate, preferred_element_type=jnp.float32)
        + jnp.einsum("secf,edf->secd", grad_up_act, w_up, preferred_element_type=jnp.float32)
    ).astype(jnp.bfloat16)
    grad_w_gate = jnp.einsum(
        "secd,secf->edf", arrived, grad_gate_act, preferred_element_type=jnp.float32
    )
    grad_w_up = jnp.einsum(
        "secd,secf->edf", arrived, grad_up_act, preferred_element_type=jnp.float32
    )
    grad_w_down = jnp.einsum(
        "secf,secd->efd", hidden, grad_arrived, preferred_element_type=jnp.float32
    )
    returned = return_rows(grad_slot_rows).reshape(expert_count * capacity, model_width)
    grad_pairs = jnp.take(returned, slot_index, axis=0, mode="fill", fill_value=0).reshape(
        token_count, TOP, model_width
    )
    grad_normed_part = jnp.sum(grad_pairs, axis=1, dtype=jnp.float32)
    grad_normed_own, grad_gates_own = (
        lax.psum_scatter(grad_normed_part, "tp", scatter_dimension=0, tiled=True),
        lax.psum_scatter(grad_gates_part, "tp", scatter_dimension=0, tiled=True),
    )
    gates_own = lax.dynamic_slice_in_dim(gates, row_start, share, 0)
    ids_own = lax.dynamic_slice_in_dim(expert_ids, row_start, share, 0)
    inner_gate = jnp.sum(gates_own * grad_gates_own, axis=-1, keepdims=True)
    grad_selected = gates_own * (grad_gates_own - inner_gate)
    own_hot = ids_own[:, :, None] == expert_line[None, None, :]
    grad_logits = jnp.sum(jnp.where(own_hot, grad_selected[:, :, None], 0.0), axis=1)
    router_f = w_router.astype(jnp.float32)
    grad_normed_own = grad_normed_own + jnp.dot(grad_logits, router_f, precision=EXACT_PRECISION)
    grad_router = jnp.dot(grad_logits.T, normed_own.astype(jnp.float32), precision=EXACT_PRECISION)
    grad_middle_back, grad_gain_ffn = norm_back(middle_own, scale_two, gain_two, grad_normed_own)
    grad_middle = cotangent.astype(jnp.float32) + grad_middle_back
    grad_attn = group_rows(grad_middle.astype(jnp.bfloat16))
    grad_w_out = jnp.einsum(
        "rf,rd->fd", head_outputs, grad_attn, preferred_element_type=jnp.float32
    )
    grad_heads = (
        jnp.einsum("rd,fd->rf", grad_attn, w_out, preferred_element_type=jnp.float32)
        .astype(jnp.bfloat16)
        .reshape(token_count, local_kv, group_factor, head_width)
    )
    grad_query, grad_keys, grad_values = attend_backward(
        query_rows, key_rows, value_rows, segment, position, log_sums, grad_heads, block_rows
    )
    grad_query_proj = (
        rotate_back(
            grad_query.reshape(token_count, local_heads, head_width), cosine_lookup, sine_lookup
        )
        .astype(jnp.bfloat16)
        .reshape(token_count, local_heads * head_width)
    )
    grad_key_proj = (
        rotate_back(grad_keys, cosine_lookup, sine_lookup)
        .astype(jnp.bfloat16)
        .reshape(token_count, local_kv * head_width)
    )
    grad_value_proj = grad_values.astype(jnp.bfloat16).reshape(token_count, local_kv * head_width)
    grad_w_query = jnp.einsum(
        "rf,rd->fd", grad_query_proj, first_normalized, preferred_element_type=jnp.float32
    )
    grad_w_key = jnp.einsum(
        "rf,rd->fd", grad_key_proj, first_normalized, preferred_element_type=jnp.float32
    )
    grad_w_value = jnp.einsum(
        "rf,rd->fd", grad_value_proj, first_normalized, preferred_element_type=jnp.float32
    )
    grad_normed_one = jnp.einsum(
        "rf,fd->rd", grad_query_proj, w_query, preferred_element_type=jnp.float32
    )
    grad_normed_one = grad_normed_one + jnp.einsum(
        "rf,fd->rd", grad_key_proj, key_projection_weight, preferred_element_type=jnp.float32
    )
    grad_normed_one = grad_normed_one + jnp.einsum(
        "rf,fd->rd", grad_value_proj, value_projection_weight, preferred_element_type=jnp.float32
    )
    grad_one_own = group_totals(grad_normed_one)
    grad_inputs_back, grad_gain_attn = norm_back(inputs_own, scale_one, gain_one, grad_one_own)
    grad_input = grad_middle + grad_inputs_back
    grad_w_query, grad_w_key, grad_w_value, grad_w_out = (
        lax.psum(grad_w_query.astype(jnp.bfloat16), "ep").astype(jnp.float32),
        lax.psum(grad_w_key.astype(jnp.bfloat16), "ep").astype(jnp.float32),
        lax.psum(grad_w_value.astype(jnp.bfloat16), "ep").astype(jnp.float32),
        lax.psum(grad_w_out.astype(jnp.bfloat16), "ep").astype(jnp.float32),
    )
    grad_gain_attn, grad_gain_ffn, grad_router = lax.psum(
        (grad_gain_attn, grad_gain_ffn, grad_router), ("ep", "tp")
    )
    return (
        output_own,
        grad_input,
        grad_gain_attn,
        grad_w_query,
        grad_w_key,
        grad_w_value,
        grad_w_out,
        grad_gain_ffn,
        grad_router,
        grad_w_gate,
        grad_w_up,
        grad_w_down,
    )


def solution(mesh):
    placed = (
        P(("ep", "tp"), None),
        P(),
        P("tp", None),
        P("tp", None),
        P("tp", None),
        P("tp", None),
        P(),
        P(),
        P("ep", None, "tp"),
        P("ep", None, "tp"),
        P("ep", "tp", None),
        P("ep", None),
        P("ep", None),
        P("ep"),
        P("ep"),
        P(("ep", "tp"), None),
    )
    return jax.shard_map(
        local,
        mesh=mesh,
        in_specs=placed,
        out_specs=(
            P(("ep", "tp"), None),
            P(("ep", "tp"), None),
            P(),
            P("tp", None),
            P("tp", None),
            P("tp", None),
            P("tp", None),
            P(),
            P(),
            P("ep", None, "tp"),
            P("ep", None, "tp"),
            P("ep", "tp", None),
        ),
        check_vma=False,
    )
```

profile of v0, /device:TPU:0, one launch (start us, length us, event | category | flops | bytes accessed | tf_op | source)
XLA Modules:
  0.0 2925.8 jit_solution(1993893032222044582)
XLA Ops:
  16.4 18.4 all-gather.6.cloned.1.call-done
  46.3 2.6 fusion.92
  49.8 15.5 scatter_custom_fusion
  65.3 4.6 reduce-window.6
  72.5 11.3 all-reduce
  83.9 3.2 reduce-scatter.6.cloned.1.call-done
  90.9 23.0 gather_fusion
  114.7 15.7 scatter_custom_fusion.1
  131.2 50.9 %gather_fusion.2 = bf16[8192,1536]{1,0:T(8,128)(2,1)} fusion(bf16[512,1536]{1,0:T(8,128)(2,1)} %all-gather.8.cloned.1.call-done, s32[8192]{0:T(1024)S(1)} %get-tuple-element.146), kind=kCustom, calls=%fused_computation.clone | custom fusion | bytes 50364416 | tf_op jit(solution)/shard_map/jit(_take)/gather | solution.py:258
  182.1 21.8 broadcast_select_fusion.2
  203.9 6.5 all-to-all-start
  211.0 21.6 all-gather.10.cloned.1.call-done
  232.6 51.0 %gather_fusion.4 = bf16[8192,1536]{1,0:T(8,128)(2,1)} fusion(bf16[512,1536]{1,0:T(8,128)(2,1)} %all-gather.10.cloned.1.call-done, s32[8192]{0:T(1024)S(1)} %get-tuple-element.146), kind=kCustom, calls=%fused_computation.2.clone | custom fusion | bytes 50364416 | tf_op jit(solution)/shard_map/jit(_take)/gather | solution.py:277
  285.7 45.5 %gather_fusion.1 = f32[8192]{0:T(1024)S(1)} fusion(f32[4096]{0:T(1024)S(1)} %div.99, s32[8192]{0:T(1024)S(1)} %copy-done.60), kind=kCustom, calls=%fused_computation.5 | custom fusion | bytes 98304 | tf_op jit(solution)/shard_map/jit(_take)/gather | solution.py:276
  331.3 23.1 multiply_convert_fusion
  354.4 398.9 %all-to-all-done = bf16[8,2,512,1536]{3,2,1,0:T(8,128)(2,1)} async-done(((bf16[8,2,512,1536]{3,2,1,0:T(8,128)(2,1)}), bf16[8,2,512,1536]{3,2,1,0:T(8,128)(2,1)}, u32[]{:S(2)}, u32[]{:S(2)}) %all-to-all-start) | async-done | bytes 25165856 | tf_op jit(solution)/shard_map/all_to_all | solution.py:83
  753.3 6.5 all-to-all-start.2
  759.9 13.0 fusion.4
  772.9 13.0 fusion.6
  785.9 516.0 %all-to-all-done.2 = bf16[8,2,512,1536]{3,2,1,0:T(8,128)(2,1)} async-done(((bf16[8,2,512,1536]{3,2,1,0:T(8,128)(2,1)}), bf16[8,2,512,1536]{3,2,1,0:T(8,128)(2,1)}, u32[]{:S(2)}, u32[]{:S(2)}) %all-to-all-start.2) | async-done | bytes 25165856 | tf_op jit(solution)/shard_map/all_to_all | solution.py:83
  1301.9 16.2 fusion.22
  1318.1 13.9 fusion.8
  1332.0 20.8 copy.80
  1352.8 6.4 all-to-all-start.1
  1359.2 20.5 fusion.59
  1379.7 27.5 fusion.9
  1407.1 20.8 copy.83
  1427.9 472.4 %all-to-all-done.1 = bf16[8,2,512,1536]{3,2,1,0:T(8,128)(2,1)} async-done(((bf16[8,2,512,1536]{3,2,1,0:T(8,128)(2,1)}), bf16[8,2,512,1536]{3,2,1,0:T(8,128)(2,1)}, u32[]{:S(2)}, u32[]{:S(2)}) %all-to-all-start.1) | async-done | bytes 25165856 | tf_op jit(solution)/shard_map/all_to_all | solution.py:87
  1900.4 6.4 all-to-all-start.3
  1907.1 36.8 %gather_fusion.3 = bf16[4096,1536]{1,0:T(8,128)(2,1)} fusion(bf16[8192,1536]{1,0:T(8,128)(2,1)} %bitcast.30, s32[4096]{0:T(1024)S(1)} %broadcast_clamp_fusion.1), kind=kCustom, calls=%fused_computation.1.clone | custom fusion | bytes 25182208 | tf_op jit(solution)/shard_map/jit(_take)/gather | solution.py:270
  1943.9 12.4 fusion.10
  1957.3 490.2 %all-to-all-done.3 = bf16[8,2,512,1536]{3,2,1,0:T(8,128)(2,1)} async-done(((bf16[8,2,512,1536]{3,2,1,0:T(8,128)(2,1)}), bf16[8,2,512,1536]{3,2,1,0:T(8,128)(2,1)}, u32[]{:S(2)}, u32[]{:S(2)}) %all-to-all-start.3) | async-done | bytes 25165856 | tf_op jit(solution)/shard_map/all_to_all | solution.py:87
  2447.4 36.7 %gather_fusion.5 = bf16[4096,1536]{1,0:T(8,128)(2,1)} fusion(bf16[8192,1536]{1,0:T(8,128)(2,1)} %bitcast.39, s32[4096]{0:T(1024)S(1)} %broadcast_clamp_fusion.1), kind=kCustom, calls=%fused_computation.3.clone | custom fusion | bytes 25182208 | tf_op jit(solution)/shard_map/jit(_take)/gather | solution.py:306
  2484.1 14.8 convert_reduce_fusion
  2499.3 6.6 fusion.12
  2510.1 27.0 reduce-scatter.10.cloned.1.call-done
  2539.6 38.2 %reduce-scatter.8.cloned.1.call-done = f32[128,1536]{1,0:T(8,128)} async-done(((f32[512,1536]{1,0:T(8,128)}), f32[128,1536]{1,0:T(8,128)}) %reduce-scatter.8.cloned.1.call-update) | async-done | bytes 786448 | tf_op jit(solution)/shard_map/reduce_scatter | solution.py:79
  2580.9 19.3 all-gather.12.cloned.1.call-done
  2602.6 4.1 fusion.45
  2609.4 2.7 fusion.16
  2625.3 16.9 convolution_bitcast_fusion
  2642.2 15.8 convolution_bitcast_fusion.1
  2658.1 12.1 fusion.34
  2671.1 80.2 %all-reduce.8.cloned.1.call-done = (bf16[384,1536]{1,0:T(8,128)(2,1)}, bf16[128,1536]{1,0:T(8,128)(2,1)}, bf16[128,1536]{1,0:T(8,128)(2,1)}, bf16[384,1536]{1,0:T(8,128)(2,1)}) async-done(((bf16[384,1536]{1,0:T(8,128)(2,1)}, bf16[128,1536]{1,0:T(8,128)(2,1)}, bf16[128,1536]{1,0:T(8,128)(2,1)}, bf16[384,1536]{1,0:T(8,128)(2,1)}), (bf16[384,1536]{1,0:T(8,128)(2,1)}, bf16[128,1536]{1,0:T(8,128)(2,1)}, ...) | async-done | bytes 3145744 | tf_op jit(solution)/shard_map/psum | solution.py:372
  2755.4 3.0 convert_element_type.167
  2760.1 30.7 %reduce-scatter.14.cloned.1.call-done = f32[128,1536]{1,0:T(8,128)} async-done(((f32[512,1536]{1,0:T(8,128)}), f32[128,1536]{1,0:T(8,128)}) %reduce-scatter.14.cloned.1.call-update) | async-done | bytes 786448 | tf_op jit(solution)/shard_map/reduce_scatter | solution.py:79
  2794.5 39.4 %all-reduce.1 = (f32[1536]{0:T(1024)}, f32[1536]{0:T(1024)}) all-reduce(f32[1536]{0:T(1024)S(1)} %get-tuple-element.111, f32[1536]{0:T(1024)S(1)} %copy-done.67), channel_id=1, replica_groups=mesh['ep'=8,'tp'=4] {'ep','tp'}, use_global_device_ids=true, to_apply=%region_28.31 | all-reduce | flops 3072 | bytes 24576 | tf_op jit(solution)/shard_map/psum | solution.py:377
  2834.0 83.6 %all-reduce.6.cloned.1.call-done = f32[16,1536]{1,0:T(8,128)} async-done(((f32[16,1536]{1,0:T(8,128)}), f32[16,1536]{1,0:T(8,128)}) %all-reduce.6.cloned.1.call-update) | async-done | bytes 98320 | tf_op jit(solution)/shard_map/psum | solution.py:377
  (294 shorter events, 72.1 us)
Async XLA Ops:
  7.2 39.2 %copy-start = (bf16[384,1536]{1,0:T(8,128)(2,1)S(1)}, bf16[384,1536]{1,0:T(8,128)(2,1)}, u32[]{:S(2)}) copy-start(bf16[384,1536]{1,0:T(8,128)(2,1)} %param.27) | copy-start | bytes 3538948
  7.2 29.8 %copy-start.24 = (bf16[384,1536]{1,0:T(8,128)(2,1)S(1)}, bf16[384,1536]{1,0:T(8,128)(2,1)}, u32[]{:S(2)}) copy-start(bf16[384,1536]{1,0:T(8,128)(2,1)} %param.24) | copy-start | bytes 3538948
  7.2 27.6 all-gather.6.cloned.1.call-start
  12.3 74.8 %reduce-scatter.6.cloned.1.call-start = ((), (), s32[]{:S(2)}) async-start(), calls=%async_computation.10 | async-start | bytes 3932160 | tf_op jit(solution)/shard_map/reduce_scatter | solution.py:79
  14.8 24.5 copy-start.16
  49.0 38.2 %copy-start.10 = (bf16[128,1536]{1,0:T(8,128)(2,1)S(1)}, bf16[128,1536]{1,0:T(8,128)(2,1)}, u32[]{:S(2)}) copy-start(bf16[128,1536]{1,0:T(8,128)(2,1)} %param.22) | copy-start | bytes 1179652
  49.0 82.2 %all-gather.8.cloned.1.call-start = ((), (), s32[]{:S(2)}) async-start(), calls=%async_computation.11 | async-start | bytes 1966080 | tf_op jit(solution)/shard_map/all_gather | solution.py:75
  49.1 64.9 %copy-start.58 = (f32[1536]{0:T(1024)}, f32[1536]{0:T(1024)S(1)}, u32[]{:S(2)}) copy-start(f32[1536]{0:T(1024)S(1)} %convert_element_type.141) | copy-start | bytes 18436
  49.7 64.3 %copy-start.45 = (s32[4096]{0:T(1024)}, s32[4096]{0:T(1024)S(1)}, u32[]{:S(2)}) copy-start(s32[4096]{0:T(1024)S(1)} %reshape.618) | copy-start | bytes 49156
  130.5 51.6 %copy-start.37 = (s32[8193]{0:T(1024)}, s32[8193]{0:T(1024)S(1)}, u32[]{:S(2)}) copy-start(s32[8193]{0:T(1024)S(1)} %scatter_custom_fusion.1) | copy-start | bytes 98320
  203.9 549.4 %all-to-all-start = ((bf16[8,2,512,1536]{3,2,1,0:T(8,128)(2,1)}), bf16[8,2,512,1536]{3,2,1,0:T(8,128)(2,1)}, u32[]{:S(2)}, u32[]{:S(2)}) async-start(bf16[8,2,512,1536]{3,2,1,0:T(8,128)(2,1)} %bitcast.219), calls=%async_computation.1 | async-start | bytes 50331648 | tf_op jit(solution)/shard_map/all_to_all | solution.py:83
  210.4 22.2 all-gather.10.cloned.1.call-start
  211.0 72.7 %copy-start.1 = (bf16[512,1536]{1,0:T(8,128)(2,1)S(1)}, bf16[512,1536]{1,0:T(8,128)(2,1)}, u32[]{:S(2)}) copy-start(bf16[512,1536]{1,0:T(8,128)(2,1)} %all-gather.8.cloned.1.call-done) | copy-start | bytes 4718596
  211.0 72.6 %copy-start.51 = (bf16[16,1536]{1,0:T(8,128)(2,1)S(1)}, bf16[16,1536]{1,0:T(8,128)(2,1)}, u32[]{:S(2)}) copy-start(bf16[16,1536]{1,0:T(8,128)(2,1)} %param.29) | copy-start | bytes 147460
  211.0 73.1 %copy-start.54 = (s32[512,8]{0,1:T(8,128)S(1)}, s32[512,8]{0,1:T(8,128)}, u32[]{:S(2)}) copy-start(s32[512,8]{0,1:T(8,128)} %param.33) | copy-start | bytes 49156
  211.0 74.7 %copy-start.60 = (s32[8192]{0:T(1024)S(1)}, s32[8192]{0:T(1024)}, u32[]{:S(2)}) copy-start(s32[8192]{0:T(1024)} %get-tuple-element.145) | copy-start | bytes 98308
  285.4 45.9 %copy-start.61 = (f32[512,8]{0,1:T(8,128)}, f32[512,8]{0,1:T(8,128)S(1)}, u32[]{:S(2)}) copy-start(f32[512,8]{0,1:T(8,128)S(1)} %fusion.72) | copy-start | bytes 49156
  285.7 45.6 %copy-start.38 = (s32[8193]{0:T(1024)S(1)}, s32[8193]{0:T(1024)}, u32[]{:S(2)}) copy-start(s32[8193]{0:T(1024)} %copy-done.37) | copy-start | bytes 98320
  753.3 548.6 %all-to-all-start.2 = ((bf16[8,2,512,1536]{3,2,1,0:T(8,128)(2,1)}), bf16[8,2,512,1536]{3,2,1,0:T(8,128)(2,1)}, u32[]{:S(2)}, u32[]{:S(2)}) async-start(bf16[8,2,512,1536]{3,2,1,0:T(8,128)(2,1)} %bitcast.218), calls=%async_computation.4 | async-start | bytes 50331648 | tf_op jit(solution)/shard_map/all_to_all | solution.py:83
  1318.1 41.1 %copy-start.6 = (bf16[8,2,512,128]{3,2,0,1:T(8,128)(2,1)}, bf16[8,2,512,128]{3,2,0,1:T(8,128)(2,1)S(1)}, u32[]{:S(2)}) copy-start(bf16[8,2,512,128]{3,2,0,1:T(8,128)(2,1)S(1)} %get-tuple-element.134) | copy-start | bytes 6291460
  1352.8 547.6 %all-to-all-start.1 = ((bf16[8,2,512,1536]{3,2,1,0:T(8,128)(2,1)}), bf16[8,2,512,1536]{3,2,1,0:T(8,128)(2,1)}, u32[]{:S(2)}, u32[]{:S(2)}) async-start(bf16[8,2,512,1536]{3,2,1,0:T(8,128)(2,1)} %copy.80), calls=%async_computation.2 | async-start | bytes 50331648 | tf_op jit(solution)/shard_map/all_to_all | solution.py:87
  1427.9 479.1 %copy-start.46 = (s32[4096]{0:T(1024)S(1)}, s32[4096]{0:T(1024)}, u32[]{:S(2)}) copy-start(s32[4096]{0:T(1024)} %copy-done.45) | copy-start | bytes 49156
  1427.9 479.1 %copy-start.48 = (s32[4096]{0:T(1024)S(1)}, s32[4096]{0:T(1024)}, u32[]{:S(2)}) copy-start(s32[4096]{0:T(1024)} %copy-done.47) | copy-start | bytes 49156
  1427.9 479.1 %copy-start.50 = (s32[4096]{0:T(1024)S(1)}, s32[4096]{0:T(1024)}, u32[]{:S(2)}) copy-start(s32[4096]{0:T(1024)} %copy-done.49) | copy-start | bytes 49156
  1900.4 547.0 %all-to-all-start.3 = ((bf16[8,2,512,1536]{3,2,1,0:T(8,128)(2,1)}), bf16[8,2,512,1536]{3,2,1,0:T(8,128)(2,1)}, u32[]{:S(2)}, u32[]{:S(2)}) async-start(bf16[8,2,512,1536]{3,2,1,0:T(8,128)(2,1)} %copy.83), calls=%async_computation.5 | async-start | bytes 50331648 | tf_op jit(solution)/shard_map/all_to_all | solution.py:87
  1906.8 602.0 %reduce-scatter.12.cloned.1.call-start = ((), (), s32[]{:S(2)}) async-start(), calls=%async_computation.15 | async-start | bytes 20480 | tf_op jit(solution)/shard_map/reduce_scatter | solution.py:312
  1907.1 36.8 %copy-start.2 = (bf16[512,1536]{1,0:T(8,128)(2,1)S(1)}, bf16[512,1536]{1,0:T(8,128)(2,1)}, u32[]{:S(2)}) copy-start(bf16[512,1536]{1,0:T(8,128)(2,1)} %all-gather.10.cloned.1.call-done) | copy-start | bytes 4718596
  1957.0 580.1 %reduce-scatter.10.cloned.1.call-start = ((), (), s32[]{:S(2)}) async-start(), calls=%async_computation.14 | async-start | bytes 3932160 | tf_op jit(solution)/shard_map/reduce_scatter | solution.py:311
  2499.0 78.8 %reduce-scatter.8.cloned.1.call-start = ((), (), s32[]{:S(2)}) async-start(), calls=%async_computation.12 | async-start | bytes 3932160 | tf_op jit(solution)/shard_map/reduce_scatter | solution.py:79
  2506.0 31.1 %copy-start.9 = (f32[128,1536]{1,0:T(8,128)S(1)}, f32[128,1536]{1,0:T(8,128)}, u32[]{:S(2)}) copy-start(f32[128,1536]{1,0:T(8,128)} %copy-done.8) | copy-start | bytes 2359300
  2506.0 31.1 %copy-start.52 = (bf16[16,1536]{1,0:T(8,128)(2,1)S(1)}, bf16[16,1536]{1,0:T(8,128)(2,1)}, u32[]{:S(2)}) copy-start(bf16[16,1536]{1,0:T(8,128)(2,1)} %param.29) | copy-start | bytes 147460
  2506.0 31.1 %copy-start.59 = (f32[1536]{0:T(1024)S(1)}, f32[1536]{0:T(1024)}, u32[]{:S(2)}) copy-start(f32[1536]{0:T(1024)} %copy-done.58) | copy-start | bytes 18436
  2506.0 31.1 %copy-start.74 = (f32[128]{0:T(128)S(1)}, f32[128]{0:T(128)}, u32[]{:S(2)}) copy-start(f32[128]{0:T(128)} %copy-done.73) | copy-start | bytes 1540
  2507.9 69.9 %copy-start.20 = (bf16[128,1536]{1,0:T(8,128)(2,1)S(1)}, bf16[128,1536]{1,0:T(8,128)(2,1)}, u32[]{:S(2)}) copy-start(bf16[128,1536]{1,0:T(8,128)(2,1)} %param.37) | copy-start | bytes 1179652
  2507.9 69.9 %copy-start.78 = (f32[128]{0:T(128)S(1)}, f32[128]{0:T(128)}, u32[]{:S(2)}) copy-start(f32[128]{0:T(128)} %get-tuple-element.154) | copy-start | bytes 1540
  2507.9 72.9 %copy-start.64 = (f32[2,3,512]{2,1,0:T(4,128)S(1)}, f32[2,3,512]{2,1,0:T(4,128)}, u32[]{:S(2)}) copy-start(f32[2,3,512]{2,1,0:T(4,128)} %copy-done.63) | copy-start | bytes 36868
  2507.9 72.9 %copy-start.66 = (f32[2,3,512]{2,1,0:T(4,128)S(1)}, f32[2,3,512]{2,1,0:T(4,128)}, u32[]{:S(2)}) copy-start(f32[2,3,512]{2,1,0:T(4,128)} %copy-done.65) | copy-start | bytes 36868
  2507.9 92.3 %all-gather.12.cloned.1.call-start = ((), (), s32[]{:S(2)}) async-start(), calls=%async_computation.16 | async-start | bytes 1966080 | tf_op jit(solution)/shard_map/all_gather | solution.py:75
  2580.4 170.9 %all-reduce.8.cloned.1.call-start = ((), (), s32[]{:S(2)}) async-start(), calls=%async_computation.19 | async-start | bytes 6291456 | tf_op jit(solution)/shard_map/psum | solution.py:372
  2580.9 25.9 copy-start.55
  2620.8 170.0 %reduce-scatter.14.cloned.1.call-start = ((), (), s32[]{:S(2)}) async-start(), calls=%async_computation.17 | async-start | bytes 3932160 | tf_op jit(solution)/shard_map/reduce_scatter | solution.py:79
  2625.1 292.4 %all-reduce.6.cloned.1.call-start = ((), (), s32[]{:S(2)}) async-start(), calls=%async_computation.18 | async-start | bytes 196608 | tf_op jit(solution)/shard_map/psum | solution.py:377
  2753.4 37.4 %copy-start.11 = (bf16[128,1536]{1,0:T(8,128)(2,1)S(1)}, bf16[128,1536]{1,0:T(8,128)(2,1)}, u32[]{:S(2)}) copy-start(bf16[128,1536]{1,0:T(8,128)(2,1)} %param.22) | copy-start | bytes 1179652
  2753.4 37.4 %copy-start.57 = (f32[1536]{0:T(1024)S(1)}, f32[1536]{0:T(1024)}, u32[]{:S(2)}) copy-start(f32[1536]{0:T(1024)} %copy-done.56) | copy-start | bytes 18436
  2753.4 37.4 %copy-start.76 = (f32[128]{0:T(128)S(1)}, f32[128]{0:T(128)}, u32[]{:S(2)}) copy-start(f32[128]{0:T(128)} %copy-done.75) | copy-start | bytes 1540
  2755.4 36.8 %copy-start.15 = (f32[128,1536]{1,0:T(8,128)S(1)}, f32[128,1536]{1,0:T(8,128)}, u32[]{:S(2)}) copy-start(f32[128,1536]{1,0:T(8,128)} %get-tuple-element.130) | copy-start | bytes 2359300
  2755.4 36.8 %copy-start.79 = (f32[128]{0:T(128)S(1)}, f32[128]{0:T(128)}, u32[]{:S(2)}) copy-start(f32[128]{0:T(128)} %get-tuple-element.152) | copy-start | bytes 1540
  2758.4 36.1 %copy-start.67 = (f32[1536]{0:T(1024)S(1)}, f32[1536]{0:T(1024)}, u32[]{:S(2)}) copy-start(f32[1536]{0:T(1024)} %get-tuple-element.109) | copy-start | bytes 18436
  (51 other events, 277.6 us)
Sparse Core Ops, SparseCore 0:
  12.4 22.3 all-gather.5
  49.1 37.9 reduce-scatter.5
  90.4 19.6 all-gather.7
  212.6 20.0 all-gather.9
  1957.1 19.9 reduce-scatter.11
  2499.1 37.9 reduce-scatter.9
  2539.8 37.9 reduce-scatter.7
  2580.5 19.6 all-gather.11
  2620.9 130.3 all-reduce.7
  2753.9 36.8 reduce-scatter.13
  2796.9 120.5 all-reduce.5
where the time goes:
time: 2940 us; the launch traced here: 2930 us
  waiting for transfers between devices  2200 us (75%)
  local copies, waits for them, and re-layouts  331 us (11%)
  matrix products  202 us (7%)
  other arithmetic  97.8 us (3%)
  blocking collectives  50.8 us (2%)
    all_to_all x2, waiting for transfers between devices, return_rows(): return lax.all_to_all(buffer, 'ep', split_axis=0, concat_axis=0, tiled=True)  963 us
    all_to_all x2, waiting for transfers between devices, deal_rows(): return lax.all_to_all(buffer, 'ep', split_axis=0, concat_axis=0, tiled=True)  915 us
    psum x1, waiting for transfers between devices, local(): lax.psum((grad_gain_attn, grad_gain_ffn, grad_router), ('ep', 'tp'))  83.6 us
    psum x1, waiting for transfers between devices, local(): lax.psum(grad_w_query.astype(jnp.bfloat16), 'ep').astype(jnp.float32)  80.2 us
    reduce_scatter x3, waiting for transfers between devices, group_totals(): return lax.psum_scatter(value_rows, 'tp', scatter_dimension=0, tiled=True)  72.1 us
    all_gather x4, waiting for transfers between devices, group_rows(): return lax.all_gather(value_rows, 'tp', axis=0, tiled=True)  59.4 us
  transfers between devices with their start and end apart: 15, of which 13 were waited for; matrix products, arithmetic and copies ran while one was open for 16% of the time, Pallas kernels for 0%

commit v1 on v0

--- a/solution.py
+++ b/solution.py
@@ -4,7 +4,6 @@
 from jax.sharding import PartitionSpec as P
 
 HEAD_DIMENSION = 64
-TOP = 8
 TREE_TOKENS = 512
 CAP = 2304
 
@@ -12,19 +11,6 @@
 EPSILON = 1e-06
 ROPE_BASE = 10000.0
 EXACT_PRECISION = lax.Precision.HIGHEST
-
-
-def carried_in(array, axis, combine, identity):
-    length, mine = (lax.axis_size(axis), lax.axis_index(axis))
-    everything = lax.all_gather(array, axis)
-    start = jnp.broadcast_to(jnp.asarray(identity, array.dtype), array.shape)
-
-    def turn(k, before):
-        reached = k < mine
-        new = combine(before, everything[k])
-        return jnp.where(reached, new, before)
-
-    return lax.fori_loop(0, length, turn, start)
 
 
 def rope_tables(position, head_width):
@@ -79,12 +65,27 @@
     return lax.psum_scatter(value_rows, "tp", scatter_dimension=0, tiled=True)
 
 
-def deal_rows(buffer):
-    return lax.all_to_all(buffer, "ep", split_axis=0, concat_axis=0, tiled=True)
-
-
-def return_rows(buffer):
-    return lax.all_to_all(buffer, "ep", split_axis=0, concat_axis=0, tiled=True)
+def gather_all(value_rows):
+    return lax.all_gather(value_rows, ("ep", "tp"), axis=0, tiled=True)
+
+
+def total_all(value_rows):
+    return lax.psum_scatter(value_rows, ("ep", "tp"), scatter_dimension=0, tiled=True)
+
+
+def kept_pairs(expert_ids, slot_order, expert_count, row_start, share):
+    experts = jnp.arange(expert_count, dtype=jnp.int32)
+    chosen = expert_ids[:, :, None] == experts[None, None, :]
+    last = jnp.int32(1 << 30)
+    order = jnp.min(jnp.where(chosen, slot_order[:, :, None], last), axis=1)
+    counts = jnp.sum((order < last).astype(jnp.int32), axis=0)
+    every = lax.all_gather(counts, "ep")
+    earlier = jnp.arange(every.shape[0], dtype=jnp.int32) < lax.axis_index("ep")
+    offsets = jnp.sum(jnp.where(earlier[:, None], every, 0), axis=0)
+    own = lax.dynamic_slice_in_dim(order, row_start, share, 0)
+    rank = jnp.sum((order[:, None, :] < own[None, :, :]).astype(jnp.int32), axis=0)
+    used = own < last
+    return used, used & (rank + offsets[None, :] < CAP)
 
 
 def visible_block(query_seg, query_pos, query_row, key_seg, key_pos, key_row):
@@ -188,11 +189,10 @@
     share = hidden_in.shape[0]
     row_start = lax.axis_index("tp") * share
     expert_count = w_router.shape[0]
-    owners = lax.axis_size("ep")
     per_owner = w_gate.shape[0]
-    capacity = 2 * token_count * TOP // expert_count
-    pair_count = token_count * TOP
     block_rows = 512
+    used, kept = kept_pairs(expert_ids, slot_order, expert_count, row_start, share)
+    cot_all = gather_all(cotangent)
     inputs_own = hidden_in.astype(jnp.float32)
     gain_one = gain_attn.astype(jnp.float32)
     gain_two = gain_ffn.astype(jnp.float32)
@@ -228,95 +228,71 @@
     )
     scale_two = norm_scale(middle_own)
     normed_own = (middle_own * scale_two * gain_two).astype(jnp.bfloat16)
-    normed_two = group_rows(normed_own)
-    logits = jnp.einsum("rd,ed->re", normed_two, w_router, preferred_element_type=jnp.float32)
-    expert_line = jnp.arange(expert_count, dtype=jnp.int32)
-    chosen = expert_ids[:, :, None] == expert_line[None, None, :]
-    selected = jnp.sum(jnp.where(chosen, logits[:, None, :], 0.0), axis=2)
-    gates = jax.nn.softmax(selected, axis=-1)
-    ids_flat = expert_ids.reshape(-1)
-    order_flat = slot_order.reshape(-1)
-    sorted_ids = jnp.zeros((pair_count,), jnp.int32).at[order_flat].set(ids_flat)
-    hits = (sorted_ids[:, None] == expert_line[None, :]).astype(jnp.int32)
-    running = jnp.cumsum(hits, axis=0)
-    rank_sorted = jnp.sum(running * hits, axis=1) - 1
-    local_rank = rank_sorted[order_flat]
-    counts = jnp.sum(hits, axis=0)
-    offsets = carried_in(
-        counts, "ep", lambda earlier, later: earlier + later, jnp.zeros_like(counts)
-    )
-    pair_hot = ids_flat[:, None] == expert_line[None, :]
-    global_rank = local_rank + jnp.sum(jnp.where(pair_hot, offsets[None, :], 0), axis=1)
-    kept = global_rank < CAP
-    slot_index = jnp.where(kept, ids_flat * capacity + local_rank, expert_count * capacity)
-    pair_of_slot = (
-        jnp.full((expert_count * capacity + 1,), pair_count, jnp.int32)
-        .at[slot_index]
-        .set(jnp.arange(pair_count, dtype=jnp.int32))[: expert_count * capacity]
-    )
-    token_of_slot = pair_of_slot // TOP
-    send_rows = jnp.take(normed_two, token_of_slot, axis=0, mode="fill", fill_value=0).reshape(
-        owners, per_owner, capacity, model_width
-    )
-    arrived = deal_rows(send_rows)
-    gate_act = jnp.einsum("secd,edf->secf", arrived, w_gate, preferred_element_type=jnp.float32)
-    up_act = jnp.einsum("secd,edf->secf", arrived, w_up, preferred_element_type=jnp.float32)
-    hidden = (jax.nn.silu(gate_act) * up_act).astype(jnp.bfloat16)
-    partial_value = jnp.einsum(
-        "secf,efd->secd", hidden, w_down, preferred_element_type=jnp.float32
-    ).astype(jnp.bfloat16)
-    cot_rows = group_rows(cotangent)
-    back_rows = return_rows(partial_value).reshape(expert_count * capacity, model_width)
-    picked = jnp.take(back_rows, slot_index, axis=0, mode="fill", fill_value=0).reshape(
-        token_count, TOP, model_width
-    )
-    combined = jnp.einsum("rk,rkd->rd", gates, picked, preferred_element_type=jnp.float32)
-    output_own = (middle_own + group_totals(combined)).astype(jnp.bfloat16)
-    grad_gates_part = jnp.einsum("rd,rkd->rk", cot_rows, picked, preferred_element_type=jnp.float32)
-    gate_slot = jnp.take(gates.reshape(-1), pair_of_slot, axis=0, mode="fill", fill_value=0.0)
-    cot_slot = jnp.take(cot_rows, token_of_slot, axis=0, mode="fill", fill_value=0)
-    grad_send = (
-        (gate_slot[:, None] * cot_slot)
-        .astype(jnp.bfloat16)
-        .reshape(owners, per_owner, capacity, model_width)
-    )
-    grad_arrived = deal_rows(grad_send)
+    normed_two = gather_all(normed_own)
+    logits = jnp.einsum("rd,ed->re", normed_own, w_router, preferred_element_type=jnp.float32)
+    top_logit = jnp.max(jnp.where(used, logits, -jnp.inf), axis=-1, keepdims=True)
+    powers = jnp.where(used, jnp.exp(logits - top_logit), 0.0)
+    gates = powers / jnp.sum(powers, axis=-1, keepdims=True)
+    first_expert = lax.axis_index("ep") * per_owner
+    kept_all = lax.dynamic_slice_in_dim(
+        gather_all(kept.astype(jnp.float32)), first_expert, per_owner, 1
+    )
+    gate_all = lax.dynamic_slice_in_dim(
+        gather_all(jnp.where(kept, gates, 0.0)), first_expert, per_owner, 1
+    )
+    units = w_gate.shape[2]
+    gate_in = jnp.concatenate([w_gate[e] for e in range(per_owner)], axis=1)
+    up_in = jnp.concatenate([w_up[e] for e in range(per_owner)], axis=1)
+    down_in = w_down.reshape(per_owner * units, model_width)
+    spread = jnp.repeat(gate_all, units, axis=1)
+    gate_act = jnp.dot(normed_two, gate_in, preferred_element_type=jnp.float32)
+    up_act = jnp.dot(normed_two, up_in, preferred_element_type=jnp.float32)
+    back_act = jnp.einsum("rd,fd->rf", cot_all, down_in, preferred_element_type=jnp.float32)
     sigma = jax.nn.sigmoid(gate_act)
-    grad_hidden = jnp.einsum(
-        "secd,efd->secf", grad_arrived, w_down, preferred_element_type=jnp.float32
-    )
+    hidden = gate_act * sigma * up_act
+    weighted_hidden = (spread * hidden).astype(jnp.bfloat16)
+    grad_hidden = spread * back_act
     grad_gate_act = (grad_hidden * up_act * sigma * (1.0 + gate_act * (1.0 - sigma))).astype(
         jnp.bfloat16
     )
     grad_up_act = (grad_hidden * gate_act * sigma).astype(jnp.bfloat16)
-    grad_slot_rows = (
-        jnp.einsum("secf,edf->secd", grad_gate_act, w_gate, preferred_element_type=jnp.float32)
-        + jnp.einsum("secf,edf->secd", grad_up_act, w_up, preferred_element_type=jnp.float32)
+    grad_gates_part = kept_all * jnp.sum(
+        (hidden * back_act).reshape(-1, per_owner, units), axis=2
+    )
+    grad_rows = (
+        jnp.einsum("rf,df->rd", grad_gate_act, gate_in, preferred_element_type=jnp.float32)
+        + jnp.einsum("rf,df->rd", grad_up_act, up_in, preferred_element_type=jnp.float32)
     ).astype(jnp.bfloat16)
+    grad_normed_own = total_all(grad_rows).astype(jnp.float32)
+    grad_gates_own = total_all(
+        lax.dynamic_update_slice_in_dim(
+            jnp.zeros((normed_two.shape[0], expert_count), jnp.float32),
+            grad_gates_part,
+            first_expert,
+            1,
+        )
+    )
+    combined = jnp.dot(weighted_hidden, down_in, preferred_element_type=jnp.float32).astype(
+        jnp.bfloat16
+    )
+    output_own = (middle_own + total_all(combined).astype(jnp.float32)).astype(jnp.bfloat16)
     grad_w_gate = jnp.einsum(
-        "secd,secf->edf", arrived, grad_gate_act, preferred_element_type=jnp.float32
+        "rd,ref->edf",
+        normed_two,
+        grad_gate_act.reshape(-1, per_owner, units),
+        preferred_element_type=jnp.float32,
     )
     grad_w_up = jnp.einsum(
-        "secd,secf->edf", arrived, grad_up_act, preferred_element_type=jnp.float32
+        "rd,ref->edf",
+        normed_two,
+        grad_up_act.reshape(-1, per_owner, units),
+        preferred_element_type=jnp.float32,
     )
     grad_w_down = jnp.einsum(
-        "secf,secd->efd", hidden, grad_arrived, preferred_element_type=jnp.float32
-    )
-    returned = return_rows(grad_slot_rows).reshape(expert_count * capacity, model_width)
-    grad_pairs = jnp.take(returned, slot_index, axis=0, mode="fill", fill_value=0).reshape(
-        token_count, TOP, model_width
-    )
-    grad_normed_part = jnp.sum(grad_pairs, axis=1, dtype=jnp.float32)
-    grad_normed_own, grad_gates_own = (
-        lax.psum_scatter(grad_normed_part, "tp", scatter_dimension=0, tiled=True),
-        lax.psum_scatter(grad_gates_part, "tp", scatter_dimension=0, tiled=True),
-    )
-    gates_own = lax.dynamic_slice_in_dim(gates, row_start, share, 0)
-    ids_own = lax.dynamic_slice_in_dim(expert_ids, row_start, share, 0)
-    inner_gate = jnp.sum(gates_own * grad_gates_own, axis=-1, keepdims=True)
-    grad_selected = gates_own * (grad_gates_own - inner_gate)
-    own_hot = ids_own[:, :, None] == expert_line[None, None, :]
-    grad_logits = jnp.sum(jnp.where(own_hot, grad_selected[:, :, None], 0.0), axis=1)
+        "rf,rd->fd", weighted_hidden, cot_all, preferred_element_type=jnp.float32
+    ).reshape(per_owner, units, model_width)
+    inner_gate = jnp.sum(gates * grad_gates_own, axis=-1, keepdims=True)
+    grad_logits = gates * (grad_gates_own - inner_gate)
     router_f = w_router.astype(jnp.float32)
     grad_normed_own = grad_normed_own + jnp.dot(grad_logits, router_f, precision=EXACT_PRECISION)
     grad_router = jnp.dot(grad_logits.T, normed_own.astype(jnp.float32), precision=EXACT_PRECISION)

time: 2940 us -> 1180 us (0.40)
  waiting for transfers between devices: 2200 us -> 812 us
  local copies, waits for them, and re-layouts: 331 us -> 23.5 us
  blocking collectives: 50.8 us -> 131 us
  matrix products: 202 us -> 135 us
  other arithmetic: 97.8 us -> 53.1 us
    all_to_all x4 -> x0, waiting for transfers between devices: 1880 us -> none  [the longest x2 963 us: return_rows(): return lax.all_to_all(buffer, 'ep', split_axis=0, concat_axis=0, tiled=True)]
    reduce_scatter x2 -> x3, waiting for transfers between devices: 27 us -> 430 us  [total_all(): lax.psum_scatter(value_rows, ('ep', 'tp'), scatter_dimension=0, tiled=True)]
    gather x6 -> x0, local copies, waits for them, and re-layouts: 244 us -> none  [the longest x1 51 us: local(): jnp.take(cot_rows, token_of_slot, axis=0, mode='fill', fill_value=0)]
    all_gather x0 -> x2, waiting for transfers between devices: none -> 99.7 us  [gather_all(): return lax.all_gather(value_rows, ('ep', 'tp'), axis=0, tiled=True)]
    all_gather x0 -> x2, blocking collectives: none -> 79.7 us  [gather_all(): return lax.all_gather(value_rows, ('ep', 'tp'), axis=0, tiled=True)]
    dot_general x12 -> x10, matrix products: 168 us -> 97.1 us  [the longest x1 15.3 us: local(): jnp.einsum('rf,df->rd', grad_up_act, up_in, preferred_element_type=jnp.fl...]
    convert_element_type x2 -> x0, local copies, waits for them, and re-layouts: 41.6 us -> none  [the longest x1 20.8 us: local(): grad_slot_rows = (jnp.einsum('secf,edf->secd', grad_gate_act, w_gate, pre...]
    scatter x2 -> x0, local copies, waits for them, and re-layouts: 31.3 us -> none  [the longest x1 15.7 us: local(): pair_of_slot = jnp.full((expert_count * capacity + 1,), pair_count, jnp.i...]
  transfers between devices with their start and end apart: 15 -> 11, of which waited for: 13 -> 11; matrix products, arithmetic and copies ran while one was open for 16% -> 9% of each run, Pallas kernels for 0% -> 0%
where the time goes in v1:
time: 1180 us; the launch traced here: 1170 us
  waiting for transfers between devices  812 us (69%)
  matrix products  135 us (11%)
  blocking collectives  131 us (11%)
  other arithmetic  53.1 us (4%)
  local copies, waits for them, and re-layouts  23.5 us (2%)
  between operations  15.5 us (1%)
    reduce_scatter x3, waiting for transfers between devices, total_all(): lax.psum_scatter(value_rows, ('ep', 'tp'), scatter_dimension=0, tiled=True)  430 us
    all_gather x2, waiting for transfers between devices, gather_all(): return lax.all_gather(value_rows, ('ep', 'tp'), axis=0, tiled=True)  99.7 us
    psum x1, waiting for transfers between devices, local(): lax.psum(grad_w_query.astype(jnp.bfloat16), 'ep').astype(jnp.float32)  92 us
    psum x1, waiting for transfers between devices, local(): lax.psum((grad_gain_attn, grad_gain_ffn, grad_router), ('ep', 'tp'))  83.6 us
    all_gather x2, blocking collectives, gather_all(): return lax.all_gather(value_rows, ('ep', 'tp'), axis=0, tiled=True)  79.7 us
    reduce_scatter x2, waiting for transfers between devices, group_totals(): return lax.psum_scatter(value_rows, 'tp', scatter_dimension=0, tiled=True)  69.5 us
    psum x1, blocking collectives, local(): lax.psum((grad_gain_attn, grad_gain_ffn, grad_router), ('ep', 'tp'))  39.4 us
    all_gather x2, waiting for transfers between devices, group_rows(): return lax.all_gather(value_rows, 'tp', axis=0, tiled=True)  36.3 us
  transfers between devices with their start and end apart: 11, of which 11 were waited for; matrix products, arithmetic and copies ran while one was open for 9% of the time, Pallas kernels for 0%

profile of v1, /device:TPU:0, one launch (start us, length us, event | category | flops | bytes accessed | tf_op | source)
XLA Modules:
  0.0 1170.8 jit_solution(3175409998038890623)
XLA Ops:
  9.8 1.9 fusion.31
  15.8 18.4 %all-gather.6.cloned.1.call-done = bf16[512,1536]{1,0:T(8,128)(2,1)} async-done(((bf16[128,1536]{1,0:T(8,128)(2,1)}), bf16[512,1536]{1,0:T(8,128)(2,1)}) %all-gather.6.cloned.1.call-update) | async-done | bytes 1572880 | tf_op jit(solution)/shard_map/all_gather | solution.py:61
  34.3 2.1 fusion.66
  36.5 2.2 fusion.67
  45.8 2.6 fusion.68
  49.1 37.4 %reduce-scatter.6.cloned.1.call-done = f32[128,1536]{1,0:T(8,128)} async-done(((f32[512,1536]{1,0:T(8,128)}), f32[128,1536]{1,0:T(8,128)}) %reduce-scatter.6.cloned.1.call-update) | async-done | bytes 786448 | tf_op jit(solution)/shard_map/reduce_scatter | solution.py:65
  98.7 12.1 %all-reduce = s32[128]{0:T(128)} all-reduce(s32[128]{0:T(128)} %dynamic-update-slice), channel_id=2, replica_groups=mesh['ep'=8,'tp'=4] {'ep'}, use_global_device_ids=true, to_apply=%add | all-reduce | flops 128 | bytes 1024
  113.6 4.3 convert_reduce_fusion
  119.3 42.5 %all_gather.30 = f32[4096,16]{0,1:T(8,128)} all-gather(f32[128,16]{0,1:T(8,128)S(1)} %get-tuple-element.48), channel_id=1, replica_groups=mesh['ep'=8,'tp'=4] {'ep','tp'}, dimensions={0}, use_global_device_ids=true | all-gather | bytes 270336 | tf_op jit(solution)/shard_map/all_gather | solution.py:69
  161.8 2.0 slice_bitcast_fusion.3
  163.9 2.0 slice_bitcast_fusion.1
  165.9 22.4 %all-gather.8.cloned.1.call-done = bf16[4096,1536]{1,0:T(8,128)(2,1)} async-done(((bf16[128,1536]{1,0:T(8,128)(2,1)}), bf16[4096,1536]{1,0:T(8,128)(2,1)}) %all-gather.8.cloned.1.call-update) | async-done | bytes 12582928 | tf_op jit(solution)/shard_map/all_gather | solution.py:69
  188.3 10.3 fusion.38
  198.6 10.2 fusion.40
  208.8 77.3 %all-gather.10.cloned.1.call-done = bf16[4096,1536]{1,0:T(8,128)(2,1)} async-done(((bf16[128,1536]{1,0:T(8,128)(2,1)}), bf16[4096,1536]{1,0:T(8,128)(2,1)}) %all-gather.10.cloned.1.call-update) | async-done | bytes 12582928 | tf_op jit(solution)/shard_map/all_gather | solution.py:69
  286.1 12.7 %bitcast_reduce_fusion = (f32[4096,2]{0,1:T(2,128)S(1)}, f32[4096,256]{0,1:T(8,128)}) fusion(f32[4096,256]{0,1:T(8,128)} %fusion.38, f32[4096,256]{0,1:T(8,128)} %fusion.40, bf16[4096,1536]{1,0:T(8,128)(2,1)} %all-gather.10.cloned.1.call-done, bf16[256,1536]{1,0:T(8,128)(2,1)} %bitcast.149), kind=kOutput, calls=%fused_computation.19 | convolution fusion | flops 3228557312 | bytes 25985024 | tf_op jit(solution)/shard_map/rd,fd->rf/dot_general | solution.py:250
  304.1 128.7 %reduce-scatter.12.cloned.1.call-done = f32[128,16]{0,1:T(8,128)} async-done(((f32[4096,16]{0,1:T(8,128)}), f32[128,16]{0,1:T(8,128)}) %reduce-scatter.12.cloned.1.call-update) | async-done | bytes 8208 | tf_op jit(solution)/shard_map/reduce_scatter | solution.py:73
  434.1 37.2 %all_gather.27 = f32[4096,16]{0,1:T(8,128)S(1)} all-gather(f32[128,16]{0,1:T(8,128)S(1)} %get-tuple-element.70), channel_id=1, replica_groups=mesh['ep'=8,'tp'=4] {'ep','tp'}, dimensions={0}, use_global_device_ids=true | all-gather | bytes 270336 | tf_op jit(solution)/shard_map/all_gather | solution.py:69
  471.3 7.3 multiply_convert_fusion
  478.7 10.4 fusion.39
  489.0 15.3 %add_convert_fusion = bf16[4096,1536]{1,0:T(8,128)(2,1)} fusion(f32[4096,1536]{1,0:T(8,128)} %fusion.39, bf16[4096,256]{0,1:T(8,128)(2,1)} %get-tuple-element.53, bf16[1536,128]{1,0:T(8,128)(2,1)} %get-tuple-element.64, bf16[1536,128]{1,0:T(8,128)(2,1)} %get-tuple-element.63), kind=kOutput, calls=%fused_computation | convolution fusion | flops 3235381248 | bytes 40632320 | tf_op jit(solution)/shard_map/rf,df->rd/dot_general | solution.py:264
  504.4 10.2 convolution_convert_fusion
  514.7 143.0 %reduce-scatter.10.cloned.1.call-done = bf16[128,1536]{1,0:T(8,128)(2,1)} async-done(((bf16[4096,1536]{1,0:T(8,128)(2,1)}), bf16[128,1536]{1,0:T(8,128)(2,1)}) %reduce-scatter.10.cloned.1.call-update) | async-done | bytes 393232 | tf_op jit(solution)/shard_map/reduce_scatter | solution.py:73
  657.7 3.2 multiply_reduce_fusion
  661.5 158.1 %reduce-scatter.8.cloned.1.call-done = bf16[128,1536]{1,0:T(8,128)(2,1)} async-done(((bf16[4096,1536]{1,0:T(8,128)(2,1)}), bf16[128,1536]{1,0:T(8,128)(2,1)}) %reduce-scatter.8.cloned.1.call-update) | async-done | bytes 393232 | tf_op jit(solution)/shard_map/reduce_scatter | solution.py:73
  819.5 2.9 fusion.62
  823.5 17.8 %all-gather.12.cloned.1.call-done = bf16[512,1536]{1,0:T(8,128)(2,1)} async-done(((bf16[128,1536]{1,0:T(8,128)(2,1)}), bf16[512,1536]{1,0:T(8,128)(2,1)}) %all-gather.12.cloned.1.call-update) | async-done | bytes 1572880 | tf_op jit(solution)/shard_map/all_gather | solution.py:61
  841.3 2.4 convolution_convert_fusion.5
  843.7 4.1 fusion.26
  847.9 4.5 fusion.4
  852.4 4.7 fusion.6
  859.7 1.8 convolution_convert_fusion.1
  863.8 1.8 convolution_convert_fusion.2
  865.7 2.3 fusion.69
  869.0 2.2 convolution_add_fusion
  871.6 7.1 fusion.17
  880.3 9.9 fusion.14
  890.1 3.1 copy.43
  894.2 9.9 fusion.70
  904.1 92.0 %all-reduce.8.cloned.1.call-done = (bf16[384,1536]{1,0:T(8,128)(2,1)}, bf16[128,1536]{1,0:T(8,128)(2,1)}, bf16[128,1536]{1,0:T(8,128)(2,1)}, bf16[384,1536]{1,0:T(8,128)(2,1)}) async-done(((bf16[384,1536]{1,0:T(8,128)(2,1)}, bf16[128,1536]{1,0:T(8,128)(2,1)}, bf16[128,1536]{1,0:T(8,128)(2,1)}, bf16[384,1536]{1,0:T(8,128)(2,1)}), (bf16[384,1536]{1,0:T(8,128)(2,1)}, bf16[128,1536]{1,0:T(8,128)(2,1)}, ...) | async-done | bytes 3145744 | tf_op jit(solution)/shard_map/psum | solution.py:348
  996.1 2.1 convert_element_type.156
  998.2 2.0 convert_element_type.158
  1000.2 1.7 convert_element_type.154
  1001.9 1.7 convert_element_type.160
  1003.6 32.0 %reduce-scatter.14.cloned.1.call-done = f32[128,1536]{1,0:T(8,128)} async-done(((f32[512,1536]{1,0:T(8,128)}), f32[128,1536]{1,0:T(8,128)}) %reduce-scatter.14.cloned.1.call-update) | async-done | bytes 786448 | tf_op jit(solution)/shard_map/reduce_scatter | solution.py:65
  1037.0 2.4 fusion.34
  1039.4 39.4 %all-reduce.1 = (f32[1536]{0:T(1024)}, f32[1536]{0:T(1024)}) all-reduce(f32[1536]{0:T(1024)S(1)} %get-tuple-element.38, f32[1536]{0:T(1024)S(1)} %copy-done.40), channel_id=1, replica_groups=mesh['ep'=8,'tp'=4] {'ep','tp'}, use_global_device_ids=true, to_apply=%region_21.22 | all-reduce | flops 3072 | bytes 24576 | tf_op jit(solution)/shard_map/psum | solution.py:353
  1078.8 83.6 %all-reduce.6.cloned.1.call-done = f32[16,1536]{1,0:T(8,128)} async-done(((f32[16,1536]{1,0:T(8,128)}), f32[16,1536]{1,0:T(8,128)}) %all-reduce.6.cloned.1.call-update) | async-done | bytes 98320 | tf_op jit(solution)/shard_map/psum | solution.py:353
  (181 shorter events, 49.9 us)
Async XLA Ops:
  7.2 38.6 %copy-start = (bf16[384,1536]{1,0:T(8,128)(2,1)S(1)}, bf16[384,1536]{1,0:T(8,128)(2,1)}, u32[]{:S(2)}) copy-start(bf16[384,1536]{1,0:T(8,128)(2,1)} %param.21) | copy-start | bytes 3538948
  7.2 29.2 %copy-start.20 = (bf16[384,1536]{1,0:T(8,128)(2,1)S(1)}, bf16[384,1536]{1,0:T(8,128)(2,1)}, u32[]{:S(2)}) copy-start(bf16[384,1536]{1,0:T(8,128)(2,1)} %param.18) | copy-start | bytes 3538948
  7.2 27.1 %all-gather.6.cloned.1.call-start = ((), (), s32[]{:S(2)}) async-start(), calls=%async_computation.5 | async-start | bytes 1966080 | tf_op jit(solution)/shard_map/all_gather | solution.py:61
  9.1 2.6 copy-start.46
  11.8 74.8 %reduce-scatter.6.cloned.1.call-start = ((), (), s32[]{:S(2)}) async-start(), calls=%async_computation.6 | async-start | bytes 3932160 | tf_op jit(solution)/shard_map/reduce_scatter | solution.py:65
  14.2 24.5 %copy-start.9 = (f32[512,32]{0,1:T(8,128)}, f32[512,32]{0,1:T(8,128)S(1)}, u32[]{:S(2)}) copy-start(f32[512,32]{0,1:T(8,128)S(1)} %get-tuple-element.71) | copy-start | bytes 196612
  14.2 24.5 %copy-start.11 = (f32[512,32]{0,1:T(8,128)}, f32[512,32]{0,1:T(8,128)S(1)}, u32[]{:S(2)}) copy-start(f32[512,32]{0,1:T(8,128)S(1)} %get-tuple-element.72) | copy-start | bytes 196612
  15.8 23.0 %copy-start.6 = (pred[512,512]{0,1:T(8,128)(4,1)}, pred[512,512]{0,1:T(8,128)(4,1)S(1)}, u32[]{:S(2)}) copy-start(pred[512,512]{0,1:T(8,128)(4,1)S(1)} %compare_and_fusion) | copy-start | bytes 786436
  36.4 2.5 copy-start.31
  36.4 2.5 copy-start.33
  40.1 3.6 copy-start.1
  40.1 3.6 copy-start.38
  40.2 2.6 copy-start.2
  40.2 3.0 copy-start.17
  48.4 139.9 %all-gather.8.cloned.1.call-start = ((), (), s32[]{:S(2)}) async-start(), calls=%async_computation.7 | async-start | bytes 12976128 | tf_op jit(solution)/shard_map/all_gather | solution.py:69
  49.1 114.8 %copy-start.35 = (f32[1536]{0:T(1024)}, f32[1536]{0:T(1024)S(1)}, u32[]{:S(2)}) copy-start(f32[1536]{0:T(1024)S(1)} %convert_element_type.133) | copy-start | bytes 18436
  90.0 196.0 %all-gather.10.cloned.1.call-start = ((), (), s32[]{:S(2)}) async-start(), calls=%async_computation.9 | async-start | bytes 12976128 | tf_op jit(solution)/shard_map/all_gather | solution.py:69
  90.6 342.3 %reduce-scatter.12.cloned.1.call-start = ((), (), s32[]{:S(2)}) async-start(), calls=%async_computation.11 | async-start | bytes 270336 | tf_op jit(solution)/shard_map/reduce_scatter | solution.py:73
  188.3 10.3 copy-start.13
  188.3 10.3 copy-start.15
  301.1 356.6 %reduce-scatter.10.cloned.1.call-start = ((), (), s32[]{:S(2)}) async-start(), calls=%async_computation.10 | async-start | bytes 12976128 | tf_op jit(solution)/shard_map/reduce_scatter | solution.py:73
  471.3 7.4 copy-start.14
  471.3 7.3 copy-start.16
  478.7 10.4 copy-start.3
  504.4 315.2 %reduce-scatter.8.cloned.1.call-start = ((), (), s32[]{:S(2)}) async-start(), calls=%async_computation.8 | async-start | bytes 12976128 | tf_op jit(solution)/shard_map/reduce_scatter | solution.py:73
  514.6 326.7 %all-gather.12.cloned.1.call-start = ((), (), s32[]{:S(2)}) async-start(), calls=%async_computation.12 | async-start | bytes 1966080 | tf_op jit(solution)/shard_map/all_gather | solution.py:61
  822.4 21.2 %copy-start.7 = (pred[512,512]{0,1:T(8,128)(4,1)S(1)}, pred[512,512]{0,1:T(8,128)(4,1)}, u32[]{:S(2)}) copy-start(pred[512,512]{0,1:T(8,128)(4,1)} %copy-done.6) | copy-start | bytes 786436
  822.5 173.7 %all-reduce.8.cloned.1.call-start = ((), (), s32[]{:S(2)}) async-start(), calls=%async_computation.15 | async-start | bytes 6291456 | tf_op jit(solution)/shard_map/psum | solution.py:348
  841.3 6.5 slice-start
  843.7 4.1 slice-start.1
  843.7 4.1 copy-start.30
  852.4 4.7 copy-start.26
  852.4 4.7 copy-start.28
  865.6 170.0 %reduce-scatter.14.cloned.1.call-start = ((), (), s32[]{:S(2)}) async-start(), calls=%async_computation.13 | async-start | bytes 3932160 | tf_op jit(solution)/shard_map/reduce_scatter | solution.py:65
  871.3 291.2 %all-reduce.6.cloned.1.call-start = ((), (), s32[]{:S(2)}) async-start(), calls=%async_computation.14 | async-start | bytes 196608 | tf_op jit(solution)/shard_map/psum | solution.py:353
  890.1 3.1 copy-start.5
  890.1 3.1 copy-start.36
  890.1 3.1 copy-start.37
  890.1 3.1 copy-start.42
  890.1 3.1 copy-start.43
  890.1 3.1 copy-start.45
  996.1 4.1 copy-start.22
  996.1 5.8 copy-start.21
  1000.2 35.4 %copy-start.4 = (bf16[128,1536]{1,0:T(8,128)(2,1)S(1)}, bf16[128,1536]{1,0:T(8,128)(2,1)}, u32[]{:S(2)}) copy-start(bf16[128,1536]{1,0:T(8,128)(2,1)} %param.16) | copy-start | bytes 1179652
  1000.2 35.4 %copy-start.47 = (f32[128]{0:T(128)S(1)}, f32[128]{0:T(128)}, u32[]{:S(2)}) copy-start(f32[128]{0:T(128)} %copy-done.46) | copy-start | bytes 1540
  1001.9 35.1 %copy-start.8 = (f32[128,1536]{1,0:T(8,128)S(1)}, f32[128,1536]{1,0:T(8,128)}, u32[]{:S(2)}) copy-start(f32[128,1536]{1,0:T(8,128)} %get-tuple-element.47) | copy-start | bytes 2359300
  1001.9 35.1 %copy-start.49 = (f32[128]{0:T(128)S(1)}, f32[128]{0:T(128)}, u32[]{:S(2)}) copy-start(f32[128]{0:T(128)} %get-tuple-element.76) | copy-start | bytes 1540
  1001.9 37.5 %copy-start.40 = (f32[1536]{0:T(1024)S(1)}, f32[1536]{0:T(1024)}, u32[]{:S(2)}) copy-start(f32[1536]{0:T(1024)} %get-tuple-element.36) | copy-start | bytes 18436
  (16 other events, 20.0 us)
Sparse Core Ops, SparseCore 0:
  11.9 22.3 all-gather.5
  48.5 37.9 reduce-scatter.5
  90.4 97.9 all-gather.7
  191.5 94.5 all-gather.9
  301.2 131.6 reduce-scatter.11
  504.5 153.1 reduce-scatter.9
  664.8 154.7 reduce-scatter.7
  822.6 18.7 all-gather.11
  865.7 130.3 all-reduce.7
  998.7 36.8 reduce-scatter.13
  1041.8 120.5 all-reduce.5

commit v2 on v1

--- a/solution.py
+++ b/solution.py
@@ -1,6 +1,10 @@
+import functools
+
 import jax
 import jax.numpy as jnp
 from jax import lax
+from jax.experimental import pallas as pl
+from jax.experimental.pallas import tpu as pltpu
 from jax.sharding import PartitionSpec as P
 
 HEAD_DIMENSION = 64
@@ -65,27 +69,443 @@
     return lax.psum_scatter(value_rows, "tp", scatter_dimension=0, tiled=True)
 
 
-def gather_all(value_rows):
+MESH = pl.DeviceIdType.MESH
+
+
+class Place:
+    def __init__(self, ep_size):
+        self.depth = ep_size // 2
+        ep, tp = lax.axis_index("ep"), lax.axis_index("tp")
+        self.z, self.y = ep // 2, ep % 2
+        self.x, self.c = tp // 2, tp % 2
+
+    def device(self, z=None, y=None, x=None, c=None):
+        z = self.z if z is None else z
+        y = self.y if y is None else y
+        x = self.x if x is None else x
+        c = self.c if c is None else c
+        return (z * 2 + y, x * 2 + c)
+
+    def sibling(self):
+        return self.device(c=1 - self.c)
+
+    def x_peer(self):
+        return self.device(x=1 - self.x)
+
+    def y_peer(self):
+        return self.device(y=1 - self.y)
+
+    def after(self, step):
+        return lax.rem(self.z + step, self.depth)
+
+    def before(self, step):
+        return lax.rem(self.z + self.depth - step, self.depth)
+
+
+def meet(devices):
+    barrier = pltpu.get_barrier_semaphore()
+    for device in devices:
+        pl.semaphore_signal(barrier, inc=1, device_id=device, device_id_type=MESH)
+    pl.semaphore_wait(barrier, len(devices))
+
+
+def send(src, dst, send_sem, recv_sem, device):
+    copy = pltpu.make_async_remote_copy(
+        src_ref=src,
+        dst_ref=dst,
+        send_sem=send_sem,
+        recv_sem=recv_sem,
+        device_id=device,
+        device_id_type=MESH,
+    )
+    copy.start()
+    return copy
+
+
+def gather_kernel(ep_size, own, out, own_sem, z_sems, pair_sems, core_sems):
+    me = Place(ep_size)
+    depth = me.depth
+    half = own.shape[0] // 2
+    z_send, z_recv = z_sems.at[0], z_sems.at[1]
+    pair_send, pair_recv = pair_sems.at[0], pair_sems.at[1]
+    core_send, core_recv = core_sems.at[0], core_sems.at[1]
+    meet(
+        [me.sibling(), me.x_peer(), me.y_peer()]
+        + [me.device(z=me.after(s)) for s in range(1, depth)]
+    )
+
+    def rows(part):
+        return pl.ds(part * half, half)
+
+    def block(step, y, x, part, c=None):
+        return out.at[me.before(step), y, x, me.c if c is None else c, rows(part)]
+
+    started = []
+
+    def forward(source, target, sems, slot, device):
+        started.append(send(source, target, sems[0].at[slot], sems[1].at[slot], device))
+
+    for s in range(1, depth):
+        for part in range(2):
+            forward(
+                own.at[rows(part)],
+                out.at[me.z, me.y, me.x, me.c, rows(part)],
+                (z_send, z_recv),
+                (s - 1) * 2 + part,
+                me.device(z=me.after(s)),
+            )
+    local = pltpu.make_async_copy(own, out.at[me.z, me.y, me.x, me.c], own_sem)
+    local.start()
+    local.wait()
+
+    kinds = [
+        (me.y, me.x, 0),
+        (me.y, me.x, 1),
+        (1 - me.y, me.x, 0),
+        (me.y, 1 - me.x, 1),
+        (1 - me.y, me.x, 1),
+        (1 - me.y, 1 - me.x, 1),
+        (me.y, 1 - me.x, 0),
+        (1 - me.y, 1 - me.x, 0),
+    ]
+    x_route = {0: 6, 2: 7, 1: 3}
+    y_route = {0: 2, 1: 4, 3: 5}
+
+    def landed(step, kind):
+        y, x, part = kinds[kind]
+        place = block(step, y, x, part)
+        if kind < 2:
+            if step > 0:
+                sem = z_recv.at[(step - 1) * 2 + part]
+                pltpu.make_async_copy(place, place, sem).wait()
+        else:
+            pltpu.make_async_copy(place, place, pair_recv.at[step * 8 + kind]).wait()
+
+    def pass_on(step, kind):
+        y, x, part = kinds[kind]
+        place = block(step, y, x, part)
+        if kind in x_route:
+            forward(place, place, (pair_send, pair_recv), step * 8 + x_route[kind], me.x_peer())
+        if kind in y_route:
+            forward(place, place, (pair_send, pair_recv), step * 8 + y_route[kind], me.y_peer())
+        forward(place, place, (core_send, core_recv), step * 8 + kind, me.sibling())
+
+    for turn in range(depth + 2):
+        for step, group in ((turn, (0, 1)), (turn - 1, (2, 3)), (turn - 2, (4, 5, 6, 7))):
+            if 0 <= step < depth:
+                for kind in group:
+                    landed(step, kind)
+                    pass_on(step, kind)
+    for step in range(depth):
+        for kind in range(8):
+            y, x, part = kinds[kind]
+            place = block(step, y, x, part, 1 - me.c)
+            pltpu.make_async_copy(place, place, core_recv.at[step * 8 + kind]).wait()
+    for copy in started:
+        copy.wait_send()
+
+
+def gather_by_links(value_rows, ep_size):
+    rows, width = value_rows.shape
+    depth = ep_size // 2
+    dma = pltpu.SemaphoreType.DMA
+    every = pl.pallas_call(
+        functools.partial(gather_kernel, ep_size),
+        out_shape=jax.ShapeDtypeStruct((depth, 2, 2, 2, rows, width), value_rows.dtype),
+        in_specs=[pl.BlockSpec(memory_space=pl.ANY)],
+        out_specs=pl.BlockSpec(memory_space=pl.ANY),
+        scratch_shapes=[
+            dma,
+            dma((2, 2 * depth - 2)),
+            dma((2, 8 * depth)),
+            dma((2, 8 * depth)),
+        ],
+        compiler_params=pltpu.CompilerParams(collective_id=1, has_side_effects=True),
+        name="gather_by_links",
+    )(value_rows)
+    return every.reshape(-1, width)
+
+
+def add_into(target, other):
+    rows = target.shape[-2]
+
+    def tile(i, carry):
+        at = pl.ds(pl.multiple_of(i * 32, 32), 32)
+        target[at, :] = target[at, :] + other[at, :]
+        return carry
+
+    lax.fori_loop(0, rows // 32, tile, 0)
+
+
+def total_kernel(
+    ep_size,
+    first_in,
+    second_in,
+    small_in,
+    first_out,
+    second_out,
+    small_out,
+    parts,
+    core_got,
+    pair_got,
+    last_got,
+    z_got,
+    small_got,
+    load_sems,
+    core_sems,
+    pair_sems,
+    last_sems,
+    z_sems,
+    small_sems,
+    own_sem,
+):
+    me = Place(ep_size)
+    depth = me.depth
+    others = []
+    for k in range(1, ep_size * 4):
+        ep = lax.rem(lax.axis_index("ep") + k // 4, ep_size)
+        tp = lax.rem(lax.axis_index("tp") + k % 4, 4)
+        others.append((ep, tp))
+    meet(others)
+    small = []
+    my_place = lax.axis_index("ep") * 4 + lax.axis_index("tp")
+    for k, device in enumerate(others):
+        small.append(
+            send(
+                small_in.at[device[0] * 4 + device[1]],
+                small_got.at[my_place],
+                small_sems.at[0, k],
+                small_sems.at[1, k],
+                device,
+            )
+        )
+    own_small = pltpu.make_async_copy(small_in.at[my_place], small_got.at[my_place], own_sem)
+    own_small.start()
+
+    def load(step, which):
+        source = (first_in, second_in)[which]
+        slot = lax.rem(step, 2)
+        return pltpu.make_async_copy(
+            source.at[me.after(step + 1)], parts.at[slot, which], load_sems.at[slot, which]
+        )
+
+    def core_copy(step):
+        return pltpu.make_async_remote_copy(
+            src_ref=parts.at[lax.rem(step, 2), :, :, :, 1 - me.c],
+            dst_ref=core_got.at[step],
+            send_sem=core_sems.at[0, step],
+            recv_sem=core_sems.at[1, step],
+            device_id=me.sibling(),
+            device_id_type=MESH,
+        )
+
+    def pair_copy(step, which):
+        source = (core_got.at[step, 0, :, 1 - me.x], core_got.at[step, 1, 1 - me.y])[which]
+        return pltpu.make_async_remote_copy(
+            src_ref=source,
+            dst_ref=pair_got.at[step, which],
+            send_sem=pair_sems.at[0, step, which],
+            recv_sem=pair_sems.at[1, step, which],
+            device_id=(me.x_peer(), me.y_peer())[which],
+            device_id_type=MESH,
+        )
+
+    def last_copy(step, which):
+        return pltpu.make_async_remote_copy(
+            src_ref=pair_got.at[step, which, (1 - me.y, 1 - me.x)[which]],
+            dst_ref=last_got.at[step, which],
+            send_sem=last_sems.at[0, step, which],
+            recv_sem=last_sems.at[1, step, which],
+            device_id=(me.y_peer(), me.x_peer())[which],
+            device_id_type=MESH,
+        )
+
+    def z_copy(step):
+        return pltpu.make_async_remote_copy(
+            src_ref=last_got.at[step],
+            dst_ref=z_got.at[step],
+            send_sem=z_sems.at[0, step],
+            recv_sem=z_sems.at[1, step],
+            device_id=me.device(z=me.after(step + 1)),
+            device_id_type=MESH,
+        )
+
+    def turn(i, carry):
+        @pl.when(i < depth)
+        def _():
+            for which in range(2):
+                load(i, which).start()
+            for which in range(2):
+                load(i, which).wait()
+            core_copy(i).start()
+
+        @pl.when((i >= 1) & (i <= depth))
+        def _():
+            step = i - 1
+            core_copy(step).wait_recv()
+            for y in range(2):
+                for x in range(2):
+                    for which in range(2):
+                        add_into(
+                            core_got.at[step, which, y, x],
+                            parts.at[lax.rem(step, 2), which, y, x, me.c],
+                        )
+            for which in range(2):
+                pair_copy(step, which).start()
+            core_copy(step).wait_send()
+
+        @pl.when((i >= 2) & (i <= depth + 1))
+        def _():
+            step = i - 2
+            for which in range(2):
+                pair_copy(step, which).wait_recv()
+                for k in range(2):
+                    mine = (core_got.at[step, 0, k, me.x], core_got.at[step, 1, me.y, k])[which]
+                    add_into(pair_got.at[step, which, k], mine)
+                last_copy(step, which).start()
+
+        @pl.when(i >= 3)
+        def _():
+            step = i - 3
+            for which in range(2):
+                last_copy(step, which).wait_recv()
+                add_into(last_got.at[step, which], pair_got.at[step, which, (me.y, me.x)[which]])
+
+            @pl.when(step < depth - 1)
+            def _():
+                z_copy(step).start()
+
+        return carry
+
+    lax.fori_loop(0, depth + 3, turn, 0)
+    for step in range(depth - 1):
+        z_copy(step).wait_recv()
+
+    def finish(which, target):
+        def tile(i, carry):
+            at = pl.ds(pl.multiple_of(i * 16, 16), 16)
+            total = last_got[depth - 1, which, at, :].astype(jnp.float32)
+            for step in range(depth - 1):
+                total = total + z_got[step, which, at, :].astype(jnp.float32)
+            target[at, :] = total
+            return carry
+
+        lax.fori_loop(0, target.shape[0] // 16, tile, 0)
+
+    finish(0, first_out)
+    finish(1, second_out)
+    own_small.wait()
+    for copy in small:
+        copy.wait()
+    for ep in range(ep_size):
+        total = small_got[ep * 4]
+        for tp in range(1, 4):
+            total = total + small_got[ep * 4 + tp]
+        small_out[ep] = total
+    for step in range(depth):
+        for which in range(2):
+            pair_copy(step, which).wait_send()
+            last_copy(step, which).wait_send()
+        if step < depth - 1:
+            z_copy(step).wait_send()
+
+
+def totals_by_links(first, second, small, ep_size):
+    total_rows, width = first.shape
+    depth = ep_size // 2
+    rows = total_rows // (4 * ep_size)
+    whole = (depth, 2, 2, 2, rows, width)
+    bf16, f32 = jnp.bfloat16, jnp.float32
+    dma = pltpu.SemaphoreType.DMA
+    vmem = pl.BlockSpec(memory_space=pltpu.VMEM)
+    anywhere = pl.BlockSpec(memory_space=pl.ANY)
+    return pl.pallas_call(
+        functools.partial(total_kernel, ep_size),
+        out_shape=(
+            jax.ShapeDtypeStruct((rows, width), f32),
+            jax.ShapeDtypeStruct((rows, width), f32),
+            jax.ShapeDtypeStruct((ep_size,) + small.shape[1:], f32),
+        ),
+        in_specs=[anywhere, anywhere, vmem],
+        out_specs=(vmem, vmem, vmem),
+        scratch_shapes=[
+            pltpu.VMEM((2, 2, 2, 2, 2, rows, width), bf16),
+            pltpu.VMEM((depth, 2, 2, 2, rows, width), bf16),
+            pltpu.VMEM((depth, 2, 2, rows, width), bf16),
+            pltpu.VMEM((depth, 2, rows, width), bf16),
+            pltpu.VMEM((depth - 1, 2, rows, width), bf16),
+            pltpu.VMEM(small.shape, f32),
+            dma((2, 2)),
+            dma((2, depth)),
+            dma((2, depth, 2)),
+            dma((2, depth, 2)),
+            dma((2, depth - 1)),
+            dma((2, 4 * ep_size - 1)),
+            dma,
+        ],
+        compiler_params=pltpu.CompilerParams(
+            collective_id=2, has_side_effects=True, vmem_limit_bytes=56 * 1024 * 1024
+        ),
+        name="totals_by_links",
+    )(first.reshape(whole), second.reshape(whole), small)
+
+
+def gather_all(value_rows, by_links):
+    if by_links:
+        return gather_by_links(value_rows, lax.axis_size("ep"))
     return lax.all_gather(value_rows, ("ep", "tp"), axis=0, tiled=True)
 
 
-def total_all(value_rows):
-    return lax.psum_scatter(value_rows, ("ep", "tp"), scatter_dimension=0, tiled=True)
-
-
-def kept_pairs(expert_ids, slot_order, expert_count, row_start, share):
+def totals(first, second, small, by_links):
+    ep_size, tp_size = lax.axis_size("ep"), lax.axis_size("tp")
+    if by_links:
+        rows = small.shape[1] // (ep_size * tp_size)
+        blocks = small.reshape(small.shape[0], ep_size * tp_size, rows).swapaxes(0, 1)
+        blocks = jnp.pad(blocks, ((0, 0), (0, -small.shape[0] % 8), (0, 0)))
+        first, second, got = totals_by_links(first, second, blocks, ep_size)
+        return first, second, got[:, : small.shape[0]].reshape(-1, rows).T
+
+    def scatter(value_rows):
+        return lax.psum_scatter(value_rows, ("ep", "tp"), scatter_dimension=0, tiled=True)
+
+    columns = jnp.zeros((small.shape[1], small.shape[0] * ep_size), jnp.float32)
+    columns = lax.dynamic_update_slice_in_dim(
+        columns, small.T, lax.axis_index("ep") * small.shape[0], 1
+    )
+    return (
+        scatter(first).astype(jnp.float32),
+        scatter(second).astype(jnp.float32),
+        scatter(columns),
+    )
+
+
+LAST = 1 << 30
+
+
+def pair_order(expert_ids, slot_order, expert_count):
     experts = jnp.arange(expert_count, dtype=jnp.int32)
-    chosen = expert_ids[:, :, None] == experts[None, None, :]
-    last = jnp.int32(1 << 30)
-    order = jnp.min(jnp.where(chosen, slot_order[:, :, None], last), axis=1)
-    counts = jnp.sum((order < last).astype(jnp.int32), axis=0)
-    every = lax.all_gather(counts, "ep")
-    earlier = jnp.arange(every.shape[0], dtype=jnp.int32) < lax.axis_index("ep")
-    offsets = jnp.sum(jnp.where(earlier[:, None], every, 0), axis=0)
-    own = lax.dynamic_slice_in_dim(order, row_start, share, 0)
-    rank = jnp.sum((order[:, None, :] < own[None, :, :]).astype(jnp.int32), axis=0)
-    used = own < last
-    return used, used & (rank + offsets[None, :] < CAP)
+    chosen = expert_ids.T[None, :, :] == experts[:, None, None]
+    return jnp.min(jnp.where(chosen, slot_order.T[None, :, :], LAST), axis=1)
+
+
+def kept_pairs(order):
+    used = order < LAST
+    counts = jnp.sum(used.astype(jnp.int32), axis=2)
+    block = jnp.arange(order.shape[0], dtype=jnp.int32)
+    earlier = block[None, :] < block[:, None]
+    offsets = jnp.sum(jnp.where(earlier[:, :, None], counts[None, :, :], 0), axis=1)
+    whole = offsets + counts <= CAP
+    edge = (offsets < CAP) & ~whole
+    edge_order = jnp.sum(jnp.where(edge[:, :, None], order, 0), axis=0)
+    rank = jnp.sum((edge_order[:, :, None] < edge_order[:, None, :]).astype(jnp.int32), axis=1)
+    early = offsets[:, :, None] + rank[None, :, :] < CAP
+    return used & (whole[:, :, None] | (edge[:, :, None] & early))
+
+
+def masked_softmax(logits, used):
+    top = jnp.max(jnp.where(used, logits, -jnp.inf), axis=-1, keepdims=True)
+    powers = jnp.where(used, jnp.exp(logits - top), 0.0)
+    return powers / jnp.sum(powers, axis=-1, keepdims=True)
 
 
 def visible_block(query_seg, query_pos, query_row, key_seg, key_pos, key_row):
@@ -191,8 +611,10 @@
     expert_count = w_router.shape[0]
     per_owner = w_gate.shape[0]
     block_rows = 512
-    used, kept = kept_pairs(expert_ids, slot_order, expert_count, row_start, share)
-    cot_all = gather_all(cotangent)
+    by_links = lax.axis_size("tp") == 4 and lax.axis_size("ep") == 8
+    order = pair_order(expert_ids, slot_order, expert_count)
+    order_all = lax.all_gather(order, "ep")
+    cot_all = gather_all(cotangent, False)
     inputs_own = hidden_in.astype(jnp.float32)
     gain_one = gain_attn.astype(jnp.float32)
     gain_two = gain_ffn.astype(jnp.float32)
@@ -228,17 +650,21 @@
     )
     scale_two = norm_scale(middle_own)
     normed_own = (middle_own * scale_two * gain_two).astype(jnp.bfloat16)
-    normed_two = gather_all(normed_own)
-    logits = jnp.einsum("rd,ed->re", normed_own, w_router, preferred_element_type=jnp.float32)
-    top_logit = jnp.max(jnp.where(used, logits, -jnp.inf), axis=-1, keepdims=True)
-    powers = jnp.where(used, jnp.exp(logits - top_logit), 0.0)
-    gates = powers / jnp.sum(powers, axis=-1, keepdims=True)
+    normed_two = gather_all(normed_own, by_links)
     first_expert = lax.axis_index("ep") * per_owner
-    kept_all = lax.dynamic_slice_in_dim(
-        gather_all(kept.astype(jnp.float32)), first_expert, per_owner, 1
-    )
-    gate_all = lax.dynamic_slice_in_dim(
-        gather_all(jnp.where(kept, gates, 0.0)), first_expert, per_owner, 1
+    used = lax.dynamic_slice_in_dim(order, row_start, share, 1).T < LAST
+    gates = masked_softmax(
+        jnp.einsum("rd,ed->re", normed_own, w_router, preferred_element_type=jnp.float32), used
+    )
+    kept_all = kept_pairs(
+        lax.dynamic_slice_in_dim(order_all, first_expert, per_owner, 1)
+    ).swapaxes(0, 1).reshape(per_owner, -1)
+    all_gates = masked_softmax(
+        jnp.einsum("rd,ed->re", normed_two, w_router, preferred_element_type=jnp.float32),
+        order_all.swapaxes(1, 2).reshape(-1, expert_count) < LAST,
+    )
+    gate_all = jnp.where(
+        kept_all.T, lax.dynamic_slice_in_dim(all_gates, first_expert, per_owner, 1), 0.0
     )
     units = w_gate.shape[2]
     gate_in = jnp.concatenate([w_gate[e] for e in range(per_owner)], axis=1)
@@ -256,26 +682,20 @@
         jnp.bfloat16
     )
     grad_up_act = (grad_hidden * gate_act * sigma).astype(jnp.bfloat16)
-    grad_gates_part = kept_all * jnp.sum(
-        (hidden * back_act).reshape(-1, per_owner, units), axis=2
+    grad_gates_part = jnp.where(
+        kept_all, jnp.sum((hidden * back_act).reshape(-1, per_owner, units), axis=2).T, 0.0
     )
     grad_rows = (
         jnp.einsum("rf,df->rd", grad_gate_act, gate_in, preferred_element_type=jnp.float32)
         + jnp.einsum("rf,df->rd", grad_up_act, up_in, preferred_element_type=jnp.float32)
     ).astype(jnp.bfloat16)
-    grad_normed_own = total_all(grad_rows).astype(jnp.float32)
-    grad_gates_own = total_all(
-        lax.dynamic_update_slice_in_dim(
-            jnp.zeros((normed_two.shape[0], expert_count), jnp.float32),
-            grad_gates_part,
-            first_expert,
-            1,
-        )
-    )
     combined = jnp.dot(weighted_hidden, down_in, preferred_element_type=jnp.float32).astype(
         jnp.bfloat16
     )
-    output_own = (middle_own + total_all(combined).astype(jnp.float32)).astype(jnp.bfloat16)
+    grad_normed_own, combined_own, grad_gates_own = totals(
+        grad_rows, combined, grad_gates_part, by_links
+    )
+    output_own = (middle_own + combined_own).astype(jnp.bfloat16)
     grad_w_gate = jnp.einsum(
         "rd,ref->edf",
         normed_two,

time: 1180 us -> 770 us (0.65)
  waiting for transfers between devices: 812 us -> 245 us
  Pallas kernels: 0 us -> 231 us
  blocking collectives: 131 us -> 71 us
    reduce_scatter x3 -> x0, waiting for transfers between devices: 430 us -> none  [total_all(): lax.psum_scatter(value_rows, ('ep', 'tp'), scatter_dimension=0, tiled=True)]
    pallas_call x0 -> x2, Pallas kernels: none -> 231 us  [the longest x1 139 us: totals_by_links(): pl.pallas_call(functools.partial(total_kernel, ep_size), out_shape=(jax.S...]
    all_gather x2 -> x1, waiting for transfers between devices: 99.7 us -> 0.01 us  [gather_all(): return lax.all_gather(value_rows, ('ep', 'tp'), axis=0, tiled=True)]
    all_gather x2 -> x1, blocking collectives: 79.7 us -> 31.5 us  [local(): order_all = lax.all_gather(order, 'ep')]
    reduce_scatter x2, waiting for transfers between devices: 69.5 us -> 31.9 us  [group_totals(): return lax.psum_scatter(value_rows, 'tp', scatter_dimension=0, tiled=True)]
    unnamed x1 -> x0, blocking collectives: 12.1 us -> none
  transfers between devices with their start and end apart: 11 -> 7, of which waited for: 11 -> 5; matrix products, arithmetic and copies ran while one was open for 9% -> 11% of each run, Pallas kernels for 0% -> 12%
where the time goes in v2:
time: 770 us; the launch traced here: 763 us
  waiting for transfers between devices  245 us (32%)
  Pallas kernels  231 us (30%)
  matrix products  133 us (17%)
  blocking collectives  71 us (9%)
  other arithmetic  43.8 us (6%)
  local copies, waits for them, and re-layouts  21.8 us (3%)
  between operations  16.7 us (2%)
    pallas_call x1, Pallas kernels, totals_by_links(): pl.pallas_call(functools.partial(total_kernel, ep_size), out_shape=(jax.S...  139 us
    pallas_call x1, Pallas kernels, gather_by_links(): pl.pallas_call(functools.partial(gather_kernel, ep_size), out_shape=jax.S...  92.8 us
    psum x1, waiting for transfers between devices, local(): lax.psum(grad_w_query.astype(jnp.bfloat16), 'ep').astype(jnp.float32)  92.1 us
    psum x1, waiting for transfers between devices, local(): lax.psum((grad_gain_attn, grad_gain_ffn, grad_router), ('ep', 'tp'))  84.4 us
    psum x1, blocking collectives, local(): lax.psum((grad_gain_attn, grad_gain_ffn, grad_router), ('ep', 'tp'))  39.5 us
    all_gather x2, waiting for transfers between devices, group_rows(): return lax.all_gather(value_rows, 'tp', axis=0, tiled=True)  35.9 us
    reduce_scatter x2, waiting for transfers between devices, group_totals(): return lax.psum_scatter(value_rows, 'tp', scatter_dimension=0, tiled=True)  31.9 us
    all_gather x1, blocking collectives, local(): order_all = lax.all_gather(order, 'ep')  31.5 us
  transfers between devices with their start and end apart: 7, of which 5 were waited for; matrix products, arithmetic and copies ran while one was open for 11% of the time, Pallas kernels for 12%

profile of v2, /device:TPU:0, one launch (start us, length us, event | category | flops | bytes accessed | tf_op | source)
XLA Modules:
  0.0 763.3 jit_solution(17263197393058041824)
XLA Ops:
  10.7 1.9 fusion.21
  15.1 1.6 compare_and_fusion
  16.7 18.4 %all-gather.5.cloned.1.call-done = bf16[512,1536]{1,0:T(8,128)(2,1)} async-done(((bf16[128,1536]{1,0:T(8,128)(2,1)}), bf16[512,1536]{1,0:T(8,128)(2,1)}) %all-gather.5.cloned.1.call-update) | async-done | bytes 1572880 | tf_op jit(solution)/shard_map/all_gather | solution.py:65
  35.1 2.1 fusion.61
  37.3 2.3 fusion.62
  41.9 1.7 copy-done.2
  46.6 2.6 fusion.63
  51.5 31.5 %all-gather = s32[128,512]{1,0:T(8,128)S(1)} all-gather(s32[16,512]{1,0:T(8,128)S(1)} %select_reduce_fusion.1), channel_id=2, replica_groups=mesh['ep'=8,'tp'=4] {'ep'}, dimensions={0}, use_global_device_ids=true | all-gather | bytes 294912 | tf_op jit(solution)/shard_map/all_gather | solution.py:616
  88.6 2.0 slice_bitcast_fusion.3
  90.6 1.4 multiply_reduce_fusion.2
  94.0 92.8 %gather_by_links.1 = bf16[4,2,2,2,128,1536]{5,4,3,2,1,0:T(8,128)(2,1)} custom-call(bf16[128,1536]{1,0:T(8,128)(2,1)} %multiply_convert_fusion.2.own), custom_call_target="tpu_custom_call" | custom-call | tf_op jit(solution)/shard_map/gather_by_links/pallas_call | solution.py:212
  189.4 8.3 %select_reduce_fusion = (f32[4096]{0:T(1024)S(1)}, f32[4096,16]{0,1:T(8,128)S(1)}) fusion(pred[4096,16]{0,1:T(8,128)(4,1)} %bitcast.192, bf16[4096,1536]{1,0:T(8,128)(2,1)} %bitcast.164, bf16[16,1536]{1,0:T(8,128)(2,1)} %param.23), kind=kOutput, calls=%fused_computation.81 | convolution fusion | flops 201453568 | bytes 12976128 | tf_op jit(solution)/shard_map/rd,ed->re/dot_general | solution.py:663
  198.4 10.1 %fusion.29 = f32[4096,256]{0,1:T(8,128)} fusion(bf16[4096,1536]{1,0:T(8,128)(2,1)} %bitcast.165, bf16[1536,128]{1,0:T(8,128)(2,1)S(1)} %copy-done.19, bf16[1536,128]{1,0:T(8,128)(2,1)S(1)} %copy-done.17), kind=kOutput, calls=%fused_computation.68 | convolution fusion | flops 3222798336 | bytes 17563648 | tf_op jit(solution)/shard_map/dot_general | solution.py:674
  208.5 10.3 %fusion.64 = f32[4096,256]{0,1:T(8,128)} fusion(bf16[4096,1536]{1,0:T(8,128)(2,1)} %all-gather.7.cloned.1.call-done, bf16[256,1536]{1,0:T(8,128)(2,1)} %bitcast.185), kind=kOutput, calls=%fused_computation.158 | convolution fusion | flops 3221225472 | bytes 17563648 | tf_op jit(solution)/shard_map/rd,fd->rf/dot_general | solution.py:676
  218.8 11.4 %fusion.4 = (bf16[4096,256]{0,1:T(8,128)(2,1)}, bf16[4096,256]{0,1:T(8,128)(2,1)S(1)}, bf16[4096,256]{0,1:T(8,128)(2,1)}, f32[4096,256]{0,1:T(8,128)}) fusion(f32[4096,2]{0,1:T(2,128)S(1)} %copy-done.50, f32[4096,256]{0,1:T(8,128)S(1)} %copy-done.3, f32[4096,256]{0,1:T(8,128)} %fusion.64, bf16[4096,1536]{1,0:T(8,128)(2,1)} %bitcast.166, ...), kind=kOutput, calls=%fused_computation.14 | convolution fusion | flops 3241672704 | bytes 32276480 | tf_op jit(solution)/shard_map/dot_general | solution.py:675
  230.2 5.8 bitcast_reduce_fusion
  236.1 6.4 convolution_convert_fusion
  242.5 10.4 %fusion.28 = f32[4096,1536]{1,0:T(8,128)} fusion(bf16[4096,256]{0,1:T(8,128)(2,1)S(1)} %get-tuple-element.65, bf16[1536,128]{1,0:T(8,128)(2,1)S(1)} %copy-done.20, bf16[1536,128]{1,0:T(8,128)(2,1)S(1)} %copy-done.18), kind=kOutput, calls=%fused_computation.67 | convolution fusion | flops 3222798336 | bytes 28049408 | tf_op jit(solution)/shard_map/rf,df->rd/dot_general | solution.py:689
  253.5 15.4 %add_convert_fusion = bf16[4096,1536]{1,0:T(8,128)(2,1)} fusion(f32[4096,1536]{1,0:T(8,128)} %fusion.28, bf16[4096,256]{0,1:T(8,128)(2,1)} %get-tuple-element.66, bf16[1536,128]{1,0:T(8,128)(2,1)} %get-tuple-element.73, bf16[1536,128]{1,0:T(8,128)(2,1)} %get-tuple-element.72), kind=kOutput, calls=%fused_computation | convolution fusion | flops 3235381248 | bytes 40632320 | tf_op jit(solution)/shard_map/rf,df->rd/dot_general | solution.py:690
  269.0 138.6 %totals_by_links.1 = (f32[128,1536]{1,0:T(8,128)}, f32[128,1536]{1,0:T(8,128)}, f32[8,8,128]{2,1,0:T(8,128)}) custom-call(bf16[4,2,2,2,128,1536]{5,4,3,2,1,0:T(8,128)(2,1)} %bitcast.169, bf16[4,2,2,2,128,1536]{5,4,3,2,1,0:T(8,128)(2,1)} %bitcast.170, f32[32,8,128]{2,1,0:T(8,128)} %pad.4.small_in), custom_call_target="tpu_custom_call" | custom-call | tf_op jit(solution)/shard_map/totals_by_links/pallas_call | solution.py:422
  408.4 2.5 multiply_reduce_fusion
  410.9 2.6 fusion.57
  414.8 17.5 %all-gather.9.cloned.1.call-done = bf16[512,1536]{1,0:T(8,128)(2,1)} async-done(((bf16[128,1536]{1,0:T(8,128)(2,1)}), bf16[512,1536]{1,0:T(8,128)(2,1)}) %all-gather.9.cloned.1.call-update) | async-done | bytes 1572880 | tf_op jit(solution)/shard_map/all_gather | solution.py:65
  432.3 2.4 convolution_convert_fusion.5
  434.7 4.1 fusion.16
  438.8 4.5 fusion
  443.4 4.7 fusion.2
  450.7 1.9 convolution_convert_fusion.1
  454.8 1.8 convolution_convert_fusion.2
  459.9 2.2 convolution_add_fusion
  462.4 1.5 copy-done.6
  464.0 7.5 convolution_bitcast_fusion.1
  471.5 3.2 copy.43
  474.7 7.6 convolution_bitcast_fusion
  482.3 3.2 copy.44
  485.5 1.9 fusion.39
  487.5 7.6 fusion.67
  495.1 92.1 %all-reduce.8.cloned.1.call-done = (bf16[384,1536]{1,0:T(8,128)(2,1)}, bf16[128,1536]{1,0:T(8,128)(2,1)}, bf16[128,1536]{1,0:T(8,128)(2,1)}, bf16[384,1536]{1,0:T(8,128)(2,1)}) async-done(((bf16[384,1536]{1,0:T(8,128)(2,1)}, bf16[128,1536]{1,0:T(8,128)(2,1)}, bf16[128,1536]{1,0:T(8,128)(2,1)}, bf16[384,1536]{1,0:T(8,128)(2,1)}), (bf16[384,1536]{1,0:T(8,128)(2,1)}, bf16[128,1536]{1,0:T(8,128)(2,1)}, ...) | async-done | bytes 3145744 | tf_op jit(solution)/shard_map/psum | solution.py:768
  587.2 2.1 convert_element_type.146
  589.3 2.0 convert_element_type.148
  591.3 1.7 convert_element_type.144
  593.0 1.7 convert_element_type.150
  594.7 31.8 %reduce-scatter.5.cloned.1.call-done = f32[128,1536]{1,0:T(8,128)} async-done(((f32[512,1536]{1,0:T(8,128)}), f32[128,1536]{1,0:T(8,128)}) %reduce-scatter.5.cloned.1.call-update) | async-done | bytes 786448 | tf_op jit(solution)/shard_map/reduce_scatter | solution.py:69
  626.5 1.4 fusion.27
  627.9 2.4 fusion.24
  630.3 39.5 %all-reduce.1 = (f32[1536]{0:T(1024)}, f32[1536]{0:T(1024)}) all-reduce(f32[1536]{0:T(1024)S(1)} %get-tuple-element.44, f32[1536]{0:T(1024)S(1)} %copy-done.58), channel_id=1, replica_groups=mesh['ep'=8,'tp'=4] {'ep','tp'}, use_global_device_ids=true, to_apply=%region_21.22 | all-reduce | flops 3072 | bytes 24576 | tf_op jit(solution)/shard_map/psum | solution.py:773
  669.8 84.4 %all-reduce.6.cloned.1.call-done = f32[16,1536]{1,0:T(8,128)} async-done(((f32[16,1536]{1,0:T(8,128)}), f32[16,1536]{1,0:T(8,128)}) %all-reduce.6.cloned.1.call-update) | async-done | bytes 98320 | tf_op jit(solution)/shard_map/psum | solution.py:773
  754.1 1.5 copy.61
  (217 shorter events, 34.5 us)
Async XLA Ops:
  8.0 38.6 %copy-start = (bf16[384,1536]{1,0:T(8,128)(2,1)S(1)}, bf16[384,1536]{1,0:T(8,128)(2,1)}, u32[]{:S(2)}) copy-start(bf16[384,1536]{1,0:T(8,128)(2,1)} %param.21) | copy-start | bytes 3538948
  8.0 29.2 %copy-start.25 = (bf16[384,1536]{1,0:T(8,128)(2,1)S(1)}, bf16[384,1536]{1,0:T(8,128)(2,1)}, u32[]{:S(2)}) copy-start(bf16[384,1536]{1,0:T(8,128)(2,1)} %param.18) | copy-start | bytes 3538948
  8.0 27.1 %all-gather.5.cloned.1.call-start = ((), (), s32[]{:S(2)}) async-start(), calls=%async_computation.2 | async-start | bytes 1966080 | tf_op jit(solution)/shard_map/all_gather | solution.py:65
  12.6 78.0 %reduce-scatter.3.cloned.1.call-start = ((), (), s32[]{:S(2)}) async-start(), calls=%async_computation.3 | async-start | bytes 3932160 | tf_op jit(solution)/shard_map/reduce_scatter | solution.py:69
  15.0 24.5 %copy-start.13 = (f32[512,32]{0,1:T(8,128)}, f32[512,32]{0,1:T(8,128)S(1)}, u32[]{:S(2)}) copy-start(f32[512,32]{0,1:T(8,128)S(1)} %get-tuple-element.80) | copy-start | bytes 196612
  15.1 24.5 %copy-start.15 = (f32[512,32]{0,1:T(8,128)}, f32[512,32]{0,1:T(8,128)S(1)}, u32[]{:S(2)}) copy-start(f32[512,32]{0,1:T(8,128)S(1)} %get-tuple-element.81) | copy-start | bytes 196612
  16.7 23.1 %copy-start.10 = (pred[512,512]{0,1:T(8,128)(4,1)}, pred[512,512]{0,1:T(8,128)(4,1)S(1)}, u32[]{:S(2)}) copy-start(pred[512,512]{0,1:T(8,128)(4,1)S(1)} %compare_and_fusion) | copy-start | bytes 786436
  49.3 38.4 %copy-start.32 = (bf16[2,1536,128]{2,1,0:T(8,128)(2,1)S(1)}, bf16[2,1536,128]{2,1,0:T(8,128)(2,1)}, u32[]{:S(2)}) copy-start(bf16[2,1536,128]{2,1,0:T(8,128)(2,1)} %param.24) | copy-start | bytes 2359300
  49.3 159.2 %all-gather.7.cloned.1.call-start = ((), (), s32[]{:S(2)}) async-start(), calls=%async_computation.4 | async-start | bytes 12976128 | tf_op jit(solution)/shard_map/all_gather | solution.py:456
  49.9 382.4 %all-gather.9.cloned.1.call-start = ((), (), s32[]{:S(2)}) async-start(), calls=%async_computation.5 | async-start | bytes 1966080 | tf_op jit(solution)/shard_map/all_gather | solution.py:65
  50.6 42.0 %copy-start.48 = (f32[1536]{0:T(1024)}, f32[1536]{0:T(1024)S(1)}, u32[]{:S(2)}) copy-start(f32[1536]{0:T(1024)S(1)} %convert_element_type.126) | copy-start | bytes 18436
  51.5 31.5 %copy-start.45 = (s32[16,512]{1,0:T(8,128)}, s32[16,512]{1,0:T(8,128)S(1)}, u32[]{:S(2)}) copy-start(s32[16,512]{1,0:T(8,128)S(1)} %select_reduce_fusion.1) | copy-start | bytes 98308
  189.3 8.3 %copy-start.37 = (pred[2,8,8,512]{3,1,2,0:T(8,128)(4,1)S(1)}, pred[2,8,8,512]{3,1,2,0:T(8,128)(4,1)}, u32[]{:S(2)}) copy-start(pred[2,8,8,512]{3,1,2,0:T(8,128)(4,1)} %copy.53) | copy-start | bytes 196612
  189.4 8.4 %copy-start.46 = (pred[1,2,8,512]{3,1,2,0:T(4,128)(4,1)S(1)}, pred[1,2,8,512]{3,1,2,0:T(4,128)(4,1)}, u32[]{:S(2)}) copy-start(pred[1,2,8,512]{3,1,2,0:T(4,128)(4,1)} %copy.54) | copy-start | bytes 24580
  189.4 9.1 %copy-start.17 = (bf16[1536,128]{1,0:T(8,128)(2,1)S(1)}, bf16[1536,128]{1,0:T(8,128)(2,1)}, u32[]{:S(2)}) copy-start(bf16[1536,128]{1,0:T(8,128)(2,1)} %get-tuple-element.74) | copy-start | bytes 1179652
  189.4 9.1 %copy-start.19 = (bf16[1536,128]{1,0:T(8,128)(2,1)S(1)}, bf16[1536,128]{1,0:T(8,128)(2,1)}, u32[]{:S(2)}) copy-start(bf16[1536,128]{1,0:T(8,128)(2,1)} %get-tuple-element.75) | copy-start | bytes 1179652
  208.5 10.3 %copy-start.3 = (f32[4096,256]{0,1:T(8,128)S(1)}, f32[4096,256]{0,1:T(8,128)}, u32[]{:S(2)}) copy-start(f32[4096,256]{0,1:T(8,128)} %fusion.29) | copy-start | bytes 12582916
  208.5 10.3 %copy-start.50 = (f32[4096,2]{0,1:T(2,128)S(1)}, f32[4096,2]{0,1:T(2,128)}, u32[]{:S(2)}) copy-start(f32[4096,2]{0,1:T(2,128)} %bitcast_select_fusion.1) | copy-start | bytes 98308
  230.2 12.3 %copy-start.5 = (bf16[4096,256]{0,1:T(8,128)(2,1)}, bf16[4096,256]{0,1:T(8,128)(2,1)S(1)}, u32[]{:S(2)}) copy-start(bf16[4096,256]{0,1:T(8,128)(2,1)S(1)} %get-tuple-element.65) | copy-start | bytes 6291460
  230.2 5.8 copy-start.47
  230.2 5.9 copy-start.7
  230.2 5.9 copy-start.31
  236.1 6.4 copy-start.18
  236.1 6.4 copy-start.20
  268.9 139.4 %copy-start.56 = (pred[128,16]{0,1:T(8,128)(4,1)S(1)}, pred[128,16]{0,1:T(8,128)(4,1)}, u32[]{:S(2)}) copy-start(pred[128,16]{0,1:T(8,128)(4,1)} %copy-done.55) | copy-start | bytes 6148
  268.9 139.4 %copy-start.60 = (f32[128]{0:T(128)S(1)}, f32[128]{0:T(128)}, u32[]{:S(2)}) copy-start(f32[128]{0:T(128)} %copy-done.59) | copy-start | bytes 1540
  268.9 139.4 %copy-start.62 = (f32[128]{0:T(128)S(1)}, f32[128]{0:T(128)}, u32[]{:S(2)}) copy-start(f32[128]{0:T(128)} %fusion.38) | copy-start | bytes 1540
  268.9 139.4 %copy-start.40 = (bf16[16,1536]{1,0:T(8,128)(2,1)S(1)}, bf16[16,1536]{1,0:T(8,128)(2,1)}, u32[]{:S(2)}) copy-start(bf16[16,1536]{1,0:T(8,128)(2,1)} %param.23) | copy-start | bytes 147460
  268.9 139.4 %copy-start.49 = (f32[1536]{0:T(1024)S(1)}, f32[1536]{0:T(1024)}, u32[]{:S(2)}) copy-start(f32[1536]{0:T(1024)} %copy-done.48) | copy-start | bytes 18436
  268.9 139.4 %copy-start.65 = (f32[128]{0:T(128)S(1)}, f32[128]{0:T(128)}, u32[]{:S(2)}) copy-start(f32[128]{0:T(128)} %copy-done.64) | copy-start | bytes 1540
  268.9 141.9 %copy-start.21 = (bf16[128,1536]{1,0:T(8,128)(2,1)S(1)}, bf16[128,1536]{1,0:T(8,128)(2,1)}, u32[]{:S(2)}) copy-start(bf16[128,1536]{1,0:T(8,128)(2,1)} %param.31) | copy-start | bytes 1179652
  269.0 141.9 %copy-start.70 = (f32[128]{0:T(128)S(1)}, f32[128]{0:T(128)}, u32[]{:S(2)}) copy-start(f32[128]{0:T(128)} %get-tuple-element.87) | copy-start | bytes 1540
  408.3 5.2 copy-start.51
  408.3 5.2 copy-start.66
  413.6 21.1 %copy-start.11 = (pred[512,512]{0,1:T(8,128)(4,1)S(1)}, pred[512,512]{0,1:T(8,128)(4,1)}, u32[]{:S(2)}) copy-start(pred[512,512]{0,1:T(8,128)(4,1)} %copy-done.10) | copy-start | bytes 786436
  413.6 173.7 %all-reduce.8.cloned.1.call-start = ((), (), s32[]{:S(2)}) async-start(), calls=%async_computation.8 | async-start | bytes 6291456 | tf_op jit(solution)/shard_map/psum | solution.py:768
  432.3 6.5 slice-start
  443.4 4.7 copy-start.34
  443.4 4.7 copy-start.36
  456.7 169.8 %reduce-scatter.5.cloned.1.call-start = ((), (), s32[]{:S(2)}) async-start(), calls=%async_computation.6 | async-start | bytes 3932160 | tf_op jit(solution)/shard_map/reduce_scatter | solution.py:69
  462.2 291.9 %all-reduce.6.cloned.1.call-start = ((), (), s32[]{:S(2)}) async-start(), calls=%async_computation.7 | async-start | bytes 196608 | tf_op jit(solution)/shard_map/psum | solution.py:773
  482.3 5.2 copy-start.8
  587.2 5.8 copy-start.27
  591.3 35.3 %copy-start.9 = (bf16[128,1536]{1,0:T(8,128)(2,1)S(1)}, bf16[128,1536]{1,0:T(8,128)(2,1)}, u32[]{:S(2)}) copy-start(bf16[128,1536]{1,0:T(8,128)(2,1)} %param.16) | copy-start | bytes 1179652
  591.3 35.3 %copy-start.69 = (f32[128]{0:T(128)S(1)}, f32[128]{0:T(128)}, u32[]{:S(2)}) copy-start(f32[128]{0:T(128)} %copy-done.68) | copy-start | bytes 1540
  593.0 34.9 %copy-start.12 = (f32[128,1536]{1,0:T(8,128)S(1)}, f32[128,1536]{1,0:T(8,128)}, u32[]{:S(2)}) copy-start(f32[128,1536]{1,0:T(8,128)} %get-tuple-element.53) | copy-start | bytes 2359300
  593.0 34.9 %copy-start.71 = (f32[128]{0:T(128)S(1)}, f32[128]{0:T(128)}, u32[]{:S(2)}) copy-start(f32[128]{0:T(128)} %get-tuple-element.85) | copy-start | bytes 1540
  593.0 37.3 %copy-start.58 = (f32[1536]{0:T(1024)S(1)}, f32[1536]{0:T(1024)}, u32[]{:S(2)}) copy-start(f32[1536]{0:T(1024)} %get-tuple-element.42) | copy-start | bytes 18436
  (34 other events, 75.5 us)
Sparse Core Ops, SparseCore 0:
  12.7 22.3 all-gather.4
  49.4 38.1 reduce-scatter.2
  413.7 18.5 all-gather.8
  456.8 130.3 all-reduce.7
  589.6 36.8 reduce-scatter.4
  633.5 120.6 all-reduce.5
Sparse Core Ops, SparseCore 1:
  53.0 138.7 all-gather.6

commit v3 on v2

--- a/solution.py
+++ b/solution.py
@@ -58,15 +58,7 @@
     weighted = grad_normed * gain
     inner = jnp.mean(value_rows * weighted, axis=-1, keepdims=True)
     grad_values = scale * weighted - value_rows * (scale * scale * scale) * inner
-    return (grad_values, jnp.sum(grad_normed * value_rows * scale, axis=0))
-
-
-def group_rows(value_rows):
-    return lax.all_gather(value_rows, "tp", axis=0, tiled=True)
-
-
-def group_totals(value_rows):
-    return lax.psum_scatter(value_rows, "tp", scatter_dimension=0, tiled=True)
+    return grad_values
 
 
 MESH = pl.DeviceIdType.MESH
@@ -227,14 +219,12 @@
 
 
 def add_into(target, other):
-    rows = target.shape[-2]
-
     def tile(i, carry):
-        at = pl.ds(pl.multiple_of(i * 32, 32), 32)
+        at = pl.ds(pl.multiple_of(i * 16, 16), 16)
         target[at, :] = target[at, :] + other[at, :]
         return carry
 
-    lax.fori_loop(0, rows // 32, tile, 0)
+    lax.fori_loop(0, target.shape[0] // 16, tile, 0)
 
 
 def total_kernel(
@@ -261,11 +251,7 @@
 ):
     me = Place(ep_size)
     depth = me.depth
-    others = []
-    for k in range(1, ep_size * 4):
-        ep = lax.rem(lax.axis_index("ep") + k // 4, ep_size)
-        tp = lax.rem(lax.axis_index("tp") + k % 4, 4)
-        others.append((ep, tp))
+    others = all_others(ep_size)
     meet(others)
     small = []
     my_place = lax.axis_index("ep") * 4 + lax.axis_index("tp")
@@ -450,6 +436,371 @@
     )(first.reshape(whole), second.reshape(whole), small)
 
 
+def group_gather_kernel(ep_size, pieces, own, out, own_sem, sems):
+    me = Place(ep_size)
+    size = own.shape[0] // pieces
+    meet([me.sibling(), me.x_peer()])
+    started = []
+    local = pltpu.make_async_copy(own, out.at[me.x, me.c], own_sem)
+    local.start()
+
+    def at(p):
+        return pl.ds(p * size, size)
+
+    def go(kind, p, src, dst, device):
+        slot = kind * pieces + p
+        started.append(send(src, dst, sems.at[0, slot], sems.at[1, slot], device))
+
+    for p in range(pieces):
+        go(0, p, own.at[at(p)], out.at[me.x, me.c, at(p)], me.x_peer())
+    for p in range(pieces):
+        go(1, p, own.at[at(p)], out.at[me.x, me.c, at(p)], me.sibling())
+    for p in range(pieces):
+        block = out.at[1 - me.x, me.c, at(p)]
+        pltpu.make_async_copy(block, block, sems.at[1, p]).wait()
+        go(2, p, block, block, me.sibling())
+    for p in range(pieces):
+        for kind, x in ((1, me.x), (2, 1 - me.x)):
+            block = out.at[x, 1 - me.c, at(p)]
+            pltpu.make_async_copy(block, block, sems.at[1, kind * pieces + p]).wait()
+    local.wait()
+    for copy in started:
+        copy.wait_send()
+
+
+def group_gather(value_rows, ep_size, call):
+    rows, width = value_rows.shape
+    pieces = 4
+    dma = pltpu.SemaphoreType.DMA
+    every = pl.pallas_call(
+        functools.partial(group_gather_kernel, ep_size, pieces),
+        out_shape=jax.ShapeDtypeStruct((2, 2, rows, width), value_rows.dtype),
+        in_specs=[pl.BlockSpec(memory_space=pl.ANY)],
+        out_specs=pl.BlockSpec(memory_space=pl.ANY),
+        scratch_shapes=[dma, dma((2, 3 * pieces))],
+        compiler_params=pltpu.CompilerParams(collective_id=call, has_side_effects=True),
+        name="group_gather",
+    )(value_rows)
+    return every.reshape(-1, width)
+
+
+class GroupTotal:
+    def __init__(self, me, parts, core_got, pair_got, sems):
+        self.me, self.parts, self.core_got, self.pair_got = me, parts, core_got, pair_got
+        self.core = [
+            pltpu.make_async_remote_copy(
+                src_ref=parts.at[x, 1 - me.c],
+                dst_ref=core_got.at[x],
+                send_sem=sems.at[0, k],
+                recv_sem=sems.at[1, k],
+                device_id=me.sibling(),
+                device_id_type=MESH,
+            )
+            for k, x in enumerate((1 - me.x, me.x))
+        ]
+        self.pair = pltpu.make_async_remote_copy(
+            src_ref=core_got.at[1 - me.x],
+            dst_ref=pair_got,
+            send_sem=sems.at[0, 2],
+            recv_sem=sems.at[1, 2],
+            device_id=me.x_peer(),
+            device_id_type=MESH,
+        )
+
+    def begin(self):
+        for copy in self.core:
+            copy.start()
+
+    def exchange(self):
+        self.core[0].wait_recv()
+        far = 1 - self.me.x
+        add_into(self.core_got.at[far], self.parts.at[far, self.me.c])
+        self.pair.start()
+
+    def finish(self, out):
+        self.core[1].wait_recv()
+        self.pair.wait_recv()
+
+        def tile(i, carry):
+            at = pl.ds(pl.multiple_of(i * 16, 16), 16)
+            out[at, :] = (
+                self.parts[self.me.x, self.me.c, at, :].astype(jnp.float32)
+                + self.core_got[self.me.x, at, :].astype(jnp.float32)
+                + self.pair_got[at, :].astype(jnp.float32)
+            )
+            return carry
+
+        lax.fori_loop(0, out.shape[0] // 16, tile, 0)
+
+    def sent(self):
+        for copy in self.core + [self.pair]:
+            copy.wait_send()
+
+
+def group_total_kernel(ep_size, parts, out, core_got, pair_got, sems):
+    me = Place(ep_size)
+    meet([me.sibling(), me.x_peer()])
+    total = GroupTotal(me, parts, core_got, pair_got, sems)
+    total.begin()
+    total.exchange()
+    total.finish(out)
+    total.sent()
+
+
+def group_total(value_rows, ep_size, call):
+    rows, width = value_rows.shape[0] // 4, value_rows.shape[1]
+    vmem = pl.BlockSpec(memory_space=pltpu.VMEM)
+    return pl.pallas_call(
+        functools.partial(group_total_kernel, ep_size),
+        out_shape=jax.ShapeDtypeStruct((rows, width), jnp.float32),
+        in_specs=[vmem],
+        out_specs=vmem,
+        scratch_shapes=[
+            pltpu.VMEM((2, rows, width), jnp.bfloat16),
+            pltpu.VMEM((rows, width), jnp.bfloat16),
+            pltpu.SemaphoreType.DMA((2, 3)),
+        ],
+        compiler_params=pltpu.CompilerParams(
+            collective_id=call, has_side_effects=True, vmem_limit_bytes=32 * 1024 * 1024
+        ),
+        name="group_total",
+    )(value_rows.reshape(2, 2, rows, width))
+
+
+def all_others(ep_size):
+    ep, tp = lax.axis_index("ep"), lax.axis_index("tp")
+    return [
+        (lax.rem(ep + k // 4, ep_size), lax.rem(tp + k % 4, 4)) for k in range(1, ep_size * 4)
+    ]
+
+
+def tail_kernel(
+    ep_size,
+    counts,
+    *refs,
+):
+    n = len(counts)
+    grads, rows_in, small_in = refs[:n], refs[n], refs[n + 1]
+    outs, rows_out, small_out = refs[n + 2 : 2 * n + 2], refs[2 * n + 2], refs[2 * n + 3]
+    (
+        y_got,
+        z_got,
+        final,
+        core_got,
+        pair_got,
+        small_got,
+        small_sum,
+        y_sems,
+        z_sems,
+        fz_sems,
+        fy_sems,
+        group_sems,
+        small_sems,
+        spread_sems,
+        own_sem,
+    ) = refs[2 * n + 4 :]
+    me = Place(ep_size)
+    depth = me.depth
+    starts = [sum(counts[:i]) for i in range(n)]
+    others = all_others(ep_size)
+    meet(others)
+    my_place = lax.axis_index("ep") * 4 + lax.axis_index("tp")
+
+    def y_copy(step, i):
+        return pltpu.make_async_remote_copy(
+            src_ref=grads[i].at[me.after(step + 1), 1 - me.y],
+            dst_ref=y_got.at[step, pl.ds(starts[i], counts[i])],
+            send_sem=y_sems.at[0, step, i],
+            recv_sem=y_sems.at[1, step, i],
+            device_id=me.y_peer(),
+            device_id_type=MESH,
+        )
+
+    def z_copy(step):
+        return pltpu.make_async_remote_copy(
+            src_ref=y_got.at[step],
+            dst_ref=z_got.at[step],
+            send_sem=z_sems.at[0, step],
+            recv_sem=z_sems.at[1, step],
+            device_id=me.device(z=me.after(step + 1)),
+            device_id_type=MESH,
+        )
+
+    for step in range(depth):
+        for i in range(n):
+            y_copy(step, i).start()
+    group = GroupTotal(me, rows_in, core_got, pair_got, group_sems)
+    group.begin()
+    small = [
+        send(
+            small_in.at[device[0] * 4 + device[1]],
+            small_got.at[my_place],
+            small_sems.at[0, k],
+            small_sems.at[1, k],
+            device,
+        )
+        for k, device in enumerate(others)
+    ]
+    own_small = pltpu.make_async_copy(small_in.at[my_place], small_got.at[my_place], own_sem)
+    own_small.start()
+    group.exchange()
+
+    def y_sum(step):
+        for i in range(n):
+            y_copy(step, i).wait_recv()
+            add_into(
+                y_got.at[step, pl.ds(starts[i], counts[i])],
+                grads[i].at[me.after(step + 1), me.y],
+            )
+
+    for step in range(depth - 1):
+        y_sum(step)
+        z_copy(step).start()
+    own_small.wait()
+    for copy in small:
+        copy.wait_recv()
+    total = small_got[0]
+    for k in range(1, 4 * ep_size):
+        total = total + small_got[k]
+    small_sum[...] = total
+    spread = [
+        send(
+            small_sum,
+            small_out.at[my_place],
+            spread_sems.at[0, k],
+            spread_sems.at[1, k],
+            device,
+        )
+        for k, device in enumerate(others)
+    ]
+    small_out[my_place] = total
+    group.finish(rows_out)
+    y_sum(depth - 1)
+    for step in range(depth - 1):
+        z_copy(step).wait_recv()
+
+    def tile(i, carry):
+        at = pl.ds(pl.multiple_of(i * 16, 16), 16)
+        value = y_got[depth - 1, at, :].astype(jnp.float32)
+        for step in range(depth - 1):
+            value = value + z_got[step, at, :].astype(jnp.float32)
+        final[me.z, me.y, at, :] = value.astype(final.dtype)
+        return carry
+
+    lax.fori_loop(0, sum(counts) // 16, tile, 0)
+    mine = final.at[me.z, me.y]
+    finals = []
+    for s in range(1, depth):
+        finals.append(
+            send(mine, mine, fz_sems.at[0, s], fz_sems.at[1, s], me.device(z=me.after(s)))
+        )
+    finals.append(send(mine, mine, fy_sems.at[0, 0], fy_sems.at[1, 0], me.y_peer()))
+    for s in range(1, depth):
+        block = final.at[me.before(s), me.y]
+        pltpu.make_async_copy(block, block, fz_sems.at[1, s]).wait()
+        finals.append(send(block, block, fy_sems.at[0, s], fy_sems.at[1, s], me.y_peer()))
+
+    def deliver(s, y):
+        z = me.before(s)
+        for i in range(n):
+
+            def tile(t, carry):
+                at = pl.multiple_of(t * 16, 16)
+                outs[i][z, y, pl.ds(at, 16), :] = final[
+                    z, y, pl.ds(starts[i] + at, 16), :
+                ].astype(jnp.float32)
+                return carry
+
+            lax.fori_loop(0, counts[i] // 16, tile, 0)
+
+    for s in range(depth):
+        deliver(s, me.y)
+    for s in range(depth):
+        block = final.at[me.before(s), 1 - me.y]
+        pltpu.make_async_copy(block, block, fy_sems.at[1, s]).wait()
+        deliver(s, 1 - me.y)
+    for copy in spread:
+        copy.wait()
+    for copy in small + finals:
+        copy.wait_send()
+    group.sent()
+    for step in range(depth):
+        for i in range(n):
+            y_copy(step, i).wait_send()
+        if step < depth - 1:
+            z_copy(step).wait_send()
+
+
+def tail_by_links(grads, rows_part, small, ep_size):
+    width = rows_part.shape[1]
+    depth = ep_size // 2
+    rows = rows_part.shape[0] // 4
+    counts = [g.shape[0] // ep_size for g in grads]
+    total = sum(counts)
+    places = 4 * ep_size
+    bf16, f32 = jnp.bfloat16, jnp.float32
+    dma = pltpu.SemaphoreType.DMA
+    vmem = pl.BlockSpec(memory_space=pltpu.VMEM)
+    lanes = width // 128
+    blocks = jnp.pad(small, ((0, places - small.shape[0]), (0, 0))).reshape(places, lanes, 128)
+    got = pl.pallas_call(
+        functools.partial(tail_kernel, ep_size, counts),
+        out_shape=tuple(jax.ShapeDtypeStruct((depth, 2, k, width), f32) for k in counts)
+        + (
+            jax.ShapeDtypeStruct((rows, width), f32),
+            jax.ShapeDtypeStruct(blocks.shape, f32),
+        ),
+        in_specs=[vmem] * (len(grads) + 2),
+        out_specs=(vmem,) * (len(grads) + 2),
+        scratch_shapes=[
+            pltpu.VMEM((depth, total, width), bf16),
+            pltpu.VMEM((depth - 1, total, width), bf16),
+            pltpu.VMEM((depth, 2, total, width), bf16),
+            pltpu.VMEM((2, rows, width), bf16),
+            pltpu.VMEM((rows, width), bf16),
+            pltpu.VMEM(blocks.shape, f32),
+            pltpu.VMEM(blocks.shape[1:], f32),
+            dma((2, depth, len(grads))),
+            dma((2, depth)),
+            dma((2, depth)),
+            dma((2, depth)),
+            dma((2, 3)),
+            dma((2, places - 1)),
+            dma((2, places - 1)),
+            dma,
+        ],
+        compiler_params=pltpu.CompilerParams(
+            collective_id=5, has_side_effects=True, vmem_limit_bytes=56 * 1024 * 1024
+        ),
+        name="tail_by_links",
+    )(
+        *[g.reshape(depth, 2, k, width) for g, k in zip(grads, counts)],
+        rows_part.reshape(2, 2, rows, width),
+        blocks,
+    )
+    sums = [g.reshape(-1, width) for g in got[: len(grads)]]
+    return sums, got[-2], got[-1].reshape(places, width)[: small.shape[0]]
+
+
+def group_rows(value_rows, by_links, call):
+    if by_links:
+        return group_gather(value_rows, lax.axis_size("ep"), call)
+    return lax.all_gather(value_rows, "tp", axis=0, tiled=True)
+
+
+def group_totals(value_rows, by_links, call):
+    if by_links:
+        return group_total(value_rows, lax.axis_size("ep"), call)
+    return lax.psum_scatter(value_rows, "tp", scatter_dimension=0, tiled=True).astype(jnp.float32)
+
+
+def tail_totals(grads, rows_part, small, by_links):
+    if by_links:
+        return tail_by_links(grads, rows_part, small, lax.axis_size("ep"))
+    sums = [lax.psum(g, "ep").astype(jnp.float32) for g in grads]
+    return sums, group_totals(rows_part, by_links, None), lax.psum(small, ("ep", "tp"))
+
+
 def gather_all(value_rows, by_links):
     if by_links:
         return gather_by_links(value_rows, lax.axis_size("ep"))
@@ -619,7 +970,9 @@
     gain_one = gain_attn.astype(jnp.float32)
     gain_two = gain_ffn.astype(jnp.float32)
     scale_one = norm_scale(inputs_own)
-    first_normalized = group_rows((inputs_own * scale_one * gain_one).astype(jnp.bfloat16))
+    first_normalized = group_rows(
+        (inputs_own * scale_one * gain_one).astype(jnp.bfloat16), by_links, 6
+    )
     cosine_lookup, sine_lookup = rope_tables(position, head_width)
     query_proj = jnp.einsum(
         "rd,fd->rf", first_normalized, w_query, preferred_element_type=jnp.float32
@@ -646,7 +999,9 @@
     head_outputs, log_sums = attend_forward(query_rows, key_rows, value_rows, segment, position)
     head_outputs = head_outputs.reshape(token_count, local_heads * head_width)
     middle_own = inputs_own + group_totals(
-        jnp.dot(head_outputs, w_out, preferred_element_type=jnp.float32)
+        jnp.dot(head_outputs, w_out, preferred_element_type=jnp.float32).astype(jnp.bfloat16),
+        by_links,
+        3,
     )
     scale_two = norm_scale(middle_own)
     normed_own = (middle_own * scale_two * gain_two).astype(jnp.bfloat16)
@@ -716,12 +1071,15 @@
     router_f = w_router.astype(jnp.float32)
     grad_normed_own = grad_normed_own + jnp.dot(grad_logits, router_f, precision=EXACT_PRECISION)
     grad_router = jnp.dot(grad_logits.T, normed_own.astype(jnp.float32), precision=EXACT_PRECISION)
-    grad_middle_back, grad_gain_ffn = norm_back(middle_own, scale_two, gain_two, grad_normed_own)
-    grad_middle = cotangent.astype(jnp.float32) + grad_middle_back
-    grad_attn = group_rows(grad_middle.astype(jnp.bfloat16))
+    grad_gain_ffn = jnp.sum(grad_normed_own * middle_own * scale_two, axis=0)
+    grad_middle = cotangent.astype(jnp.float32) + norm_back(
+        middle_own, scale_two, gain_two, grad_normed_own
+    )
+    grad_attn = group_rows(grad_middle.astype(jnp.bfloat16), by_links, 7)
     grad_w_out = jnp.einsum(
         "rf,rd->fd", head_outputs, grad_attn, preferred_element_type=jnp.float32
     )
+    grad_w_out = lax.psum(grad_w_out.astype(jnp.bfloat16), "ep").astype(jnp.float32)
     grad_heads = (
         jnp.einsum("rd,fd->rf", grad_attn, w_out, preferred_element_type=jnp.float32)
         .astype(jnp.bfloat16)
@@ -761,18 +1119,19 @@
     grad_normed_one = grad_normed_one + jnp.einsum(
         "rf,fd->rd", grad_value_proj, value_projection_weight, preferred_element_type=jnp.float32
     )
-    grad_one_own = group_totals(grad_normed_one)
-    grad_inputs_back, grad_gain_attn = norm_back(inputs_own, scale_one, gain_one, grad_one_own)
-    grad_input = grad_middle + grad_inputs_back
-    grad_w_query, grad_w_key, grad_w_value, grad_w_out = (
-        lax.psum(grad_w_query.astype(jnp.bfloat16), "ep").astype(jnp.float32),
-        lax.psum(grad_w_key.astype(jnp.bfloat16), "ep").astype(jnp.float32),
-        lax.psum(grad_w_value.astype(jnp.bfloat16), "ep").astype(jnp.float32),
-        lax.psum(grad_w_out.astype(jnp.bfloat16), "ep").astype(jnp.float32),
-    )
-    grad_gain_attn, grad_gain_ffn, grad_router = lax.psum(
-        (grad_gain_attn, grad_gain_ffn, grad_router), ("ep", "tp")
-    )
+    grad_gain_attn = jnp.sum(grad_normed_one * first_normalized.astype(jnp.float32), axis=0)
+    small = jnp.concatenate(
+        [grad_router, grad_gain_ffn[None, :], (grad_gain_attn / gain_one)[None, :]], axis=0
+    )
+    (grad_w_query, grad_w_key, grad_w_value), grad_one_own, small = tail_totals(
+        [g.astype(jnp.bfloat16) for g in (grad_w_query, grad_w_key, grad_w_value)],
+        grad_normed_one.astype(jnp.bfloat16),
+        small,
+        by_links,
+    )
+    grad_router = small[:expert_count]
+    grad_gain_ffn, grad_gain_attn = small[expert_count], small[expert_count + 1]
+    grad_input = grad_middle + norm_back(inputs_own, scale_one, gain_one, grad_one_own)
     return (
         output_own,
         grad_input,

time: 770 us -> 589 us (0.76)
  waiting for transfers between devices: 245 us -> 0.7 us
  Pallas kernels: 231 us -> 354 us
  blocking collectives: 71 us -> 33.3 us
  other arithmetic: 43.8 us -> 31.8 us
  matrix products: 133 us -> 124 us
    psum x2 -> x1, waiting for transfers between devices: 177 us -> 0.01 us  [local(): lax.psum(grad_w_out.astype(jnp.bfloat16), 'ep').astype(jnp.float32)]
    pallas_call x0 -> x4, Pallas kernels: none -> 135 us  [the longest x1 81.9 us: tail_by_links(): pl.pallas_call(functools.partial(tail_kernel, ep_size, counts), out_shape...]
    psum x1 -> x0, blocking collectives: 39.5 us -> none  [local(): lax.psum((grad_gain_attn, grad_gain_ffn, grad_router), ('ep', 'tp'))]
    all_gather x2 -> x0, waiting for transfers between devices: 35.9 us -> none  [group_rows(): return lax.all_gather(value_rows, 'tp', axis=0, tiled=True)]
    reduce_scatter x2 -> x0, waiting for transfers between devices: 31.9 us -> none  [group_totals(): return lax.psum_scatter(value_rows, 'tp', scatter_dimension=0, tiled=True)]
    pallas_call x1, Pallas kernels: 92.8 us -> 74.8 us  [gather_by_links(): pl.pallas_call(functools.partial(gather_kernel, ep_size), out_shape=jax.S...]
    unnamed x155 -> x170, local copies, waits for them, and re-layouts: 16.5 us -> 14.2 us
  transfers between devices with their start and end apart: 7 -> 2, of which waited for: 5 -> 0; matrix products, arithmetic and copies ran while one was open for 11% -> 11% of each run, Pallas kernels for 12% -> 34%
where the time goes in v3:
time: 589 us; the launch traced here: 578 us
  Pallas kernels  354 us (60%)
  matrix products  124 us (21%)
  blocking collectives  33.3 us (6%)
  other arithmetic  31.8 us (5%)
  local copies, waits for them, and re-layouts  18.3 us (3%)
  between operations  15.3 us (3%)
    pallas_call x1, Pallas kernels, totals_by_links(): pl.pallas_call(functools.partial(total_kernel, ep_size), out_shape=(jax.S...  145 us
    pallas_call x1, Pallas kernels, tail_by_links(): pl.pallas_call(functools.partial(tail_kernel, ep_size, counts), out_shape...  81.9 us
    pallas_call x1, Pallas kernels, gather_by_links(): pl.pallas_call(functools.partial(gather_kernel, ep_size), out_shape=jax.S...  74.8 us
    all_gather x1, blocking collectives, local(): order_all = lax.all_gather(order, 'ep')  33.3 us
    pallas_call x2, Pallas kernels, group_gather(): pl.pallas_call(functools.partial(group_gather_kernel, ep_size, pieces), o...  30.9 us
    pallas_call x1, Pallas kernels, group_total(): pl.pallas_call(functools.partial(group_total_kernel, ep_size), out_shape=...  21.9 us
    dot_general x1, matrix products, local(): jnp.einsum('rf,df->rd', grad_up_act, up_in, preferred_element_type=jnp.fl...  15 us
    unnamed x170, local copies, waits for them, and re-layouts  14.2 us
  transfers between devices with their start and end apart: 2, of which 0 were waited for; matrix products, arithmetic and copies ran while one was open for 11% of the time, Pallas kernels for 34%

profile of v3, /device:TPU:0, one launch (start us, length us, event | category | flops | bytes accessed | tf_op | source)
XLA Modules:
  0.0 577.8 jit_solution(8964799582246750618)
XLA Ops:
  10.9 33.3 %all-gather = s32[128,512]{1,0:T(8,128)S(1)} all-gather(s32[16,512]{1,0:T(8,128)S(1)} %select_reduce_fusion.1), channel_id=2, replica_groups=mesh['ep'=8,'tp'=4] {'ep'}, dimensions={0}, use_global_device_ids=true | all-gather | bytes 294912 | tf_op jit(solution)/shard_map/all_gather | solution.py:967
  45.5 1.2 fusion.19
  47.3 1.9 fusion.21.own
  49.2 16.2 %group_gather.2 = bf16[2,2,128,1536]{3,2,1,0:T(8,128)(2,1)} custom-call(bf16[128,1536]{1,0:T(8,128)(2,1)} %fusion.21.own), custom_call_target="tpu_custom_call" | custom-call | tf_op jit(solution)/shard_map/group_gather/pallas_call | solution.py:475
  66.6 2.0 fusion.59
  70.5 1.2 fusion.58
  71.7 0.9 fusion.3
  72.6 1.9 copy-done.1
  74.5 1.2 fusion.10
  76.1 1.0 convolution_convert_fusion.1
  77.1 21.9 %group_total.1 = f32[128,1536]{1,0:T(8,128)S(1)} custom-call(bf16[2,2,128,1536]{3,2,1,0:T(8,128)(2,1)S(1)} %bitcast.186), custom_call_target="tpu_custom_call" | custom-call | tf_op jit(solution)/shard_map/group_total/pallas_call | solution.py:553
  100.1 0.9 multiply_convert_fusion.2.own
  101.0 74.8 %gather_by_links.1 = bf16[4,2,2,2,128,1536]{5,4,3,2,1,0:T(8,128)(2,1)} custom-call(bf16[128,1536]{1,0:T(8,128)(2,1)} %multiply_convert_fusion.2.own), custom_call_target="tpu_custom_call" | custom-call | tf_op jit(solution)/shard_map/gather_by_links/pallas_call | solution.py:204
  177.3 8.1 %select_reduce_fusion = (f32[4096]{0:T(1024)S(1)}, f32[4096,16]{0,1:T(8,128)S(1)}) fusion(pred[4096,16]{0,1:T(8,128)(4,1)S(1)} %bitcast.228, bf16[4096,1536]{1,0:T(8,128)(2,1)} %bitcast.187, bf16[16,1536]{1,0:T(8,128)(2,1)S(1)} %copy-done.45), kind=kOutput, calls=%fused_computation.81 | convolution fusion | flops 201453568 | bytes 12976128 | tf_op jit(solution)/shard_map/rd,ed->re/dot_general | solution.py:1018
  185.6 1.0 slice_bitcast_fusion.3
  186.7 10.0 %fusion.27 = f32[4096,256]{0,1:T(8,128)} fusion(bf16[4096,1536]{1,0:T(8,128)(2,1)} %bitcast.188, bf16[1536,128]{1,0:T(8,128)(2,1)S(1)} %get-tuple-element.91, bf16[1536,128]{1,0:T(8,128)(2,1)S(1)} %get-tuple-element.90), kind=kOutput, calls=%fused_computation.68 | convolution fusion | flops 3222798336 | bytes 17563648 | tf_op jit(solution)/shard_map/dot_general | solution.py:1029
  196.8 7.1 %fusion.61 = f32[4096,256]{0,1:T(8,128)S(1)} fusion(bf16[4096,1536]{1,0:T(8,128)(2,1)} %all-gather.3.cloned.1.call-done, bf16[256,1536]{1,0:T(8,128)(2,1)} %bitcast.220), kind=kOutput, calls=%fused_computation.163 | convolution fusion | flops 3221225472 | bytes 17563648 | tf_op jit(solution)/shard_map/rd,fd->rf/dot_general | solution.py:1031
  203.9 10.8 %fusion.4 = (bf16[4096,256]{0,1:T(8,128)(2,1)}, bf16[4096,256]{0,1:T(8,128)(2,1)}, bf16[4096,256]{0,1:T(8,128)(2,1)}, f32[4096,256]{0,1:T(8,128)}) fusion(f32[4096,2]{0,1:T(2,128)S(1)} %bitcast_select_fusion.1, f32[4096,256]{0,1:T(8,128)S(1)} %copy-done.6, f32[4096,256]{0,1:T(8,128)S(1)} %fusion.61, bf16[4096,1536]{1,0:T(8,128)(2,1)} %bitcast.189, ...), kind=kOutput, calls=%fused_computation.14 | convolution fusion | flops 3241672704 | bytes 32276480 | tf_op jit(solution)/shard_map/dot_general | solution.py:1030
  214.8 3.9 bitcast_reduce_fusion
  218.7 7.7 %convolution_convert_fusion = bf16[4096,1536]{1,0:T(8,128)(2,1)} fusion(bf16[4096,256]{0,1:T(8,128)(2,1)S(1)} %copy-done.13, bf16[256,1536]{1,0:T(8,128)(2,1)} %bitcast.221), kind=kOutput, calls=%fused_computation.1 | convolution fusion | flops 3227516928 | bytes 15466496 | tf_op jit(solution)/shard_map/dot_general | solution.py:1047
  226.4 10.3 %fusion.26 = f32[4096,1536]{1,0:T(8,128)} fusion(bf16[4096,256]{0,1:T(8,128)(2,1)S(1)} %copy-done.11, bf16[1536,128]{1,0:T(8,128)(2,1)S(1)} %copy-done.28, bf16[1536,128]{1,0:T(8,128)(2,1)S(1)} %copy-done.26), kind=kOutput, calls=%fused_computation.67 | convolution fusion | flops 3222798336 | bytes 28049408 | tf_op jit(solution)/shard_map/rf,df->rd/dot_general | solution.py:1044
  237.4 15.0 %add_convert_fusion = bf16[4096,1536]{1,0:T(8,128)(2,1)} fusion(f32[4096,1536]{1,0:T(8,128)} %fusion.26, bf16[4096,256]{0,1:T(8,128)(2,1)S(1)} %copy-done.7, bf16[1536,128]{1,0:T(8,128)(2,1)} %get-tuple-element.89, bf16[1536,128]{1,0:T(8,128)(2,1)} %get-tuple-element.88), kind=kOutput, calls=%fused_computation | convolution fusion | flops 3235381248 | bytes 40632320 | tf_op jit(solution)/shard_map/rf,df->rd/dot_general | solution.py:1045
  252.5 144.8 %totals_by_links.1 = (f32[128,1536]{1,0:T(8,128)}, f32[128,1536]{1,0:T(8,128)}, f32[8,8,128]{2,1,0:T(8,128)}) custom-call(bf16[4,2,2,2,128,1536]{5,4,3,2,1,0:T(8,128)(2,1)} %bitcast.194, bf16[4,2,2,2,128,1536]{5,4,3,2,1,0:T(8,128)(2,1)} %bitcast.195, f32[32,8,128]{2,1,0:T(8,128)} %pad.8.small_in), custom_call_target="tpu_custom_call" | custom-call | tf_op jit(solution)/shard_map/totals_by_links/pallas_call | solution.py:408
  398.2 0.9 fusion.37
  399.1 2.5 multiply_reduce_fusion.1
  401.6 1.5 fusion.55
  403.1 14.7 %group_gather.3 = bf16[2,2,128,1536]{3,2,1,0:T(8,128)(2,1)} custom-call(bf16[128,1536]{1,0:T(8,128)(2,1)} %get-tuple-element.66.own), custom_call_target="tpu_custom_call" | custom-call | tf_op jit(solution)/shard_map/group_gather/pallas_call | solution.py:475
  417.8 3.1 convolution_convert_fusion.6
  420.9 1.8 convolution_convert_fusion.2
  422.7 4.9 fusion.16
  427.6 4.4 fusion
  432.0 6.5 %fusion.2 = bf16[2,3,512,512]{2,3,1,0:T(8,128)(2,1)} fusion(f32[2,512,512,3]{2,1,3,0:T(8,128)} %get-tuple-element.114, f32[2,3,512,512]{2,3,1,0:T(8,128)S(1)} %bitcast.197, f32[2,3,512]{2,1,0:T(4,128)S(1)} %get-tuple-element.113, f32[2,3,512]{2,1,0:T(4,128)S(1)} %copy-done.57, pred[512,512]{0,1:T(8,128)(4,1)S(1)} %compare_and_fusion), kind=kLoop, calls=%fused_computation.6 | loop fusion | flops 7864320 | bytes 16015360 | tf_op jit(solution)/shard_map/convert_element_type | solution.py:922
  438.6 3.3 fusion.15
  443.3 1.8 convolution_convert_fusion.3
  445.1 2.6 fusion.63
  447.8 4.6 convolution_bitcast_fusion
  452.4 4.8 convolution_bitcast_fusion.1
  457.3 1.1 convolution_convert_fusion.4
  458.5 1.1 convolution_convert_fusion.5
  460.6 1.9 multiply_reduce_fusion
  463.3 81.9 %tail_by_links.1 = (f32[4,2,48,1536]{3,2,1,0:T(8,128)}, f32[4,2,16,1536]{3,2,1,0:T(8,128)}, f32[4,2,16,1536]{3,2,1,0:T(8,128)}, f32[128,1536]{1,0:T(8,128)}, f32[32,12,128]{2,1,0:T(8,128)}) custom-call(bf16[4,2,48,1536]{3,2,1,0:T(8,128)(2,1)} %bitcast.217, bf16[4,2,16,1536]{3,2,1,0:T(8,128)(2,1)} %bitcast.214, bf16[4,2,16,1536]{3,2,1,0:T(8,128)(2,1)} %bitcast.213, ...), custom_call_target="tpu_custom_call" | custom-call | tf_op jit(solution)/shard_map/tail_by_links/pallas_call | solution.py:746
  545.3 1.4 fusion.25
  546.7 2.4 fusion.24
  549.7 3.2 copy.52
  552.9 3.0 copy.53
  556.6 7.6 %fusion.64 = f32[256,1536]{1,0:T(8,128)} fusion(bf16[4096,256]{0,1:T(8,128)(2,1)S(1)} %copy-done.14, bf16[4096,1536]{1,0:T(8,128)(2,1)} %all-gather.3.cloned.1.call-done), kind=kOutput, calls=%fused_computation.166 | convolution fusion | flops 3221225472 | bytes 16252928 | tf_op jit(solution)/shard_map/rf,rd->fd/dot_general | solution.py:1066
  564.2 3.1 convert_element_type.172
  567.3 1.4 copy.72
  (225 shorter events, 19.6 us)
Async XLA Ops:
  7.2 61.6 %copy-start = (bf16[384,1536]{1,0:T(8,128)(2,1)S(1)}, bf16[384,1536]{1,0:T(8,128)(2,1)}, u32[]{:S(2)}) copy-start(bf16[384,1536]{1,0:T(8,128)(2,1)} %param.18) | copy-start | bytes 3538948
  7.2 58.6 %copy-start.65 = (s32[512]{0:T(512)S(1)}, s32[512]{0:T(512)}, u32[]{:S(2)}) copy-start(s32[512]{0:T(512)} %param.30) | copy-start | bytes 6148
  7.2 58.2 %copy-start.63 = (s32[512]{0:T(512)S(1)}, s32[512]{0:T(512)}, u32[]{:S(2)}) copy-start(s32[512]{0:T(512)} %param.29) | copy-start | bytes 6148
  7.2 59.4 %copy-start.50 = (bf16[128,1536]{1,0:T(8,128)(2,1)S(1)}, bf16[128,1536]{1,0:T(8,128)(2,1)}, u32[]{:S(2)}) copy-start(bf16[128,1536]{1,0:T(8,128)(2,1)} %param.19) | copy-start | bytes 1179652
  7.2 189.5 %all-gather.3.cloned.1.call-start = ((), (), s32[]{:S(2)}) async-start(), calls=%async_computation | async-start | bytes 12976128 | tf_op jit(solution)/shard_map/all_gather | solution.py:807
  8.0 556.2 %all-reduce.4.cloned.1.call-start = ((), (), s32[]{:S(2)}) async-start(), calls=%async_computation.1 | async-start | bytes 2359296 | tf_op jit(solution)/shard_map/psum | solution.py:1082
  10.1 58.6 %copy-start.58 = (f32[1536]{0:T(1024)}, f32[1536]{0:T(1024)S(1)}, u32[]{:S(2)}) copy-start(f32[1536]{0:T(1024)S(1)} %convert_element_type.137) | copy-start | bytes 18436
  47.3 18.2 %copy-start.72 = (f32[128]{0:T(128)}, f32[128]{0:T(128)S(1)}, u32[]{:S(2)}) copy-start(f32[128]{0:T(128)S(1)} %get-tuple-element.104) | copy-start | bytes 1540
  75.7 23.6 %copy-start.47 = (bf16[2,64,3,512]{3,1,2,0:T(8,128)(2,1)}, bf16[2,64,3,512]{3,1,2,0:T(8,128)(2,1)S(1)}, u32[]{:S(2)}) copy-start(bf16[2,64,3,512]{3,1,2,0:T(8,128)(2,1)S(1)} %fusion.10) | copy-start | bytes 1179652
  75.7 23.4 %copy-start.15 = (bf16[128,1536]{1,0:T(8,128)(2,1)S(1)}, bf16[128,1536]{1,0:T(8,128)(2,1)}, u32[]{:S(2)}) copy-start(bf16[128,1536]{1,0:T(8,128)(2,1)} %param.16) | copy-start | bytes 1179652
  99.9 76.0 %copy-start.70 = (f32[128]{0:T(128)}, f32[128]{0:T(128)S(1)}, u32[]{:S(2)}) copy-start(f32[128]{0:T(128)S(1)} %get-tuple-element.106) | copy-start | bytes 1540
  101.0 74.9 %copy-start.17 = (bf16[128,1536]{1,0:T(8,128)(2,1)S(1)}, bf16[128,1536]{1,0:T(8,128)(2,1)}, u32[]{:S(2)}) copy-start(bf16[128,1536]{1,0:T(8,128)(2,1)} %multiply_convert_fusion.2.own) | copy-start | bytes 1179652
  101.0 74.9 %copy-start.45 = (bf16[16,1536]{1,0:T(8,128)(2,1)S(1)}, bf16[16,1536]{1,0:T(8,128)(2,1)}, u32[]{:S(2)}) copy-start(bf16[16,1536]{1,0:T(8,128)(2,1)} %param.23) | copy-start | bytes 147460
  176.1 9.2 %copy-start.61 = (pred[128,16]{0,1:T(8,128)(4,1)}, pred[128,16]{0,1:T(8,128)(4,1)S(1)}, u32[]{:S(2)}) copy-start(pred[128,16]{0,1:T(8,128)(4,1)S(1)} %get-tuple-element.69) | copy-start | bytes 6148
  176.2 9.2 %copy-start.67 = (f32[128]{0:T(128)}, f32[128]{0:T(128)S(1)}, u32[]{:S(2)}) copy-start(f32[128]{0:T(128)S(1)} %get-tuple-element.68) | copy-start | bytes 1540
  177.3 8.2 %copy-start.36 = (bf16[2,1536,128]{2,1,0:T(8,128)(2,1)S(1)}, bf16[2,1536,128]{2,1,0:T(8,128)(2,1)}, u32[]{:S(2)}) copy-start(bf16[2,1536,128]{2,1,0:T(8,128)(2,1)} %param.24) | copy-start | bytes 2359300
  177.3 8.3 %copy-start.37 = (bf16[2,1536,128]{2,1,0:T(8,128)(2,1)S(1)}, bf16[2,1536,128]{2,1,0:T(8,128)(2,1)}, u32[]{:S(2)}) copy-start(bf16[2,1536,128]{2,1,0:T(8,128)(2,1)} %param.25) | copy-start | bytes 2359300
  196.8 7.2 %copy-start.6 = (f32[4096,256]{0,1:T(8,128)S(1)}, f32[4096,256]{0,1:T(8,128)}, u32[]{:S(2)}) copy-start(f32[4096,256]{0,1:T(8,128)} %fusion.27) | copy-start | bytes 12582916
  218.7 7.7 %copy-start.11 = (bf16[4096,256]{0,1:T(8,128)(2,1)S(1)}, bf16[4096,256]{0,1:T(8,128)(2,1)}, u32[]{:S(2)}) copy-start(bf16[4096,256]{0,1:T(8,128)(2,1)} %get-tuple-element.79) | copy-start | bytes 6291460
  218.7 7.7 %copy-start.26 = (bf16[1536,128]{1,0:T(8,128)(2,1)S(1)}, bf16[1536,128]{1,0:T(8,128)(2,1)}, u32[]{:S(2)}) copy-start(bf16[1536,128]{1,0:T(8,128)(2,1)} %copy-done.25) | copy-start | bytes 1179652
  218.7 7.7 %copy-start.28 = (bf16[1536,128]{1,0:T(8,128)(2,1)S(1)}, bf16[1536,128]{1,0:T(8,128)(2,1)}, u32[]{:S(2)}) copy-start(bf16[1536,128]{1,0:T(8,128)(2,1)} %copy-done.27) | copy-start | bytes 1179652
  226.4 11.0 %copy-start.7 = (bf16[4096,256]{0,1:T(8,128)(2,1)S(1)}, bf16[4096,256]{0,1:T(8,128)(2,1)}, u32[]{:S(2)}) copy-start(bf16[4096,256]{0,1:T(8,128)(2,1)} %get-tuple-element.80) | copy-start | bytes 6291460
  252.4 145.8 %copy-start.62 = (pred[128,16]{0,1:T(8,128)(4,1)S(1)}, pred[128,16]{0,1:T(8,128)(4,1)}, u32[]{:S(2)}) copy-start(pred[128,16]{0,1:T(8,128)(4,1)} %copy-done.61) | copy-start | bytes 6148
  252.4 145.8 %copy-start.68 = (f32[128]{0:T(128)S(1)}, f32[128]{0:T(128)}, u32[]{:S(2)}) copy-start(f32[128]{0:T(128)} %copy-done.67) | copy-start | bytes 1540
  252.4 145.8 %copy-start.69 = (f32[128]{0:T(128)S(1)}, f32[128]{0:T(128)}, u32[]{:S(2)}) copy-start(f32[128]{0:T(128)} %fusion.36) | copy-start | bytes 1540
  252.4 145.8 %copy-start.18 = (bf16[128,1536]{1,0:T(8,128)(2,1)S(1)}, bf16[128,1536]{1,0:T(8,128)(2,1)}, u32[]{:S(2)}) copy-start(bf16[128,1536]{1,0:T(8,128)(2,1)} %multiply_convert_fusion.2.own) | copy-start | bytes 1179652
  252.4 146.7 %copy-start.10 = (f32[128,1536]{1,0:T(8,128)S(1)}, f32[128,1536]{1,0:T(8,128)}, u32[]{:S(2)}) copy-start(f32[128,1536]{1,0:T(8,128)} %copy-done.9) | copy-start | bytes 2359300
  252.4 146.7 %copy-start.46 = (bf16[16,1536]{1,0:T(8,128)(2,1)S(1)}, bf16[16,1536]{1,0:T(8,128)(2,1)}, u32[]{:S(2)}) copy-start(bf16[16,1536]{1,0:T(8,128)(2,1)} %param.23) | copy-start | bytes 147460
  252.4 146.7 %copy-start.71 = (f32[128]{0:T(128)S(1)}, f32[128]{0:T(128)}, u32[]{:S(2)}) copy-start(f32[128]{0:T(128)} %copy-done.70) | copy-start | bytes 1540
  252.5 149.2 %copy-start.74 = (f32[128]{0:T(128)S(1)}, f32[128]{0:T(128)}, u32[]{:S(2)}) copy-start(f32[128]{0:T(128)} %get-tuple-element.105) | copy-start | bytes 1540
  397.3 4.3 copy-start.29
  401.6 16.2 %copy-start.34 = (bf16[384,1536]{1,0:T(8,128)(2,1)S(1)}, bf16[384,1536]{1,0:T(8,128)(2,1)}, u32[]{:S(2)}) copy-start(bf16[384,1536]{1,0:T(8,128)(2,1)} %param.21) | copy-start | bytes 3538948
  420.9 6.7 %slice-start.3 = ((s8[6291456]{0:T(1024)(128)(4,1)}), s8[2097152]{0:T(1024)(128)(4,1)S(1)}, s32[]{:S(2)}) async-start(s8[6291456]{0:T(1024)(128)(4,1)} %bitcast.196), calls=%async_computation.5 | async-start | bytes 4194304
  422.7 4.9 slice-start.4
  422.7 4.9 copy-start.43
  422.7 4.9 copy-start.52
  432.0 15.7 %slice-start = ((s8[12582912]{0:T(1024)(128)(4,1)}), s8[4194304]{0:T(1024)(128)(4,1)S(1)}, s32[]{:S(2)}) async-start(s8[12582912]{0:T(1024)(128)(4,1)} %bitcast.190), calls=%async_computation.2 | async-start | bytes 8388608
  432.0 15.7 %slice-start.1 = ((s8[12582912]{0:T(1024)(128)(4,1)}), s8[4194304]{0:T(1024)(128)(4,1)S(1)}, s32[]{:S(2)}) async-start(s8[12582912]{0:T(1024)(128)(4,1)} %bitcast.190), calls=%async_computation.3 | async-start | bytes 8388608
  442.6 5.2 slice-start.2
  447.8 4.6 copy-start.12
  452.4 4.8 copy-start.64
  452.4 4.9 copy-start.44
  462.5 82.8 %copy-start.16 = (bf16[128,1536]{1,0:T(8,128)(2,1)S(1)}, bf16[128,1536]{1,0:T(8,128)(2,1)}, u32[]{:S(2)}) copy-start(bf16[128,1536]{1,0:T(8,128)(2,1)} %param.16) | copy-start | bytes 1179652
  462.5 82.8 %copy-start.59 = (f32[1536]{0:T(1024)S(1)}, f32[1536]{0:T(1024)}, u32[]{:S(2)}) copy-start(f32[1536]{0:T(1024)} %copy-done.58) | copy-start | bytes 18436
  462.5 84.1 %copy-start.19 = (f32[128,1536]{1,0:T(8,128)S(1)}, f32[128,1536]{1,0:T(8,128)}, u32[]{:S(2)}) copy-start(f32[128,1536]{1,0:T(8,128)} %get-tuple-element.67) | copy-start | bytes 2359300
  462.5 84.2 %copy-start.73 = (f32[128]{0:T(128)S(1)}, f32[128]{0:T(128)}, u32[]{:S(2)}) copy-start(f32[128]{0:T(128)} %copy-done.72) | copy-start | bytes 1540
  462.5 84.2 %copy-start.75 = (f32[128]{0:T(128)S(1)}, f32[128]{0:T(128)}, u32[]{:S(2)}) copy-start(f32[128]{0:T(128)} %get-tuple-element.103) | copy-start | bytes 1540
  549.7 6.9 %copy-start.14 = (bf16[4096,256]{0,1:T(8,128)(2,1)S(1)}, bf16[4096,256]{0,1:T(8,128)(2,1)}, u32[]{:S(2)}) copy-start(bf16[4096,256]{0,1:T(8,128)(2,1)} %get-tuple-element.78) | copy-start | bytes 6291460
  (35 other events, 88.0 us)
Sparse Core Ops, SparseCore 0:
  10.9 135.0 all-gather.2
  457.4 106.2 all-reduce.3

commit v4 on v3

--- a/solution.py
+++ b/solution.py
@@ -227,219 +227,54 @@
     lax.fori_loop(0, target.shape[0] // 16, tile, 0)
 
 
-def total_kernel(
-    ep_size,
-    first_in,
-    second_in,
-    small_in,
-    first_out,
-    second_out,
-    small_out,
-    parts,
-    core_got,
-    pair_got,
-    last_got,
-    z_got,
-    small_got,
-    load_sems,
-    core_sems,
-    pair_sems,
-    last_sems,
-    z_sems,
-    small_sems,
-    own_sem,
+def front_gather_kernel(
+    ep_size, pieces, own, table, out, tables, own_sem, sems, table_own_sem, table_sems
 ):
     me = Place(ep_size)
-    depth = me.depth
-    others = all_others(ep_size)
-    meet(others)
-    small = []
-    my_place = lax.axis_index("ep") * 4 + lax.axis_index("tp")
-    for k, device in enumerate(others):
-        small.append(
-            send(
-                small_in.at[device[0] * 4 + device[1]],
-                small_got.at[my_place],
-                small_sems.at[0, k],
-                small_sems.at[1, k],
-                device,
-            )
-        )
-    own_small = pltpu.make_async_copy(small_in.at[my_place], small_got.at[my_place], own_sem)
-    own_small.start()
-
-    def load(step, which):
-        source = (first_in, second_in)[which]
-        slot = lax.rem(step, 2)
-        return pltpu.make_async_copy(
-            source.at[me.after(step + 1)], parts.at[slot, which], load_sems.at[slot, which]
-        )
-
-    def core_copy(step):
-        return pltpu.make_async_remote_copy(
-            src_ref=parts.at[lax.rem(step, 2), :, :, :, 1 - me.c],
-            dst_ref=core_got.at[step],
-            send_sem=core_sems.at[0, step],
-            recv_sem=core_sems.at[1, step],
-            device_id=me.sibling(),
-            device_id_type=MESH,
-        )
-
-    def pair_copy(step, which):
-        source = (core_got.at[step, 0, :, 1 - me.x], core_got.at[step, 1, 1 - me.y])[which]
-        return pltpu.make_async_remote_copy(
-            src_ref=source,
-            dst_ref=pair_got.at[step, which],
-            send_sem=pair_sems.at[0, step, which],
-            recv_sem=pair_sems.at[1, step, which],
-            device_id=(me.x_peer(), me.y_peer())[which],
-            device_id_type=MESH,
-        )
-
-    def last_copy(step, which):
-        return pltpu.make_async_remote_copy(
-            src_ref=pair_got.at[step, which, (1 - me.y, 1 - me.x)[which]],
-            dst_ref=last_got.at[step, which],
-            send_sem=last_sems.at[0, step, which],
-            recv_sem=last_sems.at[1, step, which],
-            device_id=(me.y_peer(), me.x_peer())[which],
-            device_id_type=MESH,
-        )
-
-    def z_copy(step):
-        return pltpu.make_async_remote_copy(
-            src_ref=last_got.at[step],
-            dst_ref=z_got.at[step],
-            send_sem=z_sems.at[0, step],
-            recv_sem=z_sems.at[1, step],
-            device_id=me.device(z=me.after(step + 1)),
-            device_id_type=MESH,
-        )
-
-    def turn(i, carry):
-        @pl.when(i < depth)
-        def _():
-            for which in range(2):
-                load(i, which).start()
-            for which in range(2):
-                load(i, which).wait()
-            core_copy(i).start()
-
-        @pl.when((i >= 1) & (i <= depth))
-        def _():
-            step = i - 1
-            core_copy(step).wait_recv()
-            for y in range(2):
-                for x in range(2):
-                    for which in range(2):
-                        add_into(
-                            core_got.at[step, which, y, x],
-                            parts.at[lax.rem(step, 2), which, y, x, me.c],
-                        )
-            for which in range(2):
-                pair_copy(step, which).start()
-            core_copy(step).wait_send()
-
-        @pl.when((i >= 2) & (i <= depth + 1))
-        def _():
-            step = i - 2
-            for which in range(2):
-                pair_copy(step, which).wait_recv()
-                for k in range(2):
-                    mine = (core_got.at[step, 0, k, me.x], core_got.at[step, 1, me.y, k])[which]
-                    add_into(pair_got.at[step, which, k], mine)
-                last_copy(step, which).start()
-
-        @pl.when(i >= 3)
-        def _():
-            step = i - 3
-            for which in range(2):
-                last_copy(step, which).wait_recv()
-                add_into(last_got.at[step, which], pair_got.at[step, which, (me.y, me.x)[which]])
-
-            @pl.when(step < depth - 1)
-            def _():
-                z_copy(step).start()
-
-        return carry
-
-    lax.fori_loop(0, depth + 3, turn, 0)
-    for step in range(depth - 1):
-        z_copy(step).wait_recv()
-
-    def finish(which, target):
-        def tile(i, carry):
-            at = pl.ds(pl.multiple_of(i * 16, 16), 16)
-            total = last_got[depth - 1, which, at, :].astype(jnp.float32)
-            for step in range(depth - 1):
-                total = total + z_got[step, which, at, :].astype(jnp.float32)
-            target[at, :] = total
-            return carry
-
-        lax.fori_loop(0, target.shape[0] // 16, tile, 0)
-
-    finish(0, first_out)
-    finish(1, second_out)
-    own_small.wait()
-    for copy in small:
+    mine = lax.axis_index("ep")
+    tp = lax.axis_index("tp")
+    peers = [(lax.rem(mine + k, ep_size), tp) for k in range(1, ep_size)]
+    meet([me.sibling(), me.x_peer()] + peers)
+    local = pltpu.make_async_copy(table, tables.at[mine], table_own_sem)
+    local.start()
+    copies = [
+        send(table, tables.at[mine], table_sems.at[0, k], table_sems.at[1, k], device)
+        for k, device in enumerate(peers)
+    ]
+    group_gather_body(me, pieces, own, out, own_sem, sems)
+    local.wait()
+    for copy in copies:
         copy.wait()
-    for ep in range(ep_size):
-        total = small_got[ep * 4]
-        for tp in range(1, 4):
-            total = total + small_got[ep * 4 + tp]
-        small_out[ep] = total
-    for step in range(depth):
-        for which in range(2):
-            pair_copy(step, which).wait_send()
-            last_copy(step, which).wait_send()
-        if step < depth - 1:
-            z_copy(step).wait_send()
-
-
-def totals_by_links(first, second, small, ep_size):
-    total_rows, width = first.shape
-    depth = ep_size // 2
-    rows = total_rows // (4 * ep_size)
-    whole = (depth, 2, 2, 2, rows, width)
-    bf16, f32 = jnp.bfloat16, jnp.float32
+
+
+def front_gather(value_rows, table, ep_size):
+    rows, width = value_rows.shape
+    pieces = 4
     dma = pltpu.SemaphoreType.DMA
-    vmem = pl.BlockSpec(memory_space=pltpu.VMEM)
     anywhere = pl.BlockSpec(memory_space=pl.ANY)
-    return pl.pallas_call(
-        functools.partial(total_kernel, ep_size),
+    every, tables = pl.pallas_call(
+        functools.partial(front_gather_kernel, ep_size, pieces),
         out_shape=(
-            jax.ShapeDtypeStruct((rows, width), f32),
-            jax.ShapeDtypeStruct((rows, width), f32),
-            jax.ShapeDtypeStruct((ep_size,) + small.shape[1:], f32),
+            jax.ShapeDtypeStruct((2, 2, rows, width), value_rows.dtype),
+            jax.ShapeDtypeStruct((ep_size,) + table.shape, table.dtype),
         ),
-        in_specs=[anywhere, anywhere, vmem],
-        out_specs=(vmem, vmem, vmem),
-        scratch_shapes=[
-            pltpu.VMEM((2, 2, 2, 2, 2, rows, width), bf16),
-            pltpu.VMEM((depth, 2, 2, 2, rows, width), bf16),
-            pltpu.VMEM((depth, 2, 2, rows, width), bf16),
-            pltpu.VMEM((depth, 2, rows, width), bf16),
-            pltpu.VMEM((depth - 1, 2, rows, width), bf16),
-            pltpu.VMEM(small.shape, f32),
-            dma((2, 2)),
-            dma((2, depth)),
-            dma((2, depth, 2)),
-            dma((2, depth, 2)),
-            dma((2, depth - 1)),
-            dma((2, 4 * ep_size - 1)),
-            dma,
-        ],
-        compiler_params=pltpu.CompilerParams(
-            collective_id=2, has_side_effects=True, vmem_limit_bytes=56 * 1024 * 1024
-        ),
-        name="totals_by_links",
-    )(first.reshape(whole), second.reshape(whole), small)
+        in_specs=[anywhere] * 2,
+        out_specs=(anywhere,) * 2,
+        scratch_shapes=[dma, dma((2, 3 * pieces)), dma, dma((2, ep_size - 1))],
+        compiler_params=pltpu.CompilerParams(collective_id=6, has_side_effects=True),
+        name="front_gather",
+    )(value_rows, table)
+    return every.reshape(-1, width), tables
 
 
 def group_gather_kernel(ep_size, pieces, own, out, own_sem, sems):
     me = Place(ep_size)
+    meet([me.sibling(), me.x_peer()])
+    group_gather_body(me, pieces, own, out, own_sem, sems)
+
+
+def group_gather_body(me, pieces, own, out, own_sem, sems):
     size = own.shape[0] // pieces
-    meet([me.sibling(), me.x_peer()])
     started = []
     local = pltpu.make_async_copy(own, out.at[me.x, me.c], own_sem)
     local.start()
@@ -572,6 +407,360 @@
     return [
         (lax.rem(ep + k // 4, ep_size), lax.rem(tp + k % 4, 4)) for k in range(1, ep_size * 4)
     ]
+
+
+def experts_kernel(
+    ep_size,
+    per_owner,
+    rows_in,
+    cots_in,
+    code_in,
+    router,
+    enter,
+    leave,
+    grad_out,
+    sum_out,
+    small_out,
+    gate_out,
+    up_out,
+    down_out,
+    rows_buf,
+    cots_buf,
+    weighted,
+    turned,
+    enter_sum,
+    parts,
+    core_got,
+    pair_got,
+    last_got,
+    z_got,
+    small_in,
+    small_got,
+    load_sems,
+    core_sems,
+    pair_sems,
+    last_sems,
+    z_sems,
+    small_sems,
+    own_sem,
+):
+    me = Place(ep_size)
+    depth = me.depth
+    blocks = 2 * depth
+    width = router.shape[1]
+    tokens = rows_buf.shape[1]
+    share = tokens // 4
+    units = leave.shape[0] // per_owner
+    hidden = per_owner * units
+    f32, bf16 = jnp.float32, jnp.bfloat16
+    others = all_others(ep_size)
+    meet(others)
+    my_place = lax.axis_index("ep") * 4 + lax.axis_index("tp")
+
+    def where(b):
+        return me.after(b // 2 + 1), lax.rem(1 - me.y + b % 2, 2)
+
+    def load(b, which):
+        z, y = where(b)
+        source, target = ((rows_in, rows_buf), (cots_in, cots_buf))[which]
+        slot = lax.rem(b, 2)
+        return pltpu.make_async_copy(
+            source.at[z, y], target.at[slot], load_sems.at[slot, which]
+        )
+
+    def core_copy(b):
+        y = where(b)[1]
+        return pltpu.make_async_remote_copy(
+            src_ref=parts.at[lax.rem(b, 2), :, :, 1 - me.c],
+            dst_ref=core_got.at[b // 2, y],
+            send_sem=core_sems.at[0, b],
+            recv_sem=core_sems.at[1, b],
+            device_id=me.sibling(),
+            device_id_type=MESH,
+        )
+
+    def grad_pair(b):
+        y = where(b)[1]
+        return pltpu.make_async_remote_copy(
+            src_ref=core_got.at[b // 2, y, 0, 1 - me.x],
+            dst_ref=pair_got.at[b // 2, 0, y],
+            send_sem=pair_sems.at[0, b],
+            recv_sem=pair_sems.at[1, b],
+            device_id=me.x_peer(),
+            device_id_type=MESH,
+        )
+
+    def sum_pair(step):
+        return pltpu.make_async_remote_copy(
+            src_ref=core_got.at[step, 1 - me.y, 1],
+            dst_ref=pair_got.at[step, 1],
+            send_sem=pair_sems.at[0, blocks + step],
+            recv_sem=pair_sems.at[1, blocks + step],
+            device_id=me.y_peer(),
+            device_id_type=MESH,
+        )
+
+    def last_copy(step, which):
+        return pltpu.make_async_remote_copy(
+            src_ref=pair_got.at[step, which, (1 - me.y, 1 - me.x)[which]],
+            dst_ref=last_got.at[step, which],
+            send_sem=last_sems.at[0, step, which],
+            recv_sem=last_sems.at[1, step, which],
+            device_id=(me.y_peer(), me.x_peer())[which],
+            device_id_type=MESH,
+        )
+
+    def z_copy(step):
+        return pltpu.make_async_remote_copy(
+            src_ref=last_got.at[step],
+            dst_ref=z_got.at[step],
+            send_sem=z_sems.at[0, step],
+            recv_sem=z_sems.at[1, step],
+            device_id=me.device(z=me.after(step + 1)),
+            device_id_type=MESH,
+        )
+
+    def small_copy(k, device):
+        return pltpu.make_async_remote_copy(
+            src_ref=small_in.at[device[0] * 4 + device[1]],
+            dst_ref=small_got.at[my_place],
+            send_sem=small_sems.at[0, k],
+            recv_sem=small_sems.at[1, k],
+            device_id=device,
+            device_id_type=MESH,
+        )
+
+    def dot(a, b, contract):
+        return lax.dot_general(
+            a, b, ((contract[:1], contract[1:]), ((), ())), preferred_element_type=f32
+        )
+
+    def spread(columns):
+        return jnp.concatenate(
+            [jnp.broadcast_to(columns[:, e : e + 1], (tokens, units)) for e in range(per_owner)],
+            axis=1,
+        )
+
+    def compute(b):
+        z, y = where(b)
+        slot = lax.rem(b, 2)
+        rows, cots = rows_buf[slot], cots_buf[slot]
+        code = code_in[pl.ds(pl.multiple_of((z * 2 + y) * tokens, tokens), tokens), :].astype(f32)
+        used = code >= 0.0
+        logits = jnp.where(used, dot(rows, router[...], (1, 1)), -1e30)
+        top = jnp.max(logits, axis=1, keepdims=True)
+        powers = jnp.where(used, jnp.exp(logits - top), 0.0)
+        kept = jnp.where(code == 0.0, 1.0, 0.0)
+        gates = spread(kept * powers / jnp.sum(powers, axis=1, keepdims=True))
+        act = dot(rows, enter[...], (1, 0))
+        gate_act, up_act = act[:, :hidden], act[:, hidden:]
+        back_act = dot(cots, leave[...], (1, 1))
+        sigma = jax.nn.sigmoid(gate_act)
+        swish = gate_act * sigma
+        value = swish * up_act
+        gate_parts = spread(kept) * (value * back_act)
+        lane = lax.broadcasted_iota(jnp.int32, (8, hidden), 1)
+        pick = lax.broadcasted_iota(jnp.int32, (8, hidden), 0)
+        mine = jnp.where((lane >= pick * units) & (lane < (pick + 1) * units), 1.0, 0.0)
+        grad_gates = lax.dot_general(
+            mine,
+            gate_parts,
+            (((1,), (1,)), ((), ())),
+            precision=EXACT_PRECISION,
+            preferred_element_type=f32,
+        )
+        for k in range(4):
+            small_in[(z * 2 + y) * 4 + k] = grad_gates[:, k * share : (k + 1) * share]
+        weighted[...] = (gates * value).astype(bf16)
+        grad_hidden = gates * back_act
+        turned[:, :hidden] = (
+            grad_hidden * up_act * sigma * (1.0 + gate_act * (1.0 - sigma))
+        ).astype(bf16)
+        turned[:, hidden:] = (grad_hidden * swish).astype(bf16)
+        tile = 512
+        for n in range(width // tile):
+            cols = slice(n * tile, (n + 1) * tile)
+            grads = dot(turned[...], enter[cols, :], (1, 1)).astype(bf16)
+            sums = dot(weighted[...], leave[:, cols], (1, 0)).astype(bf16)
+            for x in range(2):
+                for c in range(2):
+                    at = slice((x * 2 + c) * share, (x * 2 + c + 1) * share)
+                    parts[slot, 0, x, c, :, cols] = grads[at]
+                    parts[slot, 1, x, c, :, cols] = sums[at]
+
+    def weight_sums(b):
+        slot = lax.rem(b, 2)
+        tile = 512
+        for n in range(width // tile):
+            cols = slice(n * tile, (n + 1) * tile)
+            enter_sum[:, cols] += dot(turned[...], rows_buf[slot, :, cols], (0, 0))
+            down_out[:, cols] += dot(weighted[...], cots_buf[slot, :, cols], (0, 0))
+
+    enter_sum[...] = jnp.zeros_like(enter_sum)
+    down_out[...] = jnp.zeros_like(down_out)
+    for which in range(2):
+        load(0, which).start()
+
+    def turn(b, carry):
+        @pl.when(b < blocks)
+        def _():
+            for which in range(2):
+                load(b, which).wait()
+
+            @pl.when(b + 1 < blocks)
+            def _():
+                for which in range(2):
+                    load(b + 1, which).start()
+
+            compute(b)
+            core_copy(b).start()
+            weight_sums(b)
+
+        @pl.when((b >= 1) & (b <= blocks))
+        def _():
+            j = b - 1
+            y = where(j)[1]
+            core_copy(j).wait_recv()
+            for which in range(2):
+                for x in range(2):
+                    add_into(
+                        core_got.at[j // 2, y, which, x],
+                        parts.at[lax.rem(j, 2), which, x, me.c],
+                    )
+            grad_pair(j).start()
+
+            @pl.when(j % 2 == 0)
+            def _():
+                sum_pair(j // 2).start()
+
+            core_copy(j).wait_send()
+
+        @pl.when((b >= 2) & (b <= blocks + 1))
+        def _():
+            j = b - 2
+            y = where(j)[1]
+            step = j // 2
+            grad_pair(j).wait_recv()
+            add_into(pair_got.at[step, 0, y], core_got.at[step, y, 0, me.x])
+
+            @pl.when(j % 2 == 0)
+            def _():
+                last_copy(step, 0).start()
+                sum_pair(step).wait_recv()
+                for x in range(2):
+                    add_into(pair_got.at[step, 1, x], core_got.at[step, me.y, 1, x])
+                last_copy(step, 1).start()
+
+        @pl.when((b >= 4) & (b % 2 == 0))
+        def _():
+            step = (b - 4) // 2
+            for which in range(2):
+                last_copy(step, which).wait_recv()
+                add_into(last_got.at[step, which], pair_got.at[step, which, (me.y, me.x)[which]])
+
+            @pl.when(step < depth - 1)
+            def _():
+                z_copy(step).start()
+
+        @pl.when(b == blocks)
+        def _():
+            for k, device in enumerate(others):
+                small_copy(k, device).start()
+            pltpu.make_async_copy(
+                small_in.at[my_place], small_got.at[my_place], own_sem
+            ).start()
+            for e in range(per_owner):
+                gate_out[e] = enter_sum[e * units : (e + 1) * units, :].T
+                up_out[e] = enter_sum[hidden + e * units : hidden + (e + 1) * units, :].T
+
+        return carry
+
+    lax.fori_loop(0, blocks + 3, turn, 0)
+    pltpu.make_async_copy(small_in.at[my_place], small_got.at[my_place], own_sem).wait()
+    for k, device in enumerate(others):
+        small_copy(k, device).wait()
+    for ep in range(ep_size):
+        total = small_got[ep * 4]
+        for tp in range(1, 4):
+            total = total + small_got[ep * 4 + tp]
+        small_out[ep] = total
+    for step in range(depth - 1):
+        z_copy(step).wait_recv()
+
+    def finish(which, target):
+        def tile(i, carry):
+            at = pl.ds(pl.multiple_of(i * 16, 16), 16)
+            total = last_got[depth - 1, which, at, :].astype(f32)
+            for step in range(depth - 1):
+                total = total + z_got[step, which, at, :].astype(f32)
+            target[at, :] = total
+            return carry
+
+        lax.fori_loop(0, target.shape[0] // 16, tile, 0)
+
+    finish(0, grad_out)
+    finish(1, sum_out)
+    for step in range(depth):
+        grad_pair(2 * step).wait_send()
+        grad_pair(2 * step + 1).wait_send()
+        sum_pair(step).wait_send()
+        for which in range(2):
+            last_copy(step, which).wait_send()
+        if step < depth - 1:
+            z_copy(step).wait_send()
+
+
+def experts_by_links(rows_all, cots_all, code, router, enter, leave, per_owner, ep_size):
+    total_rows, width = rows_all.shape
+    depth = ep_size // 2
+    tokens = total_rows // ep_size
+    rows = tokens // 4
+    hidden = leave.shape[0]
+    units = hidden // per_owner
+    bf16, f32 = jnp.bfloat16, jnp.float32
+    dma = pltpu.SemaphoreType.DMA
+    vmem = pl.BlockSpec(memory_space=pltpu.VMEM)
+    anywhere = pl.BlockSpec(memory_space=pl.ANY)
+    places = 4 * ep_size
+    blocks = (depth, 2, tokens, width)
+    return pl.pallas_call(
+        functools.partial(experts_kernel, ep_size, per_owner),
+        out_shape=(
+            jax.ShapeDtypeStruct((rows, width), f32),
+            jax.ShapeDtypeStruct((rows, width), f32),
+            jax.ShapeDtypeStruct((ep_size, 8, rows), f32),
+            jax.ShapeDtypeStruct((per_owner, width, units), f32),
+            jax.ShapeDtypeStruct((per_owner, width, units), f32),
+            jax.ShapeDtypeStruct((hidden, width), f32),
+        ),
+        in_specs=[anywhere, anywhere, vmem, vmem, vmem, vmem],
+        out_specs=(vmem,) * 6,
+        scratch_shapes=[
+            pltpu.VMEM((2, tokens, width), bf16),
+            pltpu.VMEM((2, tokens, width), bf16),
+            pltpu.VMEM((tokens, hidden), bf16),
+            pltpu.VMEM((tokens, 2 * hidden), bf16),
+            pltpu.VMEM((2 * hidden, width), f32),
+            pltpu.VMEM((2, 2, 2, 2, rows, width), bf16),
+            pltpu.VMEM((depth, 2, 2, 2, rows, width), bf16),
+            pltpu.VMEM((depth, 2, 2, rows, width), bf16),
+            pltpu.VMEM((depth, 2, rows, width), bf16),
+            pltpu.VMEM((depth - 1, 2, rows, width), bf16),
+            pltpu.VMEM((places, 8, rows), f32),
+            pltpu.VMEM((places, 8, rows), f32),
+            dma((2, 2)),
+            dma((2, 2 * depth)),
+            dma((2, 3 * depth)),
+            dma((2, depth, 2)),
+            dma((2, depth - 1)),
+            dma((2, places - 1)),
+            dma,
+        ],
+        compiler_params=pltpu.CompilerParams(
+            collective_id=2, has_side_effects=True, vmem_limit_bytes=60 * 1024 * 1024
+        ),
+        name="experts_by_links",
+    )(rows_all.reshape(blocks), cots_all.reshape(blocks), code, router, enter, leave)
 
 
 def tail_kernel(
@@ -807,29 +996,6 @@
     return lax.all_gather(value_rows, ("ep", "tp"), axis=0, tiled=True)
 
 
-def totals(first, second, small, by_links):
-    ep_size, tp_size = lax.axis_size("ep"), lax.axis_size("tp")
-    if by_links:
-        rows = small.shape[1] // (ep_size * tp_size)
-        blocks = small.reshape(small.shape[0], ep_size * tp_size, rows).swapaxes(0, 1)
-        blocks = jnp.pad(blocks, ((0, 0), (0, -small.shape[0] % 8), (0, 0)))
-        first, second, got = totals_by_links(first, second, blocks, ep_size)
-        return first, second, got[:, : small.shape[0]].reshape(-1, rows).T
-
-    def scatter(value_rows):
-        return lax.psum_scatter(value_rows, ("ep", "tp"), scatter_dimension=0, tiled=True)
-
-    columns = jnp.zeros((small.shape[1], small.shape[0] * ep_size), jnp.float32)
-    columns = lax.dynamic_update_slice_in_dim(
-        columns, small.T, lax.axis_index("ep") * small.shape[0], 1
-    )
-    return (
-        scatter(first).astype(jnp.float32),
-        scatter(second).astype(jnp.float32),
-        scatter(columns),
-    )
-
-
 LAST = 1 << 30
 
 
@@ -854,9 +1020,90 @@
 
 
 def masked_softmax(logits, used):
-    top = jnp.max(jnp.where(used, logits, -jnp.inf), axis=-1, keepdims=True)
+    top = jnp.max(jnp.where(used, logits, -1e30), axis=-1, keepdims=True)
     powers = jnp.where(used, jnp.exp(logits - top), 0.0)
     return powers / jnp.sum(powers, axis=-1, keepdims=True)
+
+
+def pair_codes(order_all, per_owner):
+    expert_count = order_all.shape[1]
+    first = lax.axis_index("ep") * per_owner
+    turned = jnp.roll(order_all, -first, axis=1)
+    kept = kept_pairs(turned[:, :per_owner])
+    dropped = jnp.pad(~kept, ((0, 0), (0, expert_count - per_owner), (0, 0)))
+    code = jnp.where(turned < LAST, dropped.astype(jnp.float32), -1.0)
+    code = code.swapaxes(1, 2).reshape(-1, expert_count)
+    lanes = -expert_count % 128
+    return jnp.pad(code, ((0, 0), (0, lanes)), constant_values=-1.0).astype(jnp.bfloat16)
+
+
+def run_experts(rows_all, cots_all, code, w_router, w_gate, w_up, w_down, by_links):
+    per_owner, width, units = w_gate.shape
+    expert_count = w_router.shape[0]
+    ep_size, tp_size = lax.axis_size("ep"), lax.axis_size("tp")
+    hidden = per_owner * units
+    router = jnp.roll(w_router, -lax.axis_index("ep") * per_owner, axis=0)
+    router = jnp.pad(router, ((0, -expert_count % 128), (0, 0)))
+    enter = jnp.concatenate([w[e] for w in (w_gate, w_up) for e in range(per_owner)], axis=1)
+    leave = w_down.reshape(hidden, width)
+    if by_links:
+        grads, sums, small, gate, up, down = experts_by_links(
+            rows_all, cots_all, code, router, enter, leave, per_owner, ep_size
+        )
+        share = grads.shape[0]
+        return (
+            grads,
+            sums,
+            small[:, :per_owner].reshape(expert_count, share).T,
+            gate,
+            up,
+            down.reshape(w_down.shape),
+        )
+    used, kept = code >= 0, (code == 0).astype(jnp.float32)
+    logits = jnp.einsum("rd,ed->re", rows_all, router, preferred_element_type=jnp.float32)
+    gates = jnp.repeat((kept * masked_softmax(logits, used))[:, :per_owner], units, axis=1)
+    act = jnp.dot(rows_all, enter, preferred_element_type=jnp.float32)
+    gate_act, up_act = act[:, :hidden], act[:, hidden:]
+    back_act = jnp.einsum("rd,fd->rf", cots_all, leave, preferred_element_type=jnp.float32)
+    sigma = jax.nn.sigmoid(gate_act)
+    value = gate_act * sigma * up_act
+    weighted = (gates * value).astype(jnp.bfloat16)
+    grad_hidden = gates * back_act
+    turned = jnp.concatenate(
+        [
+            grad_hidden * up_act * sigma * (1.0 + gate_act * (1.0 - sigma)),
+            grad_hidden * gate_act * sigma,
+        ],
+        axis=1,
+    ).astype(jnp.bfloat16)
+    small = kept[:, :per_owner] * jnp.sum((value * back_act).reshape(-1, per_owner, units), axis=2)
+    grads = jnp.einsum("rf,df->rd", turned, enter, preferred_element_type=jnp.float32)
+    sums = jnp.dot(weighted, leave, preferred_element_type=jnp.float32)
+
+    def scatter(value_rows):
+        return lax.psum_scatter(value_rows, ("ep", "tp"), scatter_dimension=0, tiled=True)
+
+    columns = lax.dynamic_update_slice_in_dim(
+        jnp.zeros((small.shape[0], expert_count), jnp.float32),
+        small,
+        lax.axis_index("ep") * per_owner,
+        1,
+    )
+    both = jnp.einsum(
+        "rd,rwef->wedf",
+        rows_all,
+        turned.reshape(-1, 2, per_owner, units),
+        preferred_element_type=jnp.float32,
+    )
+    down = jnp.einsum("rf,rd->fd", weighted, cots_all, preferred_element_type=jnp.float32)
+    return (
+        scatter(grads.astype(jnp.bfloat16)).astype(jnp.float32),
+        scatter(sums.astype(jnp.bfloat16)).astype(jnp.float32),
+        scatter(columns),
+        both[0],
+        both[1],
+        down.reshape(w_down.shape),
+    )
 
 
 def visible_block(query_seg, query_pos, query_row, key_seg, key_pos, key_row):
@@ -964,15 +1211,18 @@
     block_rows = 512
     by_links = lax.axis_size("tp") == 4 and lax.axis_size("ep") == 8
     order = pair_order(expert_ids, slot_order, expert_count)
-    order_all = lax.all_gather(order, "ep")
     cot_all = gather_all(cotangent, False)
     inputs_own = hidden_in.astype(jnp.float32)
     gain_one = gain_attn.astype(jnp.float32)
     gain_two = gain_ffn.astype(jnp.float32)
     scale_one = norm_scale(inputs_own)
-    first_normalized = group_rows(
-        (inputs_own * scale_one * gain_one).astype(jnp.bfloat16), by_links, 6
-    )
+    first_own = (inputs_own * scale_one * gain_one).astype(jnp.bfloat16)
+    if by_links:
+        first_normalized, order_all = front_gather(first_own, order, lax.axis_size("ep"))
+    else:
+        first_normalized = group_rows(first_own, by_links, None)
+        order_all = lax.all_gather(order, "ep")
+    code = pair_codes(order_all, per_owner)
     cosine_lookup, sine_lookup = rope_tables(position, head_width)
     query_proj = jnp.einsum(
         "rd,fd->rf", first_normalized, w_query, preferred_element_type=jnp.float32
@@ -1006,66 +1256,14 @@
     scale_two = norm_scale(middle_own)
     normed_own = (middle_own * scale_two * gain_two).astype(jnp.bfloat16)
     normed_two = gather_all(normed_own, by_links)
-    first_expert = lax.axis_index("ep") * per_owner
     used = lax.dynamic_slice_in_dim(order, row_start, share, 1).T < LAST
     gates = masked_softmax(
         jnp.einsum("rd,ed->re", normed_own, w_router, preferred_element_type=jnp.float32), used
     )
-    kept_all = kept_pairs(
-        lax.dynamic_slice_in_dim(order_all, first_expert, per_owner, 1)
-    ).swapaxes(0, 1).reshape(per_owner, -1)
-    all_gates = masked_softmax(
-        jnp.einsum("rd,ed->re", normed_two, w_router, preferred_element_type=jnp.float32),
-        order_all.swapaxes(1, 2).reshape(-1, expert_count) < LAST,
-    )
-    gate_all = jnp.where(
-        kept_all.T, lax.dynamic_slice_in_dim(all_gates, first_expert, per_owner, 1), 0.0
-    )
-    units = w_gate.shape[2]
-    gate_in = jnp.concatenate([w_gate[e] for e in range(per_owner)], axis=1)
-    up_in = jnp.concatenate([w_up[e] for e in range(per_owner)], axis=1)
-    down_in = w_down.reshape(per_owner * units, model_width)
-    spread = jnp.repeat(gate_all, units, axis=1)
-    gate_act = jnp.dot(normed_two, gate_in, preferred_element_type=jnp.float32)
-    up_act = jnp.dot(normed_two, up_in, preferred_element_type=jnp.float32)
-    back_act = jnp.einsum("rd,fd->rf", cot_all, down_in, preferred_element_type=jnp.float32)
-    sigma = jax.nn.sigmoid(gate_act)
-    hidden = gate_act * sigma * up_act
-    weighted_hidden = (spread * hidden).astype(jnp.bfloat16)
-    grad_hidden = spread * back_act
-    grad_gate_act = (grad_hidden * up_act * sigma * (1.0 + gate_act * (1.0 - sigma))).astype(
-        jnp.bfloat16
-    )
-    grad_up_act = (grad_hidden * gate_act * sigma).astype(jnp.bfloat16)
-    grad_gates_part = jnp.where(
-        kept_all, jnp.sum((hidden * back_act).reshape(-1, per_owner, units), axis=2).T, 0.0
-    )
-    grad_rows = (
-        jnp.einsum("rf,df->rd", grad_gate_act, gate_in, preferred_element_type=jnp.float32)
-        + jnp.einsum("rf,df->rd", grad_up_act, up_in, preferred_element_type=jnp.float32)
-    ).astype(jnp.bfloat16)
-    combined = jnp.dot(weighted_hidden, down_in, preferred_element_type=jnp.float32).astype(
-        jnp.bfloat16
-    )
-    grad_normed_own, combined_own, grad_gates_own = totals(
-        grad_rows, combined, grad_gates_part, by_links
+    grad_normed_own, combined_own, grad_gates_own, grad_w_gate, grad_w_up, grad_w_down = (
+        run_experts(normed_two, cot_all, code, w_router, w_gate, w_up, w_down, by_links)
     )
     output_own = (middle_own + combined_own).astype(jnp.bfloat16)
-    grad_w_gate = jnp.einsum(
-        "rd,ref->edf",
-        normed_two,
-        grad_gate_act.reshape(-1, per_owner, units),
-        preferred_element_type=jnp.float32,
-    )
-    grad_w_up = jnp.einsum(
-        "rd,ref->edf",
-        normed_two,
-        grad_up_act.reshape(-1, per_owner, units),
-        preferred_element_type=jnp.float32,
-    )
-    grad_w_down = jnp.einsum(
-        "rf,rd->fd", weighted_hidden, cot_all, preferred_element_type=jnp.float32
-    ).reshape(per_owner, units, model_width)
     inner_gate = jnp.sum(gates * grad_gates_own, axis=-1, keepdims=True)
     grad_logits = gates * (grad_gates_own - inner_gate)
     router_f = w_router.astype(jnp.float32)

time: 589 us -> 485 us (0.82); the launches traced: 578 us -> 484 us
  matrix products: 124 us -> 33.5 us
  blocking collectives: 33.3 us -> 0 us
  Pallas kernels: 354 us -> 376 us
  waiting for transfers between devices: 0.7 us -> 12.4 us
    dot_general x10 -> x0, matrix products: 86 us -> none  [the longest x1 15 us: local(): jnp.einsum('rf,df->rd', grad_up_act, up_in, preferred_element_type=jnp.fl...]
    pallas_call x1 -> x2, Pallas kernels: 145 us -> 180 us  [the longest x1 159 us: experts_by_links(): pl.pallas_call(functools.partial(experts_kernel, ep_size, per_owner), out...]
    all_gather x1 -> x0, blocking collectives: 33.3 us -> none  [local(): order_all = lax.all_gather(order, 'ep')]
    pallas_call x2 -> x1, Pallas kernels: 30.9 us -> 14 us  [group_gather(): pl.pallas_call(functools.partial(group_gather_kernel, ep_size, pieces), o...]
    psum x1, waiting for transfers between devices: 0.01 us -> 11.7 us  [local(): lax.psum(grad_w_out.astype(jnp.bfloat16), 'ep').astype(jnp.float32)]
    pallas_call x1, Pallas kernels: 74.8 us -> 84.9 us  [gather_by_links(): pl.pallas_call(functools.partial(gather_kernel, ep_size), out_shape=jax.S...]
    pallas_call x1, Pallas kernels: 21.9 us -> 13.4 us  [group_total(): pl.pallas_call(functools.partial(group_total_kernel, ep_size), out_shape=...]
    unnamed x170 -> x117, local copies, waits for them, and re-layouts: 14.2 us -> 10.5 us
  transfers between devices with their start and end apart: 2 -> 2, of which waited for: 0 -> 1; matrix products, arithmetic and copies ran while one was open for 11% -> 9% of each run, Pallas kernels for 34% -> 42%
where the time goes in v4:
time: 485 us; the launch traced here: 484 us
  Pallas kernels  376 us (78%)
  matrix products  33.5 us (7%)
  other arithmetic  26 us (5%)
  local copies, waits for them, and re-layouts  20.5 us (4%)
  between operations  14.8 us (3%)
  waiting for transfers between devices  12.4 us (3%)
    pallas_call x1, Pallas kernels, experts_by_links(): pl.pallas_call(functools.partial(experts_kernel, ep_size, per_owner), out...  159 us
    pallas_call x1, Pallas kernels, gather_by_links(): pl.pallas_call(functools.partial(gather_kernel, ep_size), out_shape=jax.S...  84.9 us
    pallas_call x1, Pallas kernels, tail_by_links(): pl.pallas_call(functools.partial(tail_kernel, ep_size, counts), out_shape...  83.6 us
    pallas_call x1, Pallas kernels, front_gather(): pl.pallas_call(functools.partial(front_gather_kernel, ep_size, pieces), o...  21.1 us
    pallas_call x1, Pallas kernels, group_gather(): pl.pallas_call(functools.partial(group_gather_kernel, ep_size, pieces), o...  14 us
    pallas_call x1, Pallas kernels, group_total(): pl.pallas_call(functools.partial(group_total_kernel, ep_size), out_shape=...  13.4 us
    psum x1, waiting for transfers between devices, local(): lax.psum(grad_w_out.astype(jnp.bfloat16), 'ep').astype(jnp.float32)  11.7 us
    unnamed x117, local copies, waits for them, and re-layouts  10.5 us
  transfers between devices with their start and end apart: 2, of which 1 were waited for; matrix products, arithmetic and copies ran while one was open for 9% of the time, Pallas kernels for 42%

profile of v4, /device:TPU:0, one launch (start us, length us, event | category | flops | bytes accessed | tf_op | source)
XLA Modules:
  0.0 483.6 jit_solution(18212171473074440848)
XLA Ops:
  10.1 1.5 select_reduce_fusion.table
  11.6 1.2 fusion.18
  13.3 1.9 fusion.20.own
  15.2 21.1 %front_gather.1 = (bf16[2,2,128,1536]{3,2,1,0:T(8,128)(2,1)}, s32[8,16,512]{2,1,0:T(8,128)}) custom-call(bf16[128,1536]{1,0:T(8,128)(2,1)} %fusion.20.own, s32[16,512]{1,0:T(8,128)} %select_reduce_fusion.table), custom_call_target="tpu_custom_call" | custom-call | tf_op jit(solution)/shard_map/front_gather/pallas_call | solution.py:255
  36.4 1.2 fusion.25
  38.6 1.1 fusion.26
  39.7 1.3 copy.51
  42.2 2.1 fusion.47
  46.0 1.2 fusion.46
  47.3 0.9 fusion.3
  48.2 1.8 copy-done.1
  50.0 1.2 fusion.9
  51.2 1.0 convolution_convert_fusion
  52.2 13.4 %group_total.1 = f32[128,1536]{1,0:T(8,128)S(1)} custom-call(bf16[2,2,128,1536]{3,2,1,0:T(8,128)(2,1)S(1)} %bitcast.133), custom_call_target="tpu_custom_call" | custom-call | tf_op jit(solution)/shard_map/group_total/pallas_call | solution.py:388
  65.9 0.9 multiply_convert_fusion.own
  66.8 84.9 %gather_by_links.1 = bf16[4,2,2,2,128,1536]{5,4,3,2,1,0:T(8,128)(2,1)} custom-call(bf16[128,1536]{1,0:T(8,128)(2,1)} %multiply_convert_fusion.own), custom_call_target="tpu_custom_call" | custom-call | tf_op jit(solution)/shard_map/gather_by_links/pallas_call | solution.py:204
  152.5 2.4 pad.18.code_in
  155.9 1.5 slice_bitcast_fusion.1
  157.4 1.3 pad_maximum_fusion.enter
  158.7 159.3 %experts_by_links.1 = (f32[128,1536]{1,0:T(8,128)}, f32[128,1536]{1,0:T(8,128)}, f32[8,8,128]{2,1,0:T(8,128)}, f32[2,1536,128]{2,1,0:T(8,128)}, f32[2,1536,128]{2,1,0:T(8,128)}, /*index=5*/f32[256,1536]{1,0:T(8,128)}) custom-call(bf16[4,2,512,1536]{3,2,1,0:T(8,128)(2,1)} %bitcast.136, bf16[4,2,512,1536]{3,2,1,0:T(8,128)(2,1)} %bitcast.143, ...), custom_call_target="tpu_custom_call" | custom-call | tf_op jit(solution)/shard_map/experts_by_links/pallas_call | solution.py:726
  318.9 0.9 fusion.31
  319.8 2.5 multiply_reduce_fusion.1
  322.3 1.5 fusion.44
  323.8 14.0 %group_gather.1 = bf16[2,2,128,1536]{3,2,1,0:T(8,128)(2,1)} custom-call(bf16[128,1536]{1,0:T(8,128)(2,1)} %get-tuple-element.40.own), custom_call_target="tpu_custom_call" | custom-call | tf_op jit(solution)/shard_map/group_gather/pallas_call | solution.py:310
  337.8 3.4 convolution_convert_fusion.5
  341.3 1.8 convolution_convert_fusion.1
  343.1 4.9 %fusion.15 = bf16[2,64,512]{2,1,0:T(8,128)(2,1)} fusion(bf16[512,2,3,64]{0,3,2,1:T(8,128)(2,1)} %bitcast.173, f32[2,3,512,512]{2,3,1,0:T(8,128)} %copy-done.1, f32[2,3,512]{2,1,0:T(4,128)S(1)} %log_add_fusion, pred[512,512]{0,1:T(8,128)(4,1)S(1)} %compare_and_fusion), kind=kOutput, calls=%fused_computation.37 | convolution fusion | flops 206110720 | bytes 7090176 | tf_op jit(solution)/shard_map/kgqp,qkgd->pkd/dot_general | solution.py:1159
  348.0 2.0 fusion
  350.0 1.8 fusion.2
  351.9 1.1 fusion.14
  354.4 1.8 convolution_convert_fusion.2
  356.2 2.6 fusion.50
  358.9 1.1 convolution_convert_fusion.3
  360.1 1.1 convolution_convert_fusion.4
  362.2 1.9 multiply_reduce_fusion
  364.9 83.6 %tail_by_links.1 = (f32[4,2,48,1536]{3,2,1,0:T(8,128)}, f32[4,2,16,1536]{3,2,1,0:T(8,128)}, f32[4,2,16,1536]{3,2,1,0:T(8,128)}, f32[128,1536]{1,0:T(8,128)}, f32[32,12,128]{2,1,0:T(8,128)}) custom-call(bf16[4,2,48,1536]{3,2,1,0:T(8,128)(2,1)} %bitcast.155, bf16[4,2,16,1536]{3,2,1,0:T(8,128)(2,1)} %bitcast.151, bf16[4,2,16,1536]{3,2,1,0:T(8,128)(2,1)} %bitcast.150, ...), custom_call_target="tpu_custom_call" | custom-call | tf_op jit(solution)/shard_map/tail_by_links/pallas_call | solution.py:935
  448.6 0.9 slice.77
  450.2 1.3 fusion.24
  451.6 1.3 slice_bitcast_fusion.4
  452.9 2.4 fusion.23
  455.2 11.7 %all-reduce.6.cloned.1.call-done = bf16[384,1536]{1,0:T(8,128)(2,1)} async-done(((bf16[384,1536]{1,0:T(8,128)(2,1)}), bf16[384,1536]{1,0:T(8,128)(2,1)}) %all-reduce.6.cloned.1.call-update) | async-done | bytes 1179664 | tf_op jit(solution)/shard_map/psum | solution.py:1280
  466.9 3.0 convert_element_type.159
  469.9 1.4 copy.73
  471.5 0.9 copy.74
  472.4 0.9 copy.75
  473.3 1.1 copy.76
  474.4 1.1 copy.77
  475.6 1.1 copy.78
  (161 shorter events, 14.5 us)
Async XLA Ops:
  7.2 37.2 %copy-start = (bf16[384,1536]{1,0:T(8,128)(2,1)S(1)}, bf16[384,1536]{1,0:T(8,128)(2,1)}, u32[]{:S(2)}) copy-start(bf16[384,1536]{1,0:T(8,128)(2,1)} %param.18) | copy-start | bytes 3538948
  7.2 34.2 %copy-start.48 = (s32[512]{0:T(512)S(1)}, s32[512]{0:T(512)}, u32[]{:S(2)}) copy-start(s32[512]{0:T(512)} %param.30) | copy-start | bytes 6148
  7.2 33.8 %copy-start.46 = (s32[512]{0:T(512)S(1)}, s32[512]{0:T(512)}, u32[]{:S(2)}) copy-start(s32[512]{0:T(512)} %param.29) | copy-start | bytes 6148
  7.2 151.5 %all-gather.2.cloned.1.call-start = ((), (), s32[]{:S(2)}) async-start(), calls=%async_computation | async-start | bytes 12976128 | tf_op jit(solution)/shard_map/all_gather | solution.py:996
  7.9 459.0 %all-reduce.6.cloned.1.call-start = ((), (), s32[]{:S(2)}) async-start(), calls=%async_computation.1 | async-start | bytes 2359296 | tf_op jit(solution)/shard_map/psum | solution.py:1280
  9.4 56.5 %copy-start.44 = (f32[1536]{0:T(1024)}, f32[1536]{0:T(1024)S(1)}, u32[]{:S(2)}) copy-start(f32[1536]{0:T(1024)S(1)} %convert_element_type.136) | copy-start | bytes 18436
  10.1 5.1 %copy-start.42 = (f32[1536]{0:T(1024)}, f32[1536]{0:T(1024)S(1)}, u32[]{:S(2)}) copy-start(f32[1536]{0:T(1024)S(1)} %convert_element_type.128) | copy-start | bytes 18436
  13.3 24.5 %copy-start.50 = (f32[128]{0:T(128)}, f32[128]{0:T(128)S(1)}, u32[]{:S(2)}) copy-start(f32[128]{0:T(128)S(1)} %get-tuple-element.71) | copy-start | bytes 1540
  36.4 8.0 %copy-start.2 = (bf16[2,2,128,1536]{3,2,1,0:T(8,128)(2,1)S(1)}, bf16[2,2,128,1536]{3,2,1,0:T(8,128)(2,1)}, u32[]{:S(2)}) copy-start(bf16[2,2,128,1536]{3,2,1,0:T(8,128)(2,1)} %get-tuple-element.25) | copy-start | bytes 4718596
  41.3 3.8 copy-start.10
  41.3 3.8 copy-start.12
  45.3 1.9 copy-start.25
  45.3 1.9 copy-start.27
  46.0 2.2 copy-start.29
  47.3 2.7 copy-start.1
  51.2 14.7 %copy-start.33 = (bf16[2,64,3,512]{3,1,2,0:T(8,128)(2,1)}, bf16[2,64,3,512]{3,1,2,0:T(8,128)(2,1)S(1)}, u32[]{:S(2)}) copy-start(bf16[2,64,3,512]{3,1,2,0:T(8,128)(2,1)S(1)} %fusion.9) | copy-start | bytes 1179652
  51.2 14.5 %copy-start.5 = (bf16[128,1536]{1,0:T(8,128)(2,1)S(1)}, bf16[128,1536]{1,0:T(8,128)(2,1)}, u32[]{:S(2)}) copy-start(bf16[128,1536]{1,0:T(8,128)(2,1)} %param.16) | copy-start | bytes 1179652
  66.8 84.9 %copy-start.32 = (bf16[16,1536]{1,0:T(8,128)(2,1)S(1)}, bf16[16,1536]{1,0:T(8,128)(2,1)}, u32[]{:S(2)}) copy-start(bf16[16,1536]{1,0:T(8,128)(2,1)} %param.23) | copy-start | bytes 147460
  66.8 88.2 %copy-start.7 = (bf16[128,1536]{1,0:T(8,128)(2,1)S(1)}, bf16[128,1536]{1,0:T(8,128)(2,1)}, u32[]{:S(2)}) copy-start(bf16[128,1536]{1,0:T(8,128)(2,1)} %multiply_convert_fusion.own) | copy-start | bytes 1179652
  158.7 161.1 %copy-start.45 = (f32[1536]{0:T(1024)S(1)}, f32[1536]{0:T(1024)}, u32[]{:S(2)}) copy-start(f32[1536]{0:T(1024)} %copy-done.44) | copy-start | bytes 18436
  318.0 4.3 copy-start.17
  318.0 4.3 copy-start.22
  337.8 3.5 copy-start.18
  337.8 3.4 copy-start.34
  341.3 6.7 %slice-start = ((s8[6291456]{0:T(1024)(128)(4,1)}), s8[2097152]{0:T(1024)(128)(4,1)S(1)}, s32[]{:S(2)}) async-start(s8[6291456]{0:T(1024)(128)(4,1)} %bitcast.134), calls=%async_computation.2 | async-start | bytes 4194304
  343.1 4.9 %slice-start.1 = ((s8[6291456]{0:T(1024)(128)(4,1)}), s8[4194304]{0:T(1024)(128)(4,1)S(1)}, s32[]{:S(2)}) async-start(s8[6291456]{0:T(1024)(128)(4,1)} %bitcast.134), calls=%async_computation.3 | async-start | bytes 8388608
  343.1 4.9 %copy-start.30 = (bf16[512,128]{0,1:T(8,128)(2,1)S(1)}, bf16[512,128]{0,1:T(8,128)(2,1)}, u32[]{:S(2)}) copy-start(bf16[512,128]{0,1:T(8,128)(2,1)} %copy-done.29) | copy-start | bytes 393220
  343.1 4.9 %copy-start.37 = (bf16[512,384]{0,1:T(8,128)(2,1)S(1)}, bf16[512,384]{0,1:T(8,128)(2,1)}, u32[]{:S(2)}) copy-start(bf16[512,384]{0,1:T(8,128)(2,1)} %convolution_convert_fusion.5) | copy-start | bytes 1179652
  350.0 1.9 copy-start.26
  350.0 1.9 copy-start.28
  351.9 1.8 copy-start.11
  351.9 1.8 copy-start.13
  356.2 2.7 copy-start.47
  356.2 2.7 copy-start.31
  358.9 2.3 copy-start.4
  358.9 2.3 copy-start.36
  362.2 1.9 copy-start.49
  362.2 1.9 copy-start.35
  364.1 86.1 %copy-start.6 = (bf16[128,1536]{1,0:T(8,128)(2,1)S(1)}, bf16[128,1536]{1,0:T(8,128)(2,1)}, u32[]{:S(2)}) copy-start(bf16[128,1536]{1,0:T(8,128)(2,1)} %param.16) | copy-start | bytes 1179652
  364.1 86.1 %copy-start.43 = (f32[1536]{0:T(1024)S(1)}, f32[1536]{0:T(1024)}, u32[]{:S(2)}) copy-start(f32[1536]{0:T(1024)} %copy-done.42) | copy-start | bytes 18436
  364.1 88.7 %copy-start.8 = (f32[128,1536]{1,0:T(8,128)S(1)}, f32[128,1536]{1,0:T(8,128)}, u32[]{:S(2)}) copy-start(f32[128,1536]{1,0:T(8,128)} %get-tuple-element.41) | copy-start | bytes 2359300
  364.2 88.7 %copy-start.51 = (f32[128]{0:T(128)S(1)}, f32[128]{0:T(128)}, u32[]{:S(2)}) copy-start(f32[128]{0:T(128)} %copy-done.50) | copy-start | bytes 1540
  364.2 88.7 %copy-start.52 = (f32[128]{0:T(128)S(1)}, f32[128]{0:T(128)}, u32[]{:S(2)}) copy-start(f32[128]{0:T(128)} %get-tuple-element.70) | copy-start | bytes 1540
  455.2 14.6 %copy-start.9 = (f32[4,2,48,1536]{3,2,1,0:T(8,128)S(1)}, f32[4,2,48,1536]{3,2,1,0:T(8,128)}, u32[]{:S(2)}) copy-start(f32[4,2,48,1536]{3,2,1,0:T(8,128)} %get-tuple-element.32) | copy-start | bytes 7077892
  469.9 2.5 copy-start.23
  469.9 3.4 copy-start.16
  471.5 2.9 copy-start.15
  473.3 2.3 copy-start.14
  (9 other events, 12.0 us)
Sparse Core Ops, SparseCore 0:
  10.9 130.7 all-gather.1
  359.0 107.8 all-reduce.5

commit v5 on v4

--- a/solution.py
+++ b/solution.py
@@ -446,10 +446,11 @@
 ):
     me = Place(ep_size)
     depth = me.depth
-    blocks = 2 * depth
+    steps = 2 * depth
+    blocks = 2 * steps
     width = router.shape[1]
-    tokens = rows_buf.shape[1]
-    share = tokens // 4
+    share = rows_buf.shape[2]
+    tokens = 4 * share
     units = leave.shape[0] // per_owner
     hidden = per_owner * units
     f32, bf16 = jnp.float32, jnp.bfloat16
@@ -458,14 +459,17 @@
     my_place = lax.axis_index("ep") * 4 + lax.axis_index("tp")
 
     def where(b):
-        return me.after(b // 2 + 1), lax.rem(1 - me.y + b % 2, 2)
+        return me.after(b // 4 + 1), lax.rem(1 - me.y + b % 2, 2)
+
+    def half(b):
+        return pl.ds(pl.multiple_of(b // 2 % 2 * share, share), share)
 
     def load(b, which):
         z, y = where(b)
         source, target = ((rows_in, rows_buf), (cots_in, cots_buf))[which]
         slot = lax.rem(b, 2)
         return pltpu.make_async_copy(
-            source.at[z, y], target.at[slot], load_sems.at[slot, which]
+            source.at[z, y, :, half(b)], target.at[slot], load_sems.at[slot, which]
         )
 
     def core_copy(b):
@@ -510,13 +514,13 @@
             device_id_type=MESH,
         )
 
-    def z_copy(step):
+    def z_copy(step, which):
         return pltpu.make_async_remote_copy(
-            src_ref=last_got.at[step],
-            dst_ref=z_got.at[step],
-            send_sem=z_sems.at[0, step],
-            recv_sem=z_sems.at[1, step],
-            device_id=me.device(z=me.after(step + 1)),
+            src_ref=last_got.at[step, which],
+            dst_ref=z_got.at[step, which],
+            send_sem=z_sems.at[0, step, which],
+            recv_sem=z_sems.at[1, step, which],
+            device_id=me.device(z=me.after(step // 2 + 1)),
             device_id_type=MESH,
         )
 
@@ -544,8 +548,9 @@
     def compute(b):
         z, y = where(b)
         slot = lax.rem(b, 2)
-        rows, cots = rows_buf[slot], cots_buf[slot]
-        code = code_in[pl.ds(pl.multiple_of((z * 2 + y) * tokens, tokens), tokens), :].astype(f32)
+        rows = rows_buf[slot].reshape(tokens, width)
+        cots = cots_buf[slot].reshape(tokens, width)
+        code = code_in[z * 2 + y, :, half(b), :].astype(f32).reshape(tokens, -1)
         used = code >= 0.0
         logits = jnp.where(used, dot(rows, router[...], (1, 1)), -1e30)
         top = jnp.max(logits, axis=1, keepdims=True)
@@ -570,7 +575,9 @@
             preferred_element_type=f32,
         )
         for k in range(4):
-            small_in[(z * 2 + y) * 4 + k] = grad_gates[:, k * share : (k + 1) * share]
+            small_in[(z * 2 + y) * 4 + k, b // 2 % 2, :, :share] = grad_gates[
+                :, k * share : (k + 1) * share
+            ]
         weighted[...] = (gates * value).astype(bf16)
         grad_hidden = gates * back_act
         turned[:, :hidden] = (
@@ -593,89 +600,101 @@
         tile = 512
         for n in range(width // tile):
             cols = slice(n * tile, (n + 1) * tile)
-            enter_sum[:, cols] += dot(turned[...], rows_buf[slot, :, cols], (0, 0))
-            down_out[:, cols] += dot(weighted[...], cots_buf[slot, :, cols], (0, 0))
+            rows = rows_buf[slot, :, :, cols].reshape(tokens, tile)
+            cots = cots_buf[slot, :, :, cols].reshape(tokens, tile)
+            enter_sum[:, cols] += dot(turned[...], rows, (0, 0))
+            down_out[:, cols] += dot(weighted[...], cots, (0, 0))
 
     enter_sum[...] = jnp.zeros_like(enter_sum)
     down_out[...] = jnp.zeros_like(down_out)
+    small_in[...] = jnp.zeros_like(small_in)
     for which in range(2):
         load(0, which).start()
 
-    def turn(b, carry):
-        @pl.when(b < blocks)
+    def during(i, lag, body, even=False):
+        b = i - lag
+        inside = (b >= 0) & (b < blocks)
+        if even:
+            inside &= b % 2 == 0
+        pl.when(inside)(lambda: body(b))
+
+    def finish_sum(which):
+        def body(b):
+            step = b // 2
+            last_copy(step, which).wait_recv()
+            add_into(last_got.at[step, which], pair_got.at[step, which, (me.y, me.x)[which]])
+
+            @pl.when(step < steps - 2)
+            def _():
+                z_copy(step, which).start()
+
+        return body
+
+    def work(b):
+        for which in range(2):
+            load(b, which).wait()
+
+        @pl.when(b + 1 < blocks)
         def _():
             for which in range(2):
-                load(b, which).wait()
-
-            @pl.when(b + 1 < blocks)
-            def _():
-                for which in range(2):
-                    load(b + 1, which).start()
-
-            compute(b)
-            core_copy(b).start()
-            weight_sums(b)
-
-        @pl.when((b >= 1) & (b <= blocks))
+                load(b + 1, which).start()
+
+        compute(b)
+        core_copy(b).start()
+        weight_sums(b)
+
+    def core_sum(b):
+        y = where(b)[1]
+        core_copy(b).wait_recv()
+        for which in range(2):
+            for x in range(2):
+                add_into(
+                    core_got.at[b // 2, y, which, x], parts.at[lax.rem(b, 2), which, x, me.c]
+                )
+        grad_pair(b).start()
+
+        @pl.when(b % 2 == 0)
         def _():
-            j = b - 1
-            y = where(j)[1]
-            core_copy(j).wait_recv()
-            for which in range(2):
-                for x in range(2):
-                    add_into(
-                        core_got.at[j // 2, y, which, x],
-                        parts.at[lax.rem(j, 2), which, x, me.c],
-                    )
-            grad_pair(j).start()
-
-            @pl.when(j % 2 == 0)
-            def _():
-                sum_pair(j // 2).start()
-
-            core_copy(j).wait_send()
-
-        @pl.when((b >= 2) & (b <= blocks + 1))
+            sum_pair(b // 2).start()
+
+        core_copy(b).wait_send()
+
+    def out_pair(b):
+        step = b // 2
+        sum_pair(step).wait_recv()
+        for x in range(2):
+            add_into(pair_got.at[step, 1, x], core_got.at[step, me.y, 1, x])
+        last_copy(step, 1).start()
+
+    def back_pair(b):
+        y = where(b)[1]
+        step = b // 2
+        grad_pair(b).wait_recv()
+        add_into(pair_got.at[step, 0, y], core_got.at[step, y, 0, me.x])
+
+        @pl.when(b % 2 == 0)
         def _():
-            j = b - 2
-            y = where(j)[1]
-            step = j // 2
-            grad_pair(j).wait_recv()
-            add_into(pair_got.at[step, 0, y], core_got.at[step, y, 0, me.x])
-
-            @pl.when(j % 2 == 0)
-            def _():
-                last_copy(step, 0).start()
-                sum_pair(step).wait_recv()
-                for x in range(2):
-                    add_into(pair_got.at[step, 1, x], core_got.at[step, me.y, 1, x])
-                last_copy(step, 1).start()
-
-        @pl.when((b >= 4) & (b % 2 == 0))
-        def _():
-            step = (b - 4) // 2
-            for which in range(2):
-                last_copy(step, which).wait_recv()
-                add_into(last_got.at[step, which], pair_got.at[step, which, (me.y, me.x)[which]])
-
-            @pl.when(step < depth - 1)
-            def _():
-                z_copy(step).start()
-
-        @pl.when(b == blocks)
-        def _():
-            for k, device in enumerate(others):
-                small_copy(k, device).start()
-            pltpu.make_async_copy(
-                small_in.at[my_place], small_got.at[my_place], own_sem
-            ).start()
-            for e in range(per_owner):
-                gate_out[e] = enter_sum[e * units : (e + 1) * units, :].T
-                up_out[e] = enter_sum[hidden + e * units : hidden + (e + 1) * units, :].T
-
+            last_copy(step, 0).start()
+
+    def small_send(b):
+        for k, device in enumerate(others):
+            small_copy(k, device).start()
+        pltpu.make_async_copy(small_in.at[my_place], small_got.at[my_place], own_sem).start()
+        for e in range(per_owner):
+            gate_out[e] = enter_sum[e * units : (e + 1) * units, :].T
+            up_out[e] = enter_sum[hidden + e * units : hidden + (e + 1) * units, :].T
+
+    def turn(i, carry):
+        during(i, 6, finish_sum(1), True)
+        during(i, 0, work)
+        during(i, 1, core_sum)
+        during(i, 7, finish_sum(0), True)
+        during(i, 3, out_pair, True)
+        during(i, 4, back_pair)
+        pl.when(i == blocks)(lambda: small_send(i))
         return carry
 
-    lax.fori_loop(0, blocks + 3, turn, 0)
+    lax.fori_loop(0, blocks + 7, turn, 0)
     pltpu.make_async_copy(small_in.at[my_place], small_got.at[my_place], own_sem).wait()
     for k, device in enumerate(others):
         small_copy(k, device).wait()
@@ -684,30 +703,40 @@
         for tp in range(1, 4):
             total = total + small_got[ep * 4 + tp]
         small_out[ep] = total
-    for step in range(depth - 1):
-        z_copy(step).wait_recv()
-
-    def finish(which, target):
+    for step in range(steps - 2):
+        for which in range(2):
+            z_copy(step, which).wait_recv()
+
+    def finish(which, part, target):
         def tile(i, carry):
-            at = pl.ds(pl.multiple_of(i * 16, 16), 16)
-            total = last_got[depth - 1, which, at, :].astype(f32)
+            at = pl.multiple_of(i * 16, 16)
+            total = last_got[steps - 2 + part, which, pl.ds(at, 16), :].astype(f32)
             for step in range(depth - 1):
-                total = total + z_got[step, which, at, :].astype(f32)
-            target[at, :] = total
+                total = total + z_got[2 * step + part, which, pl.ds(at, 16), :].astype(f32)
+            target[pl.ds(part * share + at, 16), :] = total
             return carry
 
-        lax.fori_loop(0, target.shape[0] // 16, tile, 0)
-
-    finish(0, grad_out)
-    finish(1, sum_out)
-    for step in range(depth):
+        lax.fori_loop(0, share // 16, tile, 0)
+
+    for part in range(2):
+        finish(0, part, grad_out)
+        finish(1, part, sum_out)
+
+    def sent(step, carry):
         grad_pair(2 * step).wait_send()
         grad_pair(2 * step + 1).wait_send()
         sum_pair(step).wait_send()
         for which in range(2):
             last_copy(step, which).wait_send()
-        if step < depth - 1:
-            z_copy(step).wait_send()
+
+        @pl.when(step < steps - 2)
+        def _():
+            for which in range(2):
+                z_copy(step, which).wait_send()
+
+        return carry
+
+    lax.fori_loop(0, steps, sent, 0)
 
 
 def experts_by_links(rows_all, cots_all, code, router, enter, leave, per_owner, ep_size):
@@ -715,6 +744,7 @@
     depth = ep_size // 2
     tokens = total_rows // ep_size
     rows = tokens // 4
+    half, steps = rows // 2, 2 * depth
     hidden = leave.shape[0]
     units = hidden // per_owner
     bf16, f32 = jnp.bfloat16, jnp.float32
@@ -722,13 +752,13 @@
     vmem = pl.BlockSpec(memory_space=pltpu.VMEM)
     anywhere = pl.BlockSpec(memory_space=pl.ANY)
     places = 4 * ep_size
-    blocks = (depth, 2, tokens, width)
+    blocks = (depth, 2, 4, rows, width)
     return pl.pallas_call(
         functools.partial(experts_kernel, ep_size, per_owner),
         out_shape=(
             jax.ShapeDtypeStruct((rows, width), f32),
             jax.ShapeDtypeStruct((rows, width), f32),
-            jax.ShapeDtypeStruct((ep_size, 8, rows), f32),
+            jax.ShapeDtypeStruct((ep_size, 2, 8, 128), f32),
             jax.ShapeDtypeStruct((per_owner, width, units), f32),
             jax.ShapeDtypeStruct((per_owner, width, units), f32),
             jax.ShapeDtypeStruct((hidden, width), f32),
@@ -736,23 +766,23 @@
         in_specs=[anywhere, anywhere, vmem, vmem, vmem, vmem],
         out_specs=(vmem,) * 6,
         scratch_shapes=[
-            pltpu.VMEM((2, tokens, width), bf16),
-            pltpu.VMEM((2, tokens, width), bf16),
-            pltpu.VMEM((tokens, hidden), bf16),
-            pltpu.VMEM((tokens, 2 * hidden), bf16),
+            pltpu.VMEM((2, 4, half, width), bf16),
+            pltpu.VMEM((2, 4, half, width), bf16),
+            pltpu.VMEM((4 * half, hidden), bf16),
+            pltpu.VMEM((4 * half, 2 * hidden), bf16),
             pltpu.VMEM((2 * hidden, width), f32),
-            pltpu.VMEM((2, 2, 2, 2, rows, width), bf16),
-            pltpu.VMEM((depth, 2, 2, 2, rows, width), bf16),
-            pltpu.VMEM((depth, 2, 2, rows, width), bf16),
-            pltpu.VMEM((depth, 2, rows, width), bf16),
-            pltpu.VMEM((depth - 1, 2, rows, width), bf16),
-            pltpu.VMEM((places, 8, rows), f32),
-            pltpu.VMEM((places, 8, rows), f32),
+            pltpu.VMEM((2, 2, 2, 2, half, width), bf16),
+            pltpu.VMEM((steps, 2, 2, 2, half, width), bf16),
+            pltpu.VMEM((steps, 2, 2, half, width), bf16),
+            pltpu.VMEM((steps, 2, half, width), bf16),
+            pltpu.VMEM((steps - 2, 2, half, width), bf16),
+            pltpu.VMEM((places, 2, 8, 128), f32),
+            pltpu.VMEM((places, 2, 8, 128), f32),
             dma((2, 2)),
-            dma((2, 2 * depth)),
-            dma((2, 3 * depth)),
-            dma((2, depth, 2)),
-            dma((2, depth - 1)),
+            dma((2, 2 * steps)),
+            dma((2, 3 * steps)),
+            dma((2, steps, 2)),
+            dma((2, steps - 2, 2)),
             dma((2, places - 1)),
             dma,
         ],
@@ -760,7 +790,14 @@
             collective_id=2, has_side_effects=True, vmem_limit_bytes=60 * 1024 * 1024
         ),
         name="experts_by_links",
-    )(rows_all.reshape(blocks), cots_all.reshape(blocks), code, router, enter, leave)
+    )(
+        rows_all.reshape(blocks),
+        cots_all.reshape(blocks),
+        code.reshape(ep_size, 4, rows, -1),
+        router,
+        enter,
+        leave,
+    )
 
 
 def tail_kernel(
@@ -1054,7 +1091,7 @@
         return (
             grads,
             sums,
-            small[:, :per_owner].reshape(expert_count, share).T,
+            small[:, :, :per_owner, : share // 2].swapaxes(1, 2).reshape(expert_count, share).T,
             gate,
             up,
             down.reshape(w_down.shape),

time: 485 us -> 460 us (0.948)
  Pallas kernels: 376 us -> 351 us
    pallas_call x1, Pallas kernels: 159 us -> 137 us  [experts_by_links(): pl.pallas_call(functools.partial(experts_kernel, ep_size, per_owner), out...]
    unnamed x117 -> x118, local copies, waits for them, and re-layouts: 10.5 us -> 11.9 us
  transfers between devices with their start and end apart: 2 -> 2, of which waited for: 1 -> 1; matrix products, arithmetic and copies ran while one was open for 9% -> 9% of each run, Pallas kernels for 42% -> 43%
where the time goes in v5:
time: 460 us; the launch traced here: 459 us
  Pallas kernels  351 us (76%)
  matrix products  33.5 us (7%)
  other arithmetic  26.1 us (6%)
  local copies, waits for them, and re-layouts  20.6 us (4%)
  between operations  14.8 us (3%)
  waiting for transfers between devices  12.6 us (3%)
    pallas_call x1, Pallas kernels, experts_by_links(): pl.pallas_call(functools.partial(experts_kernel, ep_size, per_owner), out...  137 us
    pallas_call x1, Pallas kernels, gather_by_links(): pl.pallas_call(functools.partial(gather_kernel, ep_size), out_shape=jax.S...  84.7 us
    pallas_call x1, Pallas kernels, tail_by_links(): pl.pallas_call(functools.partial(tail_kernel, ep_size, counts), out_shape...  80.3 us
    pallas_call x1, Pallas kernels, front_gather(): pl.pallas_call(functools.partial(front_gather_kernel, ep_size, pieces), o...  21.1 us
    pallas_call x1, Pallas kernels, group_gather(): pl.pallas_call(functools.partial(group_gather_kernel, ep_size, pieces), o...  14.6 us
    pallas_call x1, Pallas kernels, group_total(): pl.pallas_call(functools.partial(group_total_kernel, ep_size), out_shape=...  13.3 us
    psum x1, waiting for transfers between devices, local(): lax.psum(grad_w_out.astype(jnp.bfloat16), 'ep').astype(jnp.float32)  11.9 us
    unnamed x118, local copies, waits for them, and re-layouts  11.9 us
  transfers between devices with their start and end apart: 2, of which 1 were waited for; matrix products, arithmetic and copies ran while one was open for 9% of the time, Pallas kernels for 43%

profile of v5, /device:TPU:0, one launch (start us, length us, event | category | flops | bytes accessed | tf_op | source)
XLA Modules:
  0.0 459.2 jit_solution(3873603908512924906)
XLA Ops:
  10.1 1.5 select_reduce_fusion.table
  11.6 1.2 fusion.18
  13.3 1.9 fusion.20.own
  15.2 21.1 %front_gather.1 = (bf16[2,2,128,1536]{3,2,1,0:T(8,128)(2,1)}, s32[8,16,512]{2,1,0:T(8,128)}) custom-call(bf16[128,1536]{1,0:T(8,128)(2,1)} %fusion.20.own, s32[16,512]{1,0:T(8,128)} %select_reduce_fusion.table), custom_call_target="tpu_custom_call" | custom-call | tf_op jit(solution)/shard_map/front_gather/pallas_call | solution.py:255
  36.3 1.2 fusion.25
  38.5 1.1 fusion.26
  39.6 1.3 copy.69
  41.3 1.0 compare_and_fusion
  42.3 2.1 fusion.51
  46.2 1.2 fusion.50
  47.4 0.9 fusion.3
  48.3 1.8 copy-done.1
  50.1 1.2 fusion.9
  51.4 1.0 convolution_convert_fusion
  52.4 13.3 %group_total.1 = f32[128,1536]{1,0:T(8,128)S(1)} custom-call(bf16[2,2,128,1536]{3,2,1,0:T(8,128)(2,1)S(1)} %bitcast.144), custom_call_target="tpu_custom_call" | custom-call | tf_op jit(solution)/shard_map/group_total/pallas_call | solution.py:388
  65.9 0.9 multiply_convert_fusion.own
  66.8 84.7 %gather_by_links.1 = bf16[4,2,2,2,128,1536]{5,4,3,2,1,0:T(8,128)(2,1)} custom-call(bf16[128,1536]{1,0:T(8,128)(2,1)} %multiply_convert_fusion.own), custom_call_target="tpu_custom_call" | custom-call | tf_op jit(solution)/shard_map/gather_by_links/pallas_call | solution.py:204
  152.4 2.4 pad.18.clone
  155.7 1.5 slice_bitcast_fusion.1
  157.2 1.3 pad_maximum_fusion.enter
  158.5 137.3 %experts_by_links.1 = (f32[128,1536]{1,0:T(8,128)}, f32[128,1536]{1,0:T(8,128)}, f32[8,2,8,128]{3,2,1,0:T(8,128)}, f32[2,1536,128]{2,1,0:T(8,128)}, f32[2,1536,128]{2,1,0:T(8,128)}, /*index=5*/f32[256,1536]{1,0:T(8,128)}) custom-call(bf16[4,2,4,128,1536]{4,3,2,1,0:T(8,128)(2,1)} %bitcast.147, bf16[4,2,4,128,1536]{4,3,2,1,0:T(8,128)(2,1)} %bitcast.154, ...), custom_call_target="tpu_custom_call" | custom-call | tf_op jit(solution)/shard_map/experts_by_links/pallas_call | solution.py:756
  295.9 0.9 slice_bitcast_fusion.4
  296.9 0.9 fusion.33
  297.8 2.5 multiply_reduce_fusion.1
  300.3 1.5 fusion.48
  301.8 14.6 %group_gather.1 = bf16[2,2,128,1536]{3,2,1,0:T(8,128)(2,1)} custom-call(bf16[128,1536]{1,0:T(8,128)(2,1)} %get-tuple-element.40.own), custom_call_target="tpu_custom_call" | custom-call | tf_op jit(solution)/shard_map/group_gather/pallas_call | solution.py:310
  316.4 3.4 convolution_convert_fusion.5
  319.9 1.8 convolution_convert_fusion.1
  321.7 4.9 %fusion.15 = bf16[2,64,512]{2,1,0:T(8,128)(2,1)} fusion(bf16[512,2,3,64]{0,3,2,1:T(8,128)(2,1)} %bitcast.185, f32[2,3,512,512]{2,3,1,0:T(8,128)} %copy-done.1, f32[2,3,512]{2,1,0:T(4,128)S(1)} %log_add_fusion, pred[512,512]{0,1:T(8,128)(4,1)S(1)} %compare_and_fusion), kind=kOutput, calls=%fused_computation.37 | convolution fusion | flops 206110720 | bytes 7090176 | tf_op jit(solution)/shard_map/kgqp,qkgd->pkd/dot_general | solution.py:1196
  326.6 2.0 fusion
  328.6 1.8 fusion.2
  330.5 1.1 fusion.14
  333.0 1.8 convolution_convert_fusion.2
  334.8 2.6 fusion.54
  337.5 1.1 convolution_convert_fusion.3
  338.7 1.1 convolution_convert_fusion.4
  340.9 1.9 multiply_reduce_fusion
  343.6 80.3 %tail_by_links.1 = (f32[4,2,48,1536]{3,2,1,0:T(8,128)}, f32[4,2,16,1536]{3,2,1,0:T(8,128)}, f32[4,2,16,1536]{3,2,1,0:T(8,128)}, f32[128,1536]{1,0:T(8,128)}, f32[32,12,128]{2,1,0:T(8,128)}) custom-call(bf16[4,2,48,1536]{3,2,1,0:T(8,128)(2,1)} %bitcast.167, bf16[4,2,16,1536]{3,2,1,0:T(8,128)(2,1)} %bitcast.163, bf16[4,2,16,1536]{3,2,1,0:T(8,128)(2,1)} %bitcast.162, ...), custom_call_target="tpu_custom_call" | custom-call | tf_op jit(solution)/shard_map/tail_by_links/pallas_call | solution.py:972
  423.9 0.9 slice.77
  425.5 1.4 fusion.24
  426.9 1.3 slice_bitcast_fusion.5
  428.2 2.4 fusion.23
  430.6 11.9 %all-reduce.6.cloned.1.call-done = bf16[384,1536]{1,0:T(8,128)(2,1)} async-done(((bf16[384,1536]{1,0:T(8,128)(2,1)}), bf16[384,1536]{1,0:T(8,128)(2,1)}) %all-reduce.6.cloned.1.call-update) | async-done | bytes 1179664 | tf_op jit(solution)/shard_map/psum | solution.py:1317
  442.5 3.0 convert_element_type.159
  445.5 1.4 copy.81
  448.9 1.1 copy.84
  450.0 1.1 copy.85
  451.2 1.1 copy.86
  (163 shorter events, 14.6 us)
Async XLA Ops:
  7.2 37.3 %copy-start = (bf16[384,1536]{1,0:T(8,128)(2,1)S(1)}, bf16[384,1536]{1,0:T(8,128)(2,1)}, u32[]{:S(2)}) copy-start(bf16[384,1536]{1,0:T(8,128)(2,1)} %param.18) | copy-start | bytes 3538948
  7.2 34.1 %copy-start.48 = (s32[512]{0:T(512)S(1)}, s32[512]{0:T(512)}, u32[]{:S(2)}) copy-start(s32[512]{0:T(512)} %param.30) | copy-start | bytes 6148
  7.2 33.7 %copy-start.46 = (s32[512]{0:T(512)S(1)}, s32[512]{0:T(512)}, u32[]{:S(2)}) copy-start(s32[512]{0:T(512)} %param.29) | copy-start | bytes 6148
  7.2 151.3 %all-gather.2.cloned.1.call-start = ((), (), s32[]{:S(2)}) async-start(), calls=%async_computation | async-start | bytes 12976128 | tf_op jit(solution)/shard_map/all_gather | solution.py:1033
  7.9 434.5 %all-reduce.6.cloned.1.call-start = ((), (), s32[]{:S(2)}) async-start(), calls=%async_computation.1 | async-start | bytes 2359296 | tf_op jit(solution)/shard_map/psum | solution.py:1317
  9.4 56.5 %copy-start.44 = (f32[1536]{0:T(1024)}, f32[1536]{0:T(1024)S(1)}, u32[]{:S(2)}) copy-start(f32[1536]{0:T(1024)S(1)} %convert_element_type.136) | copy-start | bytes 18436
  10.1 5.0 %copy-start.42 = (f32[1536]{0:T(1024)}, f32[1536]{0:T(1024)S(1)}, u32[]{:S(2)}) copy-start(f32[1536]{0:T(1024)S(1)} %convert_element_type.128) | copy-start | bytes 18436
  13.3 24.5 %copy-start.50 = (f32[128]{0:T(128)}, f32[128]{0:T(128)S(1)}, u32[]{:S(2)}) copy-start(f32[128]{0:T(128)S(1)} %get-tuple-element.71) | copy-start | bytes 1540
  36.3 8.2 %copy-start.2 = (bf16[2,2,128,1536]{3,2,1,0:T(8,128)(2,1)S(1)}, bf16[2,2,128,1536]{3,2,1,0:T(8,128)(2,1)}, u32[]{:S(2)}) copy-start(bf16[2,2,128,1536]{3,2,1,0:T(8,128)(2,1)} %get-tuple-element.25) | copy-start | bytes 4718596
  41.3 4.0 copy-start.10
  41.3 4.0 copy-start.12
  45.4 1.9 copy-start.25
  45.5 1.9 copy-start.27
  46.1 2.2 copy-start.29
  47.4 2.7 copy-start.1
  51.3 14.6 %copy-start.33 = (bf16[2,64,3,512]{3,1,2,0:T(8,128)(2,1)}, bf16[2,64,3,512]{3,1,2,0:T(8,128)(2,1)S(1)}, u32[]{:S(2)}) copy-start(bf16[2,64,3,512]{3,1,2,0:T(8,128)(2,1)S(1)} %fusion.9) | copy-start | bytes 1179652
  51.3 14.4 %copy-start.5 = (bf16[128,1536]{1,0:T(8,128)(2,1)S(1)}, bf16[128,1536]{1,0:T(8,128)(2,1)}, u32[]{:S(2)}) copy-start(bf16[128,1536]{1,0:T(8,128)(2,1)} %param.16) | copy-start | bytes 1179652
  66.8 84.7 %copy-start.32 = (bf16[16,1536]{1,0:T(8,128)(2,1)S(1)}, bf16[16,1536]{1,0:T(8,128)(2,1)}, u32[]{:S(2)}) copy-start(bf16[16,1536]{1,0:T(8,128)(2,1)} %param.23) | copy-start | bytes 147460
  66.8 87.9 %copy-start.7 = (bf16[128,1536]{1,0:T(8,128)(2,1)S(1)}, bf16[128,1536]{1,0:T(8,128)(2,1)}, u32[]{:S(2)}) copy-start(bf16[128,1536]{1,0:T(8,128)(2,1)} %multiply_convert_fusion.own) | copy-start | bytes 1179652
  158.5 139.3 %copy-start.45 = (f32[1536]{0:T(1024)S(1)}, f32[1536]{0:T(1024)}, u32[]{:S(2)}) copy-start(f32[1536]{0:T(1024)} %copy-done.44) | copy-start | bytes 18436
  295.9 4.4 copy-start.17
  296.9 3.4 copy-start.22
  316.4 3.5 copy-start.18
  316.4 3.5 copy-start.34
  319.9 6.7 %slice-start = ((s8[6291456]{0:T(1024)(128)(4,1)}), s8[2097152]{0:T(1024)(128)(4,1)S(1)}, s32[]{:S(2)}) async-start(s8[6291456]{0:T(1024)(128)(4,1)} %bitcast.145), calls=%async_computation.2 | async-start | bytes 4194304
  321.7 4.9 %slice-start.1 = ((s8[6291456]{0:T(1024)(128)(4,1)}), s8[4194304]{0:T(1024)(128)(4,1)S(1)}, s32[]{:S(2)}) async-start(s8[6291456]{0:T(1024)(128)(4,1)} %bitcast.145), calls=%async_computation.3 | async-start | bytes 8388608
  321.7 4.9 %copy-start.30 = (bf16[512,128]{0,1:T(8,128)(2,1)S(1)}, bf16[512,128]{0,1:T(8,128)(2,1)}, u32[]{:S(2)}) copy-start(bf16[512,128]{0,1:T(8,128)(2,1)} %copy-done.29) | copy-start | bytes 393220
  321.7 4.9 %copy-start.37 = (bf16[512,384]{0,1:T(8,128)(2,1)S(1)}, bf16[512,384]{0,1:T(8,128)(2,1)}, u32[]{:S(2)}) copy-start(bf16[512,384]{0,1:T(8,128)(2,1)} %convolution_convert_fusion.5) | copy-start | bytes 1179652
  328.6 1.9 copy-start.26
  328.6 1.9 copy-start.28
  330.5 1.8 copy-start.11
  330.5 1.8 copy-start.13
  334.8 2.6 copy-start.47
  334.8 2.7 copy-start.31
  337.5 2.3 copy-start.4
  337.5 2.3 copy-start.36
  340.9 1.9 copy-start.49
  340.9 1.9 copy-start.35
  342.8 82.7 %copy-start.6 = (bf16[128,1536]{1,0:T(8,128)(2,1)S(1)}, bf16[128,1536]{1,0:T(8,128)(2,1)}, u32[]{:S(2)}) copy-start(bf16[128,1536]{1,0:T(8,128)(2,1)} %param.16) | copy-start | bytes 1179652
  342.8 82.7 %copy-start.43 = (f32[1536]{0:T(1024)S(1)}, f32[1536]{0:T(1024)}, u32[]{:S(2)}) copy-start(f32[1536]{0:T(1024)} %copy-done.42) | copy-start | bytes 18436
  342.8 85.4 %copy-start.8 = (f32[128,1536]{1,0:T(8,128)S(1)}, f32[128,1536]{1,0:T(8,128)}, u32[]{:S(2)}) copy-start(f32[128,1536]{1,0:T(8,128)} %get-tuple-element.41) | copy-start | bytes 2359300
  342.8 85.4 %copy-start.51 = (f32[128]{0:T(128)S(1)}, f32[128]{0:T(128)}, u32[]{:S(2)}) copy-start(f32[128]{0:T(128)} %copy-done.50) | copy-start | bytes 1540
  342.8 85.4 %copy-start.52 = (f32[128]{0:T(128)S(1)}, f32[128]{0:T(128)}, u32[]{:S(2)}) copy-start(f32[128]{0:T(128)} %get-tuple-element.70) | copy-start | bytes 1540
  430.6 14.9 %copy-start.9 = (f32[4,2,48,1536]{3,2,1,0:T(8,128)S(1)}, f32[4,2,48,1536]{3,2,1,0:T(8,128)}, u32[]{:S(2)}) copy-start(f32[4,2,48,1536]{3,2,1,0:T(8,128)} %get-tuple-element.32) | copy-start | bytes 7077892
  445.5 2.5 copy-start.23
  445.5 3.4 copy-start.16
  447.1 2.9 copy-start.15
  448.9 2.3 copy-start.14
  (9 other events, 12.0 us)
Sparse Core Ops, SparseCore 0:
  10.9 130.7 all-gather.1
  337.6 104.8 all-reduce.5

commit v6 on v5

--- a/solution.py
+++ b/solution.py
@@ -267,12 +267,6 @@
     return every.reshape(-1, width), tables
 
 
-def group_gather_kernel(ep_size, pieces, own, out, own_sem, sems):
-    me = Place(ep_size)
-    meet([me.sibling(), me.x_peer()])
-    group_gather_body(me, pieces, own, out, own_sem, sems)
-
-
 def group_gather_body(me, pieces, own, out, own_sem, sems):
     size = own.shape[0] // pieces
     started = []
@@ -301,22 +295,6 @@
     local.wait()
     for copy in started:
         copy.wait_send()
-
-
-def group_gather(value_rows, ep_size, call):
-    rows, width = value_rows.shape
-    pieces = 4
-    dma = pltpu.SemaphoreType.DMA
-    every = pl.pallas_call(
-        functools.partial(group_gather_kernel, ep_size, pieces),
-        out_shape=jax.ShapeDtypeStruct((2, 2, rows, width), value_rows.dtype),
-        in_specs=[pl.BlockSpec(memory_space=pl.ANY)],
-        out_specs=pl.BlockSpec(memory_space=pl.ANY),
-        scratch_shapes=[dma, dma((2, 3 * pieces))],
-        compiler_params=pltpu.CompilerParams(collective_id=call, has_side_effects=True),
-        name="group_gather",
-    )(value_rows)
-    return every.reshape(-1, width)
 
 
 class GroupTotal:
@@ -352,17 +330,18 @@
         add_into(self.core_got.at[far], self.parts.at[far, self.me.c])
         self.pair.start()
 
-    def finish(self, out):
+    def finish(self, out, change=lambda value, at: value):
         self.core[1].wait_recv()
         self.pair.wait_recv()
 
         def tile(i, carry):
             at = pl.ds(pl.multiple_of(i * 16, 16), 16)
-            out[at, :] = (
+            value = (
                 self.parts[self.me.x, self.me.c, at, :].astype(jnp.float32)
                 + self.core_got[self.me.x, at, :].astype(jnp.float32)
                 + self.pair_got[at, :].astype(jnp.float32)
             )
+            out[at, :] = change(value, at)
             return carry
 
         lax.fori_loop(0, out.shape[0] // 16, tile, 0)
@@ -800,66 +779,298 @@
     )
 
 
-def tail_kernel(
+class EpSum:
+    def __init__(self, me, grads, outs, y_got, z_got, final, sems):
+        self.me, self.grads, self.outs = me, grads, outs
+        self.y_got, self.z_got, self.final = y_got, z_got, final
+        self.y_sems, self.z_sems, self.fz_sems, self.fy_sems = sems
+        self.counts = [g.shape[2] for g in grads]
+        self.starts = [sum(self.counts[:i]) for i in range(len(grads))]
+        self.finals = []
+
+    def y_copy(self, step, i):
+        me = self.me
+        return pltpu.make_async_remote_copy(
+            src_ref=self.grads[i].at[me.after(step + 1), 1 - me.y],
+            dst_ref=self.y_got.at[step, pl.ds(self.starts[i], self.counts[i])],
+            send_sem=self.y_sems.at[0, step, i],
+            recv_sem=self.y_sems.at[1, step, i],
+            device_id=me.y_peer(),
+            device_id_type=MESH,
+        )
+
+    def z_copy(self, step):
+        return pltpu.make_async_remote_copy(
+            src_ref=self.y_got.at[step],
+            dst_ref=self.z_got.at[step],
+            send_sem=self.z_sems.at[0, step],
+            recv_sem=self.z_sems.at[1, step],
+            device_id=self.me.device(z=self.me.after(step + 1)),
+            device_id_type=MESH,
+        )
+
+    def begin(self):
+        for step in range(self.me.depth):
+            for i in range(len(self.grads)):
+                self.y_copy(step, i).start()
+
+    def fold(self, step):
+        me = self.me
+        for i in range(len(self.grads)):
+            self.y_copy(step, i).wait_recv()
+            add_into(
+                self.y_got.at[step, pl.ds(self.starts[i], self.counts[i])],
+                self.grads[i].at[me.after(step + 1), me.y],
+            )
+        if step < me.depth - 1:
+            self.z_copy(step).start()
+
+    def settle(self):
+        me, depth = self.me, self.me.depth
+        for step in range(depth - 1):
+            self.z_copy(step).wait_recv()
+
+        def tile(i, carry):
+            at = pl.ds(pl.multiple_of(i * 16, 16), 16)
+            value = self.y_got[depth - 1, at, :].astype(jnp.float32)
+            for step in range(depth - 1):
+                value = value + self.z_got[step, at, :].astype(jnp.float32)
+            self.final[me.z, me.y, at, :] = value.astype(self.final.dtype)
+            return carry
+
+        lax.fori_loop(0, sum(self.counts) // 16, tile, 0)
+        mine = self.final.at[me.z, me.y]
+        for s in range(1, depth):
+            self.spread(mine, self.fz_sems, s, me.device(z=me.after(s)))
+        self.spread(mine, self.fy_sems, 0, me.y_peer())
+
+    def spread(self, block, sems, slot, device):
+        self.finals.append(send(block, block, sems.at[0, slot], sems.at[1, slot], device))
+
+    def pass_on(self):
+        me = self.me
+        for s in range(1, me.depth):
+            block = self.final.at[me.before(s), me.y]
+            pltpu.make_async_copy(block, block, self.fz_sems.at[1, s]).wait()
+            self.spread(block, self.fy_sems, s, me.y_peer())
+
+    def deliver(self, y):
+        me = self.me
+        for s in range(me.depth):
+            z = me.before(s)
+            for i, out in enumerate(self.outs):
+
+                def tile(t, carry):
+                    at = pl.multiple_of(t * 16, 16)
+                    out[z, y, pl.ds(at, 16), :] = self.final[
+                        z, y, pl.ds(self.starts[i] + at, 16), :
+                    ].astype(jnp.float32)
+                    return carry
+
+                lax.fori_loop(0, self.counts[i] // 16, tile, 0)
+
+    def finish(self):
+        me = self.me
+        for s in range(me.depth):
+            block = self.final.at[me.before(s), 1 - me.y]
+            pltpu.make_async_copy(block, block, self.fy_sems.at[1, s]).wait()
+        self.deliver(1 - me.y)
+
+    def sent(self):
+        for copy in self.finals:
+            copy.wait_send()
+        for step in range(self.me.depth):
+            for i in range(len(self.grads)):
+                self.y_copy(step, i).wait_send()
+            if step < self.me.depth - 1:
+                self.z_copy(step).wait_send()
+
+
+def visible_columns(info_cols, info_rows):
+    key_seg, key_pos = info_cols[:, 0:1], info_cols[:, 1:2]
+    query_seg, query_pos = info_rows[0:1, :], info_rows[1:2, :]
+    parent = jnp.where(query_seg >= 5, (query_seg - 5) // 2 + 1, -1)
+    above = (key_seg == query_seg) | (key_seg == 0) | (key_seg == parent)
+    return above & (key_pos <= query_pos)
+
+
+def back_kernel(
     ep_size,
-    counts,
-    *refs,
+    heads,
+    last_row,
+    datt_own,
+    heads_in,
+    w_out,
+    queries,
+    keys,
+    values,
+    log_sums,
+    info_cols,
+    info_rows,
+    cosine,
+    sine,
+    rows_in,
+    w_query,
+    w_key,
+    w_value,
+    small_in,
+    gain,
+    inputs,
+    middle,
+    query_out,
+    key_out,
+    value_out,
+    out_out,
+    grad_input,
+    small_out,
+    datt,
+    bias,
+    grad_heads,
+    grad_proj,
+    key_sum,
+    value_sum,
+    part_query,
+    part_key,
+    part_value,
+    part_out,
+    y_got,
+    z_got,
+    final,
+    y_got_out,
+    z_got_out,
+    final_out,
+    parts,
+    core_got,
+    pair_got,
+    small_src,
+    small_got,
+    small_sum,
+    own_sem,
+    gather_sems,
+    y_sems,
+    z_sems,
+    fz_sems,
+    fy_sems,
+    y_sems_out,
+    z_sems_out,
+    fz_sems_out,
+    fy_sems_out,
+    group_sems,
+    small_sems,
+    spread_sems,
+    own_small_sem,
 ):
-    n = len(counts)
-    grads, rows_in, small_in = refs[:n], refs[n], refs[n + 1]
-    outs, rows_out, small_out = refs[n + 2 : 2 * n + 2], refs[2 * n + 2], refs[2 * n + 3]
-    (
+    me = Place(ep_size)
+    depth = me.depth
+    f32, bf16 = jnp.float32, jnp.bfloat16
+    others = all_others(ep_size)
+    meet(others)
+    my_place = lax.axis_index("ep") * 4 + lax.axis_index("tp")
+    tokens, width = rows_in.shape
+    share = datt_own.shape[0]
+    size = HEAD_DIMENSION
+    groups = keys.shape[1] // size
+    per_group = heads // groups
+    scale = size ** (-0.5)
+    tile = 512
+
+    def dot(a, b, contract):
+        return lax.dot_general(
+            a, b, ((contract[:1], contract[1:]), ((), ())), preferred_element_type=f32
+        )
+
+    bias[...] = jnp.where(visible_columns(info_cols[...], info_rows[...]), 0.0, -1e30)
+    group_gather_body(me, 4, datt_own, datt, own_sem, gather_sems)
+    for n in range(width // tile):
+        cols = slice(n * tile, (n + 1) * tile)
+        grads = dot(heads_in[...], datt[:, :, :, cols].reshape(tokens, tile), (0, 0))
+        part_out[:, :, :, cols] = grads.astype(bf16).reshape(depth, 2, -1, tile)
+    out_sum = EpSum(
+        me,
+        [part_out],
+        [out_out],
+        y_got_out,
+        z_got_out,
+        final_out,
+        (y_sems_out, z_sems_out, fz_sems_out, fy_sems_out),
+    )
+    out_sum.begin()
+    for x in range(2):
+        for c in range(2):
+            at = pl.ds((x * 2 + c) * share, share)
+            grad_heads[at, :] = dot(datt[x, c], w_out[...], (1, 1)).astype(bf16)
+
+    def rotate_back_rows(grads):
+        turned = jnp.concatenate([grads[:, size // 2 :], grads[:, : size // 2]], axis=1)
+        return (grads * cosine[...] + turned * sine[...]).astype(bf16)
+
+    for head in range(heads):
+        group = head // per_group
+        mine = slice(head * size, (head + 1) * size)
+        shared = slice(group * size, (group + 1) * size)
+        query, grad_head = queries[:, mine], grad_heads[:, mine]
+        key, value = keys[:, shared], values[:, shared]
+        scores = dot(key, query, (1, 1)) * scale + bias[...]
+        probs = jnp.exp(scores - log_sums[head : head + 1, :])
+        grad_probs = dot(value, grad_head, (1, 1))
+        inner = jnp.sum(probs * grad_probs, axis=0, keepdims=True)
+        grad_scores = (probs * (grad_probs - inner)).astype(bf16)
+        grad_value = dot(probs.astype(bf16), grad_head, (1, 0))
+        grad_key = dot(grad_scores, query, (1, 0)) * scale
+        if head % per_group:
+            grad_value = grad_value + value_sum[...]
+            grad_key = grad_key + key_sum[...]
+        value_sum[...] = grad_value
+        key_sum[...] = grad_key
+        grad_query = dot(grad_scores, key, (0, 0)) * scale
+        grad_proj[:, mine] = rotate_back_rows(grad_query)
+        if head % per_group == per_group - 1:
+            at = heads * size + group * size
+            grad_proj[:, at : at + size] = rotate_back_rows(grad_key)
+            at += groups * size
+            grad_proj[:, at : at + size] = grad_value.astype(bf16)
+        if 1 <= head <= depth:
+            out_sum.fold(head - 1)
+    for step in range(max(heads - 1, 0), depth):
+        out_sum.fold(step)
+    out_sum.settle()
+
+    ends = (heads * size, (heads + groups) * size, (heads + 2 * groups) * size)
+    for n in range(width // tile):
+        cols = slice(n * tile, (n + 1) * tile)
+        grads = dot(grad_proj[...], rows_in[:, cols], (0, 0)).astype(bf16)
+        part_query[:, :, :, cols] = grads[: ends[0]].reshape(depth, 2, -1, tile)
+        part_key[:, :, :, cols] = grads[ends[0] : ends[1]].reshape(depth, 2, -1, tile)
+        part_value[:, :, :, cols] = grads[ends[1] :].reshape(depth, 2, -1, tile)
+    all_sum = EpSum(
+        me,
+        [part_query, part_key, part_value],
+        [query_out, key_out, value_out],
         y_got,
         z_got,
         final,
-        core_got,
-        pair_got,
-        small_got,
-        small_sum,
-        y_sems,
-        z_sems,
-        fz_sems,
-        fy_sems,
-        group_sems,
-        small_sems,
-        spread_sems,
-        own_sem,
-    ) = refs[2 * n + 4 :]
-    me = Place(ep_size)
-    depth = me.depth
-    starts = [sum(counts[:i]) for i in range(n)]
-    others = all_others(ep_size)
-    meet(others)
-    my_place = lax.axis_index("ep") * 4 + lax.axis_index("tp")
-
-    def y_copy(step, i):
-        return pltpu.make_async_remote_copy(
-            src_ref=grads[i].at[me.after(step + 1), 1 - me.y],
-            dst_ref=y_got.at[step, pl.ds(starts[i], counts[i])],
-            send_sem=y_sems.at[0, step, i],
-            recv_sem=y_sems.at[1, step, i],
-            device_id=me.y_peer(),
-            device_id_type=MESH,
-        )
-
-    def z_copy(step):
-        return pltpu.make_async_remote_copy(
-            src_ref=y_got.at[step],
-            dst_ref=z_got.at[step],
-            send_sem=z_sems.at[0, step],
-            recv_sem=z_sems.at[1, step],
-            device_id=me.device(z=me.after(step + 1)),
-            device_id_type=MESH,
-        )
-
-    for step in range(depth):
-        for i in range(n):
-            y_copy(step, i).start()
-    group = GroupTotal(me, rows_in, core_got, pair_got, group_sems)
+        (y_sems, z_sems, fz_sems, fy_sems),
+    )
+    all_sum.begin()
+    small_src[...] = small_in[...]
+    for n in range(width // tile):
+        cols = slice(n * tile, (n + 1) * tile)
+        grads = (
+            dot(grad_proj[:, : ends[0]], w_query[:, cols], (1, 0))
+            + dot(grad_proj[:, ends[0] : ends[1]], w_key[:, cols], (1, 0))
+            + dot(grad_proj[:, ends[1] :], w_value[:, cols], (1, 0))
+        )
+        parts[:, :, :, cols] = grads.astype(bf16).reshape(2, 2, share, tile)
+        gained = jnp.sum(grads * rows_in[:, cols].astype(f32), axis=0, keepdims=True)
+        gained = gained / gain[:, cols]
+        for k in range(tile // 128):
+            row = n * (tile // 128) + k
+            small_src[last_row, row : row + 1, :] = gained[:, k * 128 : (k + 1) * 128]
+    group = GroupTotal(me, parts, core_got, pair_got, group_sems)
     group.begin()
     small = [
         send(
-            small_in.at[device[0] * 4 + device[1]],
+            small_src.at[device[0] * 4 + device[1]],
             small_got.at[my_place],
             small_sems.at[0, k],
             small_sems.at[1, k],
@@ -867,21 +1078,15 @@
         )
         for k, device in enumerate(others)
     ]
-    own_small = pltpu.make_async_copy(small_in.at[my_place], small_got.at[my_place], own_sem)
+    own_small = pltpu.make_async_copy(
+        small_src.at[my_place], small_got.at[my_place], own_small_sem
+    )
     own_small.start()
     group.exchange()
-
-    def y_sum(step):
-        for i in range(n):
-            y_copy(step, i).wait_recv()
-            add_into(
-                y_got.at[step, pl.ds(starts[i], counts[i])],
-                grads[i].at[me.after(step + 1), me.y],
-            )
-
-    for step in range(depth - 1):
-        y_sum(step)
-        z_copy(step).start()
+    all_sum.fold(0)
+    out_sum.pass_on()
+    for step in range(1, depth):
+        all_sum.fold(step)
     own_small.wait()
     for copy in small:
         copy.wait_recv()
@@ -900,117 +1105,142 @@
         for k, device in enumerate(others)
     ]
     small_out[my_place] = total
-    group.finish(rows_out)
-    y_sum(depth - 1)
-    for step in range(depth - 1):
-        z_copy(step).wait_recv()
-
-    def tile(i, carry):
-        at = pl.ds(pl.multiple_of(i * 16, 16), 16)
-        value = y_got[depth - 1, at, :].astype(jnp.float32)
-        for step in range(depth - 1):
-            value = value + z_got[step, at, :].astype(jnp.float32)
-        final[me.z, me.y, at, :] = value.astype(final.dtype)
-        return carry
-
-    lax.fori_loop(0, sum(counts) // 16, tile, 0)
-    mine = final.at[me.z, me.y]
-    finals = []
-    for s in range(1, depth):
-        finals.append(
-            send(mine, mine, fz_sems.at[0, s], fz_sems.at[1, s], me.device(z=me.after(s)))
-        )
-    finals.append(send(mine, mine, fy_sems.at[0, 0], fy_sems.at[1, 0], me.y_peer()))
-    for s in range(1, depth):
-        block = final.at[me.before(s), me.y]
-        pltpu.make_async_copy(block, block, fz_sems.at[1, s]).wait()
-        finals.append(send(block, block, fy_sems.at[0, s], fy_sems.at[1, s], me.y_peer()))
-
-    def deliver(s, y):
-        z = me.before(s)
-        for i in range(n):
-
-            def tile(t, carry):
-                at = pl.multiple_of(t * 16, 16)
-                outs[i][z, y, pl.ds(at, 16), :] = final[
-                    z, y, pl.ds(starts[i] + at, 16), :
-                ].astype(jnp.float32)
-                return carry
-
-            lax.fori_loop(0, counts[i] // 16, tile, 0)
-
-    for s in range(depth):
-        deliver(s, me.y)
-    for s in range(depth):
-        block = final.at[me.before(s), 1 - me.y]
-        pltpu.make_async_copy(block, block, fy_sems.at[1, s]).wait()
-        deliver(s, 1 - me.y)
+
+    def last(value, at):
+        values_own = inputs[at, :].astype(f32)
+        factor = norm_scale(values_own)
+        return middle[at, :] + norm_back(values_own, factor, gain[...], value)
+
+    group.finish(grad_input, last)
+    out_sum.deliver(me.y)
+    out_sum.finish()
+    all_sum.settle()
+    all_sum.pass_on()
+    all_sum.deliver(me.y)
+    all_sum.finish()
     for copy in spread:
         copy.wait()
-    for copy in small + finals:
+    for copy in small:
         copy.wait_send()
     group.sent()
-    for step in range(depth):
-        for i in range(n):
-            y_copy(step, i).wait_send()
-        if step < depth - 1:
-            z_copy(step).wait_send()
-
-
-def tail_by_links(grads, rows_part, small, ep_size):
-    width = rows_part.shape[1]
+    out_sum.sent()
+    all_sum.sent()
+
+
+def back_by_links(
+    datt_own,
+    heads_in,
+    w_out,
+    queries,
+    keys,
+    values,
+    log_sums,
+    segment,
+    position,
+    rows_in,
+    w_query,
+    w_key,
+    w_value,
+    small,
+    gain,
+    inputs,
+    middle,
+    ep_size,
+):
+    tokens, width = rows_in.shape
+    share = datt_own.shape[0]
     depth = ep_size // 2
-    rows = rows_part.shape[0] // 4
-    counts = [g.shape[0] // ep_size for g in grads]
-    total = sum(counts)
+    heads = queries.shape[1] // HEAD_DIMENSION
     places = 4 * ep_size
     bf16, f32 = jnp.bfloat16, jnp.float32
     dma = pltpu.SemaphoreType.DMA
     vmem = pl.BlockSpec(memory_space=pltpu.VMEM)
-    lanes = width // 128
-    blocks = jnp.pad(small, ((0, places - small.shape[0]), (0, 0))).reshape(places, lanes, 128)
+    cosine, sine = rope_tables(position, HEAD_DIMENSION)
+    cosine = jnp.concatenate([cosine[:, 0], cosine[:, 0]], axis=1)
+    sine = jnp.concatenate([sine[:, 0], -sine[:, 0]], axis=1)
+    table = jnp.stack([segment, position])
+    info_rows = jnp.pad(table, ((0, 6), (0, 0)))
+    info_cols = jnp.pad(table.T, ((0, 0), (0, 126)))
+    blocks = jnp.pad(small, ((0, places - small.shape[0]), (0, 0))).reshape(places, -1, 128)
+    sizes = [w.shape[0] // ep_size for w in (w_query, w_key, w_value, w_out)]
+    total = sum(sizes[:3])
+
+    def partial(rows, dtype):
+        return (depth, 2, rows, width), dtype
+
+    def ep_buffers(rows):
+        return [
+            pltpu.VMEM((depth, rows, width), bf16),
+            pltpu.VMEM((depth - 1, rows, width), bf16),
+            pltpu.VMEM((depth, 2, rows, width), bf16),
+        ]
+
+    def ep_sems(arrays):
+        return [dma((2, depth, arrays)), dma((2, depth)), dma((2, depth)), dma((2, depth))]
+
     got = pl.pallas_call(
-        functools.partial(tail_kernel, ep_size, counts),
-        out_shape=tuple(jax.ShapeDtypeStruct((depth, 2, k, width), f32) for k in counts)
+        functools.partial(back_kernel, ep_size, heads, small.shape[0]),
+        out_shape=tuple(jax.ShapeDtypeStruct(*partial(k, f32)) for k in sizes)
         + (
-            jax.ShapeDtypeStruct((rows, width), f32),
+            jax.ShapeDtypeStruct((share, width), f32),
             jax.ShapeDtypeStruct(blocks.shape, f32),
         ),
-        in_specs=[vmem] * (len(grads) + 2),
-        out_specs=(vmem,) * (len(grads) + 2),
+        in_specs=[vmem] * 19,
+        out_specs=(vmem,) * 6,
         scratch_shapes=[
-            pltpu.VMEM((depth, total, width), bf16),
-            pltpu.VMEM((depth - 1, total, width), bf16),
-            pltpu.VMEM((depth, 2, total, width), bf16),
-            pltpu.VMEM((2, rows, width), bf16),
-            pltpu.VMEM((rows, width), bf16),
+            pltpu.VMEM((2, 2, share, width), bf16),
+            pltpu.VMEM((tokens, tokens), f32),
+            pltpu.VMEM(queries.shape, bf16),
+            pltpu.VMEM((tokens, queries.shape[1] + 2 * keys.shape[1]), bf16),
+            pltpu.VMEM((tokens, HEAD_DIMENSION), f32),
+            pltpu.VMEM((tokens, HEAD_DIMENSION), f32),
+        ]
+        + [pltpu.VMEM(*partial(k, bf16)) for k in sizes]
+        + ep_buffers(total)
+        + ep_buffers(sizes[3])
+        + [
+            pltpu.VMEM((2, 2, share, width), bf16),
+            pltpu.VMEM((2, share, width), bf16),
+            pltpu.VMEM((share, width), bf16),
+            pltpu.VMEM(blocks.shape, f32),
             pltpu.VMEM(blocks.shape, f32),
             pltpu.VMEM(blocks.shape[1:], f32),
-            dma((2, depth, len(grads))),
-            dma((2, depth)),
-            dma((2, depth)),
-            dma((2, depth)),
-            dma((2, 3)),
-            dma((2, places - 1)),
-            dma((2, places - 1)),
             dma,
-        ],
+            dma((2, 12)),
+        ]
+        + ep_sems(3)
+        + ep_sems(1)
+        + [dma((2, 3)), dma((2, places - 1)), dma((2, places - 1)), dma],
         compiler_params=pltpu.CompilerParams(
-            collective_id=5, has_side_effects=True, vmem_limit_bytes=56 * 1024 * 1024
+            collective_id=5, has_side_effects=True, vmem_limit_bytes=60 * 1024 * 1024
         ),
-        name="tail_by_links",
+        name="back_by_links",
     )(
-        *[g.reshape(depth, 2, k, width) for g, k in zip(grads, counts)],
-        rows_part.reshape(2, 2, rows, width),
+        datt_own,
+        heads_in,
+        w_out,
+        queries,
+        keys,
+        values,
+        log_sums,
+        info_cols,
+        info_rows,
+        cosine,
+        sine,
+        rows_in,
+        w_query,
+        w_key,
+        w_value,
         blocks,
-    )
-    sums = [g.reshape(-1, width) for g in got[: len(grads)]]
-    return sums, got[-2], got[-1].reshape(places, width)[: small.shape[0]]
-
-
-def group_rows(value_rows, by_links, call):
-    if by_links:
-        return group_gather(value_rows, lax.axis_size("ep"), call)
+        gain[None, :],
+        inputs,
+        middle,
+    )
+    sums = [g.reshape(-1, width) for g in got[:4]]
+    return sums, got[4], got[5].reshape(places, width)[: small.shape[0] + 1]
+
+
+def group_rows(value_rows):
     return lax.all_gather(value_rows, "tp", axis=0, tiled=True)
 
 
@@ -1018,13 +1248,6 @@
     if by_links:
         return group_total(value_rows, lax.axis_size("ep"), call)
     return lax.psum_scatter(value_rows, "tp", scatter_dimension=0, tiled=True).astype(jnp.float32)
-
-
-def tail_totals(grads, rows_part, small, by_links):
-    if by_links:
-        return tail_by_links(grads, rows_part, small, lax.axis_size("ep"))
-    sums = [lax.psum(g, "ep").astype(jnp.float32) for g in grads]
-    return sums, group_totals(rows_part, by_links, None), lax.psum(small, ("ep", "tp"))
 
 
 def gather_all(value_rows, by_links):
@@ -1257,7 +1480,7 @@
     if by_links:
         first_normalized, order_all = front_gather(first_own, order, lax.axis_size("ep"))
     else:
-        first_normalized = group_rows(first_own, by_links, None)
+        first_normalized = group_rows(first_own)
         order_all = lax.all_gather(order, "ep")
     code = pair_codes(order_all, per_owner)
     cosine_lookup, sine_lookup = rope_tables(position, head_width)
@@ -1310,63 +1533,85 @@
     grad_middle = cotangent.astype(jnp.float32) + norm_back(
         middle_own, scale_two, gain_two, grad_normed_own
     )
-    grad_attn = group_rows(grad_middle.astype(jnp.bfloat16), by_links, 7)
-    grad_w_out = jnp.einsum(
-        "rf,rd->fd", head_outputs, grad_attn, preferred_element_type=jnp.float32
-    )
-    grad_w_out = lax.psum(grad_w_out.astype(jnp.bfloat16), "ep").astype(jnp.float32)
-    grad_heads = (
-        jnp.einsum("rd,fd->rf", grad_attn, w_out, preferred_element_type=jnp.float32)
-        .astype(jnp.bfloat16)
-        .reshape(token_count, local_kv, group_factor, head_width)
-    )
-    grad_query, grad_keys, grad_values = attend_backward(
-        query_rows, key_rows, value_rows, segment, position, log_sums, grad_heads, block_rows
-    )
-    grad_query_proj = (
-        rotate_back(
-            grad_query.reshape(token_count, local_heads, head_width), cosine_lookup, sine_lookup
-        )
-        .astype(jnp.bfloat16)
-        .reshape(token_count, local_heads * head_width)
-    )
-    grad_key_proj = (
-        rotate_back(grad_keys, cosine_lookup, sine_lookup)
-        .astype(jnp.bfloat16)
-        .reshape(token_count, local_kv * head_width)
-    )
-    grad_value_proj = grad_values.astype(jnp.bfloat16).reshape(token_count, local_kv * head_width)
-    grad_w_query = jnp.einsum(
-        "rf,rd->fd", grad_query_proj, first_normalized, preferred_element_type=jnp.float32
-    )
-    grad_w_key = jnp.einsum(
-        "rf,rd->fd", grad_key_proj, first_normalized, preferred_element_type=jnp.float32
-    )
-    grad_w_value = jnp.einsum(
-        "rf,rd->fd", grad_value_proj, first_normalized, preferred_element_type=jnp.float32
-    )
-    grad_normed_one = jnp.einsum(
-        "rf,fd->rd", grad_query_proj, w_query, preferred_element_type=jnp.float32
-    )
-    grad_normed_one = grad_normed_one + jnp.einsum(
-        "rf,fd->rd", grad_key_proj, key_projection_weight, preferred_element_type=jnp.float32
-    )
-    grad_normed_one = grad_normed_one + jnp.einsum(
-        "rf,fd->rd", grad_value_proj, value_projection_weight, preferred_element_type=jnp.float32
-    )
-    grad_gain_attn = jnp.sum(grad_normed_one * first_normalized.astype(jnp.float32), axis=0)
-    small = jnp.concatenate(
-        [grad_router, grad_gain_ffn[None, :], (grad_gain_attn / gain_one)[None, :]], axis=0
-    )
-    (grad_w_query, grad_w_key, grad_w_value), grad_one_own, small = tail_totals(
-        [g.astype(jnp.bfloat16) for g in (grad_w_query, grad_w_key, grad_w_value)],
-        grad_normed_one.astype(jnp.bfloat16),
-        small,
-        by_links,
-    )
+    if by_links:
+        (grad_w_query, grad_w_key, grad_w_value, grad_w_out), grad_input, small = back_by_links(
+            grad_middle.astype(jnp.bfloat16),
+            head_outputs,
+            w_out,
+            query_rows.reshape(token_count, -1),
+            key_rows.reshape(token_count, -1),
+            value_rows.reshape(token_count, -1),
+            jnp.pad(log_sums[0].reshape(local_heads, token_count), ((0, -local_heads % 8), (0, 0))),
+            segment,
+            position,
+            first_normalized,
+            w_query,
+            key_projection_weight,
+            value_projection_weight,
+            jnp.concatenate([grad_router, grad_gain_ffn[None, :]], axis=0),
+            gain_one,
+            hidden_in,
+            grad_middle,
+            lax.axis_size("ep"),
+        )
+    else:
+        grad_attn = group_rows(grad_middle.astype(jnp.bfloat16))
+        grad_w_out = jnp.einsum(
+            "rf,rd->fd", head_outputs, grad_attn, preferred_element_type=jnp.float32
+        )
+        grad_w_out = lax.psum(grad_w_out.astype(jnp.bfloat16), "ep").astype(jnp.float32)
+        grad_heads = (
+            jnp.einsum("rd,fd->rf", grad_attn, w_out, preferred_element_type=jnp.float32)
+            .astype(jnp.bfloat16)
+            .reshape(token_count, local_kv, group_factor, head_width)
+        )
+        grad_query, grad_keys, grad_values = attend_backward(
+            query_rows, key_rows, value_rows, segment, position, log_sums, grad_heads, block_rows
+        )
+        grad_query_proj = (
+            rotate_back(
+                grad_query.reshape(token_count, local_heads, head_width), cosine_lookup, sine_lookup
+            )
+            .astype(jnp.bfloat16)
+            .reshape(token_count, local_heads * head_width)
+        )
+        grad_key_proj = (
+            rotate_back(grad_keys, cosine_lookup, sine_lookup)
+            .astype(jnp.bfloat16)
+            .reshape(token_count, local_kv * head_width)
+        )
+        grad_value_proj = grad_values.astype(jnp.bfloat16).reshape(token_count, local_kv * head_width)
+        grad_w_query = jnp.einsum(
+            "rf,rd->fd", grad_query_proj, first_normalized, preferred_element_type=jnp.float32
+        )
+        grad_w_key = jnp.einsum(
+            "rf,rd->fd", grad_key_proj, first_normalized, preferred_element_type=jnp.float32
+        )
+        grad_w_value = jnp.einsum(
+            "rf,rd->fd", grad_value_proj, first_normalized, preferred_element_type=jnp.float32
+        )
+        grad_normed_one = jnp.einsum(
+            "rf,fd->rd", grad_query_proj, w_query, preferred_element_type=jnp.float32
+        )
+        grad_normed_one = grad_normed_one + jnp.einsum(
+            "rf,fd->rd", grad_key_proj, key_projection_weight, preferred_element_type=jnp.float32
+        )
+        grad_normed_one = grad_normed_one + jnp.einsum(
+            "rf,fd->rd", grad_value_proj, value_projection_weight, preferred_element_type=jnp.float32
+        )
+        grad_gain_attn = jnp.sum(grad_normed_one * first_normalized.astype(jnp.float32), axis=0)
+        small = jnp.concatenate(
+            [grad_router, grad_gain_ffn[None, :], (grad_gain_attn / gain_one)[None, :]], axis=0
+        )
+        grad_w_query, grad_w_key, grad_w_value = (
+            lax.psum(g.astype(jnp.bfloat16), "ep").astype(jnp.float32)
+            for g in (grad_w_query, grad_w_key, grad_w_value)
+        )
+        grad_one_own = group_totals(grad_normed_one.astype(jnp.bfloat16), by_links, None)
+        small = lax.psum(small, ("ep", "tp"))
+        grad_input = grad_middle + norm_back(inputs_own, scale_one, gain_one, grad_one_own)
     grad_router = small[:expert_count]
     grad_gain_ffn, grad_gain_attn = small[expert_count], small[expert_count + 1]
-    grad_input = grad_middle + norm_back(inputs_own, scale_one, gain_one, grad_one_own)
     return (
         output_own,
         grad_input,

time: 460 us -> 450 us (0.978)
  Pallas kernels: 351 us -> 376 us
  matrix products: 33.5 us -> 10 us
  waiting for transfers between devices: 12.6 us -> 0.68 us
  other arithmetic: 26.1 us -> 16.5 us
  local copies, waits for them, and re-layouts: 20.6 us -> 28.7 us
    dot_general x12 -> x0, matrix products: 23 us -> none  [the longest x1 4.88 us: attend_backward(): jnp.einsum('kgqp,qkgd->pkd', probs.astype(jnp.bfloat16), grad_heads, pref...]
    pallas_call x2 -> x1, Pallas kernels: 94.8 us -> 116 us  [back_by_links(): pl.pallas_call(functools.partial(back_kernel, ep_size, heads, small.shape...]
    psum x1 -> x0, waiting for transfers between devices: 11.9 us -> none  [local(): lax.psum(grad_w_out.astype(jnp.bfloat16), 'ep').astype(jnp.float32)]
    convert_element_type x5 -> x2, other arithmetic: 6.34 us -> 1.49 us  [the longest x1 1.48 us: local(): grad_middle.astype(jnp.bfloat16)]
    unnamed x118 -> x77, local copies, waits for them, and re-layouts: 11.9 us -> 16.4 us
  transfers between devices with their start and end apart: 2 -> 1, of which waited for: 1 -> 0; matrix products, arithmetic and copies ran while one was open for 9% -> 7% of each run, Pallas kernels for 43% -> 28%
where the time goes in v6:
time: 450 us; the launch traced here: 446 us
  Pallas kernels  376 us (84%)
  local copies, waits for them, and re-layouts  28.7 us (6%)
  other arithmetic  16.5 us (4%)
  between operations  14.6 us (3%)
  matrix products  10 us (2%)
    pallas_call x1, Pallas kernels, experts_by_links(): pl.pallas_call(functools.partial(experts_kernel, ep_size, per_owner), out...  134 us
    pallas_call x1, Pallas kernels, back_by_links(): pl.pallas_call(functools.partial(back_kernel, ep_size, heads, small.shape...  116 us
    pallas_call x1, Pallas kernels, gather_by_links(): pl.pallas_call(functools.partial(gather_kernel, ep_size), out_shape=jax.S...  86.2 us
    pallas_call x1, Pallas kernels, front_gather(): pl.pallas_call(functools.partial(front_gather_kernel, ep_size, pieces), o...  21.1 us
    pallas_call x1, Pallas kernels, group_total(): pl.pallas_call(functools.partial(group_total_kernel, ep_size), out_shape=...  17.3 us
    unnamed x77, local copies, waits for them, and re-layouts  16.4 us
  transfers between devices with their start and end apart: 1, of which 0 were waited for; matrix products, arithmetic and copies ran while one was open for 7% of the time, Pallas kernels for 28%

profile of v6, /device:TPU:0, one launch (start us, length us, event | category | flops | bytes accessed | tf_op | source)
XLA Modules:
  0.0 446.1 jit_solution(12855963488550341501)
XLA Ops:
  7.2 0.7 all-gather.2.cloned.1.call-update
  8.0 0.7 convert_element_type.77
  8.7 1.3 broadcast_in_dim.127.gain
  9.9 0.7 convert_element_type.80
  10.6 1.8 fusion.14
  12.6 1.6 select_reduce_fusion.table
  14.2 1.2 fusion.4
  15.4 0.9 fusion.6.own
  16.3 21.1 %front_gather.1 = (bf16[2,2,128,1536]{3,2,1,0:T(8,128)(2,1)}, s32[8,16,512]{2,1,0:T(8,128)}) custom-call(bf16[128,1536]{1,0:T(8,128)(2,1)} %fusion.6.own, s32[16,512]{1,0:T(8,128)} %select_reduce_fusion.table), custom_call_target="tpu_custom_call" | custom-call | tf_op jit(solution)/shard_map/front_gather/pallas_call | solution.py:255
  37.4 2.1 convolution_convert_fusion.1.values
  39.7 0.8 compare_and_fusion
  41.3 0.8 fusion.39
  42.2 1.2 fusion.1
  43.4 1.3 fusion
  44.7 2.0 fusion.3
  46.7 0.9 copy.103.heads_in
  47.6 1.0 convolution_convert_fusion
  48.6 17.3 %group_total.1 = f32[128,1536]{1,0:T(8,128)S(1)} custom-call(bf16[2,2,128,1536]{3,2,1,0:T(8,128)(2,1)S(1)} %bitcast.99), custom_call_target="tpu_custom_call" | custom-call | tf_op jit(solution)/shard_map/group_total/pallas_call | solution.py:367
  68.5 0.9 multiply_convert_fusion.own
  69.3 86.2 %gather_by_links.1 = bf16[4,2,2,2,128,1536]{5,4,3,2,1,0:T(8,128)(2,1)} custom-call(bf16[128,1536]{1,0:T(8,128)(2,1)} %multiply_convert_fusion.own), custom_call_target="tpu_custom_call" | custom-call | tf_op jit(solution)/shard_map/gather_by_links/pallas_call | solution.py:204
  155.7 0.9 copy.104.queries
  156.6 0.7 copy.105.keys
  157.5 0.7 pad.33.clone.info_cols
  158.9 1.2 pad.30.clone
  160.1 0.8 pad.31.router
  161.7 0.7 select_reduce_fusion.2
  162.5 1.0 pad_maximum_fusion.2
  163.6 1.3 pad_maximum_fusion.enter
  164.9 134.5 %experts_by_links.1 = (f32[128,1536]{1,0:T(8,128)}, f32[128,1536]{1,0:T(8,128)}, f32[8,2,8,128]{3,2,1,0:T(8,128)}, f32[2,1536,128]{2,1,0:T(8,128)}, f32[2,1536,128]{2,1,0:T(8,128)}, /*index=5*/f32[256,1536]{1,0:T(8,128)}) custom-call(bf16[4,2,4,128,1536]{4,3,2,1,0:T(8,128)(2,1)} %bitcast.100, bf16[4,2,4,128,1536]{4,3,2,1,0:T(8,128)(2,1)} %bitcast.101, ...), custom_call_target="tpu_custom_call" | custom-call | tf_op jit(solution)/shard_map/experts_by_links/pallas_call | solution.py:735
  299.4 0.9 slice_bitcast_fusion.4
  300.7 1.9 multiply_reduce_fusion
  302.7 0.7 reshape.477.small_in
  303.4 1.5 fusion.36
  304.9 116.5 %back_by_links.1 = (f32[4,2,48,1536]{3,2,1,0:T(8,128)}, f32[4,2,16,1536]{3,2,1,0:T(8,128)}, f32[4,2,16,1536]{3,2,1,0:T(8,128)}, f32[4,2,48,1536]{3,2,1,0:T(8,128...) custom-call(bf16[128,1536]{1,0:T(8,128)(2,1)} %get-tuple-element.42.datt_own, bf16[512,384]{1,0:T(8,128)(2,1)} %copy.103.heads_in, ...), custom_call_target="tpu_custom_call" | custom-call | tf_op jit(solution)/shard_map/back_by_links/pallas_call | solution.py:1181
  421.4 0.9 slice.61
  422.3 1.3 slice_bitcast_fusion.5
  423.6 0.7 copy.117
  424.3 2.1 copy.126
  426.3 3.3 copy.127
  429.7 0.9 copy.128
  430.6 0.9 copy.129
  431.9 1.4 copy.130
  433.3 0.9 copy-done.12
  434.1 1.1 copy.131
  435.3 0.8 copy-done.11
  436.1 1.1 copy.132
  437.3 0.8 copy-done.10
  438.1 1.1 copy.133
  (109 shorter events, 6.4 us)
Async XLA Ops:
  7.2 8.2 %copy-start = (bf16[128,1536]{1,0:T(8,128)(2,1)S(1)}, bf16[128,1536]{1,0:T(8,128)(2,1)}, u32[]{:S(2)}) copy-start(bf16[128,1536]{1,0:T(8,128)(2,1)} %inputs.1) | copy-start | bytes 1179652
  7.2 30.2 %copy-start.9 = (bf16[128,1536]{1,0:T(8,128)(2,1)S(1)}, bf16[128,1536]{1,0:T(8,128)(2,1)}, u32[]{:S(2)}) copy-start(bf16[128,1536]{1,0:T(8,128)(2,1)} %w_value.1) | copy-start | bytes 1179652
  7.2 157.7 %all-gather.2.cloned.1.call-start = ((), (), s32[]{:S(2)}) async-start(), calls=%async_computation | async-start | bytes 12976128 | tf_op jit(solution)/shard_map/all_gather | solution.py:1256
  12.4 27.3 %copy-start.4 = (f32[512,32]{1,0:T(8,128)}, f32[512,32]{1,0:T(8,128)S(1)}, u32[]{:S(2)}) copy-start(f32[512,32]{1,0:T(8,128)S(1)} %get-tuple-element.64) | copy-start | bytes 196612
  12.4 27.3 %copy-start.6 = (f32[512,32]{1,0:T(8,128)}, f32[512,32]{1,0:T(8,128)S(1)}, u32[]{:S(2)}) copy-start(f32[512,32]{1,0:T(8,128)S(1)} %get-tuple-element.65) | copy-start | bytes 196612
  12.4 27.2 %copy-start.27 = (s32[512]{0:T(512)S(1)}, s32[512]{0:T(512)}, u32[]{:S(2)}) copy-start(s32[512]{0:T(512)} %param.29) | copy-start | bytes 6148
  12.4 27.3 %copy-start.28 = (s32[512]{0:T(512)S(1)}, s32[512]{0:T(512)}, u32[]{:S(2)}) copy-start(s32[512]{0:T(512)} %param.30) | copy-start | bytes 6148
  12.5 28.0 %copy-start.24 = (bf16[128,1536]{1,0:T(8,128)(2,1)S(1)}, bf16[128,1536]{1,0:T(8,128)(2,1)}, u32[]{:S(2)}) copy-start(bf16[128,1536]{1,0:T(8,128)(2,1)} %w_key.1) | copy-start | bytes 1179652
  37.4 3.1 copy-start.2
  39.5 2.6 copy-start.14
  39.7 1.6 copy-start.15
  41.2 1.0 copy-start.25
  44.7 2.9 copy-start.3
  47.6 18.3 %copy-start.31 = (bf16[1536]{0:T(1024)(128)(2,1)S(1)}, bf16[1536]{0:T(1024)(128)(2,1)}, u32[]{:S(2)}) copy-start(bf16[1536]{0:T(1024)(128)(2,1)} %param.22) | copy-start | bytes 9220
  47.6 18.3 %copy-start.16 = (s32[8,16,512]{2,1,0:T(8,128)S(1)}, s32[8,16,512]{2,1,0:T(8,128)}, u32[]{:S(2)}) copy-start(s32[8,16,512]{2,1,0:T(8,128)} %get-tuple-element.27) | copy-start | bytes 786436
  68.5 87.1 %copy-start.29 = (f32[128]{0:T(128)}, f32[128]{0:T(128)S(1)}, u32[]{:S(2)}) copy-start(f32[128]{0:T(128)S(1)} %get-tuple-element.70) | copy-start | bytes 1540
  69.3 87.2 %copy-start.26 = (bf16[512,2,32]{0,2,1:T(8,128)(2,1)S(1)}, bf16[512,2,32]{0,2,1:T(8,128)(2,1)}, u32[]{:S(2)}) copy-start(bf16[512,2,32]{0,2,1:T(8,128)(2,1)} %copy-done.25) | copy-start | bytes 196612
  155.6 4.4 copy-start.23
  155.7 5.8 %copy-start.1 = (bf16[128,1536]{1,0:T(8,128)(2,1)S(1)}, bf16[128,1536]{1,0:T(8,128)(2,1)}, u32[]{:S(2)}) copy-start(bf16[128,1536]{1,0:T(8,128)(2,1)} %multiply_convert_fusion.own) | copy-start | bytes 1179652
  156.6 5.9 %copy-start.5 = (f32[512,32]{1,0:T(8,128)S(1)}, f32[512,32]{1,0:T(8,128)}, u32[]{:S(2)}) copy-start(f32[512,32]{1,0:T(8,128)} %copy-done.4) | copy-start | bytes 196612
  156.6 5.9 %copy-start.7 = (f32[512,32]{1,0:T(8,128)S(1)}, f32[512,32]{1,0:T(8,128)}, u32[]{:S(2)}) copy-start(f32[512,32]{1,0:T(8,128)} %copy-done.6) | copy-start | bytes 196612
  156.6 5.9 %copy-start.17 = (f32[512,32]{1,0:T(8,128)S(1)}, f32[512,32]{1,0:T(8,128)}, u32[]{:S(2)}) copy-start(f32[512,32]{1,0:T(8,128)} %get-tuple-element.63) | copy-start | bytes 196612
  160.0 3.4 copy-start.21
  160.0 3.4 copy-start.22
  164.9 135.8 %copy-start.30 = (f32[128]{0:T(128)S(1)}, f32[128]{0:T(128)}, u32[]{:S(2)}) copy-start(f32[128]{0:T(128)} %copy-done.29) | copy-start | bytes 1540
  299.4 4.0 copy-start.13
  299.4 4.0 copy-start.18
  299.4 4.0 copy-start.32
  426.3 3.3 copy-start.20
  426.3 4.2 copy-start.19
  429.7 2.2 copy-start.8
  431.9 2.3 copy-start.12
  434.1 2.0 copy-start.11
  436.1 2.0 copy-start.10
Sparse Core Ops, SparseCore 0:
  10.9 133.0 all-gather.1

commit v7 on v6

--- a/solution.py
+++ b/solution.py
@@ -780,8 +780,8 @@
 
 
 class EpSum:
-    def __init__(self, me, grads, outs, y_got, z_got, final, sems):
-        self.me, self.grads, self.outs = me, grads, outs
+    def __init__(self, me, grads, y_got, z_got, final, sems):
+        self.me, self.grads = me, grads
         self.y_got, self.z_got, self.final = y_got, z_got, final
         self.y_sems, self.z_sems, self.fz_sems, self.fy_sems = sems
         self.counts = [g.shape[2] for g in grads]
@@ -854,27 +854,11 @@
             pltpu.make_async_copy(block, block, self.fz_sems.at[1, s]).wait()
             self.spread(block, self.fy_sems, s, me.y_peer())
 
-    def deliver(self, y):
-        me = self.me
-        for s in range(me.depth):
-            z = me.before(s)
-            for i, out in enumerate(self.outs):
-
-                def tile(t, carry):
-                    at = pl.multiple_of(t * 16, 16)
-                    out[z, y, pl.ds(at, 16), :] = self.final[
-                        z, y, pl.ds(self.starts[i] + at, 16), :
-                    ].astype(jnp.float32)
-                    return carry
-
-                lax.fori_loop(0, self.counts[i] // 16, tile, 0)
-
     def finish(self):
         me = self.me
         for s in range(me.depth):
             block = self.final.at[me.before(s), 1 - me.y]
             pltpu.make_async_copy(block, block, self.fy_sems.at[1, s]).wait()
-        self.deliver(1 - me.y)
 
     def sent(self):
         for copy in self.finals:
@@ -917,10 +901,9 @@
     gain,
     inputs,
     middle,
-    query_out,
-    key_out,
-    value_out,
-    out_out,
+    first_final,
+    second_final,
+    out_final,
     grad_input,
     small_out,
     datt,
@@ -935,10 +918,8 @@
     part_out,
     y_got,
     z_got,
-    final,
     y_got_out,
     z_got_out,
-    final_out,
     parts,
     core_got,
     pair_got,
@@ -988,10 +969,9 @@
     out_sum = EpSum(
         me,
         [part_out],
-        [out_out],
         y_got_out,
         z_got_out,
-        final_out,
+        out_final,
         (y_sems_out, z_sems_out, fz_sems_out, fy_sems_out),
     )
     out_sum.begin()
@@ -1033,25 +1013,30 @@
             out_sum.fold(head - 1)
     for step in range(max(heads - 1, 0), depth):
         out_sum.fold(step)
-    out_sum.settle()
 
     ends = (heads * size, (heads + groups) * size, (heads + 2 * groups) * size)
-    for n in range(width // tile):
-        cols = slice(n * tile, (n + 1) * tile)
+    wide = width // 2
+    sums = []
+    for n, final in enumerate((first_final, second_final)):
+        cols = slice(n * wide, (n + 1) * wide)
         grads = dot(grad_proj[...], rows_in[:, cols], (0, 0)).astype(bf16)
-        part_query[:, :, :, cols] = grads[: ends[0]].reshape(depth, 2, -1, tile)
-        part_key[:, :, :, cols] = grads[ends[0] : ends[1]].reshape(depth, 2, -1, tile)
-        part_value[:, :, :, cols] = grads[ends[1] :].reshape(depth, 2, -1, tile)
-    all_sum = EpSum(
-        me,
-        [part_query, part_key, part_value],
-        [query_out, key_out, value_out],
-        y_got,
-        z_got,
-        final,
-        (y_sems, z_sems, fz_sems, fy_sems),
-    )
-    all_sum.begin()
+        part_query[n] = grads[: ends[0]].reshape(depth, 2, -1, wide)
+        part_key[n] = grads[ends[0] : ends[1]].reshape(depth, 2, -1, wide)
+        part_value[n] = grads[ends[1] :].reshape(depth, 2, -1, wide)
+        sums.append(
+            EpSum(
+                me,
+                [part_query.at[n], part_key.at[n], part_value.at[n]],
+                y_got.at[n],
+                z_got.at[n],
+                final,
+                (y_sems.at[n], z_sems.at[n], fz_sems.at[n], fy_sems.at[n]),
+            )
+        )
+        sums[n].begin()
+        if n == 0:
+            out_sum.settle()
+    first_sum, second_sum = sums
     small_src[...] = small_in[...]
     for n in range(width // tile):
         cols = slice(n * tile, (n + 1) * tile)
@@ -1083,10 +1068,11 @@
     )
     own_small.start()
     group.exchange()
-    all_sum.fold(0)
+    first_sum.fold(0)
     out_sum.pass_on()
     for step in range(1, depth):
-        all_sum.fold(step)
+        first_sum.fold(step)
+    second_sum.fold(0)
     own_small.wait()
     for copy in small:
         copy.wait_recv()
@@ -1112,19 +1098,23 @@
         return middle[at, :] + norm_back(values_own, factor, gain[...], value)
 
     group.finish(grad_input, last)
-    out_sum.deliver(me.y)
+    second_sum.fold(1)
+    first_sum.settle()
+    for step in range(2, depth):
+        second_sum.fold(step)
+    first_sum.pass_on()
+    second_sum.settle()
     out_sum.finish()
-    all_sum.settle()
-    all_sum.pass_on()
-    all_sum.deliver(me.y)
-    all_sum.finish()
+    second_sum.pass_on()
+    first_sum.finish()
+    second_sum.finish()
     for copy in spread:
         copy.wait()
     for copy in small:
         copy.wait_send()
     group.sent()
-    out_sum.sent()
-    all_sum.sent()
+    for each in [out_sum] + sums:
+        each.sent()
 
 
 def back_by_links(
@@ -1165,28 +1155,21 @@
     sizes = [w.shape[0] // ep_size for w in (w_query, w_key, w_value, w_out)]
     total = sum(sizes[:3])
 
-    def partial(rows, dtype):
-        return (depth, 2, rows, width), dtype
-
-    def ep_buffers(rows):
-        return [
-            pltpu.VMEM((depth, rows, width), bf16),
-            pltpu.VMEM((depth - 1, rows, width), bf16),
-            pltpu.VMEM((depth, 2, rows, width), bf16),
-        ]
-
-    def ep_sems(arrays):
-        return [dma((2, depth, arrays)), dma((2, depth)), dma((2, depth)), dma((2, depth))]
-
+    def partial(rows, columns):
+        return (depth, 2, rows, columns), bf16
+
+    wide = width // 2
     got = pl.pallas_call(
         functools.partial(back_kernel, ep_size, heads, small.shape[0]),
-        out_shape=tuple(jax.ShapeDtypeStruct(*partial(k, f32)) for k in sizes)
-        + (
+        out_shape=(
+            jax.ShapeDtypeStruct(*partial(total, wide)),
+            jax.ShapeDtypeStruct(*partial(total, wide)),
+            jax.ShapeDtypeStruct(*partial(sizes[3], width)),
             jax.ShapeDtypeStruct((share, width), f32),
             jax.ShapeDtypeStruct(blocks.shape, f32),
         ),
         in_specs=[vmem] * 19,
-        out_specs=(vmem,) * 6,
+        out_specs=(vmem,) * 5,
         scratch_shapes=[
             pltpu.VMEM((2, 2, share, width), bf16),
             pltpu.VMEM((tokens, tokens), f32),
@@ -1195,10 +1178,13 @@
             pltpu.VMEM((tokens, HEAD_DIMENSION), f32),
             pltpu.VMEM((tokens, HEAD_DIMENSION), f32),
         ]
-        + [pltpu.VMEM(*partial(k, bf16)) for k in sizes]
-        + ep_buffers(total)
-        + ep_buffers(sizes[3])
+        + [pltpu.VMEM((2, depth, 2, k, wide), bf16) for k in sizes[:3]]
         + [
+            pltpu.VMEM((depth, 2, sizes[3], width), bf16),
+            pltpu.VMEM((2, depth, total, wide), bf16),
+            pltpu.VMEM((2, depth - 1, total, wide), bf16),
+            pltpu.VMEM((depth, sizes[3], width), bf16),
+            pltpu.VMEM((depth - 1, sizes[3], width), bf16),
             pltpu.VMEM((2, 2, share, width), bf16),
             pltpu.VMEM((2, share, width), bf16),
             pltpu.VMEM((share, width), bf16),
@@ -1208,8 +1194,10 @@
             dma,
             dma((2, 12)),
         ]
-        + ep_sems(3)
-        + ep_sems(1)
+        + [dma((2, 2, depth, 3))]
+        + [dma((2, 2, depth))] * 3
+        + [dma((2, depth, 1))]
+        + [dma((2, depth))] * 3
         + [dma((2, 3)), dma((2, places - 1)), dma((2, places - 1)), dma],
         compiler_params=pltpu.CompilerParams(
             collective_id=5, has_side_effects=True, vmem_limit_bytes=60 * 1024 * 1024
@@ -1236,8 +1224,114 @@
         inputs,
         middle,
     )
-    sums = [g.reshape(-1, width) for g in got[:4]]
-    return sums, got[4], got[5].reshape(places, width)[: small.shape[0] + 1]
+    return got
+
+
+def deliver_kernel(
+    ep_size,
+    sizes,
+    gate_in,
+    up_in,
+    down_in,
+    rows_in,
+    sums_in,
+    first,
+    second,
+    third,
+    small,
+    gate_out,
+    up_out,
+    down_out,
+    rows_out,
+    sums_out,
+    query_out,
+    key_out,
+    value_out,
+    out_out,
+    router_out,
+    first_gain,
+    second_gain,
+    query,
+    key,
+    value,
+    out,
+    sems,
+):
+    pairs = ((gate_in, gate_out), (up_in, up_out), (down_in, down_out), (rows_in, rows_out))
+    pairs += ((sums_in, sums_out),)
+    copies = [
+        pltpu.make_async_copy(source, target, sems.at[i]) for i, (source, target) in enumerate(pairs)
+    ]
+    for copy in copies:
+        copy.start()
+    wide = first.shape[2]
+    f32 = jnp.float32
+
+    def leave(source, target, i):
+        copies.append(pltpu.make_async_copy(source, target, sems.at[i]))
+        copies[-1].start()
+
+    out[...] = third[...].astype(f32)
+    leave(out, out_out, 5)
+    at = 0
+    for i, (source, target) in enumerate(((query, query_out), (key, key_out), (value, value_out))):
+        for n, part in enumerate((first, second)):
+            source[:, :, n * wide : (n + 1) * wide] = part[:, at : at + sizes[i], :].astype(f32)
+        at += sizes[i]
+        leave(source, target, 6 + i)
+    experts = router_out.shape[0]
+    for j in range(small.shape[1]):
+        cols = slice(j * 128, (j + 1) * 128)
+        router_out[:, cols] = small[:experts, j, :]
+        first_gain[:, cols] = small[experts + 1 : experts + 2, j, :]
+        second_gain[:, cols] = small[experts : experts + 1, j, :]
+    for copy in copies:
+        copy.wait()
+
+
+def deliver(gate, up, down, rows, sums, got, small, sizes, expert_count, ep_size):
+    width = rows.shape[1]
+    f32 = jnp.float32
+    vmem, anywhere = pl.BlockSpec(memory_space=pltpu.VMEM), pl.BlockSpec(memory_space=pl.ANY)
+    first, second, third = (g.reshape((ep_size,) + g.shape[2:]) for g in got)
+
+    def like(value):
+        return jax.ShapeDtypeStruct(value.shape, value.dtype)
+
+    shapes = [(ep_size, k, width) for k in sizes]
+    results = pl.pallas_call(
+        functools.partial(deliver_kernel, ep_size, sizes),
+        out_shape=(like(gate), like(up), like(down), like(rows), like(sums))
+        + tuple(jax.ShapeDtypeStruct(shape, f32) for shape in shapes)
+        + (
+            jax.ShapeDtypeStruct((expert_count, width), f32),
+            jax.ShapeDtypeStruct((1, width), f32),
+            jax.ShapeDtypeStruct((1, width), f32),
+        ),
+        in_specs=[anywhere] * 5 + [vmem] * 4,
+        out_specs=(anywhere,) * 9 + (vmem,) * 3,
+        scratch_shapes=[pltpu.VMEM(shape, f32) for shape in shapes]
+        + [pltpu.SemaphoreType.DMA((9,))],
+        compiler_params=pltpu.CompilerParams(vmem_limit_bytes=32 * 1024 * 1024),
+        name="deliver",
+    )(gate, up, down, rows, sums, first, second, third, small)
+    gate, up, down, rows, sums = results[:5]
+    query, key, value, out = (g.reshape(-1, width) for g in results[5:9])
+    router, first_gain, second_gain = results[9:]
+    return (
+        sums,
+        rows,
+        first_gain[0],
+        query,
+        key,
+        value,
+        out,
+        second_gain[0],
+        router,
+        gate,
+        up,
+        down,
+    )
 
 
 def group_rows(value_rows):
@@ -1534,7 +1628,7 @@
         middle_own, scale_two, gain_two, grad_normed_own
     )
     if by_links:
-        (grad_w_query, grad_w_key, grad_w_value, grad_w_out), grad_input, small = back_by_links(
+        *got, grad_input, small = back_by_links(
             grad_middle.astype(jnp.bfloat16),
             head_outputs,
             w_out,
@@ -1554,62 +1648,75 @@
             grad_middle,
             lax.axis_size("ep"),
         )
-    else:
-        grad_attn = group_rows(grad_middle.astype(jnp.bfloat16))
-        grad_w_out = jnp.einsum(
-            "rf,rd->fd", head_outputs, grad_attn, preferred_element_type=jnp.float32
-        )
-        grad_w_out = lax.psum(grad_w_out.astype(jnp.bfloat16), "ep").astype(jnp.float32)
-        grad_heads = (
-            jnp.einsum("rd,fd->rf", grad_attn, w_out, preferred_element_type=jnp.float32)
-            .astype(jnp.bfloat16)
-            .reshape(token_count, local_kv, group_factor, head_width)
-        )
-        grad_query, grad_keys, grad_values = attend_backward(
-            query_rows, key_rows, value_rows, segment, position, log_sums, grad_heads, block_rows
-        )
-        grad_query_proj = (
-            rotate_back(
-                grad_query.reshape(token_count, local_heads, head_width), cosine_lookup, sine_lookup
-            )
-            .astype(jnp.bfloat16)
-            .reshape(token_count, local_heads * head_width)
-        )
-        grad_key_proj = (
-            rotate_back(grad_keys, cosine_lookup, sine_lookup)
-            .astype(jnp.bfloat16)
-            .reshape(token_count, local_kv * head_width)
-        )
-        grad_value_proj = grad_values.astype(jnp.bfloat16).reshape(token_count, local_kv * head_width)
-        grad_w_query = jnp.einsum(
-            "rf,rd->fd", grad_query_proj, first_normalized, preferred_element_type=jnp.float32
-        )
-        grad_w_key = jnp.einsum(
-            "rf,rd->fd", grad_key_proj, first_normalized, preferred_element_type=jnp.float32
-        )
-        grad_w_value = jnp.einsum(
-            "rf,rd->fd", grad_value_proj, first_normalized, preferred_element_type=jnp.float32
-        )
-        grad_normed_one = jnp.einsum(
-            "rf,fd->rd", grad_query_proj, w_query, preferred_element_type=jnp.float32
-        )
-        grad_normed_one = grad_normed_one + jnp.einsum(
-            "rf,fd->rd", grad_key_proj, key_projection_weight, preferred_element_type=jnp.float32
-        )
-        grad_normed_one = grad_normed_one + jnp.einsum(
-            "rf,fd->rd", grad_value_proj, value_projection_weight, preferred_element_type=jnp.float32
-        )
-        grad_gain_attn = jnp.sum(grad_normed_one * first_normalized.astype(jnp.float32), axis=0)
-        small = jnp.concatenate(
-            [grad_router, grad_gain_ffn[None, :], (grad_gain_attn / gain_one)[None, :]], axis=0
-        )
-        grad_w_query, grad_w_key, grad_w_value = (
-            lax.psum(g.astype(jnp.bfloat16), "ep").astype(jnp.float32)
-            for g in (grad_w_query, grad_w_key, grad_w_value)
-        )
-        grad_one_own = group_totals(grad_normed_one.astype(jnp.bfloat16), by_links, None)
-        small = lax.psum(small, ("ep", "tp"))
-        grad_input = grad_middle + norm_back(inputs_own, scale_one, gain_one, grad_one_own)
+        ep_size = lax.axis_size("ep")
+        weights = (w_query, key_projection_weight, value_projection_weight, w_out)
+        return deliver(
+            grad_w_gate,
+            grad_w_up,
+            grad_w_down,
+            grad_input,
+            output_own,
+            got,
+            small,
+            [w.shape[0] // ep_size for w in weights],
+            expert_count,
+            ep_size,
+        )
+    grad_attn = group_rows(grad_middle.astype(jnp.bfloat16))
+    grad_w_out = jnp.einsum(
+        "rf,rd->fd", head_outputs, grad_attn, preferred_element_type=jnp.float32
+    )
+    grad_w_out = lax.psum(grad_w_out.astype(jnp.bfloat16), "ep").astype(jnp.float32)
+    grad_heads = (
+        jnp.einsum("rd,fd->rf", grad_attn, w_out, preferred_element_type=jnp.float32)
+        .astype(jnp.bfloat16)
+        .reshape(token_count, local_kv, group_factor, head_width)
+    )
+    grad_query, grad_keys, grad_values = attend_backward(
+        query_rows, key_rows, value_rows, segment, position, log_sums, grad_heads, block_rows
+    )
+    grad_query_proj = (
+        rotate_back(
+            grad_query.reshape(token_count, local_heads, head_width), cosine_lookup, sine_lookup
+        )
+        .astype(jnp.bfloat16)
+        .reshape(token_count, local_heads * head_width)
+    )
+    grad_key_proj = (
+        rotate_back(grad_keys, cosine_lookup, sine_lookup)
+        .astype(jnp.bfloat16)
+        .reshape(token_count, local_kv * head_width)
+    )
+    grad_value_proj = grad_values.astype(jnp.bfloat16).reshape(token_count, local_kv * head_width)
+    grad_w_query = jnp.einsum(
+        "rf,rd->fd", grad_query_proj, first_normalized, preferred_element_type=jnp.float32
+    )
+    grad_w_key = jnp.einsum(
+        "rf,rd->fd", grad_key_proj, first_normalized, preferred_element_type=jnp.float32
+    )
+    grad_w_value = jnp.einsum(
+        "rf,rd->fd", grad_value_proj, first_normalized, preferred_element_type=jnp.float32
+    )
+    grad_normed_one = jnp.einsum(
+        "rf,fd->rd", grad_query_proj, w_query, preferred_element_type=jnp.float32
+    )
+    grad_normed_one = grad_normed_one + jnp.einsum(
+        "rf,fd->rd", grad_key_proj, key_projection_weight, preferred_element_type=jnp.float32
+    )
+    grad_normed_one = grad_normed_one + jnp.einsum(
+        "rf,fd->rd", grad_value_proj, value_projection_weight, preferred_element_type=jnp.float32
+    )
+    grad_gain_attn = jnp.sum(grad_normed_one * first_normalized.astype(jnp.float32), axis=0)
+    small = jnp.concatenate(
+        [grad_router, grad_gain_ffn[None, :], (grad_gain_attn / gain_one)[None, :]], axis=0
+    )
+    grad_w_query, grad_w_key, grad_w_value = (
+        lax.psum(g.astype(jnp.bfloat16), "ep").astype(jnp.float32)
+        for g in (grad_w_query, grad_w_key, grad_w_value)
+    )
+    grad_one_own = group_totals(grad_normed_one.astype(jnp.bfloat16), by_links, None)
+    small = lax.psum(small, ("ep", "tp"))
+    grad_input = grad_middle + norm_back(inputs_own, scale_one, gain_one, grad_one_own)
     grad_router = small[:expert_count]
     grad_gain_ffn, grad_gain_attn = small[expert_count], small[expert_count + 1]
     return (

time: 450 us -> 445 us (0.989)
  local copies, waits for them, and re-layouts: 28.7 us -> 18.8 us
  Pallas kernels: 376 us -> 382 us
    unnamed x77 -> x80, local copies, waits for them, and re-layouts: 16.4 us -> 7.95 us
    pallas_call x0 -> x1, Pallas kernels: none -> 5.16 us  [deliver(): pl.pallas_call(functools.partial(deliver_kernel, ep_size, sizes), out_sha...]
  transfers between devices with their start and end apart: 1 -> 1, of which waited for: 0 -> 0; matrix products, arithmetic and copies ran while one was open for 7% -> 7% of each run, Pallas kernels for 28% -> 27%
where the time goes in v7:
time: 445 us; the launch traced here: 444 us
  Pallas kernels  382 us (86%)
  local copies, waits for them, and re-layouts  18.8 us (4%)
  other arithmetic  16.4 us (4%)
  between operations  14.7 us (3%)
  matrix products  11.3 us (3%)
    pallas_call x1, Pallas kernels, experts_by_links(): pl.pallas_call(functools.partial(experts_kernel, ep_size, per_owner), out...  136 us
    pallas_call x1, Pallas kernels, back_by_links(): pl.pallas_call(functools.partial(back_kernel, ep_size, heads, small.shape...  119 us
    pallas_call x1, Pallas kernels, gather_by_links(): pl.pallas_call(functools.partial(gather_kernel, ep_size), out_shape=jax.S...  85.3 us
    pallas_call x1, Pallas kernels, front_gather(): pl.pallas_call(functools.partial(front_gather_kernel, ep_size, pieces), o...  21.1 us
    pallas_call x1, Pallas kernels, group_total(): pl.pallas_call(functools.partial(group_total_kernel, ep_size), out_shape=...  15.5 us
  transfers between devices with their start and end apart: 1, of which 0 were waited for; matrix products, arithmetic and copies ran while one was open for 7% of the time, Pallas kernels for 27%

profile of v7, /device:TPU:0, one launch (start us, length us, event | category | flops | bytes accessed | tf_op | source)
XLA Modules:
  0.0 443.8 jit_solution(17112275793329115550)
XLA Ops:
  7.2 0.7 all-gather.2.cloned.1.call-update
  8.0 0.7 convert_element_type.77
  8.7 1.3 broadcast_in_dim.127.gain
  9.9 0.7 convert_element_type.80
  10.6 1.0 fusion.14
  11.9 1.5 select_reduce_fusion.table
  13.4 1.2 fusion.4
  14.6 0.9 fusion.6.own
  15.5 21.1 %front_gather.1 = (bf16[2,2,128,1536]{3,2,1,0:T(8,128)(2,1)}, s32[8,16,512]{2,1,0:T(8,128)}) custom-call(bf16[128,1536]{1,0:T(8,128)(2,1)} %fusion.6.own, s32[16,512]{1,0:T(8,128)} %select_reduce_fusion.table), custom_call_target="tpu_custom_call" | custom-call | tf_op jit(solution)/shard_map/front_gather/pallas_call | solution.py:255
  36.6 2.1 convolution_convert_fusion.1.values
  38.7 0.8 copy.89
  39.5 1.0 compare_and_fusion
  40.5 0.6 fusion.38
  41.3 2.1 fusion.39
  43.6 1.2 fusion.1
  44.8 1.3 fusion
  46.1 2.0 fusion.3
  48.1 0.9 copy.103.heads_in
  49.0 1.0 convolution_convert_fusion
  50.0 15.5 %group_total.1 = f32[128,1536]{1,0:T(8,128)S(1)} custom-call(bf16[2,2,128,1536]{3,2,1,0:T(8,128)(2,1)S(1)} %bitcast.94), custom_call_target="tpu_custom_call" | custom-call | tf_op jit(solution)/shard_map/group_total/pallas_call | solution.py:367
  66.9 0.5 copy.113
  67.6 0.9 multiply_convert_fusion.own
  68.5 85.3 %gather_by_links.1 = bf16[4,2,2,2,128,1536]{5,4,3,2,1,0:T(8,128)(2,1)} custom-call(bf16[128,1536]{1,0:T(8,128)(2,1)} %multiply_convert_fusion.own), custom_call_target="tpu_custom_call" | custom-call | tf_op jit(solution)/shard_map/gather_by_links/pallas_call | solution.py:204
  154.0 0.9 copy.104.queries
  155.0 0.8 copy.105.keys
  155.9 0.7 pad.33.clone.info_cols
  156.6 0.6 pad.34.info_rows
  157.2 1.2 pad.30.clone
  158.4 0.8 pad.31.router
  159.2 0.6 pad.32.log_sums
  160.0 0.7 select_reduce_fusion.2
  160.8 1.0 pad_maximum_fusion.2
  161.9 1.3 pad_maximum_fusion.enter
  163.2 136.2 %experts_by_links.1 = (f32[128,1536]{1,0:T(8,128)}, f32[128,1536]{1,0:T(8,128)}, f32[8,2,8,128]{3,2,1,0:T(8,128)}, f32[2,1536,128]{2,1,0:T(8,128)}, f32[2,1536,128]{2,1,0:T(8,128)}, /*index=5*/f32[256,1536]{1,0:T(8,128)}) custom-call(bf16[4,2,4,128,1536]{4,3,2,1,0:T(8,128)(2,1)} %bitcast.99, bf16[4,2,4,128,1536]{4,3,2,1,0:T(8,128)(2,1)} %bitcast.100, ...), custom_call_target="tpu_custom_call" | custom-call | tf_op jit(solution)/shard_map/experts_by_links/pallas_call | solution.py:735
  299.5 0.9 slice_bitcast_fusion.4
  300.8 1.9 multiply_reduce_fusion
  302.7 0.7 reshape.480.small_in
  303.5 1.3 fusion.36
  304.8 118.6 %back_by_links.1 = (bf16[4,2,80,768]{3,2,1,0:T(8,128)(2,1)}, bf16[4,2,80,768]{3,2,1,0:T(8,128)(2,1)}, bf16[4,2,48,1536]{3,2,1,0:T(8,128)(2,1)}, f32[128,1536]{1,0:T(8,128)}, f32[32,12,128]{2,1,0:T(8,128)}) custom-call(bf16[128,1536]{1,0:T(8,128)(2,1)} %get-tuple-element.64.datt_own, bf16[512,384]{1,0:T(8,128)(2,1)} %copy.103.heads_in, ...), custom_call_target="tpu_custom_call" | custom-call | tf_op jit(solution)/shard_map/back_by_links/pallas_call | solution.py:1162
  423.4 1.4 copy-done.2
  424.8 1.3 copy-done.3
  426.1 1.2 copy-done.4
  427.3 1.2 copy-done.5
  428.5 1.1 copy-done.6
  429.6 0.9 copy-done.7
  430.6 5.2 %deliver.1 = (f32[2,1536,128]{2,1,0:T(8,128)}, f32[2,1536,128]{2,1,0:T(8,128)}, f32[2,128,1536]{2,1,0:T(8,128)}, f32[128,1536]{1,0:T(8,128)}, bf16[128,1536]{1,0...) custom-call(f32[2,1536,128]{2,1,0:T(8,128)S(1)} %copy-done, ...), custom_call_target="tpu_custom_call" | custom-call | tf_op jit(solution)/shard_map/deliver/pallas_call | solution.py:1302
  435.7 0.6 reduce
  436.4 0.6 reduce.1
  (113 shorter events, 3.1 us)
Async XLA Ops:
  7.2 7.4 %copy-start.8 = (bf16[128,1536]{1,0:T(8,128)(2,1)S(1)}, bf16[128,1536]{1,0:T(8,128)(2,1)}, u32[]{:S(2)}) copy-start(bf16[128,1536]{1,0:T(8,128)(2,1)} %inputs.1) | copy-start | bytes 1179652
  7.2 29.4 %copy-start.14 = (bf16[128,1536]{1,0:T(8,128)(2,1)S(1)}, bf16[128,1536]{1,0:T(8,128)(2,1)}, u32[]{:S(2)}) copy-start(bf16[128,1536]{1,0:T(8,128)(2,1)} %w_value.1) | copy-start | bytes 1179652
  7.2 156.0 %all-gather.2.cloned.1.call-start = ((), (), s32[]{:S(2)}) async-start(), calls=%async_computation | async-start | bytes 12976128 | tf_op jit(solution)/shard_map/all_gather | solution.py:1350
  11.6 3.8 copy-start.12
  11.7 27.8 %copy-start.36 = (s32[512]{0:T(512)S(1)}, s32[512]{0:T(512)}, u32[]{:S(2)}) copy-start(s32[512]{0:T(512)} %param.29) | copy-start | bytes 6148
  11.7 27.9 %copy-start.37 = (s32[512]{0:T(512)S(1)}, s32[512]{0:T(512)}, u32[]{:S(2)}) copy-start(s32[512]{0:T(512)} %param.30) | copy-start | bytes 6148
  11.8 28.7 %copy-start.26 = (bf16[128,1536]{1,0:T(8,128)(2,1)S(1)}, bf16[128,1536]{1,0:T(8,128)(2,1)}, u32[]{:S(2)}) copy-start(bf16[128,1536]{1,0:T(8,128)(2,1)} %w_key.1) | copy-start | bytes 1179652
  36.6 3.9 copy-start.10
  38.7 4.7 %copy-start.16 = (bf16[512,128]{1,0:T(8,128)(2,1)}, bf16[512,128]{1,0:T(8,128)(2,1)S(1)}, u32[]{:S(2)}) copy-start(bf16[512,128]{1,0:T(8,128)(2,1)S(1)} %convolution_convert_fusion.1.values) | copy-start | bytes 393220
  41.2 2.3 copy-start.27
  41.3 2.3 copy-start.29
  43.5 1.2 copy-start.19
  43.5 1.2 copy-start.21
  44.8 1.4 copy-start.32
  44.8 1.4 copy-start.31
  46.1 2.0 copy-start.34
  46.1 2.9 copy-start.11
  49.0 16.6 %copy-start.38 = (bf16[1536]{0:T(1024)(128)(2,1)S(1)}, bf16[1536]{0:T(1024)(128)(2,1)}, u32[]{:S(2)}) copy-start(bf16[1536]{0:T(1024)(128)(2,1)} %param.22) | copy-start | bytes 9220
  49.0 16.6 %copy-start.17 = (s32[8,16,512]{2,1,0:T(8,128)S(1)}, s32[8,16,512]{2,1,0:T(8,128)}, u32[]{:S(2)}) copy-start(s32[8,16,512]{2,1,0:T(8,128)} %get-tuple-element.38) | copy-start | bytes 786436
  68.5 85.4 %copy-start.33 = (f32[2,3,512]{2,1,0:T(4,128)S(1)}, f32[2,3,512]{2,1,0:T(4,128)}, u32[]{:S(2)}) copy-start(f32[2,3,512]{2,1,0:T(4,128)} %copy-done.32) | copy-start | bytes 36868
  68.5 85.4 %copy-start.35 = (f32[2,3,512]{2,1,0:T(4,128)S(1)}, f32[2,3,512]{2,1,0:T(4,128)}, u32[]{:S(2)}) copy-start(f32[2,3,512]{2,1,0:T(4,128)} %copy-done.34) | copy-start | bytes 36868
  68.5 85.4 %copy-start.20 = (bf16[512,6,32]{0,2,1:T(8,128)(2,1)S(1)}, bf16[512,6,32]{0,2,1:T(8,128)(2,1)}, u32[]{:S(2)}) copy-start(bf16[512,6,32]{0,2,1:T(8,128)(2,1)} %copy-done.19) | copy-start | bytes 589828
  68.5 85.5 %copy-start.22 = (bf16[512,6,32]{0,2,1:T(8,128)(2,1)S(1)}, bf16[512,6,32]{0,2,1:T(8,128)(2,1)}, u32[]{:S(2)}) copy-start(bf16[512,6,32]{0,2,1:T(8,128)(2,1)} %copy-done.21) | copy-start | bytes 589828
  68.5 86.4 %copy-start.28 = (bf16[512,2,32]{0,2,1:T(8,128)(2,1)S(1)}, bf16[512,2,32]{0,2,1:T(8,128)(2,1)}, u32[]{:S(2)}) copy-start(bf16[512,2,32]{0,2,1:T(8,128)(2,1)} %copy-done.27) | copy-start | bytes 196612
  68.5 86.4 %copy-start.30 = (bf16[512,2,32]{0,2,1:T(8,128)(2,1)S(1)}, bf16[512,2,32]{0,2,1:T(8,128)(2,1)}, u32[]{:S(2)}) copy-start(bf16[512,2,32]{0,2,1:T(8,128)(2,1)} %copy-done.29) | copy-start | bytes 196612
  154.0 4.4 copy-start.25
  154.0 5.8 %copy-start.9 = (bf16[128,1536]{1,0:T(8,128)(2,1)S(1)}, bf16[128,1536]{1,0:T(8,128)(2,1)}, u32[]{:S(2)}) copy-start(bf16[128,1536]{1,0:T(8,128)(2,1)} %multiply_convert_fusion.own) | copy-start | bytes 1179652
  154.9 5.9 %copy-start.13 = (f32[512,32]{1,0:T(8,128)S(1)}, f32[512,32]{1,0:T(8,128)}, u32[]{:S(2)}) copy-start(f32[512,32]{1,0:T(8,128)} %copy-done.12) | copy-start | bytes 196612
  158.4 3.4 copy-start.23
  158.4 3.4 copy-start.24
  299.4 4.0 copy-start.15
  299.5 4.0 copy-start.18
  304.8 118.6 %copy-start = (f32[2,1536,128]{2,1,0:T(8,128)S(1)}, f32[2,1536,128]{2,1,0:T(8,128)}, u32[]{:S(2)}) copy-start(f32[2,1536,128]{2,1,0:T(8,128)} %get-tuple-element.39.gate_in) | copy-start | bytes 4718596
  304.8 118.6 %copy-start.1 = (f32[2,1536,128]{2,1,0:T(8,128)S(1)}, f32[2,1536,128]{2,1,0:T(8,128)}, u32[]{:S(2)}) copy-start(f32[2,1536,128]{2,1,0:T(8,128)} %get-tuple-element.40.up_in) | copy-start | bytes 4718596
  423.4 1.4 copy-start.2
  424.8 1.3 copy-start.3
  426.1 1.2 copy-start.4
  427.3 1.2 copy-start.5
  428.5 1.1 copy-start.6
  429.6 0.9 copy-start.7
Sparse Core Ops, SparseCore 0:
  10.9 132.2 all-gather.1

commit v8 on v7

--- a/solution.py
+++ b/solution.py
@@ -114,108 +114,70 @@
     return copy
 
 
-def gather_kernel(ep_size, own, out, own_sem, z_sems, pair_sems, core_sems):
+def gather_kernel(ep_size, count, *refs):
+    owns, outs = refs[:count], refs[count : 2 * count]
+    own_sems, z_sems, y_sems, core_sems = refs[2 * count :]
     me = Place(ep_size)
     depth = me.depth
-    half = own.shape[0] // 2
-    z_send, z_recv = z_sems.at[0], z_sems.at[1]
-    pair_send, pair_recv = pair_sems.at[0], pair_sems.at[1]
-    core_send, core_recv = core_sems.at[0], core_sems.at[1]
-    meet(
-        [me.sibling(), me.x_peer(), me.y_peer()]
-        + [me.device(z=me.after(s)) for s in range(1, depth)]
-    )
-
-    def rows(part):
-        return pl.ds(part * half, half)
-
-    def block(step, y, x, part, c=None):
-        return out.at[me.before(step), y, x, me.c if c is None else c, rows(part)]
-
+    meet([me.sibling(), me.y_peer()] + [me.device(z=me.after(s)) for s in range(1, depth)])
     started = []
 
-    def forward(source, target, sems, slot, device):
-        started.append(send(source, target, sems[0].at[slot], sems[1].at[slot], device))
-
-    for s in range(1, depth):
-        for part in range(2):
-            forward(
-                own.at[rows(part)],
-                out.at[me.z, me.y, me.x, me.c, rows(part)],
-                (z_send, z_recv),
-                (s - 1) * 2 + part,
-                me.device(z=me.after(s)),
-            )
-    local = pltpu.make_async_copy(own, out.at[me.z, me.y, me.x, me.c], own_sem)
-    local.start()
-    local.wait()
-
-    kinds = [
-        (me.y, me.x, 0),
-        (me.y, me.x, 1),
-        (1 - me.y, me.x, 0),
-        (me.y, 1 - me.x, 1),
-        (1 - me.y, me.x, 1),
-        (1 - me.y, 1 - me.x, 1),
-        (me.y, 1 - me.x, 0),
-        (1 - me.y, 1 - me.x, 0),
-    ]
-    x_route = {0: 6, 2: 7, 1: 3}
-    y_route = {0: 2, 1: 4, 3: 5}
-
-    def landed(step, kind):
-        y, x, part = kinds[kind]
-        place = block(step, y, x, part)
-        if kind < 2:
-            if step > 0:
-                sem = z_recv.at[(step - 1) * 2 + part]
-                pltpu.make_async_copy(place, place, sem).wait()
-        else:
-            pltpu.make_async_copy(place, place, pair_recv.at[step * 8 + kind]).wait()
-
-    def pass_on(step, kind):
-        y, x, part = kinds[kind]
-        place = block(step, y, x, part)
-        if kind in x_route:
-            forward(place, place, (pair_send, pair_recv), step * 8 + x_route[kind], me.x_peer())
-        if kind in y_route:
-            forward(place, place, (pair_send, pair_recv), step * 8 + y_route[kind], me.y_peer())
-        forward(place, place, (core_send, core_recv), step * 8 + kind, me.sibling())
-
-    for turn in range(depth + 2):
-        for step, group in ((turn, (0, 1)), (turn - 1, (2, 3)), (turn - 2, (4, 5, 6, 7))):
-            if 0 <= step < depth:
-                for kind in group:
-                    landed(step, kind)
-                    pass_on(step, kind)
-    for step in range(depth):
-        for kind in range(8):
-            y, x, part = kinds[kind]
-            place = block(step, y, x, part, 1 - me.c)
-            pltpu.make_async_copy(place, place, core_recv.at[step * 8 + kind]).wait()
+    def forward(source, target, sems, a, slot, device):
+        started.append(send(source, target, sems.at[0, a, slot], sems.at[1, a, slot], device))
+
+    def landed(block, sems, a, slot):
+        pltpu.make_async_copy(block, block, sems.at[1, a, slot]).wait()
+
+    local = []
+    for a in range(count):
+        own, mine = owns[a], outs[a].at[me.z, me.y, me.c]
+        for s in range(1, depth):
+            forward(own, mine, z_sems, a, s, me.device(z=me.after(s)))
+        forward(own, mine, y_sems, a, 0, me.y_peer())
+        forward(own, mine, core_sems, a, 0, me.sibling())
+        local.append(pltpu.make_async_copy(own, mine, own_sems.at[a]))
+        local[a].start()
+    for a in range(count):
+        for s in range(1, depth):
+            block = outs[a].at[me.before(s), me.y, me.c]
+            landed(block, z_sems, a, s)
+            forward(block, block, y_sems, a, s, me.y_peer())
+            forward(block, block, core_sems, a, s, me.sibling())
+    for a in range(count):
+        for s in range(depth):
+            block = outs[a].at[me.before(s), 1 - me.y, me.c]
+            landed(block, y_sems, a, s)
+            forward(block, block, core_sems, a, depth + s, me.sibling())
+    for a in range(count):
+        local[a].wait()
+        for s in range(depth):
+            for y, slot in ((me.y, s), (1 - me.y, depth + s)):
+                landed(outs[a].at[me.before(s), y, 1 - me.c], core_sems, a, slot)
     for copy in started:
         copy.wait_send()
 
 
-def gather_by_links(value_rows, ep_size):
-    rows, width = value_rows.shape
-    depth = ep_size // 2
+def gather_by_links(arrays, ep_size):
+    rows, width = arrays[0].shape
+    depth, count = ep_size // 2, len(arrays)
     dma = pltpu.SemaphoreType.DMA
-    every = pl.pallas_call(
-        functools.partial(gather_kernel, ep_size),
-        out_shape=jax.ShapeDtypeStruct((depth, 2, 2, 2, rows, width), value_rows.dtype),
-        in_specs=[pl.BlockSpec(memory_space=pl.ANY)],
-        out_specs=pl.BlockSpec(memory_space=pl.ANY),
+    anywhere = pl.BlockSpec(memory_space=pltpu.HBM)
+    return pl.pallas_call(
+        functools.partial(gather_kernel, ep_size, count),
+        out_shape=tuple(
+            jax.ShapeDtypeStruct((depth, 2, 2, rows, width), a.dtype) for a in arrays
+        ),
+        in_specs=[anywhere] * count,
+        out_specs=(anywhere,) * count,
         scratch_shapes=[
-            dma,
-            dma((2, 2 * depth - 2)),
-            dma((2, 8 * depth)),
-            dma((2, 8 * depth)),
+            dma((count,)),
+            dma((2, count, depth)),
+            dma((2, count, depth)),
+            dma((2, count, 2 * depth)),
         ],
         compiler_params=pltpu.CompilerParams(collective_id=1, has_side_effects=True),
         name="gather_by_links",
-    )(value_rows)
-    return every.reshape(-1, width)
+    )(*arrays)
 
 
 def add_into(target, other):
@@ -251,7 +213,7 @@
     rows, width = value_rows.shape
     pieces = 4
     dma = pltpu.SemaphoreType.DMA
-    anywhere = pl.BlockSpec(memory_space=pl.ANY)
+    anywhere = pl.BlockSpec(memory_space=pltpu.HBM)
     every, tables = pl.pallas_call(
         functools.partial(front_gather_kernel, ep_size, pieces),
         out_shape=(
@@ -395,117 +357,100 @@
     cots_in,
     code_in,
     router,
-    enter,
-    leave,
+    enter_own,
+    enter_peer,
+    leave_own,
+    leave_peer,
     grad_out,
     sum_out,
     small_out,
     gate_out,
     up_out,
     down_out,
+    gate_peer,
+    up_peer,
+    down_peer,
     rows_buf,
     cots_buf,
     weighted,
     turned,
     enter_sum,
+    down_sum,
     parts,
     core_got,
-    pair_got,
-    last_got,
+    y_got,
     z_got,
     small_in,
     small_got,
     load_sems,
     core_sems,
-    pair_sems,
-    last_sems,
+    y_sems,
     z_sems,
     small_sems,
     own_sem,
 ):
     me = Place(ep_size)
     depth = me.depth
-    steps = 2 * depth
-    blocks = 2 * steps
+    blocks = 2 * depth
     width = router.shape[1]
     share = rows_buf.shape[2]
-    tokens = 4 * share
-    units = leave.shape[0] // per_owner
-    hidden = per_owner * units
+    tokens = 2 * share
+    hidden = leave_own.shape[0]
+    units = hidden // per_owner
     f32, bf16 = jnp.float32, jnp.bfloat16
-    others = all_others(ep_size)
+    ep = lax.axis_index("ep")
+    others = [
+        (lax.rem(ep + k // 2, ep_size), me.x * 2 + lax.rem(me.c + k % 2, 2))
+        for k in range(1, 2 * ep_size)
+    ]
     meet(others)
-    my_place = lax.axis_index("ep") * 4 + lax.axis_index("tp")
+    my_place = ep * 2 + me.c
+    halves = ((enter_own, leave_own), (enter_peer, leave_peer))
 
     def where(b):
-        return me.after(b // 4 + 1), lax.rem(1 - me.y + b % 2, 2)
-
-    def half(b):
-        return pl.ds(pl.multiple_of(b // 2 % 2 * share, share), share)
+        return me.after(b // 2 + 1), lax.rem(1 - me.y + b % 2, 2)
 
     def load(b, which):
         z, y = where(b)
         source, target = ((rows_in, rows_buf), (cots_in, cots_buf))[which]
         slot = lax.rem(b, 2)
         return pltpu.make_async_copy(
-            source.at[z, y, :, half(b)], target.at[slot], load_sems.at[slot, which]
+            source.at[z, y], target.at[slot], load_sems.at[slot, which]
         )
 
     def core_copy(b):
-        y = where(b)[1]
         return pltpu.make_async_remote_copy(
-            src_ref=parts.at[lax.rem(b, 2), :, :, 1 - me.c],
-            dst_ref=core_got.at[b // 2, y],
+            src_ref=parts.at[lax.rem(b, 2), :, 1 - me.c],
+            dst_ref=core_got.at[b // 2, where(b)[1]],
             send_sem=core_sems.at[0, b],
             recv_sem=core_sems.at[1, b],
             device_id=me.sibling(),
             device_id_type=MESH,
         )
 
-    def grad_pair(b):
-        y = where(b)[1]
+    def y_copy(step, which):
         return pltpu.make_async_remote_copy(
-            src_ref=core_got.at[b // 2, y, 0, 1 - me.x],
-            dst_ref=pair_got.at[b // 2, 0, y],
-            send_sem=pair_sems.at[0, b],
-            recv_sem=pair_sems.at[1, b],
-            device_id=me.x_peer(),
-            device_id_type=MESH,
-        )
-
-    def sum_pair(step):
-        return pltpu.make_async_remote_copy(
-            src_ref=core_got.at[step, 1 - me.y, 1],
-            dst_ref=pair_got.at[step, 1],
-            send_sem=pair_sems.at[0, blocks + step],
-            recv_sem=pair_sems.at[1, blocks + step],
+            src_ref=core_got.at[step, 1 - me.y, which],
+            dst_ref=y_got.at[step, which],
+            send_sem=y_sems.at[0, step, which],
+            recv_sem=y_sems.at[1, step, which],
             device_id=me.y_peer(),
             device_id_type=MESH,
         )
 
-    def last_copy(step, which):
-        return pltpu.make_async_remote_copy(
-            src_ref=pair_got.at[step, which, (1 - me.y, 1 - me.x)[which]],
-            dst_ref=last_got.at[step, which],
-            send_sem=last_sems.at[0, step, which],
-            recv_sem=last_sems.at[1, step, which],
-            device_id=(me.y_peer(), me.x_peer())[which],
-            device_id_type=MESH,
-        )
-
     def z_copy(step, which):
         return pltpu.make_async_remote_copy(
-            src_ref=last_got.at[step, which],
+            src_ref=y_got.at[step, which],
             dst_ref=z_got.at[step, which],
             send_sem=z_sems.at[0, step, which],
             recv_sem=z_sems.at[1, step, which],
-            device_id=me.device(z=me.after(step // 2 + 1)),
+            device_id=me.device(z=me.after(step + 1)),
             device_id_type=MESH,
         )
 
     def small_copy(k, device):
         return pltpu.make_async_remote_copy(
-            src_ref=small_in.at[device[0] * 4 + device[1]],
+            src_ref=small_in.at[device[0] * 2 + device[1] % 2],
             dst_ref=small_got.at[my_place],
             send_sem=small_sems.at[0, k],
             recv_sem=small_sems.at[1, k],
@@ -529,50 +474,56 @@
         slot = lax.rem(b, 2)
         rows = rows_buf[slot].reshape(tokens, width)
         cots = cots_buf[slot].reshape(tokens, width)
-        code = code_in[z * 2 + y, :, half(b), :].astype(f32).reshape(tokens, -1)
+        code = code_in[z * 2 + y, me.x].astype(f32).reshape(tokens, -1)
         used = code >= 0.0
         logits = jnp.where(used, dot(rows, router[...], (1, 1)), -1e30)
         top = jnp.max(logits, axis=1, keepdims=True)
         powers = jnp.where(used, jnp.exp(logits - top), 0.0)
         kept = jnp.where(code == 0.0, 1.0, 0.0)
         gates = spread(kept * powers / jnp.sum(powers, axis=1, keepdims=True))
-        act = dot(rows, enter[...], (1, 0))
-        gate_act, up_act = act[:, :hidden], act[:, hidden:]
-        back_act = dot(cots, leave[...], (1, 1))
-        sigma = jax.nn.sigmoid(gate_act)
-        swish = gate_act * sigma
-        value = swish * up_act
-        gate_parts = spread(kept) * (value * back_act)
+        products = jnp.zeros((tokens, hidden), f32)
+        for h, (enter, leave) in enumerate(halves):
+            act = dot(rows, enter[...], (1, 0))
+            gate_act, up_act = act[:, :hidden], act[:, hidden:]
+            back_act = dot(cots, leave[...], (1, 1))
+            sigma = jax.nn.sigmoid(gate_act)
+            swish = gate_act * sigma
+            value = swish * up_act
+            products = products + value * back_act
+            weighted[:, h * hidden : (h + 1) * hidden] = (gates * value).astype(bf16)
+            grad_hidden = gates * back_act
+            at = 2 * h * hidden
+            turned[:, at : at + hidden] = (
+                grad_hidden * up_act * sigma * (1.0 + gate_act * (1.0 - sigma))
+            ).astype(bf16)
+            turned[:, at + hidden : at + 2 * hidden] = (grad_hidden * swish).astype(bf16)
         lane = lax.broadcasted_iota(jnp.int32, (8, hidden), 1)
         pick = lax.broadcasted_iota(jnp.int32, (8, hidden), 0)
         mine = jnp.where((lane >= pick * units) & (lane < (pick + 1) * units), 1.0, 0.0)
         grad_gates = lax.dot_general(
             mine,
-            gate_parts,
+            spread(kept) * products,
             (((1,), (1,)), ((), ())),
             precision=EXACT_PRECISION,
             preferred_element_type=f32,
         )
-        for k in range(4):
-            small_in[(z * 2 + y) * 4 + k, b // 2 % 2, :, :share] = grad_gates[
-                :, k * share : (k + 1) * share
-            ]
-        weighted[...] = (gates * value).astype(bf16)
-        grad_hidden = gates * back_act
-        turned[:, :hidden] = (
-            grad_hidden * up_act * sigma * (1.0 + gate_act * (1.0 - sigma))
-        ).astype(bf16)
-        turned[:, hidden:] = (grad_hidden * swish).astype(bf16)
+        for k in range(2):
+            small_in[(z * 2 + y) * 2 + k] = grad_gates[:, k * share : (k + 1) * share]
         tile = 512
         for n in range(width // tile):
             cols = slice(n * tile, (n + 1) * tile)
-            grads = dot(turned[...], enter[cols, :], (1, 1)).astype(bf16)
-            sums = dot(weighted[...], leave[:, cols], (1, 0)).astype(bf16)
-            for x in range(2):
-                for c in range(2):
-                    at = slice((x * 2 + c) * share, (x * 2 + c + 1) * share)
-                    parts[slot, 0, x, c, :, cols] = grads[at]
-                    parts[slot, 1, x, c, :, cols] = sums[at]
+            grads = (
+                dot(turned[:, : 2 * hidden], enter_own[cols, :], (1, 1))
+                + dot(turned[:, 2 * hidden :], enter_peer[cols, :], (1, 1))
+            ).astype(bf16)
+            sums = (
+                dot(weighted[:, :hidden], leave_own[:, cols], (1, 0))
+                + dot(weighted[:, hidden:], leave_peer[:, cols], (1, 0))
+            ).astype(bf16)
+            for c in range(2):
+                at = slice(c * share, (c + 1) * share)
+                parts[slot, 0, c, :, cols] = grads[at]
+                parts[slot, 1, c, :, cols] = sums[at]
 
     def weight_sums(b):
         slot = lax.rem(b, 2)
@@ -582,11 +533,10 @@
             rows = rows_buf[slot, :, :, cols].reshape(tokens, tile)
             cots = cots_buf[slot, :, :, cols].reshape(tokens, tile)
             enter_sum[:, cols] += dot(turned[...], rows, (0, 0))
-            down_out[:, cols] += dot(weighted[...], cots, (0, 0))
+            down_sum[:, cols] += dot(weighted[...], cots, (0, 0))
 
     enter_sum[...] = jnp.zeros_like(enter_sum)
-    down_out[...] = jnp.zeros_like(down_out)
-    small_in[...] = jnp.zeros_like(small_in)
+    down_sum[...] = jnp.zeros_like(down_sum)
     for which in range(2):
         load(0, which).start()
 
@@ -597,18 +547,6 @@
             inside &= b % 2 == 0
         pl.when(inside)(lambda: body(b))
 
-    def finish_sum(which):
-        def body(b):
-            step = b // 2
-            last_copy(step, which).wait_recv()
-            add_into(last_got.at[step, which], pair_got.at[step, which, (me.y, me.x)[which]])
-
-            @pl.when(step < steps - 2)
-            def _():
-                z_copy(step, which).start()
-
-        return body
-
     def work(b):
         for which in range(2):
             load(b, which).wait()
@@ -623,145 +561,122 @@
         weight_sums(b)
 
     def core_sum(b):
-        y = where(b)[1]
+        step, y = b // 2, where(b)[1]
         core_copy(b).wait_recv()
         for which in range(2):
-            for x in range(2):
-                add_into(
-                    core_got.at[b // 2, y, which, x], parts.at[lax.rem(b, 2), which, x, me.c]
-                )
-        grad_pair(b).start()
+            add_into(core_got.at[step, y, which], parts.at[lax.rem(b, 2), which, me.c])
 
         @pl.when(b % 2 == 0)
         def _():
-            sum_pair(b // 2).start()
+            for which in range(2):
+                y_copy(step, which).start()
 
         core_copy(b).wait_send()
 
-    def out_pair(b):
-        step = b // 2
-        sum_pair(step).wait_recv()
-        for x in range(2):
-            add_into(pair_got.at[step, 1, x], core_got.at[step, me.y, 1, x])
-        last_copy(step, 1).start()
-
-    def back_pair(b):
-        y = where(b)[1]
-        step = b // 2
-        grad_pair(b).wait_recv()
-        add_into(pair_got.at[step, 0, y], core_got.at[step, y, 0, me.x])
-
-        @pl.when(b % 2 == 0)
-        def _():
-            last_copy(step, 0).start()
+    def y_sum(which):
+        def body(b):
+            step = b // 2
+            y_copy(step, which).wait_recv()
+            add_into(y_got.at[step, which], core_got.at[step, me.y, which])
+
+            @pl.when(step < depth - 1)
+            def _():
+                z_copy(step, which).start()
+
+        return body
 
     def small_send(b):
         for k, device in enumerate(others):
             small_copy(k, device).start()
         pltpu.make_async_copy(small_in.at[my_place], small_got.at[my_place], own_sem).start()
         for e in range(per_owner):
-            gate_out[e] = enter_sum[e * units : (e + 1) * units, :].T
-            up_out[e] = enter_sum[hidden + e * units : hidden + (e + 1) * units, :].T
+            own, peer = e * units, 2 * hidden + e * units
+            gate_out[e] = enter_sum[own : own + units, :].T
+            up_out[e] = enter_sum[hidden + own : hidden + own + units, :].T
+            gate_peer[e] = enter_sum[peer : peer + units, :].T.astype(bf16)
+            up_peer[e] = enter_sum[hidden + peer : hidden + peer + units, :].T.astype(bf16)
+        down_out[...] = down_sum[:hidden, :]
+        down_peer[...] = down_sum[hidden:, :].astype(bf16)
 
     def turn(i, carry):
-        during(i, 6, finish_sum(1), True)
         during(i, 0, work)
         during(i, 1, core_sum)
-        during(i, 7, finish_sum(0), True)
-        during(i, 3, out_pair, True)
-        during(i, 4, back_pair)
+        during(i, 2, y_sum(0), True)
+        during(i, 3, y_sum(1), True)
         pl.when(i == blocks)(lambda: small_send(i))
         return carry
 
-    lax.fori_loop(0, blocks + 7, turn, 0)
+    lax.fori_loop(0, blocks + 2, turn, 0)
     pltpu.make_async_copy(small_in.at[my_place], small_got.at[my_place], own_sem).wait()
     for k, device in enumerate(others):
         small_copy(k, device).wait()
-    for ep in range(ep_size):
-        total = small_got[ep * 4]
-        for tp in range(1, 4):
-            total = total + small_got[ep * 4 + tp]
-        small_out[ep] = total
-    for step in range(steps - 2):
+    for k in range(ep_size):
+        small_out[k] = small_got[2 * k] + small_got[2 * k + 1]
+    for step in range(depth - 1):
         for which in range(2):
             z_copy(step, which).wait_recv()
 
-    def finish(which, part, target):
+    def finish(which, target):
         def tile(i, carry):
-            at = pl.multiple_of(i * 16, 16)
-            total = last_got[steps - 2 + part, which, pl.ds(at, 16), :].astype(f32)
+            at = pl.ds(pl.multiple_of(i * 16, 16), 16)
+            total = y_got[depth - 1, which, at, :].astype(f32)
             for step in range(depth - 1):
-                total = total + z_got[2 * step + part, which, pl.ds(at, 16), :].astype(f32)
-            target[pl.ds(part * share + at, 16), :] = total
+                total = total + z_got[step, which, at, :].astype(f32)
+            target[at, :] = total
             return carry
 
         lax.fori_loop(0, share // 16, tile, 0)
 
-    for part in range(2):
-        finish(0, part, grad_out)
-        finish(1, part, sum_out)
-
-    def sent(step, carry):
-        grad_pair(2 * step).wait_send()
-        grad_pair(2 * step + 1).wait_send()
-        sum_pair(step).wait_send()
+    finish(0, grad_out)
+    finish(1, sum_out)
+    for step in range(depth):
         for which in range(2):
-            last_copy(step, which).wait_send()
-
-        @pl.when(step < steps - 2)
-        def _():
-            for which in range(2):
+            y_copy(step, which).wait_send()
+            if step < depth - 1:
                 z_copy(step, which).wait_send()
 
-        return carry
-
-    lax.fori_loop(0, steps, sent, 0)
-
-
-def experts_by_links(rows_all, cots_all, code, router, enter, leave, per_owner, ep_size):
-    total_rows, width = rows_all.shape
-    depth = ep_size // 2
-    tokens = total_rows // ep_size
-    rows = tokens // 4
-    half, steps = rows // 2, 2 * depth
-    hidden = leave.shape[0]
+
+def experts_by_links(rows_all, cots_all, code, router, weights, per_owner, ep_size):
+    depth, _, _, rows, width = rows_all.shape
+    hidden = weights[2].shape[0]
     units = hidden // per_owner
     bf16, f32 = jnp.bfloat16, jnp.float32
     dma = pltpu.SemaphoreType.DMA
     vmem = pl.BlockSpec(memory_space=pltpu.VMEM)
-    anywhere = pl.BlockSpec(memory_space=pl.ANY)
-    places = 4 * ep_size
-    blocks = (depth, 2, 4, rows, width)
+    anywhere = pl.BlockSpec(memory_space=pltpu.HBM)
+    places = 2 * ep_size
     return pl.pallas_call(
         functools.partial(experts_kernel, ep_size, per_owner),
         out_shape=(
             jax.ShapeDtypeStruct((rows, width), f32),
             jax.ShapeDtypeStruct((rows, width), f32),
-            jax.ShapeDtypeStruct((ep_size, 2, 8, 128), f32),
+            jax.ShapeDtypeStruct((ep_size, 8, rows), f32),
             jax.ShapeDtypeStruct((per_owner, width, units), f32),
             jax.ShapeDtypeStruct((per_owner, width, units), f32),
             jax.ShapeDtypeStruct((hidden, width), f32),
+            jax.ShapeDtypeStruct((per_owner, width, units), bf16),
+            jax.ShapeDtypeStruct((per_owner, width, units), bf16),
+            jax.ShapeDtypeStruct((hidden, width), bf16),
         ),
-        in_specs=[anywhere, anywhere, vmem, vmem, vmem, vmem],
-        out_specs=(vmem,) * 6,
+        in_specs=[anywhere, anywhere] + [vmem] * 6,
+        out_specs=(vmem,) * 9,
         scratch_shapes=[
-            pltpu.VMEM((2, 4, half, width), bf16),
-            pltpu.VMEM((2, 4, half, width), bf16),
-            pltpu.VMEM((4 * half, hidden), bf16),
-            pltpu.VMEM((4 * half, 2 * hidden), bf16),
+            pltpu.VMEM((2, 2, rows, width), bf16),
+            pltpu.VMEM((2, 2, rows, width), bf16),
+            pltpu.VMEM((2 * rows, 2 * hidden), bf16),
+            pltpu.VMEM((2 * rows, 4 * hidden), bf16),
+            pltpu.VMEM((4 * hidden, width), f32),
             pltpu.VMEM((2 * hidden, width), f32),
-            pltpu.VMEM((2, 2, 2, 2, half, width), bf16),
-            pltpu.VMEM((steps, 2, 2, 2, half, width), bf16),
-            pltpu.VMEM((steps, 2, 2, half, width), bf16),
-            pltpu.VMEM((steps, 2, half, width), bf16),
-            pltpu.VMEM((steps - 2, 2, half, width), bf16),
-            pltpu.VMEM((places, 2, 8, 128), f32),
-            pltpu.VMEM((places, 2, 8, 128), f32),
+            pltpu.VMEM((2, 2, 2, rows, width), bf16),
+            pltpu.VMEM((depth, 2, 2, rows, width), bf16),
+            pltpu.VMEM((depth, 2, rows, width), bf16),
+            pltpu.VMEM((depth - 1, 2, rows, width), bf16),
+            pltpu.VMEM((places, 8, rows), f32),
+            pltpu.VMEM((places, 8, rows), f32),
             dma((2, 2)),
-            dma((2, 2 * steps)),
-            dma((2, 3 * steps)),
-            dma((2, steps, 2)),
-            dma((2, steps - 2, 2)),
+            dma((2, 2 * depth)),
+            dma((2, depth, 2)),
+            dma((2, depth - 1, 2)),
             dma((2, places - 1)),
             dma,
         ],
@@ -769,14 +684,7 @@
             collective_id=2, has_side_effects=True, vmem_limit_bytes=60 * 1024 * 1024
         ),
         name="experts_by_links",
-    )(
-        rows_all.reshape(blocks),
-        cots_all.reshape(blocks),
-        code.reshape(ep_size, 4, rows, -1),
-        router,
-        enter,
-        leave,
-    )
+    )(rows_all, cots_all, code.reshape(ep_size, 2, 2, rows, -1), router, *weights)
 
 
 class EpSum:
@@ -901,11 +809,17 @@
     gain,
     inputs,
     middle,
+    gate_peer,
+    up_peer,
+    down_peer,
     first_final,
     second_final,
     out_final,
     grad_input,
     small_out,
+    gate_got,
+    up_got,
+    down_got,
     datt,
     bias,
     grad_heads,
@@ -940,6 +854,7 @@
     small_sems,
     spread_sems,
     own_small_sem,
+    peer_sems,
 ):
     me = Place(ep_size)
     depth = me.depth
@@ -962,6 +877,12 @@
 
     bias[...] = jnp.where(visible_columns(info_cols[...], info_rows[...]), 0.0, -1e30)
     group_gather_body(me, 4, datt_own, datt, own_sem, gather_sems)
+
+    def to_peer(i):
+        source, target = ((gate_peer, gate_got), (up_peer, up_got), (down_peer, down_got))[i]
+        return send(source, target, peer_sems.at[0, i], peer_sems.at[1, i], me.x_peer())
+
+    exchanged = [to_peer(0)]
     for n in range(width // tile):
         cols = slice(n * tile, (n + 1) * tile)
         grads = dot(heads_in[...], datt[:, :, :, cols].reshape(tokens, tile), (0, 0))
@@ -1051,8 +972,16 @@
         for k in range(tile // 128):
             row = n * (tile // 128) + k
             small_src[last_row, row : row + 1, :] = gained[:, k * 128 : (k + 1) * 128]
+        first_sum.fold(n)
+    for step in range(width // tile, depth):
+        first_sum.fold(step)
     group = GroupTotal(me, parts, core_got, pair_got, group_sems)
     group.begin()
+    second_sum.fold(0)
+    group.exchange()
+    exchanged += [to_peer(1), to_peer(2)]
+    out_sum.pass_on()
+    second_sum.fold(1)
     small = [
         send(
             small_src.at[device[0] * 4 + device[1]],
@@ -1067,12 +996,17 @@
         small_src.at[my_place], small_got.at[my_place], own_small_sem
     )
     own_small.start()
-    group.exchange()
-    first_sum.fold(0)
-    out_sum.pass_on()
-    for step in range(1, depth):
-        first_sum.fold(step)
-    second_sum.fold(0)
+    for step in range(2, depth):
+        second_sum.fold(step)
+    first_sum.settle()
+
+    def last(value, at):
+        values_own = inputs[at, :].astype(f32)
+        factor = norm_scale(values_own)
+        return middle[at, :] + norm_back(values_own, factor, gain[...], value)
+
+    group.finish(grad_input, last)
+    second_sum.settle()
     own_small.wait()
     for copy in small:
         copy.wait_recv()
@@ -1091,19 +1025,7 @@
         for k, device in enumerate(others)
     ]
     small_out[my_place] = total
-
-    def last(value, at):
-        values_own = inputs[at, :].astype(f32)
-        factor = norm_scale(values_own)
-        return middle[at, :] + norm_back(values_own, factor, gain[...], value)
-
-    group.finish(grad_input, last)
-    second_sum.fold(1)
-    first_sum.settle()
-    for step in range(2, depth):
-        second_sum.fold(step)
     first_sum.pass_on()
-    second_sum.settle()
     out_sum.finish()
     second_sum.pass_on()
     first_sum.finish()
@@ -1115,6 +1037,8 @@
     group.sent()
     for each in [out_sum] + sums:
         each.sent()
+    for copy in exchanged:
+        copy.wait()
 
 
 def back_by_links(
@@ -1135,6 +1059,7 @@
     gain,
     inputs,
     middle,
+    peers,
     ep_size,
 ):
     tokens, width = rows_in.shape
@@ -1145,6 +1070,7 @@
     bf16, f32 = jnp.bfloat16, jnp.float32
     dma = pltpu.SemaphoreType.DMA
     vmem = pl.BlockSpec(memory_space=pltpu.VMEM)
+    anywhere = pl.BlockSpec(memory_space=pltpu.HBM)
     cosine, sine = rope_tables(position, HEAD_DIMENSION)
     cosine = jnp.concatenate([cosine[:, 0], cosine[:, 0]], axis=1)
     sine = jnp.concatenate([sine[:, 0], -sine[:, 0]], axis=1)
@@ -1167,9 +1093,10 @@
             jax.ShapeDtypeStruct(*partial(sizes[3], width)),
             jax.ShapeDtypeStruct((share, width), f32),
             jax.ShapeDtypeStruct(blocks.shape, f32),
-        ),
-        in_specs=[vmem] * 19,
-        out_specs=(vmem,) * 5,
+        )
+        + tuple(jax.ShapeDtypeStruct(p.shape, p.dtype) for p in peers),
+        in_specs=[vmem] * 19 + [anywhere] * 3,
+        out_specs=(vmem,) * 5 + (anywhere,) * 3,
         scratch_shapes=[
             pltpu.VMEM((2, 2, share, width), bf16),
             pltpu.VMEM((tokens, tokens), f32),
@@ -1198,7 +1125,7 @@
         + [dma((2, 2, depth))] * 3
         + [dma((2, depth, 1))]
         + [dma((2, depth))] * 3
-        + [dma((2, 3)), dma((2, places - 1)), dma((2, places - 1)), dma],
+        + [dma((2, 3)), dma((2, places - 1)), dma((2, places - 1)), dma, dma((2, 3))],
         compiler_params=pltpu.CompilerParams(
             collective_id=5, has_side_effects=True, vmem_limit_bytes=60 * 1024 * 1024
         ),
@@ -1223,6 +1150,7 @@
         gain[None, :],
         inputs,
         middle,
+        *peers,
     )
     return got
 
@@ -1230,11 +1158,14 @@
 def deliver_kernel(
     ep_size,
     sizes,
+    rows_in,
+    sums_in,
     gate_in,
     up_in,
     down_in,
-    rows_in,
-    sums_in,
+    gate_got,
+    up_got,
+    down_got,
     first,
     second,
     third,
@@ -1255,10 +1186,12 @@
     key,
     value,
     out,
+    gate,
+    up,
+    down,
     sems,
 ):
-    pairs = ((gate_in, gate_out), (up_in, up_out), (down_in, down_out), (rows_in, rows_out))
-    pairs += ((sums_in, sums_out),)
+    pairs = ((rows_in, rows_out), (sums_in, sums_out))
     copies = [
         pltpu.make_async_copy(source, target, sems.at[i]) for i, (source, target) in enumerate(pairs)
     ]
@@ -1271,6 +1204,10 @@
         copies.append(pltpu.make_async_copy(source, target, sems.at[i]))
         copies[-1].start()
 
+    trios = ((gate, gate_in, gate_got), (up, up_in, up_got), (down, down_in, down_got))
+    for i, (total, mine, got) in enumerate(trios):
+        total[...] = mine[...] + got[...].astype(f32)
+        leave(total, (gate_out, up_out, down_out)[i], 2 + i)
     out[...] = third[...].astype(f32)
     leave(out, out_out, 5)
     at = 0
@@ -1289,10 +1226,10 @@
         copy.wait()
 
 
-def deliver(gate, up, down, rows, sums, got, small, sizes, expert_count, ep_size):
+def deliver(owned, peers, rows, sums, got, small, sizes, expert_count, ep_size):
     width = rows.shape[1]
     f32 = jnp.float32
-    vmem, anywhere = pl.BlockSpec(memory_space=pltpu.VMEM), pl.BlockSpec(memory_space=pl.ANY)
+    vmem, anywhere = pl.BlockSpec(memory_space=pltpu.VMEM), pl.BlockSpec(memory_space=pltpu.HBM)
     first, second, third = (g.reshape((ep_size,) + g.shape[2:]) for g in got)
 
     def like(value):
@@ -1301,20 +1238,22 @@
     shapes = [(ep_size, k, width) for k in sizes]
     results = pl.pallas_call(
         functools.partial(deliver_kernel, ep_size, sizes),
-        out_shape=(like(gate), like(up), like(down), like(rows), like(sums))
+        out_shape=tuple(like(a) for a in owned)
+        + (like(rows), like(sums))
         + tuple(jax.ShapeDtypeStruct(shape, f32) for shape in shapes)
         + (
             jax.ShapeDtypeStruct((expert_count, width), f32),
             jax.ShapeDtypeStruct((1, width), f32),
             jax.ShapeDtypeStruct((1, width), f32),
         ),
-        in_specs=[anywhere] * 5 + [vmem] * 4,
+        in_specs=[anywhere] * 2 + [vmem] * 10,
         out_specs=(anywhere,) * 9 + (vmem,) * 3,
         scratch_shapes=[pltpu.VMEM(shape, f32) for shape in shapes]
+        + [pltpu.VMEM(a.shape, f32) for a in owned]
         + [pltpu.SemaphoreType.DMA((9,))],
-        compiler_params=pltpu.CompilerParams(vmem_limit_bytes=32 * 1024 * 1024),
+        compiler_params=pltpu.CompilerParams(vmem_limit_bytes=40 * 1024 * 1024),
         name="deliver",
-    )(gate, up, down, rows, sums, first, second, third, small)
+    )(rows, sums, *owned, *peers, first, second, third, small)
     gate, up, down, rows, sums = results[:5]
     query, key, value, out = (g.reshape(-1, width) for g in results[5:9])
     router, first_gain, second_gain = results[9:]
@@ -1330,7 +1269,7 @@
         router,
         gate,
         up,
-        down,
+        down.reshape(gate.shape[0], -1, width),
     )
 
 
@@ -1344,9 +1283,7 @@
     return lax.psum_scatter(value_rows, "tp", scatter_dimension=0, tiled=True).astype(jnp.float32)
 
 
-def gather_all(value_rows, by_links):
-    if by_links:
-        return gather_by_links(value_rows, lax.axis_size("ep"))
+def gather_all(value_rows):
     return lax.all_gather(value_rows, ("ep", "tp"), axis=0, tiled=True)
 
 
@@ -1391,28 +1328,31 @@
     return jnp.pad(code, ((0, 0), (0, lanes)), constant_values=-1.0).astype(jnp.bfloat16)
 
 
-def run_experts(rows_all, cots_all, code, w_router, w_gate, w_up, w_down, by_links):
+def expert_weights(w_gate, w_up, w_down):
+    enter = jnp.concatenate([w[e] for w in (w_gate, w_up) for e in range(w.shape[0])], axis=1)
+    return enter, w_down.reshape(-1, w_down.shape[2])
+
+
+def run_experts(rows_all, cots_all, code, w_router, w_gate, w_up, w_down, weights, by_links):
     per_owner, width, units = w_gate.shape
     expert_count = w_router.shape[0]
     ep_size, tp_size = lax.axis_size("ep"), lax.axis_size("tp")
     hidden = per_owner * units
     router = jnp.roll(w_router, -lax.axis_index("ep") * per_owner, axis=0)
     router = jnp.pad(router, ((0, -expert_count % 128), (0, 0)))
-    enter = jnp.concatenate([w[e] for w in (w_gate, w_up) for e in range(per_owner)], axis=1)
-    leave = w_down.reshape(hidden, width)
     if by_links:
-        grads, sums, small, gate, up, down = experts_by_links(
-            rows_all, cots_all, code, router, enter, leave, per_owner, ep_size
+        grads, sums, small, *owned = experts_by_links(
+            rows_all, cots_all, code, router, weights, per_owner, ep_size
         )
         share = grads.shape[0]
         return (
             grads,
             sums,
-            small[:, :, :per_owner, : share // 2].swapaxes(1, 2).reshape(expert_count, share).T,
-            gate,
-            up,
-            down.reshape(w_down.shape),
-        )
+            small[:, :per_owner].reshape(expert_count, share).T,
+            owned[:3],
+            owned[3:],
+        )
+    enter, leave = expert_weights(w_gate, w_up, w_down)
     used, kept = code >= 0, (code == 0).astype(jnp.float32)
     logits = jnp.einsum("rd,ed->re", rows_all, router, preferred_element_type=jnp.float32)
     gates = jnp.repeat((kept * masked_softmax(logits, used))[:, :per_owner], units, axis=1)
@@ -1454,9 +1394,8 @@
         scatter(grads.astype(jnp.bfloat16)).astype(jnp.float32),
         scatter(sums.astype(jnp.bfloat16)).astype(jnp.float32),
         scatter(columns),
-        both[0],
-        both[1],
-        down.reshape(w_down.shape),
+        (both[0], both[1], down),
+        None,
     )
 
 
@@ -1565,7 +1504,12 @@
     block_rows = 512
     by_links = lax.axis_size("tp") == 4 and lax.axis_size("ep") == 8
     order = pair_order(expert_ids, slot_order, expert_count)
-    cot_all = gather_all(cotangent, False)
+    if by_links:
+        near = expert_weights(w_gate, w_up, w_down)
+        far = [lax.ppermute(w, "tp", [(0, 2), (1, 3), (2, 0), (3, 1)]) for w in near]
+        weights = (near[0], far[0], near[1], far[1])
+    else:
+        weights = None
     inputs_own = hidden_in.astype(jnp.float32)
     gain_one = gain_attn.astype(jnp.float32)
     gain_two = gain_ffn.astype(jnp.float32)
@@ -1609,13 +1553,16 @@
     )
     scale_two = norm_scale(middle_own)
     normed_own = (middle_own * scale_two * gain_two).astype(jnp.bfloat16)
-    normed_two = gather_all(normed_own, by_links)
+    if by_links:
+        normed_two, cot_all = gather_by_links([normed_own, cotangent], lax.axis_size("ep"))
+    else:
+        normed_two, cot_all = gather_all(normed_own), gather_all(cotangent)
     used = lax.dynamic_slice_in_dim(order, row_start, share, 1).T < LAST
     gates = masked_softmax(
         jnp.einsum("rd,ed->re", normed_own, w_router, preferred_element_type=jnp.float32), used
     )
-    grad_normed_own, combined_own, grad_gates_own, grad_w_gate, grad_w_up, grad_w_down = (
-        run_experts(normed_two, cot_all, code, w_router, w_gate, w_up, w_down, by_links)
+    grad_normed_own, combined_own, grad_gates_own, owned, peers = run_experts(
+        normed_two, cot_all, code, w_router, w_gate, w_up, w_down, weights, by_links
     )
     output_own = (middle_own + combined_own).astype(jnp.bfloat16)
     inner_gate = jnp.sum(gates * grad_gates_own, axis=-1, keepdims=True)
@@ -1628,7 +1575,7 @@
         middle_own, scale_two, gain_two, grad_normed_own
     )
     if by_links:
-        *got, grad_input, small = back_by_links(
+        *got, grad_input, small, gate_got, up_got, down_got = back_by_links(
             grad_middle.astype(jnp.bfloat16),
             head_outputs,
             w_out,
@@ -1646,14 +1593,14 @@
             gain_one,
             hidden_in,
             grad_middle,
+            peers,
             lax.axis_size("ep"),
         )
         ep_size = lax.axis_size("ep")
         weights = (w_query, key_projection_weight, value_projection_weight, w_out)
         return deliver(
-            grad_w_gate,
-            grad_w_up,
-            grad_w_down,
+            owned,
+            (gate_got, up_got, down_got),
             grad_input,
             output_own,
             got,
@@ -1729,9 +1676,9 @@
         grad_w_out,
         grad_gain_ffn,
         grad_router,
-        grad_w_gate,
-        grad_w_up,
-        grad_w_down,
+        owned[0],
+        owned[1],
+        owned[2].reshape(w_down.shape),
     )
 
 

time: 445 us -> 472 us (1.061)
  Pallas kernels: 382 us -> 397 us
  local copies, waits for them, and re-layouts: 18.8 us -> 32.9 us
  between operations: 14.7 us -> 1.12 us
  other arithmetic: 16.4 us -> 25.6 us
    pallas_call x1, Pallas kernels: 21.1 us -> 55.8 us  [front_gather(): pl.pallas_call(functools.partial(front_gather_kernel, ep_size, pieces), o...]
    pallas_call x1, Pallas kernels: 136 us -> 110 us  [experts_by_links(): pl.pallas_call(functools.partial(experts_kernel, ep_size, per_owner), out...]
    pallas_call x1, Pallas kernels: 119 us -> 126 us  [back_by_links(): pl.pallas_call(functools.partial(back_kernel, ep_size, heads, small.shape...]
    unnamed x80 -> x82, local copies, waits for them, and re-layouts: 7.95 us -> 14.5 us
  transfers between devices with their start and end apart: 1 -> 2, of which waited for: 0 -> 0; matrix products, arithmetic and copies ran while one was open for 7% -> 11% of each run, Pallas kernels for 27% -> 33%
where the time goes in v8:
time: 472 us; the launch traced here: 471 us
  Pallas kernels  397 us (84%)
  local copies, waits for them, and re-layouts  32.9 us (7%)
  other arithmetic  25.6 us (5%)
  matrix products  12.1 us (3%)
    pallas_call x1, Pallas kernels, back_by_links(): pl.pallas_call(functools.partial(back_kernel, ep_size, heads, small.shape...  126 us
    pallas_call x1, Pallas kernels, experts_by_links(): pl.pallas_call(functools.partial(experts_kernel, ep_size, per_owner), out...  110 us
    pallas_call x1, Pallas kernels, gather_by_links(): pl.pallas_call(functools.partial(gather_kernel, ep_size, count), out_shap...  85.7 us
    pallas_call x1, Pallas kernels, front_gather(): pl.pallas_call(functools.partial(front_gather_kernel, ep_size, pieces), o...  55.8 us
    unnamed x82, local copies, waits for them, and re-layouts  14.5 us
    pallas_call x1, Pallas kernels, group_total(): pl.pallas_call(functools.partial(group_total_kernel, ep_size), out_shape=...  13.4 us
  transfers between devices with their start and end apart: 2, of which 0 were waited for; matrix products, arithmetic and copies ran while one was open for 11% of the time, Pallas kernels for 33%

profile of v8, /device:TPU:0, one launch (start us, length us, event | category | flops | bytes accessed | tf_op | source)
XLA Modules:
  0.0 471.3 jit_solution(11433769921412614699)
XLA Ops:
  0.6 1.5 slice_bitcast_fusion.1
  2.4 3.0 collective-permute-start
  7.3 1.8 fusion.14
  10.1 0.9 fusion.6.own
  11.0 55.8 %front_gather.1 = (bf16[2,2,128,1536]{3,2,1,0:T(8,128)(2,1)}, s32[8,16,512]{2,1,0:T(8,128)}) custom-call(bf16[128,1536]{1,0:T(8,128)(2,1)} %fusion.6.own, s32[16,512]{1,0:T(8,128)} %select_reduce_fusion.table), custom_call_target="tpu_custom_call" | custom-call | tf_op jit(solution)/shard_map/front_gather/pallas_call | solution.py:217
  66.8 2.7 fusion.36
  71.7 0.8 copy.86
  72.4 0.8 pad_maximum_fusion.1
  73.9 1.5 compare_and_fusion
  75.4 2.1 fusion.1
  77.5 1.3 fusion
  79.4 2.0 fusion.3
  81.4 1.0 convolution_convert_fusion
  82.4 13.4 %group_total.1 = f32[128,1536]{1,0:T(8,128)S(1)} custom-call(bf16[2,2,128,1536]{3,2,1,0:T(8,128)(2,1)S(1)} %bitcast.82), custom_call_target="tpu_custom_call" | custom-call | tf_op jit(solution)/shard_map/group_total/pallas_call | solution.py:329
  97.7 1.4 select_reduce_fusion.3
  99.1 0.8 copy.94
  99.9 1.0 select_reduce_fusion.1
  101.1 1.0 and_not_fusion
  102.2 0.8 fusion.12
  102.9 1.9 copy.99.heads_in
  104.9 1.3 broadcast_in_dim.127.gain
  106.9 2.2 copy.109
  109.1 1.3 add.142
  110.4 0.9 copy.100.queries
  112.7 1.5 multiply_convert_fusion.refs_0_
  114.8 0.8 copy.108
  116.4 1.3 pad.34.info_rows
  117.7 2.4 pad.30.clone
  120.1 85.7 %gather_by_links.1 = (bf16[4,2,2,128,1536]{4,3,2,1,0:T(8,128)(2,1)}, bf16[4,2,2,128,1536]{4,3,2,1,0:T(8,128)(2,1)}) custom-call(bf16[128,1536]{1,0:T(8,128)(2,1)} %multiply_convert_fusion.refs_0_, bf16[128,1536]{1,0:T(8,128)(2,1)} %refs_1_.1), custom_call_target="tpu_custom_call" | custom-call | tf_op jit(solution)/shard_map/gather_by_links/pallas_call | solution.py:165
  205.8 1.6 pad.31.router
  207.4 1.3 pad.32.log_sums
  208.7 1.0 fusion.37
  210.5 1.0 pad_maximum_fusion.2
  211.5 110.2 %experts_by_links.1 = (f32[128,1536]{1,0:T(8,128)}, f32[128,1536]{1,0:T(8,128)}, f32[8,8,128]{2,1,0:T(8,128)}, f32[2,1536,128]{2,1,0:T(8,128)}, f32[2,1536,128]{...) custom-call(bf16[4,2,2,128,1536]{4,3,2,1,0:T(8,128)(2,1)} %get-tuple, ...), custom_call_target="tpu_custom_call" | custom-call | tf_op jit(solution)/shard_map/experts_by_links/pallas_call | solution.py:648
  321.7 0.9 slice.39
  322.9 1.9 multiply_reduce_fusion
  325.5 2.5 fusion.33
  328.0 126.3 %back_by_links.1 = (bf16[4,2,80,768]{3,2,1,0:T(8,128)(2,1)}, bf16[4,2,80,768]{3,2,1,0:T(8,128)(2,1)}, bf16[4,2,48,1536]{3,2,1,0:T(8,128)(2,1)}, f32[128,1536]{1,...) custom-call(bf16[128,1536]{1,0:T(8,128)(2,1)} %get-tuple-element.80., ...), custom_call_target="tpu_custom_call" | custom-call | tf_op jit(solution)/shard_map/back_by_links/pallas_call | solution.py:1088
  454.3 1.4 copy-done.2
  455.7 1.3 copy-done.3
  457.0 1.2 copy-done.4
  458.2 1.2 copy-done.5
  459.4 1.1 copy-done.6
  460.5 1.1 copy-done.7
  461.7 1.1 copy-done.8
  462.8 1.1 copy-done.9
  463.9 0.9 copy-done.10
  464.9 5.1 %deliver.1 = (f32[2,1536,128]{2,1,0:T(8,128)}, f32[2,1536,128]{2,1,0:T(8,128)}, f32[256,1536]{1,0:T(8,128)}, f32[128,1536]{1,0:T(8,128)}, bf16[128,1536]{1,0:T(8...) custom-call(f32[128,1536]{1,0:T(8,128)S(1)} %copy-done.6, ...), custom_call_target="tpu_custom_call" | custom-call | tf_op jit(solution)/shard_map/deliver/pallas_call | solution.py:1239
  (114 shorter events, 15.1 us)
Async XLA Ops:
  2.1 3.4 copy-start.32
  2.1 5.0 %copy-start.34 = (bf16[1536]{0:T(1024)(128)(2,1)S(1)}, bf16[1536]{0:T(1024)(128)(2,1)}, u32[]{:S(2)}) copy-start(bf16[1536]{0:T(1024)(128)(2,1)} %param.17) | copy-start | bytes 9220
  2.1 5.0 %copy-start.11 = (bf16[128,1536]{1,0:T(8,128)(2,1)S(1)}, bf16[128,1536]{1,0:T(8,128)(2,1)}, u32[]{:S(2)}) copy-start(bf16[128,1536]{1,0:T(8,128)(2,1)} %inputs.1) | copy-start | bytes 1179652
  2.1 5.2 %copy-start.33 = (s32[512]{0:T(512)S(1)}, s32[512]{0:T(512)}, u32[]{:S(2)}) copy-start(s32[512]{0:T(512)} %param.30) | copy-start | bytes 6148
  2.2 7.2 %copy-start.35 = (s32[512,8]{0,1:T(8,128)S(1)}, s32[512,8]{0,1:T(8,128)}, u32[]{:S(2)}) copy-start(s32[512,8]{0,1:T(8,128)} %param.28) | copy-start | bytes 49156
  2.2 7.2 %copy-start.36 = (s32[512,8]{0,1:T(8,128)S(1)}, s32[512,8]{0,1:T(8,128)}, u32[]{:S(2)}) copy-start(s32[512,8]{0,1:T(8,128)} %param.27) | copy-start | bytes 49156
  2.4 67.2 %copy-start.12 = (bf16[1536,512]{1,0:T(8,128)(2,1)}, bf16[1536,512]{1,0:T(8,128)(2,1)S(1)}, u32[]{:S(2)}) copy-start(bf16[1536,512]{1,0:T(8,128)(2,1)S(1)} %pad_maximum_fusion.enter_own) | copy-start | bytes 4718596
  2.4 209.1 %collective-permute-start = (bf16[1536,512]{1,0:T(8,128)(2,1)S(1)}, bf16[1536,512]{1,0:T(8,128)(2,1)}, u32[]{:S(2)}, u32[]{:S(2)}) collective-permute-start(bf16[1536,512]{1,0:T(8,128)(2,1)S(1)} %pad_maximum_fusion.enter_own), channel_id=1, source_target_pairs={{0,2},{1,3},{2,0},{3,1},{4,6},{5,7},{6,4},{7,5},{8,10},{9,11},{10,... | collective-permute-start | bytes 4718600 | tf_op jit(solution)/shard_map/ppermute | solution.py:1509
  5.4 206.1 %collective-permute-start.1 = (bf16[256,1536]{1,0:T(8,128)(2,1)}, bf16[256,1536]{1,0:T(8,128)(2,1)}, u32[]{:S(2)}, u32[]{:S(2)}) collective-permute-start(bf16[256,1536]{1,0:T(8,128)(2,1)} %bitcast.24.leave_own), channel_id=1, source_target_pairs={{0,2},{1,3},{2,0},{3,1},{4,6},{5,7},{6,4},{7,5},{8,10},{9,11},{10,... | collective-permute-start | bytes 2359304 | tf_op jit(solution)/shard_map/ppermute | solution.py:1509
  66.8 2.7 copy-start.14
  66.8 2.7 copy-start.29
  69.6 1.5 copy-start.17
  70.4 3.5 copy-start.24
  70.4 3.5 copy-start.37
  71.1 2.1 copy-start.30
  71.6 5.8 %copy-start.21 = (bf16[512,128]{1,0:T(8,128)(2,1)}, bf16[512,128]{1,0:T(8,128)(2,1)S(1)}, u32[]{:S(2)}) copy-start(bf16[512,128]{1,0:T(8,128)(2,1)S(1)} %convolution_convert_fusion.1.values) | copy-start | bytes 393220
  77.5 2.0 copy-start.31
  79.4 2.0 copy-start.15
  81.4 1.0 copy-start.20
  82.4 14.2 %copy-start.22 = (s32[8,16,512]{2,1,0:T(8,128)S(1)}, s32[8,16,512]{2,1,0:T(8,128)}, u32[]{:S(2)}) copy-start(s32[8,16,512]{2,1,0:T(8,128)} %get-tuple-element.48) | copy-start | bytes 786436
  96.1 14.3 %copy-start.19 = (bf16[512,6,64]{0,2,1:T(8,128)(2,1)S(1)}, bf16[512,6,64]{0,2,1:T(8,128)(2,1)}, u32[]{:S(2)}) copy-start(bf16[512,6,64]{0,2,1:T(8,128)(2,1)} %pad_maximum_fusion.1) | copy-start | bytes 1179652
  96.7 0.7 copy-start.26
  102.9 8.4 %copy-start.25 = (bf16[512,2,64]{0,2,1:T(8,128)(2,1)S(1)}, bf16[512,2,64]{0,2,1:T(8,128)(2,1)}, u32[]{:S(2)}) copy-start(bf16[512,2,64]{0,2,1:T(8,128)(2,1)} %maximum_convert_fusion) | copy-start | bytes 393220
  102.9 9.1 %copy-start.27 = (bf16[16,1536]{1,0:T(8,128)(2,1)S(1)}, bf16[16,1536]{1,0:T(8,128)(2,1)}, u32[]{:S(2)}) copy-start(bf16[16,1536]{1,0:T(8,128)(2,1)} %param.23) | copy-start | bytes 147460
  114.2 94.5 %copy-start.13 = (bf16[128,1536]{1,0:T(8,128)(2,1)S(1)}, bf16[128,1536]{1,0:T(8,128)(2,1)}, u32[]{:S(2)}) copy-start(bf16[128,1536]{1,0:T(8,128)(2,1)} %multiply_convert_fusion.refs_0_) | copy-start | bytes 1179652
  116.4 94.1 %copy-start.23 = (f32[512,32]{1,0:T(8,128)S(1)}, f32[512,32]{1,0:T(8,128)}, u32[]{:S(2)}) copy-start(f32[512,32]{1,0:T(8,128)} %get-tuple-element.99) | copy-start | bytes 196612
  211.5 111.4 %copy-start.28 = (bf16[16,1536]{1,0:T(8,128)(2,1)S(1)}, bf16[16,1536]{1,0:T(8,128)(2,1)}, u32[]{:S(2)}) copy-start(bf16[16,1536]{1,0:T(8,128)(2,1)} %param.23) | copy-start | bytes 147460
  211.5 111.4 %copy-start.38 = (f32[128]{0:T(128)S(1)}, f32[128]{0:T(128)}, u32[]{:S(2)}) copy-start(f32[128]{0:T(128)} %get-tuple-element.106) | copy-start | bytes 1540
  321.7 3.9 copy-start.16
  321.7 3.9 copy-start.18
  321.7 3.8 copy-start.39
  328.0 126.3 %copy-start = (f32[2,1536,128]{2,1,0:T(8,128)S(1)}, f32[2,1536,128]{2,1,0:T(8,128)}, u32[]{:S(2)}) copy-start(f32[2,1536,128]{2,1,0:T(8,128)} %get-tuple-element.56.gate_in) | copy-start | bytes 4718596
  328.0 126.3 %copy-start.1 = (f32[2,1536,128]{2,1,0:T(8,128)S(1)}, f32[2,1536,128]{2,1,0:T(8,128)}, u32[]{:S(2)}) copy-start(f32[2,1536,128]{2,1,0:T(8,128)} %get-tuple-element.57.up_in) | copy-start | bytes 4718596
  454.3 1.4 copy-start.2
  455.7 1.3 copy-start.3
  457.0 1.2 copy-start.4
  458.2 1.2 copy-start.5
  459.4 1.1 copy-start.6
  460.5 1.1 copy-start.7
  461.7 1.1 copy-start.8
  462.8 1.1 copy-start.9
  463.9 0.9 copy-start.10

commit v9 on v8

--- a/solution.py
+++ b/solution.py
@@ -114,72 +114,6 @@
     return copy
 
 
-def gather_kernel(ep_size, count, *refs):
-    owns, outs = refs[:count], refs[count : 2 * count]
-    own_sems, z_sems, y_sems, core_sems = refs[2 * count :]
-    me = Place(ep_size)
-    depth = me.depth
-    meet([me.sibling(), me.y_peer()] + [me.device(z=me.after(s)) for s in range(1, depth)])
-    started = []
-
-    def forward(source, target, sems, a, slot, device):
-        started.append(send(source, target, sems.at[0, a, slot], sems.at[1, a, slot], device))
-
-    def landed(block, sems, a, slot):
-        pltpu.make_async_copy(block, block, sems.at[1, a, slot]).wait()
-
-    local = []
-    for a in range(count):
-        own, mine = owns[a], outs[a].at[me.z, me.y, me.c]
-        for s in range(1, depth):
-            forward(own, mine, z_sems, a, s, me.device(z=me.after(s)))
-        forward(own, mine, y_sems, a, 0, me.y_peer())
-        forward(own, mine, core_sems, a, 0, me.sibling())
-        local.append(pltpu.make_async_copy(own, mine, own_sems.at[a]))
-        local[a].start()
-    for a in range(count):
-        for s in range(1, depth):
-            block = outs[a].at[me.before(s), me.y, me.c]
-            landed(block, z_sems, a, s)
-            forward(block, block, y_sems, a, s, me.y_peer())
-            forward(block, block, core_sems, a, s, me.sibling())
-    for a in range(count):
-        for s in range(depth):
-            block = outs[a].at[me.before(s), 1 - me.y, me.c]
-            landed(block, y_sems, a, s)
-            forward(block, block, core_sems, a, depth + s, me.sibling())
-    for a in range(count):
-        local[a].wait()
-        for s in range(depth):
-            for y, slot in ((me.y, s), (1 - me.y, depth + s)):
-                landed(outs[a].at[me.before(s), y, 1 - me.c], core_sems, a, slot)
-    for copy in started:
-        copy.wait_send()
-
-
-def gather_by_links(arrays, ep_size):
-    rows, width = arrays[0].shape
-    depth, count = ep_size // 2, len(arrays)
-    dma = pltpu.SemaphoreType.DMA
-    anywhere = pl.BlockSpec(memory_space=pltpu.HBM)
-    return pl.pallas_call(
-        functools.partial(gather_kernel, ep_size, count),
-        out_shape=tuple(
-            jax.ShapeDtypeStruct((depth, 2, 2, rows, width), a.dtype) for a in arrays
-        ),
-        in_specs=[anywhere] * count,
-        out_specs=(anywhere,) * count,
-        scratch_shapes=[
-            dma((count,)),
-            dma((2, count, depth)),
-            dma((2, count, depth)),
-            dma((2, count, 2 * depth)),
-        ],
-        compiler_params=pltpu.CompilerParams(collective_id=1, has_side_effects=True),
-        name="gather_by_links",
-    )(*arrays)
-
-
 def add_into(target, other):
     def tile(i, carry):
         at = pl.ds(pl.multiple_of(i * 16, 16), 16)
@@ -187,46 +121,6 @@
         return carry
 
     lax.fori_loop(0, target.shape[0] // 16, tile, 0)
-
-
-def front_gather_kernel(
-    ep_size, pieces, own, table, out, tables, own_sem, sems, table_own_sem, table_sems
-):
-    me = Place(ep_size)
-    mine = lax.axis_index("ep")
-    tp = lax.axis_index("tp")
-    peers = [(lax.rem(mine + k, ep_size), tp) for k in range(1, ep_size)]
-    meet([me.sibling(), me.x_peer()] + peers)
-    local = pltpu.make_async_copy(table, tables.at[mine], table_own_sem)
-    local.start()
-    copies = [
-        send(table, tables.at[mine], table_sems.at[0, k], table_sems.at[1, k], device)
-        for k, device in enumerate(peers)
-    ]
-    group_gather_body(me, pieces, own, out, own_sem, sems)
-    local.wait()
-    for copy in copies:
-        copy.wait()
-
-
-def front_gather(value_rows, table, ep_size):
-    rows, width = value_rows.shape
-    pieces = 4
-    dma = pltpu.SemaphoreType.DMA
-    anywhere = pl.BlockSpec(memory_space=pltpu.HBM)
-    every, tables = pl.pallas_call(
-        functools.partial(front_gather_kernel, ep_size, pieces),
-        out_shape=(
-            jax.ShapeDtypeStruct((2, 2, rows, width), value_rows.dtype),
-            jax.ShapeDtypeStruct((ep_size,) + table.shape, table.dtype),
-        ),
-        in_specs=[anywhere] * 2,
-        out_specs=(anywhere,) * 2,
-        scratch_shapes=[dma, dma((2, 3 * pieces)), dma, dma((2, ep_size - 1))],
-        compiler_params=pltpu.CompilerParams(collective_id=6, has_side_effects=True),
-        name="front_gather",
-    )(value_rows, table)
-    return every.reshape(-1, width), tables
 
 
 def group_gather_body(me, pieces, own, out, own_sem, sems):
@@ -311,36 +205,6 @@
     def sent(self):
         for copy in self.core + [self.pair]:
             copy.wait_send()
-
-
-def group_total_kernel(ep_size, parts, out, core_got, pair_got, sems):
-    me = Place(ep_size)
-    meet([me.sibling(), me.x_peer()])
-    total = GroupTotal(me, parts, core_got, pair_got, sems)
-    total.begin()
-    total.exchange()
-    total.finish(out)
-    total.sent()
-
-
-def group_total(value_rows, ep_size, call):
-    rows, width = value_rows.shape[0] // 4, value_rows.shape[1]
-    vmem = pl.BlockSpec(memory_space=pltpu.VMEM)
-    return pl.pallas_call(
-        functools.partial(group_total_kernel, ep_size),
-        out_shape=jax.ShapeDtypeStruct((rows, width), jnp.float32),
-        in_specs=[vmem],
-        out_specs=vmem,
-        scratch_shapes=[
-            pltpu.VMEM((2, rows, width), jnp.bfloat16),
-            pltpu.VMEM((rows, width), jnp.bfloat16),
-            pltpu.SemaphoreType.DMA((2, 3)),
-        ],
-        compiler_params=pltpu.CompilerParams(
-            collective_id=call, has_side_effects=True, vmem_limit_bytes=32 * 1024 * 1024
-        ),
-        name="group_total",
-    )(value_rows.reshape(2, 2, rows, width))
 
 
 def all_others(ep_size):
@@ -784,6 +648,321 @@
     parent = jnp.where(query_seg >= 5, (query_seg - 5) // 2 + 1, -1)
     above = (key_seg == query_seg) | (key_seg == 0) | (key_seg == parent)
     return above & (key_pos <= query_pos)
+
+
+class LinkGather:
+    def __init__(self, me, own, out, sems):
+        self.me, self.own, self.out = me, own, out
+        self.own_sem, self.z_sems, self.y_sems, self.core_sems = sems
+        self.begun = []
+        depth = me.depth
+        self.found = [(me.z, 0, None)]
+        for d in range(1, depth):
+            self.found.append((me.z - d, d, me.z >= d))
+            self.found.append((me.z + d, depth - 1 + d, me.z + d < depth))
+
+    def guard(self, *conditions):
+        given = [c for c in conditions if c is not None]
+        if not given:
+            return lambda body: body()
+        total = given[0]
+        for c in given[1:]:
+            total = total & c
+        return pl.when(total)
+
+    def go(self, source, place, sems, slot, device, *conditions):
+        def copy():
+            return pltpu.make_async_remote_copy(
+                src_ref=source,
+                dst_ref=place,
+                send_sem=sems.at[0, slot],
+                recv_sem=sems.at[1, slot],
+                device_id=device,
+                device_id_type=MESH,
+            )
+
+        self.guard(*conditions)(lambda: copy().start())
+        self.begun.append((copy, conditions))
+
+    def landed(self, place, sems, slot, condition):
+        self.guard(condition)(
+            lambda: pltpu.make_async_copy(place, place, sems.at[1, slot]).wait()
+        )
+
+    def up(self, source, place, d, condition):
+        me = self.me
+        device = me.device(z=lax.rem(me.z + 1, me.depth))
+        self.go(source, place, self.z_sems, d, device, condition, me.z < me.depth - 1)
+
+    def down(self, source, place, d, condition):
+        me = self.me
+        device = me.device(z=lax.rem(me.z + me.depth - 1, me.depth))
+        self.go(source, place, self.z_sems, me.depth - 1 + d, device, condition, me.z > 0)
+
+    def place(self, z, y, c):
+        return self.out.at[lax.rem(z + self.me.depth, self.me.depth), y, c]
+
+    def begin(self):
+        me = self.me
+        mine = self.place(me.z, me.y, me.c)
+        self.up(self.own, mine, 1, None)
+        self.down(self.own, mine, 1, None)
+        self.go(self.own, mine, self.y_sems, 0, me.y_peer())
+        self.go(self.own, mine, self.core_sems, 0, me.sibling())
+        self.local = pltpu.make_async_copy(self.own, mine, self.own_sem)
+        self.local.start()
+
+    def relay(self, d):
+        me = self.me
+        for z, slot, condition in self.found[2 * d - 1 : 2 * d + 1]:
+            block = self.place(z, me.y, me.c)
+            self.landed(block, self.z_sems, slot, condition)
+            if d < me.depth - 1:
+                (self.up if slot < me.depth else self.down)(block, block, d + 1, condition)
+            self.go(block, block, self.y_sems, slot, me.y_peer(), condition)
+            self.go(block, block, self.core_sems, slot, me.sibling(), condition)
+
+    def cross(self, first, last):
+        me = self.me
+        for z, slot, condition in self.found[first:last]:
+            block = self.place(z, 1 - me.y, me.c)
+            self.landed(block, self.y_sems, slot, condition)
+            self.go(
+                block, block, self.core_sems, 2 * me.depth - 1 + slot, me.sibling(), condition
+            )
+
+    def finish(self):
+        me = self.me
+        for z, slot, condition in self.found:
+            for y, at in ((me.y, slot), (1 - me.y, 2 * me.depth - 1 + slot)):
+                self.landed(self.place(z, y, 1 - me.c), self.core_sems, at, condition)
+        self.local.wait()
+        for copy, conditions in self.begun:
+            self.guard(*conditions)(lambda: copy().wait_send())
+
+
+def front_kernel(
+    ep_size,
+    heads,
+    inputs,
+    gain_one,
+    gain_two,
+    w_query,
+    w_key,
+    w_value,
+    w_out,
+    cosine,
+    sine,
+    info_cols,
+    info_rows,
+    table,
+    cots,
+    enter_near,
+    leave_near,
+    rows_out,
+    queries,
+    keys,
+    values,
+    heads_out,
+    log_sums,
+    middle,
+    tables,
+    cots_all,
+    normed_all,
+    normed_own,
+    enter_far,
+    leave_far,
+    first_own,
+    bias,
+    parts,
+    core_got,
+    pair_got,
+    own_sem,
+    gather_sems,
+    table_own_sem,
+    table_sems,
+    group_sems,
+    far_sems,
+    cots_sems,
+    normed_sems,
+):
+    me = Place(ep_size)
+    depth = me.depth
+    f32, bf16 = jnp.float32, jnp.bfloat16
+    share, width = inputs.shape
+    tokens = 4 * share
+    size = HEAD_DIMENSION
+    groups = keys.shape[1] // size
+    per_group = heads // groups
+    scale = size ** (-0.5)
+    ep, tp = lax.axis_index("ep"), lax.axis_index("tp")
+    peers = [(lax.rem(ep + k, ep_size), tp) for k in range(1, ep_size)]
+    meet([me.sibling(), me.x_peer()] + peers)
+
+    def dot(a, b, contract):
+        return lax.dot_general(
+            a, b, ((contract[:1], contract[1:]), ((), ())), preferred_element_type=f32
+        )
+
+    cots_gather = LinkGather(me, cots, cots_all, cots_sems)
+    cots_gather.begin()
+    for i in range(share // 16):
+        at = slice(i * 16, (i + 1) * 16)
+        value = inputs[at, :].astype(f32)
+        first_own[at, :] = (value * norm_scale(value) * gain_one[...]).astype(bf16)
+    table_local = pltpu.make_async_copy(table, tables.at[ep], table_own_sem)
+    table_local.start()
+    table_copies = [
+        send(table, tables.at[ep], table_sems.at[0, k], table_sems.at[1, k], device)
+        for k, device in enumerate(peers)
+    ]
+    bias[...] = jnp.where(visible_columns(info_cols[...], info_rows[...]), 0.0, -1e30)
+    log_sums[...] = jnp.zeros_like(log_sums)
+    group_gather_body(me, 4, first_own, rows_out, own_sem, gather_sems)
+
+    def to_peer(i):
+        source, target = ((leave_near, leave_far), (enter_near, enter_far))[i]
+        return send(source, target, far_sems.at[0, i], far_sems.at[1, i], me.x_peer())
+
+    exchanged = [to_peer(0)]
+    cots_gather.relay(1)
+    rows = rows_out[...].reshape(tokens, width)
+
+    def rotate(part):
+        turned = jnp.concatenate([part[:, size // 2 :], part[:, : size // 2]], axis=1)
+        return (part * cosine[...] - turned * sine[...]).astype(bf16)
+
+    projected = dot(rows, w_query[...], (1, 1))
+    for head in range(heads):
+        mine = slice(head * size, (head + 1) * size)
+        queries[:, mine] = rotate(projected[:, mine])
+    projected = dot(rows, w_key[...], (1, 1))
+    for group in range(groups):
+        mine = slice(group * size, (group + 1) * size)
+        keys[:, mine] = rotate(projected[:, mine])
+    values[...] = dot(rows, w_value[...], (1, 1)).astype(bf16)
+    for head in range(heads):
+        mine = slice(head * size, (head + 1) * size)
+        shared = slice(head // per_group * size, (head // per_group + 1) * size)
+        scores = dot(keys[:, shared], queries[:, mine], (1, 1)) * scale + bias[...]
+        top = jnp.max(scores, axis=0, keepdims=True)
+        powers = jnp.exp(scores - top)
+        total = jnp.sum(powers, axis=0, keepdims=True)
+        log_sums[head : head + 1, :] = top + jnp.log(total)
+        probs = (powers / total).astype(bf16)
+        heads_out[:, mine] = dot(probs, values[:, shared], (0, 0)).astype(bf16)
+        if head == 1:
+            cots_gather.relay(2)
+    tile = 512
+    for n in range(width // tile):
+        cols = slice(n * tile, (n + 1) * tile)
+        sums = dot(heads_out[...], w_out[:, cols], (1, 0)).astype(bf16)
+        parts[:, :, :, cols] = sums.reshape(2, 2, share, tile)
+    group = GroupTotal(me, parts, core_got, pair_got, group_sems)
+    group.begin()
+    for step in range(3, depth):
+        cots_gather.relay(step)
+    group.exchange()
+    exchanged.append(to_peer(1))
+    cots_gather.cross(0, 3)
+
+    def last(value, at):
+        total = inputs[at, :].astype(f32) + value
+        normed_own[at, :] = (total * norm_scale(total) * gain_two[...]).astype(bf16)
+        return total
+
+    group.finish(middle, last)
+    normed_gather = LinkGather(me, normed_own, normed_all, normed_sems)
+    normed_gather.begin()
+    cots_gather.cross(3, 2 * depth - 1)
+    for step in range(1, depth):
+        normed_gather.relay(step)
+    normed_gather.cross(0, 2 * depth - 1)
+    cots_gather.finish()
+    normed_gather.finish()
+    group.sent()
+    table_local.wait()
+    for copy in table_copies + exchanged:
+        copy.wait()
+
+
+def token_tables(segment, position):
+    cosine, sine = rope_tables(position, HEAD_DIMENSION)
+    table = jnp.stack([segment, position])
+    return (
+        jnp.concatenate([cosine[:, 0], cosine[:, 0]], axis=1),
+        jnp.concatenate([sine[:, 0], -sine[:, 0]], axis=1),
+        jnp.pad(table.T, ((0, 0), (0, 126))),
+        jnp.pad(table, ((0, 6), (0, 0))),
+    )
+
+
+def front_by_links(inputs, gains, projections, w_out, tables, order, cots, near, ep_size):
+    share, width = inputs.shape
+    depth = ep_size // 2
+    tokens = 4 * share
+    heads = w_out.shape[0] // HEAD_DIMENSION
+    bf16, f32 = jnp.bfloat16, jnp.float32
+    dma = pltpu.SemaphoreType.DMA
+    vmem, anywhere = pl.BlockSpec(memory_space=pltpu.VMEM), pl.BlockSpec(memory_space=pltpu.HBM)
+
+    def like(*shape, dtype=bf16):
+        return jax.ShapeDtypeStruct(shape, dtype)
+
+    def gather_sems():
+        return (dma, dma((2, 2 * depth)), dma((2, 2 * depth)), dma((2, 4 * depth)))
+
+    widths = [w.shape[0] for w in projections]
+    everywhere = (depth, 2, 2, share, width)
+    return pl.pallas_call(
+        functools.partial(front_kernel, ep_size, heads),
+        out_shape=(
+            like(2, 2, share, width),
+            like(tokens, widths[0]),
+            like(tokens, widths[1]),
+            like(tokens, widths[2]),
+            like(tokens, widths[0]),
+            like(8, tokens, dtype=f32),
+            like(share, width, dtype=f32),
+            like(ep_size, *order.shape, dtype=order.dtype),
+            like(*everywhere),
+            like(*everywhere),
+            like(share, width),
+            like(*near[0].shape),
+            like(*near[1].shape),
+        ),
+        in_specs=[vmem] * 11 + [anywhere] * 4,
+        out_specs=(vmem,) * 7 + (anywhere,) * 3 + (vmem,) + (anywhere,) * 2,
+        scratch_shapes=[
+            pltpu.VMEM((share, width), bf16),
+            pltpu.VMEM((tokens, tokens), f32),
+            pltpu.VMEM((2, 2, share, width), bf16),
+            pltpu.VMEM((2, share, width), bf16),
+            pltpu.VMEM((share, width), bf16),
+            dma,
+            dma((2, 12)),
+            dma,
+            dma((2, ep_size - 1)),
+            dma((2, 3)),
+            dma((2, 2)),
+            gather_sems(),
+            gather_sems(),
+        ],
+        compiler_params=pltpu.CompilerParams(
+            collective_id=6, has_side_effects=True, vmem_limit_bytes=56 * 1024 * 1024
+        ),
+        name="front_by_links",
+    )(
+        inputs,
+        gains[0][None, :],
+        gains[1][None, :],
+        *projections,
+        w_out,
+        *tables,
+        order,
+        cots,
+        *near,
+    )
 
 
 def back_kernel(
@@ -1049,8 +1228,7 @@
     keys,
     values,
     log_sums,
-    segment,
-    position,
+    tables,
     rows_in,
     w_query,
     w_key,
@@ -1071,12 +1249,7 @@
     dma = pltpu.SemaphoreType.DMA
     vmem = pl.BlockSpec(memory_space=pltpu.VMEM)
     anywhere = pl.BlockSpec(memory_space=pltpu.HBM)
-    cosine, sine = rope_tables(position, HEAD_DIMENSION)
-    cosine = jnp.concatenate([cosine[:, 0], cosine[:, 0]], axis=1)
-    sine = jnp.concatenate([sine[:, 0], -sine[:, 0]], axis=1)
-    table = jnp.stack([segment, position])
-    info_rows = jnp.pad(table, ((0, 6), (0, 0)))
-    info_cols = jnp.pad(table.T, ((0, 0), (0, 126)))
+    cosine, sine, info_cols, info_rows = tables
     blocks = jnp.pad(small, ((0, places - small.shape[0]), (0, 0))).reshape(places, -1, 128)
     sizes = [w.shape[0] // ep_size for w in (w_query, w_key, w_value, w_out)]
     total = sum(sizes[:3])
@@ -1166,9 +1339,9 @@
     gate_got,
     up_got,
     down_got,
-    first,
-    second,
-    third,
+    first_in,
+    second_in,
+    third_in,
     small,
     gate_out,
     up_out,
@@ -1189,9 +1362,34 @@
     gate,
     up,
     down,
+    gate_far,
+    up_far,
+    down_far,
+    first,
+    second,
+    third,
     sems,
+    load_sems,
 ):
     pairs = ((rows_in, rows_out), (sums_in, sums_out))
+    loads = [
+        pltpu.make_async_copy(source, target, load_sems.at[i])
+        for i, (source, target) in enumerate(
+            (
+                (third_in, third),
+                (first_in, first),
+                (second_in, second),
+                (gate_in, gate),
+                (gate_got, gate_far),
+                (up_in, up),
+                (up_got, up_far),
+                (down_in, down),
+                (down_got, down_far),
+            )
+        )
+    ]
+    for load in loads:
+        load.start()
     copies = [
         pltpu.make_async_copy(source, target, sems.at[i]) for i, (source, target) in enumerate(pairs)
     ]
@@ -1204,18 +1402,22 @@
         copies.append(pltpu.make_async_copy(source, target, sems.at[i]))
         copies[-1].start()
 
-    trios = ((gate, gate_in, gate_got), (up, up_in, up_got), (down, down_in, down_got))
-    for i, (total, mine, got) in enumerate(trios):
-        total[...] = mine[...] + got[...].astype(f32)
-        leave(total, (gate_out, up_out, down_out)[i], 2 + i)
+    loads[0].wait()
     out[...] = third[...].astype(f32)
     leave(out, out_out, 5)
+    for load in loads[1:3]:
+        load.wait()
     at = 0
     for i, (source, target) in enumerate(((query, query_out), (key, key_out), (value, value_out))):
         for n, part in enumerate((first, second)):
             source[:, :, n * wide : (n + 1) * wide] = part[:, at : at + sizes[i], :].astype(f32)
         at += sizes[i]
         leave(source, target, 6 + i)
+    for i, (total, far) in enumerate(((gate, gate_far), (up, up_far), (down, down_far))):
+        for load in loads[3 + 2 * i : 5 + 2 * i]:
+            load.wait()
+        total[...] = total[...] + far[...].astype(f32)
+        leave(total, (gate_out, up_out, down_out)[i], 2 + i)
     experts = router_out.shape[0]
     for j in range(small.shape[1]):
         cols = slice(j * 128, (j + 1) * 128)
@@ -1246,11 +1448,11 @@
             jax.ShapeDtypeStruct((1, width), f32),
             jax.ShapeDtypeStruct((1, width), f32),
         ),
-        in_specs=[anywhere] * 2 + [vmem] * 10,
+        in_specs=[anywhere] * 11 + [vmem],
         out_specs=(anywhere,) * 9 + (vmem,) * 3,
         scratch_shapes=[pltpu.VMEM(shape, f32) for shape in shapes]
-        + [pltpu.VMEM(a.shape, f32) for a in owned]
-        + [pltpu.SemaphoreType.DMA((9,))],
+        + [pltpu.VMEM(a.shape, a.dtype) for a in (*owned, *peers, first, second, third)]
+        + [pltpu.SemaphoreType.DMA((9,))] * 2,
         compiler_params=pltpu.CompilerParams(vmem_limit_bytes=40 * 1024 * 1024),
         name="deliver",
     )(rows, sums, *owned, *peers, first, second, third, small)
@@ -1277,9 +1479,7 @@
     return lax.all_gather(value_rows, "tp", axis=0, tiled=True)
 
 
-def group_totals(value_rows, by_links, call):
-    if by_links:
-        return group_total(value_rows, lax.axis_size("ep"), call)
+def group_totals(value_rows):
     return lax.psum_scatter(value_rows, "tp", scatter_dimension=0, tiled=True).astype(jnp.float32)
 
 
@@ -1504,59 +1704,75 @@
     block_rows = 512
     by_links = lax.axis_size("tp") == 4 and lax.axis_size("ep") == 8
     order = pair_order(expert_ids, slot_order, expert_count)
+    gain_one = gain_attn.astype(jnp.float32)
+    gain_two = gain_ffn.astype(jnp.float32)
+    inputs_own = hidden_in.astype(jnp.float32)
     if by_links:
         near = expert_weights(w_gate, w_up, w_down)
-        far = [lax.ppermute(w, "tp", [(0, 2), (1, 3), (2, 0), (3, 1)]) for w in near]
+        token_info = token_tables(segment, position)
+        (
+            first_normalized,
+            query_rows,
+            key_rows,
+            value_rows,
+            head_outputs,
+            log_sums,
+            middle_own,
+            order_all,
+            cot_all,
+            normed_two,
+            normed_own,
+            *far,
+        ) = front_by_links(
+            hidden_in,
+            (gain_one, gain_two),
+            (w_query, key_projection_weight, value_projection_weight),
+            w_out,
+            token_info,
+            order,
+            cotangent,
+            near,
+            lax.axis_size("ep"),
+        )
         weights = (near[0], far[0], near[1], far[1])
+        scale_two = norm_scale(middle_own)
     else:
         weights = None
-    inputs_own = hidden_in.astype(jnp.float32)
-    gain_one = gain_attn.astype(jnp.float32)
-    gain_two = gain_ffn.astype(jnp.float32)
-    scale_one = norm_scale(inputs_own)
-    first_own = (inputs_own * scale_one * gain_one).astype(jnp.bfloat16)
-    if by_links:
-        first_normalized, order_all = front_gather(first_own, order, lax.axis_size("ep"))
-    else:
-        first_normalized = group_rows(first_own)
+        scale_one = norm_scale(inputs_own)
+        first_normalized = group_rows((inputs_own * scale_one * gain_one).astype(jnp.bfloat16))
         order_all = lax.all_gather(order, "ep")
+        cosine_lookup, sine_lookup = rope_tables(position, head_width)
+        query_proj = jnp.einsum(
+            "rd,fd->rf", first_normalized, w_query, preferred_element_type=jnp.float32
+        ).reshape(token_count, local_heads, head_width)
+        key_proj = jnp.einsum(
+            "rd,fd->rf", first_normalized, key_projection_weight, preferred_element_type=jnp.float32
+        ).reshape(token_count, local_kv, head_width)
+        query_rows = (
+            apply_rotation(query_proj, cosine_lookup, sine_lookup)
+            .astype(jnp.bfloat16)
+            .reshape(token_count, local_kv, group_factor, head_width)
+        )
+        key_rows = apply_rotation(key_proj, cosine_lookup, sine_lookup).astype(jnp.bfloat16)
+        value_rows = (
+            jnp.einsum(
+                "rd,fd->rf",
+                first_normalized,
+                value_projection_weight,
+                preferred_element_type=jnp.float32,
+            )
+            .astype(jnp.bfloat16)
+            .reshape(token_count, local_kv, head_width)
+        )
+        head_outputs, log_sums = attend_forward(query_rows, key_rows, value_rows, segment, position)
+        head_outputs = head_outputs.reshape(token_count, local_heads * head_width)
+        middle_own = inputs_own + group_totals(
+            jnp.dot(head_outputs, w_out, preferred_element_type=jnp.float32).astype(jnp.bfloat16)
+        )
+        scale_two = norm_scale(middle_own)
+        normed_own = (middle_own * scale_two * gain_two).astype(jnp.bfloat16)
+        normed_two, cot_all = gather_all(normed_own), gather_all(cotangent)
     code = pair_codes(order_all, per_owner)
-    cosine_lookup, sine_lookup = rope_tables(position, head_width)
-    query_proj = jnp.einsum(
-        "rd,fd->rf", first_normalized, w_query, preferred_element_type=jnp.float32
-    ).reshape(token_count, local_heads, head_width)
-    key_proj = jnp.einsum(
-        "rd,fd->rf", first_normalized, key_projection_weight, preferred_element_type=jnp.float32
-    ).reshape(token_count, local_kv, head_width)
-    query_rows = (
-        apply_rotation(query_proj, cosine_lookup, sine_lookup)
-        .astype(jnp.bfloat16)
-        .reshape(token_count, local_kv, group_factor, head_width)
-    )
-    key_rows = apply_rotation(key_proj, cosine_lookup, sine_lookup).astype(jnp.bfloat16)
-    value_rows = (
-        jnp.einsum(
-            "rd,fd->rf",
-            first_normalized,
-            value_projection_weight,
-            preferred_element_type=jnp.float32,
-        )
-        .astype(jnp.bfloat16)
-        .reshape(token_count, local_kv, head_width)
-    )
-    head_outputs, log_sums = attend_forward(query_rows, key_rows, value_rows, segment, position)
-    head_outputs = head_outputs.reshape(token_count, local_heads * head_width)
-    middle_own = inputs_own + group_totals(
-        jnp.dot(head_outputs, w_out, preferred_element_type=jnp.float32).astype(jnp.bfloat16),
-        by_links,
-        3,
-    )
-    scale_two = norm_scale(middle_own)
-    normed_own = (middle_own * scale_two * gain_two).astype(jnp.bfloat16)
-    if by_links:
-        normed_two, cot_all = gather_by_links([normed_own, cotangent], lax.axis_size("ep"))
-    else:
-        normed_two, cot_all = gather_all(normed_own), gather_all(cotangent)
     used = lax.dynamic_slice_in_dim(order, row_start, share, 1).T < LAST
     gates = masked_softmax(
         jnp.einsum("rd,ed->re", normed_own, w_router, preferred_element_type=jnp.float32), used
@@ -1579,13 +1795,12 @@
             grad_middle.astype(jnp.bfloat16),
             head_outputs,
             w_out,
-            query_rows.reshape(token_count, -1),
-            key_rows.reshape(token_count, -1),
-            value_rows.reshape(token_count, -1),
-            jnp.pad(log_sums[0].reshape(local_heads, token_count), ((0, -local_heads % 8), (0, 0))),
-            segment,
-            position,
-            first_normalized,
+            query_rows,
+            key_rows,
+            value_rows,
+            log_sums,
+            token_info,
+            first_normalized.reshape(token_count, model_width),
             w_query,
             key_projection_weight,
             value_projection_weight,
@@ -1661,7 +1876,7 @@
         lax.psum(g.astype(jnp.bfloat16), "ep").astype(jnp.float32)
         for g in (grad_w_query, grad_w_key, grad_w_value)
     )
-    grad_one_own = group_totals(grad_normed_one.astype(jnp.bfloat16), by_links, None)
+    grad_one_own = group_totals(grad_normed_one.astype(jnp.bfloat16))
     small = lax.psum(small, ("ep", "tp"))
     grad_input = grad_middle + norm_back(inputs_own, scale_one, gain_one, grad_one_own)
     grad_router = small[:expert_count]

time: 472 us -> 366 us (0.78)
  Pallas kernels: 397 us -> 327 us
  local copies, waits for them, and re-layouts: 32.9 us -> 18.8 us
  other arithmetic: 25.6 us -> 14.4 us
  matrix products: 12.1 us -> 3.69 us
    pallas_call x3 -> x1, Pallas kernels: 155 us -> 91.9 us  [front_by_links(): pl.pallas_call(functools.partial(front_kernel, ep_size, heads), out_shape...]
    dot_general x6 -> x0, matrix products: 8.94 us -> none  [the longest x1 2.68 us: local(): jnp.einsum('rd,fd->rf', first_normalized, w_query, preferred_element_type...]
    pallas_call x1, Pallas kernels: 110 us -> 104 us  [experts_by_links(): pl.pallas_call(functools.partial(experts_kernel, ep_size, per_owner), out...]
    unnamed x82 -> x38, local copies, waits for them, and re-layouts: 14.5 us -> 11.2 us
  transfers between devices with their start and end apart: 2 -> 0, of which waited for: 0 -> 0; matrix products, arithmetic and copies ran while one was open for 11% -> 0% of each run, Pallas kernels for 33% -> 0%
where the time goes in v9:
time: 366 us; the launch traced here: 365 us
  Pallas kernels  327 us (89%)
  local copies, waits for them, and re-layouts  18.8 us (5%)
  other arithmetic  14.4 us (4%)
  matrix products  3.69 us (1%)
    pallas_call x1, Pallas kernels, back_by_links(): pl.pallas_call(functools.partial(back_kernel, ep_size, heads, small.shape...  125 us
    pallas_call x1, Pallas kernels, experts_by_links(): pl.pallas_call(functools.partial(experts_kernel, ep_size, per_owner), out...  104 us
    pallas_call x1, Pallas kernels, front_by_links(): pl.pallas_call(functools.partial(front_kernel, ep_size, heads), out_shape...  91.9 us
    unnamed x38, local copies, waits for them, and re-layouts  11.2 us

profile of v9, /device:TPU:0, one launch (start us, length us, event | category | flops | bytes accessed | tf_op | source)
XLA Modules:
  0.0 364.7 jit_solution(11241028539502455936)
XLA Ops:
  0.7 0.7 convert_element_type.36
  1.4 1.3 reshape.142.gain_one.gain
  2.7 1.3 broadcast_in_dim.89.gain_two
  4.0 0.7 convert_element_type.35
  4.7 0.7 pad_add_fusion
  5.4 0.6 pad.26.info_rows
  6.0 1.5 select_reduce_fusion.table
  7.4 0.8 fusion.3
  8.3 0.1 copy.58
  8.5 0.7 pad.25.clone.info_cols
  9.2 0.8 pad.29.router
  10.0 1.0 multiply_sine_fusion
  11.0 1.0 pad_maximum_fusion.1
  12.0 0.1 slice_bitcast_fusion.1
  12.1 1.3 pad_maximum_fusion.enter_near.enter_own
  13.4 91.9 %front_by_links.1 = (bf16[2,2,128,1536]{3,2,1,0:T(8,128)(2,1)}, bf16[512,384]{1,0:T(8,128)(2,1)}, bf16[512,128]{1,0:T(8,128)(2,1)}, bf16[512,128]{1,0:T(8,128)(2...) custom-call(bf16[128,1536]{1,0:T(8,128)(2,1)} %inputs.3, ...), custom_call_target="tpu_custom_call" | custom-call | tf_op jit(solution)/shard_map/front_by_links/pallas_call | solution.py:917
  105.3 1.3 multiply_reduce_fusion.2
  106.7 1.2 fusion.13
  107.8 0.7 select_reduce_fusion.2
  108.6 1.0 fusion
  109.7 0.2 convert_reduce_fusion.1
  110.0 0.1 select_reduce_fusion.3
  110.1 0.1 copy.52
  110.2 0.1 select_reduce_fusion.1
  110.3 0.3 convert_reduce_fusion
  110.6 0.1 and_not_fusion
  110.7 0.1 fusion.1
  110.8 0.5 copy.60
  111.3 1.2 pad.28.clone
  112.5 103.7 %experts_by_links.1 = (f32[128,1536]{1,0:T(8,128)}, f32[128,1536]{1,0:T(8,128)}, f32[8,8,128]{2,1,0:T(8,128)}, f32[2,1536,128]{2,1,0:T(8,128)}, f32[2,1536,128]{...) custom-call(bf16[4,2,2,128,1536]{4,3,2,1,0:T(8,128)(2,1)} %get-tuple, ...), custom_call_target="tpu_custom_call" | custom-call | tf_op jit(solution)/shard_map/experts_by_links/pallas_call | solution.py:512
  216.2 0.8 slice.23
  217.0 2.2 multiply_reduce_fusion
  219.2 0.3 fusion.7
  219.6 1.3 fusion.11
  220.9 0.7 reshape.133.small_in
  221.6 124.6 %back_by_links.1 = (bf16[4,2,80,768]{3,2,1,0:T(8,128)(2,1)}, bf16[4,2,80,768]{3,2,1,0:T(8,128)(2,1)}, bf16[4,2,48,1536]{3,2,1,0:T(8,128)(2,1)}, f32[128,1536]{1,...) custom-call(bf16[128,1536]{1,0:T(8,128)(2,1)} %get-tuple-element.98., ...), custom_call_target="tpu_custom_call" | custom-call | tf_op jit(solution)/shard_map/back_by_links/pallas_call | solution.py:1261
  346.2 1.4 copy-done.2
  347.6 1.3 copy-done.3
  348.9 1.2 copy-done.4
  350.1 1.2 copy-done.5
  351.3 1.1 copy-done.6
  352.5 1.1 copy-done.7
  353.6 1.1 copy-done.8
  354.7 1.1 copy-done.9
  355.9 0.9 copy-done.10
  356.8 6.6 %deliver.1 = (f32[2,1536,128]{2,1,0:T(8,128)}, f32[2,1536,128]{2,1,0:T(8,128)}, f32[256,1536]{1,0:T(8,128)}, f32[128,1536]{1,0:T(8,128)}, bf16[128,1536]{1,0:T(8...) custom-call(f32[128,1536]{1,0:T(8,128)S(1)} %copy-done.6, ...), custom_call_target="tpu_custom_call" | custom-call | tf_op jit(solution)/shard_map/deliver/pallas_call | solution.py:1441
  363.4 0.6 reduce
  364.1 0.6 reduce.1
  (37 shorter events, 0.3 us)
Async XLA Ops:
  8.4 3.5 copy-start.15
  8.4 3.5 copy-start.16
  13.4 93.3 %copy-start.17 = (bf16[16,1536]{1,0:T(8,128)(2,1)S(1)}, bf16[16,1536]{1,0:T(8,128)(2,1)}, u32[]{:S(2)}) copy-start(bf16[16,1536]{1,0:T(8,128)(2,1)} %param.23) | copy-start | bytes 147460
  105.3 5.4 %copy-start.14 = (s32[8,16,512]{2,1,0:T(8,128)S(1)}, s32[8,16,512]{2,1,0:T(8,128)}, u32[]{:S(2)}) copy-start(s32[8,16,512]{2,1,0:T(8,128)} %get-tuple-element.57) | copy-start | bytes 786436
  112.5 104.5 %copy-start.11 = (f32[128,1536]{1,0:T(8,128)S(1)}, f32[128,1536]{1,0:T(8,128)}, u32[]{:S(2)}) copy-start(f32[128,1536]{1,0:T(8,128)} %get-tuple-element.54) | copy-start | bytes 2359300
  217.0 2.3 copy-start.12
  217.0 2.6 copy-start.13
  221.6 124.6 %copy-start = (f32[2,1536,128]{2,1,0:T(8,128)S(1)}, f32[2,1536,128]{2,1,0:T(8,128)}, u32[]{:S(2)}) copy-start(f32[2,1536,128]{2,1,0:T(8,128)} %get-tuple-element.74.gate_in) | copy-start | bytes 4718596
  221.6 124.6 %copy-start.1 = (f32[2,1536,128]{2,1,0:T(8,128)S(1)}, f32[2,1536,128]{2,1,0:T(8,128)}, u32[]{:S(2)}) copy-start(f32[2,1536,128]{2,1,0:T(8,128)} %get-tuple-element.75.up_in) | copy-start | bytes 4718596
  346.2 1.4 copy-start.2
  347.6 1.3 copy-start.3
  348.9 1.2 copy-start.4
  350.1 1.2 copy-start.5
  351.3 1.1 copy-start.6
  352.5 1.1 copy-start.7
  353.6 1.1 copy-start.8
  354.7 1.1 copy-start.9
  355.9 0.9 copy-start.10

commit v10 on v9

--- a/solution.py
+++ b/solution.py
@@ -551,109 +551,10 @@
     )(rows_all, cots_all, code.reshape(ep_size, 2, 2, rows, -1), router, *weights)
 
 
-class EpSum:
-    def __init__(self, me, grads, y_got, z_got, final, sems):
-        self.me, self.grads = me, grads
-        self.y_got, self.z_got, self.final = y_got, z_got, final
-        self.y_sems, self.z_sems, self.fz_sems, self.fy_sems = sems
-        self.counts = [g.shape[2] for g in grads]
-        self.starts = [sum(self.counts[:i]) for i in range(len(grads))]
-        self.finals = []
-
-    def y_copy(self, step, i):
-        me = self.me
-        return pltpu.make_async_remote_copy(
-            src_ref=self.grads[i].at[me.after(step + 1), 1 - me.y],
-            dst_ref=self.y_got.at[step, pl.ds(self.starts[i], self.counts[i])],
-            send_sem=self.y_sems.at[0, step, i],
-            recv_sem=self.y_sems.at[1, step, i],
-            device_id=me.y_peer(),
-            device_id_type=MESH,
-        )
-
-    def z_copy(self, step):
-        return pltpu.make_async_remote_copy(
-            src_ref=self.y_got.at[step],
-            dst_ref=self.z_got.at[step],
-            send_sem=self.z_sems.at[0, step],
-            recv_sem=self.z_sems.at[1, step],
-            device_id=self.me.device(z=self.me.after(step + 1)),
-            device_id_type=MESH,
-        )
-
-    def begin(self):
-        for step in range(self.me.depth):
-            for i in range(len(self.grads)):
-                self.y_copy(step, i).start()
-
-    def fold(self, step):
-        me = self.me
-        for i in range(len(self.grads)):
-            self.y_copy(step, i).wait_recv()
-            add_into(
-                self.y_got.at[step, pl.ds(self.starts[i], self.counts[i])],
-                self.grads[i].at[me.after(step + 1), me.y],
-            )
-        if step < me.depth - 1:
-            self.z_copy(step).start()
-
-    def settle(self):
-        me, depth = self.me, self.me.depth
-        for step in range(depth - 1):
-            self.z_copy(step).wait_recv()
-
-        def tile(i, carry):
-            at = pl.ds(pl.multiple_of(i * 16, 16), 16)
-            value = self.y_got[depth - 1, at, :].astype(jnp.float32)
-            for step in range(depth - 1):
-                value = value + self.z_got[step, at, :].astype(jnp.float32)
-            self.final[me.z, me.y, at, :] = value.astype(self.final.dtype)
-            return carry
-
-        lax.fori_loop(0, sum(self.counts) // 16, tile, 0)
-        mine = self.final.at[me.z, me.y]
-        for s in range(1, depth):
-            self.spread(mine, self.fz_sems, s, me.device(z=me.after(s)))
-        self.spread(mine, self.fy_sems, 0, me.y_peer())
-
-    def spread(self, block, sems, slot, device):
-        self.finals.append(send(block, block, sems.at[0, slot], sems.at[1, slot], device))
-
-    def pass_on(self):
-        me = self.me
-        for s in range(1, me.depth):
-            block = self.final.at[me.before(s), me.y]
-            pltpu.make_async_copy(block, block, self.fz_sems.at[1, s]).wait()
-            self.spread(block, self.fy_sems, s, me.y_peer())
-
-    def finish(self):
-        me = self.me
-        for s in range(me.depth):
-            block = self.final.at[me.before(s), 1 - me.y]
-            pltpu.make_async_copy(block, block, self.fy_sems.at[1, s]).wait()
-
-    def sent(self):
-        for copy in self.finals:
-            copy.wait_send()
-        for step in range(self.me.depth):
-            for i in range(len(self.grads)):
-                self.y_copy(step, i).wait_send()
-            if step < self.me.depth - 1:
-                self.z_copy(step).wait_send()
-
-
-def visible_columns(info_cols, info_rows):
-    key_seg, key_pos = info_cols[:, 0:1], info_cols[:, 1:2]
-    query_seg, query_pos = info_rows[0:1, :], info_rows[1:2, :]
-    parent = jnp.where(query_seg >= 5, (query_seg - 5) // 2 + 1, -1)
-    above = (key_seg == query_seg) | (key_seg == 0) | (key_seg == parent)
-    return above & (key_pos <= query_pos)
-
-
 class LinkGather:
-    def __init__(self, me, own, out, sems):
+    def __init__(self, me, own, out, own_sem, z_sems, y_sems, core_sems):
         self.me, self.own, self.out = me, own, out
-        self.own_sem, self.z_sems, self.y_sems, self.core_sems = sems
+        self.own_sem, self.z_sems, self.y_sems, self.core_sems = own_sem, z_sems, y_sems, core_sems
         self.begun = []
         depth = me.depth
         self.found = [(me.z, 0, None)]
@@ -700,7 +601,12 @@
         self.go(source, place, self.z_sems, me.depth - 1 + d, device, condition, me.z > 0)
 
     def place(self, z, y, c):
-        return self.out.at[lax.rem(z + self.me.depth, self.me.depth), y, c]
+        at = (lax.rem(z + self.me.depth, self.me.depth), y)
+        return self.out.at[at + (c,) if self.core_sems is not None else at]
+
+    def to_sibling(self, block, slot, *conditions):
+        if self.core_sems is not None:
+            self.go(block[0], block[1], self.core_sems, slot, self.me.sibling(), *conditions)
 
     def begin(self):
         me = self.me
@@ -708,7 +614,9 @@
         self.up(self.own, mine, 1, None)
         self.down(self.own, mine, 1, None)
         self.go(self.own, mine, self.y_sems, 0, me.y_peer())
-        self.go(self.own, mine, self.core_sems, 0, me.sibling())
+        if self.core_sems is None:
+            return
+        self.to_sibling((self.own, mine), 0)
         self.local = pltpu.make_async_copy(self.own, mine, self.own_sem)
         self.local.start()
 
@@ -720,16 +628,14 @@
             if d < me.depth - 1:
                 (self.up if slot < me.depth else self.down)(block, block, d + 1, condition)
             self.go(block, block, self.y_sems, slot, me.y_peer(), condition)
-            self.go(block, block, self.core_sems, slot, me.sibling(), condition)
+            self.to_sibling((block, block), slot, condition)
 
     def cross(self, first, last):
         me = self.me
         for z, slot, condition in self.found[first:last]:
             block = self.place(z, 1 - me.y, me.c)
             self.landed(block, self.y_sems, slot, condition)
-            self.go(
-                block, block, self.core_sems, 2 * me.depth - 1 + slot, me.sibling(), condition
-            )
+            self.to_sibling((block, block), 2 * me.depth - 1 + slot, condition)
 
     def finish(self):
         me = self.me
@@ -737,8 +643,89 @@
             for y, at in ((me.y, slot), (1 - me.y, 2 * me.depth - 1 + slot)):
                 self.landed(self.place(z, y, 1 - me.c), self.core_sems, at, condition)
         self.local.wait()
+        self.sent()
+
+    def sent(self):
         for copy, conditions in self.begun:
             self.guard(*conditions)(lambda: copy().wait_send())
+
+
+class EpSum:
+    def __init__(self, me, grads, y_got, z_got, final, sems):
+        self.me, self.grads = me, grads
+        self.y_got, self.z_got, self.final = y_got, z_got, final
+        self.y_sems, self.z_sems, self.fz_sems, self.fy_sems = sems
+
+    def y_copy(self, step):
+        me = self.me
+        return pltpu.make_async_remote_copy(
+            src_ref=self.grads.at[me.after(step + 1), 1 - me.y],
+            dst_ref=self.y_got.at[step],
+            send_sem=self.y_sems.at[0, step],
+            recv_sem=self.y_sems.at[1, step],
+            device_id=me.y_peer(),
+            device_id_type=MESH,
+        )
+
+    def z_copy(self, step):
+        return pltpu.make_async_remote_copy(
+            src_ref=self.y_got.at[step],
+            dst_ref=self.z_got.at[step],
+            send_sem=self.z_sems.at[0, step],
+            recv_sem=self.z_sems.at[1, step],
+            device_id=self.me.device(z=self.me.after(step + 1)),
+            device_id_type=MESH,
+        )
+
+    def begin(self):
+        for step in range(self.me.depth):
+            self.y_copy(step).start()
+
+    def fold(self, step):
+        me = self.me
+        self.y_copy(step).wait_recv()
+        add_into(self.y_got.at[step], self.grads.at[me.after(step + 1), me.y])
+        if step < me.depth - 1:
+            self.z_copy(step).start()
+
+    def settle(self):
+        me, depth = self.me, self.me.depth
+        for step in range(depth - 1):
+            self.z_copy(step).wait_recv()
+
+        def tile(i, carry):
+            at = pl.ds(pl.multiple_of(i * 16, 16), 16)
+            value = self.y_got[depth - 1, at, :].astype(jnp.float32)
+            for step in range(depth - 1):
+                value = value + self.z_got[step, at, :].astype(jnp.float32)
+            self.final[me.z, me.y, at, :] = value.astype(self.final.dtype)
+            return carry
+
+        lax.fori_loop(0, self.final.shape[2] // 16, tile, 0)
+        mine = self.final.at[me.z, me.y]
+        self.spread = LinkGather(me, mine, self.final, None, self.fz_sems, self.fy_sems, None)
+        self.spread.begin()
+
+    def relay(self, d):
+        self.spread.relay(d)
+
+    def finish(self):
+        self.spread.cross(0, 2 * self.me.depth - 1)
+
+    def sent(self):
+        self.spread.sent()
+        for step in range(self.me.depth):
+            self.y_copy(step).wait_send()
+            if step < self.me.depth - 1:
+                self.z_copy(step).wait_send()
+
+
+def visible_columns(info_cols, info_rows):
+    key_seg, key_pos = info_cols[:, 0:1], info_cols[:, 1:2]
+    query_seg, query_pos = info_rows[0:1, :], info_rows[1:2, :]
+    parent = jnp.where(query_seg >= 5, (query_seg - 5) // 2 + 1, -1)
+    above = (key_seg == query_seg) | (key_seg == 0) | (key_seg == parent)
+    return above & (key_pos <= query_pos)
 
 
 def front_kernel(
@@ -804,7 +791,7 @@
             a, b, ((contract[:1], contract[1:]), ((), ())), preferred_element_type=f32
         )
 
-    cots_gather = LinkGather(me, cots, cots_all, cots_sems)
+    cots_gather = LinkGather(me, cots, cots_all, *cots_sems)
     cots_gather.begin()
     for i in range(share // 16):
         at = slice(i * 16, (i + 1) * 16)
@@ -872,7 +859,7 @@
         return total
 
     group.finish(middle, last)
-    normed_gather = LinkGather(me, normed_own, normed_all, normed_sems)
+    normed_gather = LinkGather(me, normed_own, normed_all, *normed_sems)
     normed_gather.begin()
     cots_gather.cross(3, 2 * depth - 1)
     for step in range(1, depth):
@@ -1005,9 +992,7 @@
     grad_proj,
     key_sum,
     value_sum,
-    part_query,
-    part_key,
-    part_value,
+    part_proj,
     part_out,
     y_got,
     z_got,
@@ -1061,14 +1046,14 @@
         source, target = ((gate_peer, gate_got), (up_peer, up_got), (down_peer, down_got))[i]
         return send(source, target, peer_sems.at[0, i], peer_sems.at[1, i], me.x_peer())
 
-    exchanged = [to_peer(0)]
+    exchanged = [to_peer(i) for i in range(3)]
     for n in range(width // tile):
         cols = slice(n * tile, (n + 1) * tile)
         grads = dot(heads_in[...], datt[:, :, :, cols].reshape(tokens, tile), (0, 0))
         part_out[:, :, :, cols] = grads.astype(bf16).reshape(depth, 2, -1, tile)
     out_sum = EpSum(
         me,
-        [part_out],
+        part_out,
         y_got_out,
         z_got_out,
         out_final,
@@ -1109,10 +1094,9 @@
             grad_proj[:, at : at + size] = rotate_back_rows(grad_key)
             at += groups * size
             grad_proj[:, at : at + size] = grad_value.astype(bf16)
-        if 1 <= head <= depth:
-            out_sum.fold(head - 1)
-    for step in range(max(heads - 1, 0), depth):
-        out_sum.fold(step)
+        if head % 2 and head // 2 < depth - 2:
+            out_sum.fold(head // 2)
+    folded = min(heads // 2, depth - 2)
 
     ends = (heads * size, (heads + groups) * size, (heads + 2 * groups) * size)
     wide = width // 2
@@ -1120,22 +1104,30 @@
     for n, final in enumerate((first_final, second_final)):
         cols = slice(n * wide, (n + 1) * wide)
         grads = dot(grad_proj[...], rows_in[:, cols], (0, 0)).astype(bf16)
-        part_query[n] = grads[: ends[0]].reshape(depth, 2, -1, wide)
-        part_key[n] = grads[ends[0] : ends[1]].reshape(depth, 2, -1, wide)
-        part_value[n] = grads[ends[1] :].reshape(depth, 2, -1, wide)
+        at, first = 0, 0
+        for end in ends:
+            piece = grads[first:end].reshape(depth, 2, -1, wide)
+            part_proj[n, :, :, at : at + piece.shape[2]] = piece
+            at, first = at + piece.shape[2], end
         sums.append(
             EpSum(
                 me,
-                [part_query.at[n], part_key.at[n], part_value.at[n]],
+                part_proj.at[n],
                 y_got.at[n],
                 z_got.at[n],
                 final,
                 (y_sems.at[n], z_sems.at[n], fz_sems.at[n], fy_sems.at[n]),
             )
         )
+        if n == 1:
+            sums[0].fold(0)
+            for step in range(max(folded, depth - 1), depth):
+                out_sum.fold(step)
+            sums[0].fold(1)
         sums[n].begin()
         if n == 0:
-            out_sum.settle()
+            for step in range(folded, depth - 1):
+                out_sum.fold(step)
     first_sum, second_sum = sums
     small_src[...] = small_in[...]
     for n in range(width // tile):
@@ -1151,16 +1143,9 @@
         for k in range(tile // 128):
             row = n * (tile // 128) + k
             small_src[last_row, row : row + 1, :] = gained[:, k * 128 : (k + 1) * 128]
-        first_sum.fold(n)
-    for step in range(width // tile, depth):
+    for step in range(2, depth - 1):
         first_sum.fold(step)
-    group = GroupTotal(me, parts, core_got, pair_got, group_sems)
-    group.begin()
-    second_sum.fold(0)
-    group.exchange()
-    exchanged += [to_peer(1), to_peer(2)]
-    out_sum.pass_on()
-    second_sum.fold(1)
+    out_sum.settle()
     small = [
         send(
             small_src.at[device[0] * 4 + device[1]],
@@ -1175,17 +1160,11 @@
         small_src.at[my_place], small_got.at[my_place], own_small_sem
     )
     own_small.start()
-    for step in range(2, depth):
-        second_sum.fold(step)
+    second_sum.fold(0)
+    first_sum.fold(depth - 1)
     first_sum.settle()
-
-    def last(value, at):
-        values_own = inputs[at, :].astype(f32)
-        factor = norm_scale(values_own)
-        return middle[at, :] + norm_back(values_own, factor, gain[...], value)
-
-    group.finish(grad_input, last)
-    second_sum.settle()
+    out_sum.relay(1)
+    second_sum.fold(1)
     own_small.wait()
     for copy in small:
         copy.wait_recv()
@@ -1204,9 +1183,31 @@
         for k, device in enumerate(others)
     ]
     small_out[my_place] = total
-    first_sum.pass_on()
+    group = GroupTotal(me, parts, core_got, pair_got, group_sems)
+    group.begin()
+    out_sum.relay(2)
+    for step in range(2, depth - 1):
+        second_sum.fold(step)
+    group.exchange()
+    first_sum.relay(1)
+    second_sum.fold(depth - 1)
+    for step in range(3, depth):
+        out_sum.relay(step)
+    second_sum.settle()
     out_sum.finish()
-    second_sum.pass_on()
+    first_sum.relay(2)
+
+    def last(value, at):
+        values_own = inputs[at, :].astype(f32)
+        factor = norm_scale(values_own)
+        return middle[at, :] + norm_back(values_own, factor, gain[...], value)
+
+    group.finish(grad_input, last)
+    second_sum.relay(1)
+    for step in range(3, depth):
+        first_sum.relay(step)
+    for step in range(2, depth):
+        second_sum.relay(step)
     first_sum.finish()
     second_sum.finish()
     for copy in spread:
@@ -1278,8 +1279,8 @@
             pltpu.VMEM((tokens, HEAD_DIMENSION), f32),
             pltpu.VMEM((tokens, HEAD_DIMENSION), f32),
         ]
-        + [pltpu.VMEM((2, depth, 2, k, wide), bf16) for k in sizes[:3]]
         + [
+            pltpu.VMEM((2, depth, 2, total, wide), bf16),
             pltpu.VMEM((depth, 2, sizes[3], width), bf16),
             pltpu.VMEM((2, depth, total, wide), bf16),
             pltpu.VMEM((2, depth - 1, total, wide), bf16),
@@ -1294,10 +1295,10 @@
             dma,
             dma((2, 12)),
         ]
-        + [dma((2, 2, depth, 3))]
-        + [dma((2, 2, depth))] * 3
-        + [dma((2, depth, 1))]
-        + [dma((2, depth))] * 3
+        + [dma((2, 2, depth)), dma((2, 2, depth))]
+        + [dma((2, 2, 2 * depth))] * 2
+        + [dma((2, depth)), dma((2, depth))]
+        + [dma((2, 2 * depth))] * 2
         + [dma((2, 3)), dma((2, places - 1)), dma((2, places - 1)), dma, dma((2, 3))],
         compiler_params=pltpu.CompilerParams(
             collective_id=5, has_side_effects=True, vmem_limit_bytes=60 * 1024 * 1024
@@ -1453,7 +1454,7 @@
         scratch_shapes=[pltpu.VMEM(shape, f32) for shape in shapes]
         + [pltpu.VMEM(a.shape, a.dtype) for a in (*owned, *peers, first, second, third)]
         + [pltpu.SemaphoreType.DMA((9,))] * 2,
-        compiler_params=pltpu.CompilerParams(vmem_limit_bytes=40 * 1024 * 1024),
+        compiler_params=pltpu.CompilerParams(vmem_limit_bytes=60 * 1024 * 1024),
         name="deliver",
     )(rows, sums, *owned, *peers, first, second, third, small)
     gate, up, down, rows, sums = results[:5]
@@ -1462,12 +1463,12 @@
     return (
         sums,
         rows,
-        first_gain[0],
+        first_gain.reshape(width),
         query,
         key,
         value,
         out,
-        second_gain[0],
+        second_gain.reshape(width),
         router,
         gate,
         up,

time: 366 us -> 371 us (1.014)
  Pallas kernels: 327 us -> 341 us
  local copies, waits for them, and re-layouts: 18.8 us -> 8.29 us
    pallas_call x1, Pallas kernels: 6.62 us -> 38.6 us  [deliver(): pl.pallas_call(functools.partial(deliver_kernel, ep_size, sizes), out_sha...]
    pallas_call x1, Pallas kernels: 125 us -> 107 us  [back_by_links(): pl.pallas_call(functools.partial(back_kernel, ep_size, heads, small.shape...]
    unnamed x38 -> x16, local copies, waits for them, and re-layouts: 11.2 us -> 0.65 us
where the time goes in v10:
time: 371 us
  Pallas kernels  341 us (92%)
  other arithmetic  15.8 us (4%)
  local copies, waits for them, and re-layouts  8.29 us (2%)
  matrix products  4.36 us (1%)
    pallas_call x1, Pallas kernels, back_by_links(): pl.pallas_call(functools.partial(back_kernel, ep_size, heads, small.shape...  107 us
    pallas_call x1, Pallas kernels, experts_by_links(): pl.pallas_call(functools.partial(experts_kernel, ep_size, per_owner), out...  104 us
    pallas_call x1, Pallas kernels, front_by_links(): pl.pallas_call(functools.partial(front_kernel, ep_size, heads), out_shape...  91.9 us
    pallas_call x1, Pallas kernels, deliver(): pl.pallas_call(functools.partial(deliver_kernel, ep_size, sizes), out_sha...  38.6 us

profile of v10, /device:TPU:0, one launch (start us, length us, event | category | flops | bytes accessed | tf_op | source)
XLA Modules:
  0.0 370.6 jit_solution(11957170758044433313)
XLA Ops:
  0.7 0.7 convert_element_type.36
  1.4 1.3 reshape.150.gain_one.gain
  2.7 1.3 broadcast_in_dim.89.gain_two
  4.0 0.7 convert_element_type.35
  4.7 0.7 pad_add_fusion
  5.4 0.6 pad.26.info_rows
  6.0 1.5 select_reduce_fusion.table
  7.4 0.8 fusion.3
  8.3 0.1 copy.58
  8.4 0.0 copy-start.4
  8.4 0.0 copy-start.5
  8.5 0.7 pad.25.clone.info_cols
  9.2 0.8 pad.29.router
  10.0 1.0 multiply_sine_fusion
  11.0 1.0 pad_maximum_fusion.1
  11.9 0.0 copy-done.4
  12.0 0.0 copy-done.5
  12.0 0.1 slice_bitcast_fusion.1
  12.1 1.3 pad_maximum_fusion.enter_near.enter_own
  13.4 91.9 %front_by_links.1 = (bf16[2,2,128,1536]{3,2,1,0:T(8,128)(2,1)}, bf16[512,384]{1,0:T(8,128)(2,1)}, bf16[512,128]{1,0:T(8,128)(2,1)}, bf16[512,128]{1,0:T(8,128)(2...) custom-call(bf16[128,1536]{1,0:T(8,128)(2,1)} %inputs.3, ...), custom_call_target="tpu_custom_call" | custom-call | tf_op jit(solution)/shard_map/front_by_links/pallas_call | solution.py:904
  105.3 0.0 copy-start.3
  105.3 1.3 multiply_reduce_fusion.2
  106.7 0.0 copy-done.6
  106.7 1.2 fusion.13
  107.8 0.7 select_reduce_fusion.2
  108.6 1.0 fusion
  109.7 0.2 convert_reduce_fusion.1
  109.9 0.1 copy.51
  110.0 0.1 select_reduce_fusion.3
  110.1 0.1 copy.52
  110.2 0.1 select_reduce_fusion.1
  110.3 0.3 convert_reduce_fusion
  110.6 0.1 and_not_fusion
  110.7 0.0 copy-done.3
  110.7 0.1 fusion.1
  110.8 0.5 copy.60
  111.3 1.2 pad.28.clone
  112.5 103.7 %experts_by_links.1 = (f32[128,1536]{1,0:T(8,128)}, f32[128,1536]{1,0:T(8,128)}, f32[8,8,128]{2,1,0:T(8,128)}, f32[2,1536,128]{2,1,0:T(8,128)}, f32[2,1536,128]{...) custom-call(bf16[4,2,2,128,1536]{4,3,2,1,0:T(8,128)(2,1)} %get-tuple, ...), custom_call_target="tpu_custom_call" | custom-call | tf_op jit(solution)/shard_map/experts_by_links/pallas_call | solution.py:512
  216.2 0.8 slice.23
  217.0 0.0 copy-start.2
  217.0 2.9 multiply_reduce_fusion
  219.9 0.3 fusion.7
  220.2 1.3 fusion.11
  221.5 0.7 reshape.139.small_in
  222.3 107.1 %back_by_links.1 = (bf16[4,2,80,768]{3,2,1,0:T(8,128)(2,1)}, bf16[4,2,80,768]{3,2,1,0:T(8,128)(2,1)}, bf16[4,2,48,1536]{3,2,1,0:T(8,128)(2,1)}, f32[128,1536]{1,...) custom-call(bf16[128,1536]{1,0:T(8,128)(2,1)} %get-tuple-element.98., ...), custom_call_target="tpu_custom_call" | custom-call | tf_op jit(solution)/shard_map/back_by_links/pallas_call | solution.py:1262
  329.3 38.6 %deliver.1 = (f32[2,1536,128]{2,1,0:T(8,128)}, f32[2,1536,128]{2,1,0:T(8,128)}, f32[256,1536]{1,0:T(8,128)}, f32[128,1536]{1,0:T(8,128)}, bf16[128,1536]{1,0:T(8...) custom-call(f32[128,1536]{1,0:T(8,128)} %get-tuple-element.72.rows_i, ...), custom_call_target="tpu_custom_call" | custom-call | tf_op jit(solution)/shard_map/deliver/pallas_call | solution.py:1442
  368.0 1.3 reduce
  369.3 1.3 reduce.1
  (15 shorter events, 0.1 us)
Async XLA Ops:
  8.4 3.5 copy-start.4
  8.4 3.5 copy-start.5
  13.4 93.3 %copy-start.6 = (bf16[16,1536]{1,0:T(8,128)(2,1)S(1)}, bf16[16,1536]{1,0:T(8,128)(2,1)}, u32[]{:S(2)}) copy-start(bf16[16,1536]{1,0:T(8,128)(2,1)} %param.23) | copy-start | bytes 147460
  105.3 5.4 %copy-start.3 = (s32[8,16,512]{2,1,0:T(8,128)S(1)}, s32[8,16,512]{2,1,0:T(8,128)}, u32[]{:S(2)}) copy-start(s32[8,16,512]{2,1,0:T(8,128)} %get-tuple-element.57) | copy-start | bytes 786436
  112.5 104.5 %copy-start = (f32[128,1536]{1,0:T(8,128)S(1)}, f32[128,1536]{1,0:T(8,128)}, u32[]{:S(2)}) copy-start(f32[128,1536]{1,0:T(8,128)} %get-tuple-element.54) | copy-start | bytes 2359300
  217.0 2.9 copy-start.1
  217.0 3.2 copy-start.2

commit v11 on v10

--- a/solution.py
+++ b/solution.py
@@ -87,11 +87,13 @@
     def y_peer(self):
         return self.device(y=1 - self.y)
 
-    def after(self, step):
-        return lax.rem(self.z + step, self.depth)
-
-    def before(self, step):
-        return lax.rem(self.z + self.depth - step, self.depth)
+    def target(self, step):
+        side = 1 - 2 * (self.z % 2)
+        offset = 2 * (1 - step % 2) + side * (1 - step // 2)
+        return lax.rem(self.z + offset + self.depth, self.depth)
+
+    def z_peer(self, step):
+        return self.device(z=self.target((1, 1, 2)[step]))
 
 
 def meet(devices):
@@ -272,7 +274,7 @@
     halves = ((enter_own, leave_own), (enter_peer, leave_peer))
 
     def where(b):
-        return me.after(b // 2 + 1), lax.rem(1 - me.y + b % 2, 2)
+        return me.target(b // 2), lax.rem(1 - me.y + b % 2, 2)
 
     def load(b, which):
         z, y = where(b)
@@ -308,7 +310,7 @@
             dst_ref=z_got.at[step, which],
             send_sem=z_sems.at[0, step, which],
             recv_sem=z_sems.at[1, step, which],
-            device_id=me.device(z=me.after(step + 1)),
+            device_id=me.z_peer(step),
             device_id_type=MESH,
         )
 
@@ -404,11 +406,11 @@
     for which in range(2):
         load(0, which).start()
 
-    def during(i, lag, body, even=False):
+    def during(i, lag, body, parity=None):
         b = i - lag
         inside = (b >= 0) & (b < blocks)
-        if even:
-            inside &= b % 2 == 0
+        if parity is not None:
+            inside &= lax.rem(b + 2 * lag, 2) == parity
         pl.when(inside)(lambda: body(b))
 
     def work(b):
@@ -442,10 +444,14 @@
             step = b // 2
             y_copy(step, which).wait_recv()
             add_into(y_got.at[step, which], core_got.at[step, me.y, which])
-
-            @pl.when(step < depth - 1)
+            for k in range(2):
+                pl.when(step == k)(lambda: z_copy(k, which).start())
+
+            @pl.when(step == 2)
             def _():
-                z_copy(step, which).start()
+                z_copy(0, which).wait_recv()
+                add_into(y_got.at[2, which], z_got.at[0, which])
+                z_copy(2, which).start()
 
         return body
 
@@ -464,9 +470,10 @@
 
     def turn(i, carry):
         during(i, 0, work)
-        during(i, 1, core_sum)
-        during(i, 2, y_sum(0), True)
-        during(i, 3, y_sum(1), True)
+        during(i, 1, core_sum, 1)
+        during(i, 2, y_sum(0), 0)
+        during(i, 3, y_sum(1), 0)
+        during(i, 0, core_sum, 0)
         pl.when(i == blocks)(lambda: small_send(i))
         return carry
 
@@ -476,7 +483,7 @@
         small_copy(k, device).wait()
     for k in range(ep_size):
         small_out[k] = small_got[2 * k] + small_got[2 * k + 1]
-    for step in range(depth - 1):
+    for step in range(1, 3):
         for which in range(2):
             z_copy(step, which).wait_recv()
 
@@ -484,7 +491,7 @@
         def tile(i, carry):
             at = pl.ds(pl.multiple_of(i * 16, 16), 16)
             total = y_got[depth - 1, which, at, :].astype(f32)
-            for step in range(depth - 1):
+            for step in range(1, 3):
                 total = total + z_got[step, which, at, :].astype(f32)
             target[at, :] = total
             return carry
@@ -659,7 +666,7 @@
     def y_copy(self, step):
         me = self.me
         return pltpu.make_async_remote_copy(
-            src_ref=self.grads.at[me.after(step + 1), 1 - me.y],
+            src_ref=self.grads.at[me.target(step), 1 - me.y],
             dst_ref=self.y_got.at[step],
             send_sem=self.y_sems.at[0, step],
             recv_sem=self.y_sems.at[1, step],
@@ -673,7 +680,7 @@
             dst_ref=self.z_got.at[step],
             send_sem=self.z_sems.at[0, step],
             recv_sem=self.z_sems.at[1, step],
-            device_id=self.me.device(z=self.me.after(step + 1)),
+            device_id=self.me.z_peer(step),
             device_id_type=MESH,
         )
 
@@ -684,19 +691,22 @@
     def fold(self, step):
         me = self.me
         self.y_copy(step).wait_recv()
-        add_into(self.y_got.at[step], self.grads.at[me.after(step + 1), me.y])
+        add_into(self.y_got.at[step], self.grads.at[me.target(step), me.y])
+        if step == 2:
+            self.z_copy(0).wait_recv()
+            add_into(self.y_got.at[2], self.z_got.at[0])
         if step < me.depth - 1:
             self.z_copy(step).start()
 
     def settle(self):
         me, depth = self.me, self.me.depth
-        for step in range(depth - 1):
+        for step in range(1, 3):
             self.z_copy(step).wait_recv()
 
         def tile(i, carry):
             at = pl.ds(pl.multiple_of(i * 16, 16), 16)
             value = self.y_got[depth - 1, at, :].astype(jnp.float32)
-            for step in range(depth - 1):
+            for step in range(1, 3):
                 value = value + self.z_got[step, at, :].astype(jnp.float32)
             self.final[me.z, me.y, at, :] = value.astype(self.final.dtype)
             return carry
@@ -720,12 +730,13 @@
                 self.z_copy(step).wait_send()
 
 
-def visible_columns(info_cols, info_rows):
-    key_seg, key_pos = info_cols[:, 0:1], info_cols[:, 1:2]
-    query_seg, query_pos = info_rows[0:1, :], info_rows[1:2, :]
+def tree_bias(segment, position):
+    query_seg, query_pos = segment[...].reshape(1, -1), position[...].reshape(1, -1)
+    table = jnp.concatenate([query_seg] * 4 + [query_pos] * 4, axis=0).astype(jnp.float32).T
+    key_seg, key_pos = table[:, 0:1].astype(jnp.int32), table[:, 4:5].astype(jnp.int32)
     parent = jnp.where(query_seg >= 5, (query_seg - 5) // 2 + 1, -1)
     above = (key_seg == query_seg) | (key_seg == 0) | (key_seg == parent)
-    return above & (key_pos <= query_pos)
+    return jnp.where(above & (key_pos <= query_pos), 0.0, -1e30)
 
 
 def front_kernel(
@@ -740,8 +751,8 @@
     w_out,
     cosine,
     sine,
-    info_cols,
-    info_rows,
+    segment,
+    position,
     table,
     cots,
     enter_near,
@@ -791,25 +802,30 @@
             a, b, ((contract[:1], contract[1:]), ((), ())), preferred_element_type=f32
         )
 
+    first_gain = gain_one[...].astype(f32).reshape(1, width)
+    second_gain = gain_two[...].astype(f32).reshape(1, width)
     cots_gather = LinkGather(me, cots, cots_all, *cots_sems)
     cots_gather.begin()
     for i in range(share // 16):
         at = slice(i * 16, (i + 1) * 16)
         value = inputs[at, :].astype(f32)
-        first_own[at, :] = (value * norm_scale(value) * gain_one[...]).astype(bf16)
+        first_own[at, :] = (value * norm_scale(value) * first_gain).astype(bf16)
     table_local = pltpu.make_async_copy(table, tables.at[ep], table_own_sem)
     table_local.start()
     table_copies = [
         send(table, tables.at[ep], table_sems.at[0, k], table_sems.at[1, k], device)
         for k, device in enumerate(peers)
     ]
-    bias[...] = jnp.where(visible_columns(info_cols[...], info_rows[...]), 0.0, -1e30)
+    bias[...] = tree_bias(segment, position)
     log_sums[...] = jnp.zeros_like(log_sums)
     group_gather_body(me, 4, first_own, rows_out, own_sem, gather_sems)
 
+    early = width // 3
+
     def to_peer(i):
-        source, target = ((leave_near, leave_far), (enter_near, enter_far))[i]
-        return send(source, target, far_sems.at[0, i], far_sems.at[1, i], me.x_peer())
+        source, target = ((leave_near, leave_far), (enter_near, enter_far))[min(i, 1)]
+        at = (pl.ds(0, leave_near.shape[0]), pl.ds(0, early), pl.ds(early, width - early))[i]
+        return send(source.at[at], target.at[at], far_sems.at[0, i], far_sems.at[1, i], me.x_peer())
 
     exchanged = [to_peer(0)]
     cots_gather.relay(1)
@@ -822,7 +838,7 @@
     projected = dot(rows, w_query[...], (1, 1))
     for head in range(heads):
         mine = slice(head * size, (head + 1) * size)
-        queries[:, mine] = rotate(projected[:, mine])
+        queries[:, mine] = rotate(projected[:, mine] * scale)
     projected = dot(rows, w_key[...], (1, 1))
     for group in range(groups):
         mine = slice(group * size, (group + 1) * size)
@@ -831,12 +847,12 @@
     for head in range(heads):
         mine = slice(head * size, (head + 1) * size)
         shared = slice(head // per_group * size, (head // per_group + 1) * size)
-        scores = dot(keys[:, shared], queries[:, mine], (1, 1)) * scale + bias[...]
+        scores = dot(keys[:, shared], queries[:, mine], (1, 1)) + bias[...]
         top = jnp.max(scores, axis=0, keepdims=True)
         powers = jnp.exp(scores - top)
         total = jnp.sum(powers, axis=0, keepdims=True)
         log_sums[head : head + 1, :] = top + jnp.log(total)
-        probs = (powers / total).astype(bf16)
+        probs = (powers * (1.0 / total)).astype(bf16)
         heads_out[:, mine] = dot(probs, values[:, shared], (0, 0)).astype(bf16)
         if head == 1:
             cots_gather.relay(2)
@@ -850,12 +866,12 @@
     for step in range(3, depth):
         cots_gather.relay(step)
     group.exchange()
-    exchanged.append(to_peer(1))
+    exchanged += [to_peer(1), to_peer(2)]
     cots_gather.cross(0, 3)
 
     def last(value, at):
         total = inputs[at, :].astype(f32) + value
-        normed_own[at, :] = (total * norm_scale(total) * gain_two[...]).astype(bf16)
+        normed_own[at, :] = (total * norm_scale(total) * second_gain).astype(bf16)
         return total
 
     group.finish(middle, last)
@@ -875,12 +891,11 @@
 
 def token_tables(segment, position):
     cosine, sine = rope_tables(position, HEAD_DIMENSION)
-    table = jnp.stack([segment, position])
     return (
         jnp.concatenate([cosine[:, 0], cosine[:, 0]], axis=1),
         jnp.concatenate([sine[:, 0], -sine[:, 0]], axis=1),
-        jnp.pad(table.T, ((0, 0), (0, 126))),
-        jnp.pad(table, ((0, 6), (0, 0))),
+        segment,
+        position,
     )
 
 
@@ -931,7 +946,7 @@
             dma,
             dma((2, ep_size - 1)),
             dma((2, 3)),
-            dma((2, 2)),
+            dma((2, 3)),
             gather_sems(),
             gather_sems(),
         ],
@@ -941,8 +956,7 @@
         name="front_by_links",
     )(
         inputs,
-        gains[0][None, :],
-        gains[1][None, :],
+        *gains,
         *projections,
         w_out,
         *tables,
@@ -963,8 +977,8 @@
     keys,
     values,
     log_sums,
-    info_cols,
-    info_rows,
+    segment,
+    position,
     cosine,
     sine,
     rows_in,
@@ -1039,7 +1053,7 @@
             a, b, ((contract[:1], contract[1:]), ((), ())), preferred_element_type=f32
         )
 
-    bias[...] = jnp.where(visible_columns(info_cols[...], info_rows[...]), 0.0, -1e30)
+    bias[...] = tree_bias(segment, position)
     group_gather_body(me, 4, datt_own, datt, own_sem, gather_sems)
 
     def to_peer(i):
@@ -1075,13 +1089,13 @@
         shared = slice(group * size, (group + 1) * size)
         query, grad_head = queries[:, mine], grad_heads[:, mine]
         key, value = keys[:, shared], values[:, shared]
-        scores = dot(key, query, (1, 1)) * scale + bias[...]
+        scores = dot(key, query, (1, 1)) + bias[...]
         probs = jnp.exp(scores - log_sums[head : head + 1, :])
         grad_probs = dot(value, grad_head, (1, 1))
         inner = jnp.sum(probs * grad_probs, axis=0, keepdims=True)
         grad_scores = (probs * (grad_probs - inner)).astype(bf16)
         grad_value = dot(probs.astype(bf16), grad_head, (1, 0))
-        grad_key = dot(grad_scores, query, (1, 0)) * scale
+        grad_key = dot(grad_scores, query, (1, 0))
         if head % per_group:
             grad_value = grad_value + value_sum[...]
             grad_key = grad_key + key_sum[...]
@@ -1130,6 +1144,7 @@
                 out_sum.fold(step)
     first_sum, second_sum = sums
     small_src[...] = small_in[...]
+    own_gain = gain[...].astype(f32).reshape(1, width)
     for n in range(width // tile):
         cols = slice(n * tile, (n + 1) * tile)
         grads = (
@@ -1139,7 +1154,7 @@
         )
         parts[:, :, :, cols] = grads.astype(bf16).reshape(2, 2, share, tile)
         gained = jnp.sum(grads * rows_in[:, cols].astype(f32), axis=0, keepdims=True)
-        gained = gained / gain[:, cols]
+        gained = gained / own_gain[:, cols]
         for k in range(tile // 128):
             row = n * (tile // 128) + k
             small_src[last_row, row : row + 1, :] = gained[:, k * 128 : (k + 1) * 128]
@@ -1200,7 +1215,7 @@
     def last(value, at):
         values_own = inputs[at, :].astype(f32)
         factor = norm_scale(values_own)
-        return middle[at, :] + norm_back(values_own, factor, gain[...], value)
+        return middle[at, :] + norm_back(values_own, factor, own_gain, value)
 
     group.finish(grad_input, last)
     second_sum.relay(1)
@@ -1250,7 +1265,7 @@
     dma = pltpu.SemaphoreType.DMA
     vmem = pl.BlockSpec(memory_space=pltpu.VMEM)
     anywhere = pl.BlockSpec(memory_space=pltpu.HBM)
-    cosine, sine, info_cols, info_rows = tables
+    cosine, sine, segment, position = tables
     blocks = jnp.pad(small, ((0, places - small.shape[0]), (0, 0))).reshape(places, -1, 128)
     sizes = [w.shape[0] // ep_size for w in (w_query, w_key, w_value, w_out)]
     total = sum(sizes[:3])
@@ -1312,8 +1327,8 @@
         keys,
         values,
         log_sums,
-        info_cols,
-        info_rows,
+        segment,
+        position,
         cosine,
         sine,
         rows_in,
@@ -1321,7 +1336,7 @@
         w_key,
         w_value,
         blocks,
-        gain[None, :],
+        gain,
         inputs,
         middle,
         *peers,
@@ -1369,10 +1384,11 @@
     first,
     second,
     third,
+    rows,
+    sums,
     sems,
     load_sems,
 ):
-    pairs = ((rows_in, rows_out), (sums_in, sums_out))
     loads = [
         pltpu.make_async_copy(source, target, load_sems.at[i])
         for i, (source, target) in enumerate(
@@ -1386,16 +1402,14 @@
                 (up_got, up_far),
                 (down_in, down),
                 (down_got, down_far),
+                (rows_in, rows),
+                (sums_in, sums),
             )
         )
     ]
     for load in loads:
         load.start()
-    copies = [
-        pltpu.make_async_copy(source, target, sems.at[i]) for i, (source, target) in enumerate(pairs)
-    ]
-    for copy in copies:
-        copy.start()
+    copies = []
     wide = first.shape[2]
     f32 = jnp.float32
 
@@ -1419,12 +1433,16 @@
             load.wait()
         total[...] = total[...] + far[...].astype(f32)
         leave(total, (gate_out, up_out, down_out)[i], 2 + i)
+    for load in loads[9:]:
+        load.wait()
+    leave(rows, rows_out, 0)
+    leave(sums, sums_out, 1)
     experts = router_out.shape[0]
     for j in range(small.shape[1]):
         cols = slice(j * 128, (j + 1) * 128)
         router_out[:, cols] = small[:experts, j, :]
-        first_gain[:, cols] = small[experts + 1 : experts + 2, j, :]
-        second_gain[:, cols] = small[experts : experts + 1, j, :]
+        first_gain[cols] = small[experts + 1, j, :]
+        second_gain[cols] = small[experts, j, :]
     for copy in copies:
         copy.wait()
 
@@ -1446,14 +1464,15 @@
         + tuple(jax.ShapeDtypeStruct(shape, f32) for shape in shapes)
         + (
             jax.ShapeDtypeStruct((expert_count, width), f32),
-            jax.ShapeDtypeStruct((1, width), f32),
-            jax.ShapeDtypeStruct((1, width), f32),
+            jax.ShapeDtypeStruct((width,), f32),
+            jax.ShapeDtypeStruct((width,), f32),
         ),
         in_specs=[anywhere] * 11 + [vmem],
         out_specs=(anywhere,) * 9 + (vmem,) * 3,
         scratch_shapes=[pltpu.VMEM(shape, f32) for shape in shapes]
         + [pltpu.VMEM(a.shape, a.dtype) for a in (*owned, *peers, first, second, third)]
-        + [pltpu.SemaphoreType.DMA((9,))] * 2,
+        + [pltpu.VMEM(a.shape, a.dtype) for a in (rows, sums)]
+        + [pltpu.SemaphoreType.DMA((9,)), pltpu.SemaphoreType.DMA((11,))],
         compiler_params=pltpu.CompilerParams(vmem_limit_bytes=60 * 1024 * 1024),
         name="deliver",
     )(rows, sums, *owned, *peers, first, second, third, small)
@@ -1463,12 +1482,12 @@
     return (
         sums,
         rows,
-        first_gain.reshape(width),
+        first_gain,
         query,
         key,
         value,
         out,
-        second_gain.reshape(width),
+        second_gain,
         router,
         gate,
         up,
@@ -1524,9 +1543,7 @@
     kept = kept_pairs(turned[:, :per_owner])
     dropped = jnp.pad(~kept, ((0, 0), (0, expert_count - per_owner), (0, 0)))
     code = jnp.where(turned < LAST, dropped.astype(jnp.float32), -1.0)
-    code = code.swapaxes(1, 2).reshape(-1, expert_count)
-    lanes = -expert_count % 128
-    return jnp.pad(code, ((0, 0), (0, lanes)), constant_values=-1.0).astype(jnp.bfloat16)
+    return code.swapaxes(1, 2).reshape(-1, expert_count).astype(jnp.bfloat16)
 
 
 def expert_weights(w_gate, w_up, w_down):
@@ -1540,7 +1557,6 @@
     ep_size, tp_size = lax.axis_size("ep"), lax.axis_size("tp")
     hidden = per_owner * units
     router = jnp.roll(w_router, -lax.axis_index("ep") * per_owner, axis=0)
-    router = jnp.pad(router, ((0, -expert_count % 128), (0, 0)))
     if by_links:
         grads, sums, small, *owned = experts_by_links(
             rows_all, cots_all, code, router, weights, per_owner, ep_size
@@ -1726,7 +1742,7 @@
             *far,
         ) = front_by_links(
             hidden_in,
-            (gain_one, gain_two),
+            (gain_attn, gain_ffn),
             (w_query, key_projection_weight, value_projection_weight),
             w_out,
             token_info,
@@ -1806,7 +1822,7 @@
             key_projection_weight,
             value_projection_weight,
             jnp.concatenate([grad_router, grad_gain_ffn[None, :]], axis=0),
-            gain_one,
+            gain_attn,
             hidden_in,
             grad_middle,
             peers,

time: 371 us -> 331 us (0.89)
  Pallas kernels: 341 us -> 309 us
  local copies, waits for them, and re-layouts: 8.29 us -> 3.13 us
    pallas_call x1, Pallas kernels: 38.6 us -> 10.6 us  [deliver(): pl.pallas_call(functools.partial(deliver_kernel, ep_size, sizes), out_sha...]
    pallas_call x1, Pallas kernels: 104 us -> 99.1 us  [experts_by_links(): pl.pallas_call(functools.partial(experts_kernel, ep_size, per_owner), out...]
where the time goes in v11:
time: 331 us
  Pallas kernels  309 us (93%)
  other arithmetic  13.2 us (4%)
  matrix products  4.34 us (1%)
    pallas_call x1, Pallas kernels, back_by_links(): pl.pallas_call(functools.partial(back_kernel, ep_size, heads, small.shape...  108 us
    pallas_call x1, Pallas kernels, experts_by_links(): pl.pallas_call(functools.partial(experts_kernel, ep_size, per_owner), out...  99.1 us
    pallas_call x1, Pallas kernels, front_by_links(): pl.pallas_call(functools.partial(front_kernel, ep_size, heads), out_shape...  91.7 us
    pallas_call x1, Pallas kernels, deliver(): pl.pallas_call(functools.partial(deliver_kernel, ep_size, sizes), out_sha...  10.6 us

profile of v11, /device:TPU:0, one launch (start us, length us, event | category | flops | bytes accessed | tf_op | source)
XLA Modules:
  0.0 330.6 jit_solution(10999148446837002544)
XLA Ops:
  0.6 0.0 copy-start.4
  0.7 0.0 copy-start.5
  0.7 0.8 convert_element_type.41
  1.5 0.7 convert_element_type.48
  2.2 1.5 select_reduce_fusion.table
  3.7 1.5 fusion.3.router
  5.1 1.0 multiply_sine_fusion
  6.1 1.0 pad_maximum_fusion.1
  7.1 0.0 copy-done.4
  7.1 0.0 copy-done.5
  7.1 0.1 slice_bitcast_fusion.1
  7.2 1.3 pad_maximum_fusion.enter_near.enter_own
  8.6 0.0 copy-start.6
  8.6 91.7 %front_by_links.1 = (bf16[2,2,128,1536]{3,2,1,0:T(8,128)(2,1)}, bf16[512,384]{1,0:T(8,128)(2,1)}, bf16[512,128]{1,0:T(8,128)(2,1)}, bf16[512,128]{1,0:T(8,128)(2...) custom-call(bf16[128,1536]{1,0:T(8,128)(2,1)} %inputs.3, ...), custom_call_target="tpu_custom_call" | custom-call | tf_op jit(solution)/shard_map/front_by_links/pallas_call | solution.py:919
  100.3 0.0 copy-start.3
  100.3 1.3 multiply_reduce_fusion.2
  101.6 0.0 copy-done.6
  101.6 1.2 fusion.12
  102.8 0.7 select_reduce_fusion.2
  103.6 1.0 fusion
  104.6 0.2 convert_reduce_fusion.1
  104.9 0.1 copy.40
  104.9 0.1 select_reduce_fusion.3
  105.1 0.1 copy.41
  105.2 0.1 select_reduce_fusion.1
  105.3 0.3 convert_reduce_fusion
  105.6 0.1 and_not_fusion
  105.7 0.0 copy-done.3
  105.7 0.1 fusion.1
  105.8 1.3 copy.44
  107.1 0.0 copy-start
  107.1 99.1 %experts_by_links.1 = (f32[128,1536]{1,0:T(8,128)}, f32[128,1536]{1,0:T(8,128)}, f32[8,8,128]{2,1,0:T(8,128)}, f32[2,1536,128]{2,1,0:T(8,128)}, f32[2,1536,128]{...) custom-call(bf16[4,2,2,128,1536]{4,3,2,1,0:T(8,128)(2,1)} %get-tuple, ...), custom_call_target="tpu_custom_call" | custom-call | tf_op jit(solution)/shard_map/experts_by_links/pallas_call | solution.py:519
  206.2 0.8 slice.23
  207.0 0.0 copy-done
  207.0 0.0 copy-start.2
  207.0 0.0 copy-start.1
  207.0 2.9 multiply_reduce_fusion
  209.9 0.0 copy-done.2
  209.9 0.3 fusion.7
  210.2 0.0 copy-done.1
  210.2 1.3 fusion.10
  211.5 0.7 reshape.128.small_in
  212.3 107.6 %back_by_links.1 = (bf16[4,2,80,768]{3,2,1,0:T(8,128)(2,1)}, bf16[4,2,80,768]{3,2,1,0:T(8,128)(2,1)}, bf16[4,2,48,1536]{3,2,1,0:T(8,128)(2,1)}, f32[128,1536]{1,...) custom-call(bf16[128,1536]{1,0:T(8,128)(2,1)} %get-tuple-element.98., ...), custom_call_target="tpu_custom_call" | custom-call | tf_op jit(solution)/shard_map/back_by_links/pallas_call | solution.py:1277
  319.9 10.6 %deliver.1 = (f32[2,1536,128]{2,1,0:T(8,128)}, f32[2,1536,128]{2,1,0:T(8,128)}, f32[256,1536]{1,0:T(8,128)}, f32[128,1536]{1,0:T(8,128)}, bf16[128,1536]{1,0:T(8...) custom-call(f32[128,1536]{1,0:T(8,128)} %get-tuple-element.72.rows_i, ...), custom_call_target="tpu_custom_call" | custom-call | tf_op jit(solution)/shard_map/deliver/pallas_call | solution.py:1460
  (9 shorter events, 0.1 us)
Async XLA Ops:
  0.6 6.5 %copy-start.4 = (bf16[2,1536,128]{2,1,0:T(8,128)(2,1)S(1)}, bf16[2,1536,128]{2,1,0:T(8,128)(2,1)}, u32[]{:S(2)}) copy-start(bf16[2,1536,128]{2,1,0:T(8,128)(2,1)} %param.25) | copy-start | bytes 2359300
  0.7 6.5 %copy-start.5 = (bf16[2,1536,128]{2,1,0:T(8,128)(2,1)S(1)}, bf16[2,1536,128]{2,1,0:T(8,128)(2,1)}, u32[]{:S(2)}) copy-start(bf16[2,1536,128]{2,1,0:T(8,128)(2,1)} %param.24) | copy-start | bytes 2359300
  8.6 93.1 %copy-start.6 = (bf16[16,1536]{1,0:T(8,128)(2,1)S(1)}, bf16[16,1536]{1,0:T(8,128)(2,1)}, u32[]{:S(2)}) copy-start(bf16[16,1536]{1,0:T(8,128)(2,1)} %param.23) | copy-start | bytes 147460
  100.3 5.4 %copy-start.3 = (s32[8,16,512]{2,1,0:T(8,128)S(1)}, s32[8,16,512]{2,1,0:T(8,128)}, u32[]{:S(2)}) copy-start(s32[8,16,512]{2,1,0:T(8,128)} %get-tuple-element.57) | copy-start | bytes 786436
  107.1 99.9 %copy-start = (f32[128,1536]{1,0:T(8,128)S(1)}, f32[128,1536]{1,0:T(8,128)}, u32[]{:S(2)}) copy-start(f32[128,1536]{1,0:T(8,128)} %get-tuple-element.54) | copy-start | bytes 2359300
  207.0 2.9 copy-start.2
  207.0 3.2 copy-start.1

commit v12 on v11

--- a/solution.py
+++ b/solution.py
@@ -9,6 +9,7 @@
 
 HEAD_DIMENSION = 64
 TREE_TOKENS = 512
+TRUNK = 256
 CAP = 2304
 
 
@@ -169,14 +170,21 @@
             )
             for k, x in enumerate((1 - me.x, me.x))
         ]
-        self.pair = pltpu.make_async_remote_copy(
-            src_ref=core_got.at[1 - me.x],
-            dst_ref=pair_got,
-            send_sem=sems.at[0, 2],
-            recv_sem=sems.at[1, 2],
-            device_id=me.x_peer(),
-            device_id_type=MESH,
-        )
+        self.half = pair_got.shape[0] // 2
+        self.pair = [
+            pltpu.make_async_remote_copy(
+                src_ref=core_got.at[1 - me.x, self.rows(part)],
+                dst_ref=pair_got.at[self.rows(part)],
+                send_sem=sems.at[0, 2 + part],
+                recv_sem=sems.at[1, 2 + part],
+                device_id=me.x_peer(),
+                device_id_type=MESH,
+            )
+            for part in range(2)
+        ]
+
+    def rows(self, part):
+        return pl.ds(part * self.half, self.half)
 
     def begin(self):
         for copy in self.core:
@@ -185,15 +193,18 @@
     def exchange(self):
         self.core[0].wait_recv()
         far = 1 - self.me.x
-        add_into(self.core_got.at[far], self.parts.at[far, self.me.c])
-        self.pair.start()
-
-    def finish(self, out, change=lambda value, at: value):
-        self.core[1].wait_recv()
-        self.pair.wait_recv()
+        for part, copy in enumerate(self.pair):
+            rows = self.rows(part)
+            add_into(self.core_got.at[far, rows], self.parts.at[far, self.me.c, rows])
+            copy.start()
+
+    def finish(self, out, change, part):
+        if part == 0:
+            self.core[1].wait_recv()
+        self.pair[part].wait_recv()
 
         def tile(i, carry):
-            at = pl.ds(pl.multiple_of(i * 16, 16), 16)
+            at = pl.ds(pl.multiple_of(part * self.half + i * 16, 16), 16)
             value = (
                 self.parts[self.me.x, self.me.c, at, :].astype(jnp.float32)
                 + self.core_got[self.me.x, at, :].astype(jnp.float32)
@@ -202,10 +213,10 @@
             out[at, :] = change(value, at)
             return carry
 
-        lax.fori_loop(0, out.shape[0] // 16, tile, 0)
+        lax.fori_loop(0, self.half // 16, tile, 0)
 
     def sent(self):
-        for copy in self.core + [self.pair]:
+        for copy in self.core + self.pair:
             copy.wait_send()
 
 
@@ -559,8 +570,10 @@
 
 
 class LinkGather:
-    def __init__(self, me, own, out, own_sem, z_sems, y_sems, core_sems):
-        self.me, self.own, self.out = me, own, out
+    def __init__(self, me, own, out, own_sem, z_sems, y_sems, core_sems, rows=None):
+        self.me, self.own, self.out, self.rows = me, own, out, rows
+        if rows is not None:
+            self.own = own.at[rows]
         self.own_sem, self.z_sems, self.y_sems, self.core_sems = own_sem, z_sems, y_sems, core_sems
         self.begun = []
         depth = me.depth
@@ -609,7 +622,9 @@
 
     def place(self, z, y, c):
         at = (lax.rem(z + self.me.depth, self.me.depth), y)
-        return self.out.at[at + (c,) if self.core_sems is not None else at]
+        if self.core_sems is not None:
+            at += (c,)
+        return self.out.at[at if self.rows is None else at + (self.rows,)]
 
     def to_sibling(self, block, slot, *conditions):
         if self.core_sems is not None:
@@ -728,6 +743,10 @@
             self.y_copy(step).wait_send()
             if step < self.me.depth - 1:
                 self.z_copy(step).wait_send()
+
+
+def parts_of_tree(tokens):
+    return ((slice(0, TRUNK), TRUNK), (slice(TRUNK, tokens), tokens))
 
 
 def tree_bias(segment, position):
@@ -782,7 +801,8 @@
     group_sems,
     far_sems,
     cots_sems,
-    normed_sems,
+    first_sems,
+    second_sems,
 ):
     me = Place(ep_size)
     depth = me.depth
@@ -847,13 +867,15 @@
     for head in range(heads):
         mine = slice(head * size, (head + 1) * size)
         shared = slice(head // per_group * size, (head // per_group + 1) * size)
-        scores = dot(keys[:, shared], queries[:, mine], (1, 1)) + bias[...]
-        top = jnp.max(scores, axis=0, keepdims=True)
-        powers = jnp.exp(scores - top)
-        total = jnp.sum(powers, axis=0, keepdims=True)
-        log_sums[head : head + 1, :] = top + jnp.log(total)
-        probs = (powers * (1.0 / total)).astype(bf16)
-        heads_out[:, mine] = dot(probs, values[:, shared], (0, 0)).astype(bf16)
+        for cols, last_key in parts_of_tree(tokens):
+            scores = dot(keys[:last_key, shared], queries[cols, mine], (1, 1))
+            scores = scores + bias[:last_key, cols]
+            top = jnp.max(scores, axis=0, keepdims=True)
+            powers = jnp.exp(scores - top)
+            total = jnp.sum(powers, axis=0, keepdims=True)
+            log_sums[head : head + 1, cols] = top + jnp.log(total)
+            probs = (powers * (1.0 / total)).astype(bf16)
+            heads_out[cols, mine] = dot(probs, values[:last_key, shared], (0, 0)).astype(bf16)
         if head == 1:
             cots_gather.relay(2)
     tile = 512
@@ -874,15 +896,20 @@
         normed_own[at, :] = (total * norm_scale(total) * second_gain).astype(bf16)
         return total
 
-    group.finish(middle, last)
-    normed_gather = LinkGather(me, normed_own, normed_all, *normed_sems)
-    normed_gather.begin()
+    halves = []
+    for part, sems in enumerate((first_sems, second_sems)):
+        group.finish(middle, last, part)
+        rows = pl.ds(part * (share // 2), share // 2)
+        halves.append(LinkGather(me, normed_own, normed_all, *sems, rows))
+        halves[part].begin()
     cots_gather.cross(3, 2 * depth - 1)
     for step in range(1, depth):
-        normed_gather.relay(step)
-    normed_gather.cross(0, 2 * depth - 1)
-    cots_gather.finish()
-    normed_gather.finish()
+        for gather in halves:
+            gather.relay(step)
+    for gather in halves:
+        gather.cross(0, 2 * depth - 1)
+    for gather in [cots_gather] + halves:
+        gather.finish()
     group.sent()
     table_local.wait()
     for copy in table_copies + exchanged:
@@ -945,8 +972,9 @@
             dma((2, 12)),
             dma,
             dma((2, ep_size - 1)),
+            dma((2, 4)),
             dma((2, 3)),
-            dma((2, 3)),
+            gather_sems(),
             gather_sems(),
             gather_sems(),
         ],
@@ -1079,33 +1107,40 @@
             at = pl.ds((x * 2 + c) * share, share)
             grad_heads[at, :] = dot(datt[x, c], w_out[...], (1, 1)).astype(bf16)
 
-    def rotate_back_rows(grads):
+    def rotate_back_rows(grads, at):
         turned = jnp.concatenate([grads[:, size // 2 :], grads[:, : size // 2]], axis=1)
-        return (grads * cosine[...] + turned * sine[...]).astype(bf16)
+        return (grads * cosine[at, :] + turned * sine[at, :]).astype(bf16)
 
     for head in range(heads):
         group = head // per_group
         mine = slice(head * size, (head + 1) * size)
         shared = slice(group * size, (group + 1) * size)
-        query, grad_head = queries[:, mine], grad_heads[:, mine]
-        key, value = keys[:, shared], values[:, shared]
-        scores = dot(key, query, (1, 1)) + bias[...]
-        probs = jnp.exp(scores - log_sums[head : head + 1, :])
-        grad_probs = dot(value, grad_head, (1, 1))
-        inner = jnp.sum(probs * grad_probs, axis=0, keepdims=True)
-        grad_scores = (probs * (grad_probs - inner)).astype(bf16)
-        grad_value = dot(probs.astype(bf16), grad_head, (1, 0))
-        grad_key = dot(grad_scores, query, (1, 0))
+        grads = []
+        for cols, last_key in parts_of_tree(tokens):
+            query, grad_head = queries[cols, mine], grad_heads[cols, mine]
+            key, value = keys[:last_key, shared], values[:last_key, shared]
+            scores = dot(key, query, (1, 1)) + bias[:last_key, cols]
+            probs = jnp.exp(scores - log_sums[head : head + 1, cols])
+            grad_probs = dot(value, grad_head, (1, 1))
+            inner = jnp.sum(probs * grad_probs, axis=0, keepdims=True)
+            grad_scores = (probs * (grad_probs - inner)).astype(bf16)
+            grads.append(
+                (dot(probs.astype(bf16), grad_head, (1, 0)), dot(grad_scores, query, (1, 0)))
+            )
+            grad_query = dot(grad_scores, key, (0, 0)) * scale
+            grad_proj[cols, mine] = rotate_back_rows(grad_query, cols)
+        grad_value, grad_key = (
+            jnp.concatenate([trunk + both[:TRUNK], both[TRUNK:]], axis=0)
+            for trunk, both in zip(*grads)
+        )
         if head % per_group:
             grad_value = grad_value + value_sum[...]
             grad_key = grad_key + key_sum[...]
         value_sum[...] = grad_value
         key_sum[...] = grad_key
-        grad_query = dot(grad_scores, key, (0, 0)) * scale
-        grad_proj[:, mine] = rotate_back_rows(grad_query)
         if head % per_group == per_group - 1:
             at = heads * size + group * size
-            grad_proj[:, at : at + size] = rotate_back_rows(grad_key)
+            grad_proj[:, at : at + size] = rotate_back_rows(grad_key, slice(0, tokens))
             at += groups * size
             grad_proj[:, at : at + size] = grad_value.astype(bf16)
         if head % 2 and head // 2 < depth - 2:
@@ -1217,7 +1252,8 @@
         factor = norm_scale(values_own)
         return middle[at, :] + norm_back(values_own, factor, own_gain, value)
 
-    group.finish(grad_input, last)
+    for part in range(2):
+        group.finish(grad_input, last, part)
     second_sum.relay(1)
     for step in range(3, depth):
         first_sum.relay(step)
@@ -1314,7 +1350,7 @@
         + [dma((2, 2, 2 * depth))] * 2
         + [dma((2, depth)), dma((2, depth))]
         + [dma((2, 2 * depth))] * 2
-        + [dma((2, 3)), dma((2, places - 1)), dma((2, places - 1)), dma, dma((2, 3))],
+        + [dma((2, 4)), dma((2, places - 1)), dma((2, places - 1)), dma, dma((2, 3))],
         compiler_params=pltpu.CompilerParams(
             collective_id=5, has_side_effects=True, vmem_limit_bytes=60 * 1024 * 1024
         ),

time: 331 us -> 331 us (level)
  no operation moved by 1% of the time
where the time goes in v12:
time: 331 us; the launch traced here: 330 us
  Pallas kernels  308 us (93%)
  other arithmetic  13.2 us (4%)
  matrix products  4.35 us (1%)
    pallas_call x1, Pallas kernels, back_by_links(): pl.pallas_call(functools.partial(back_kernel, ep_size, heads, small.shape...  109 us
    pallas_call x1, Pallas kernels, experts_by_links(): pl.pallas_call(functools.partial(experts_kernel, ep_size, per_owner), out...  99.7 us
    pallas_call x1, Pallas kernels, front_by_links(): pl.pallas_call(functools.partial(front_kernel, ep_size, heads), out_shape...  89.3 us
    pallas_call x1, Pallas kernels, deliver(): pl.pallas_call(functools.partial(deliver_kernel, ep_size, sizes), out_sha...  10.6 us

profile of v12, /device:TPU:0, one launch (start us, length us, event | category | flops | bytes accessed | tf_op | source)
XLA Modules:
  0.0 329.9 jit_solution(5144321657603190500)
XLA Ops:
  0.6 0.0 copy-start.4
  0.7 0.0 copy-start.5
  0.7 0.8 convert_element_type.41
  1.5 0.7 convert_element_type.48
  2.2 1.5 select_reduce_fusion.table
  3.7 1.5 fusion.3.router
  5.1 1.0 multiply_sine_fusion
  6.1 1.0 pad_maximum_fusion.1
  7.1 0.0 copy-done.4
  7.1 0.0 copy-done.5
  7.1 0.1 slice_bitcast_fusion.1
  7.2 1.3 pad_maximum_fusion.enter_near.enter_own
  8.6 0.0 copy-start.6
  8.6 89.3 %front_by_links.1 = (bf16[2,2,128,1536]{3,2,1,0:T(8,128)(2,1)}, bf16[512,384]{1,0:T(8,128)(2,1)}, bf16[512,128]{1,0:T(8,128)(2,1)}, bf16[512,128]{1,0:T(8,128)(2...) custom-call(bf16[128,1536]{1,0:T(8,128)(2,1)} %inputs.3, ...), custom_call_target="tpu_custom_call" | custom-call | tf_op jit(solution)/shard_map/front_by_links/pallas_call | solution.py:946
  97.9 0.0 copy-start.3
  97.9 1.3 multiply_reduce_fusion.2
  99.2 0.0 copy-done.6
  99.2 1.2 fusion.12
  100.4 0.7 select_reduce_fusion.2
  101.2 1.0 fusion
  102.2 0.2 convert_reduce_fusion.1
  102.5 0.1 copy.40
  102.5 0.1 select_reduce_fusion.3
  102.7 0.1 copy.41
  102.8 0.1 select_reduce_fusion.1
  102.9 0.3 convert_reduce_fusion
  103.2 0.1 and_not_fusion
  103.3 0.0 copy-done.3
  103.3 0.1 fusion.1
  103.4 1.3 copy.44
  104.7 0.0 copy-start
  104.7 99.7 %experts_by_links.1 = (f32[128,1536]{1,0:T(8,128)}, f32[128,1536]{1,0:T(8,128)}, f32[8,8,128]{2,1,0:T(8,128)}, f32[2,1536,128]{2,1,0:T(8,128)}, f32[2,1536,128]{...) custom-call(bf16[4,2,2,128,1536]{4,3,2,1,0:T(8,128)(2,1)} %get-tuple, ...), custom_call_target="tpu_custom_call" | custom-call | tf_op jit(solution)/shard_map/experts_by_links/pallas_call | solution.py:530
  204.5 0.8 slice.23
  205.3 0.0 copy-done
  205.3 0.0 copy-start.2
  205.3 0.0 copy-start.1
  205.3 2.9 multiply_reduce_fusion
  208.2 0.0 copy-done.2
  208.2 0.3 fusion.7
  208.5 0.0 copy-done.1
  208.5 1.3 fusion.10
  209.8 0.7 reshape.128.small_in
  210.5 108.6 %back_by_links.1 = (bf16[4,2,80,768]{3,2,1,0:T(8,128)(2,1)}, bf16[4,2,80,768]{3,2,1,0:T(8,128)(2,1)}, bf16[4,2,48,1536]{3,2,1,0:T(8,128)(2,1)}, f32[128,1536]{1,...) custom-call(bf16[128,1536]{1,0:T(8,128)(2,1)} %get-tuple-element.98., ...), custom_call_target="tpu_custom_call" | custom-call | tf_op jit(solution)/shard_map/back_by_links/pallas_call | solution.py:1313
  319.2 10.6 %deliver.1 = (f32[2,1536,128]{2,1,0:T(8,128)}, f32[2,1536,128]{2,1,0:T(8,128)}, f32[256,1536]{1,0:T(8,128)}, f32[128,1536]{1,0:T(8,128)}, bf16[128,1536]{1,0:T(8...) custom-call(f32[128,1536]{1,0:T(8,128)} %get-tuple-element.72.rows_i, ...), custom_call_target="tpu_custom_call" | custom-call | tf_op jit(solution)/shard_map/deliver/pallas_call | solution.py:1496
  (9 shorter events, 0.1 us)
Async XLA Ops:
  0.6 6.5 %copy-start.4 = (bf16[2,1536,128]{2,1,0:T(8,128)(2,1)S(1)}, bf16[2,1536,128]{2,1,0:T(8,128)(2,1)}, u32[]{:S(2)}) copy-start(bf16[2,1536,128]{2,1,0:T(8,128)(2,1)} %param.25) | copy-start | bytes 2359300
  0.7 6.5 %copy-start.5 = (bf16[2,1536,128]{2,1,0:T(8,128)(2,1)S(1)}, bf16[2,1536,128]{2,1,0:T(8,128)(2,1)}, u32[]{:S(2)}) copy-start(bf16[2,1536,128]{2,1,0:T(8,128)(2,1)} %param.24) | copy-start | bytes 2359300
  8.6 90.7 %copy-start.6 = (bf16[16,1536]{1,0:T(8,128)(2,1)S(1)}, bf16[16,1536]{1,0:T(8,128)(2,1)}, u32[]{:S(2)}) copy-start(bf16[16,1536]{1,0:T(8,128)(2,1)} %param.23) | copy-start | bytes 147460
  97.9 5.4 %copy-start.3 = (s32[8,16,512]{2,1,0:T(8,128)S(1)}, s32[8,16,512]{2,1,0:T(8,128)}, u32[]{:S(2)}) copy-start(s32[8,16,512]{2,1,0:T(8,128)} %get-tuple-element.57) | copy-start | bytes 786436
  104.7 100.5 %copy-start = (f32[128,1536]{1,0:T(8,128)S(1)}, f32[128,1536]{1,0:T(8,128)}, u32[]{:S(2)}) copy-start(f32[128,1536]{1,0:T(8,128)} %get-tuple-element.54) | copy-start | bytes 2359300
  205.3 2.9 copy-start.2
  205.3 3.2 copy-start.1

commit v13 on v12

--- a/solution.py
+++ b/solution.py
@@ -97,11 +97,14 @@
         return self.device(z=self.target((1, 1, 2)[step]))
 
 
-def meet(devices):
+def greet(devices):
     barrier = pltpu.get_barrier_semaphore()
     for device in devices:
         pl.semaphore_signal(barrier, inc=1, device_id=device, device_id_type=MESH)
-    pl.semaphore_wait(barrier, len(devices))
+
+
+def meet(devices):
+    pl.semaphore_wait(pltpu.get_barrier_semaphore(), len(devices))
 
 
 def send(src, dst, send_sem, recv_sem, device):
@@ -280,7 +283,7 @@
         (lax.rem(ep + k // 2, ep_size), me.x * 2 + lax.rem(me.c + k % 2, 2))
         for k in range(1, 2 * ep_size)
     ]
-    meet(others)
+    greet(others)
     my_place = ep * 2 + me.c
     halves = ((enter_own, leave_own), (enter_peer, leave_peer))
 
@@ -412,8 +415,6 @@
             enter_sum[:, cols] += dot(turned[...], rows, (0, 0))
             down_sum[:, cols] += dot(weighted[...], cots, (0, 0))
 
-    enter_sum[...] = jnp.zeros_like(enter_sum)
-    down_sum[...] = jnp.zeros_like(down_sum)
     for which in range(2):
         load(0, which).start()
 
@@ -434,7 +435,14 @@
                 load(b + 1, which).start()
 
         compute(b)
+        pl.when(b == 0)(lambda: meet(others))
         core_copy(b).start()
+
+        @pl.when(b == 0)
+        def _():
+            enter_sum[...] = jnp.zeros_like(enter_sum)
+            down_sum[...] = jnp.zeros_like(down_sum)
+
         weight_sums(b)
 
     def core_sum(b):
@@ -815,7 +823,8 @@
     scale = size ** (-0.5)
     ep, tp = lax.axis_index("ep"), lax.axis_index("tp")
     peers = [(lax.rem(ep + k, ep_size), tp) for k in range(1, ep_size)]
-    meet([me.sibling(), me.x_peer()] + peers)
+    friends = [me.sibling(), me.x_peer()] + peers
+    greet(friends)
 
     def dot(a, b, contract):
         return lax.dot_general(
@@ -824,12 +833,13 @@
 
     first_gain = gain_one[...].astype(f32).reshape(1, width)
     second_gain = gain_two[...].astype(f32).reshape(1, width)
-    cots_gather = LinkGather(me, cots, cots_all, *cots_sems)
-    cots_gather.begin()
     for i in range(share // 16):
         at = slice(i * 16, (i + 1) * 16)
         value = inputs[at, :].astype(f32)
         first_own[at, :] = (value * norm_scale(value) * first_gain).astype(bf16)
+    meet(friends)
+    cots_gather = LinkGather(me, cots, cots_all, *cots_sems)
+    cots_gather.begin()
     table_local = pltpu.make_async_copy(table, tables.at[ep], table_own_sem)
     table_local.start()
     table_copies = [
@@ -1066,7 +1076,7 @@
     depth = me.depth
     f32, bf16 = jnp.float32, jnp.bfloat16
     others = all_others(ep_size)
-    meet(others)
+    greet(others)
     my_place = lax.axis_index("ep") * 4 + lax.axis_index("tp")
     tokens, width = rows_in.shape
     share = datt_own.shape[0]
@@ -1082,6 +1092,7 @@
         )
 
     bias[...] = tree_bias(segment, position)
+    meet(others)
     group_gather_body(me, 4, datt_own, datt, own_sem, gather_sems)
 
     def to_peer(i):
@@ -1443,7 +1454,7 @@
             )
         )
     ]
-    for load in loads:
+    for load in loads[:3]:
         load.start()
     copies = []
     wide = first.shape[2]
@@ -1454,10 +1465,14 @@
         copies[-1].start()
 
     loads[0].wait()
+    for load in loads[3:5]:
+        load.start()
     out[...] = third[...].astype(f32)
     leave(out, out_out, 5)
     for load in loads[1:3]:
         load.wait()
+    for load in loads[5:]:
+        load.start()
     at = 0
     for i, (source, target) in enumerate(((query, query_out), (key, key_out), (value, value_out))):
         for n, part in enumerate((first, second)):

time: 331 us -> 324 us (0.979)
  Pallas kernels: 308 us -> 302 us
    pallas_call x1, Pallas kernels: 99.7 us -> 95.2 us  [experts_by_links(): pl.pallas_call(functools.partial(experts_kernel, ep_size, per_owner), out...]
where the time goes in v13:
time: 324 us
  Pallas kernels  302 us (93%)
  other arithmetic  13.2 us (4%)
  matrix products  4.35 us (1%)
    pallas_call x1, Pallas kernels, back_by_links(): pl.pallas_call(functools.partial(back_kernel, ep_size, heads, small.shape...  108 us
    pallas_call x1, Pallas kernels, experts_by_links(): pl.pallas_call(functools.partial(experts_kernel, ep_size, per_owner), out...  95.2 us
    pallas_call x1, Pallas kernels, front_by_links(): pl.pallas_call(functools.partial(front_kernel, ep_size, heads), out_shape...  88.9 us
    pallas_call x1, Pallas kernels, deliver(): pl.pallas_call(functools.partial(deliver_kernel, ep_size, sizes), out_sha...  10.5 us

profile of v13, /device:TPU:0, one launch (start us, length us, event | category | flops | bytes accessed | tf_op | source)
XLA Modules:
  0.0 323.9 jit_solution(13648260298393175780)
XLA Ops:
  0.6 0.0 copy-start.4
  0.7 0.0 copy-start.5
  0.7 0.8 convert_element_type.41
  1.5 0.7 convert_element_type.48
  2.2 1.5 select_reduce_fusion.table
  3.7 1.5 fusion.3.router
  5.1 1.0 multiply_sine_fusion
  6.1 1.0 pad_maximum_fusion.1
  7.1 0.0 copy-done.4
  7.1 0.0 copy-done.5
  7.1 0.1 slice_bitcast_fusion.1
  7.2 1.3 pad_maximum_fusion.enter_near.enter_own
  8.6 0.0 copy-start.6
  8.6 88.9 %front_by_links.1 = (bf16[2,2,128,1536]{3,2,1,0:T(8,128)(2,1)}, bf16[512,384]{1,0:T(8,128)(2,1)}, bf16[512,128]{1,0:T(8,128)(2,1)}, bf16[512,128]{1,0:T(8,128)(2...) custom-call(bf16[128,1536]{1,0:T(8,128)(2,1)} %inputs.3, ...), custom_call_target="tpu_custom_call" | custom-call | tf_op jit(solution)/shard_map/front_by_links/pallas_call | solution.py:956
  97.5 0.0 copy-start.3
  97.5 1.3 multiply_reduce_fusion.2
  98.8 0.0 copy-done.6
  98.8 1.2 fusion.12
  100.0 0.7 select_reduce_fusion.2
  100.8 1.0 fusion
  101.8 0.2 convert_reduce_fusion.1
  102.1 0.1 copy.40
  102.1 0.1 select_reduce_fusion.3
  102.3 0.1 copy.41
  102.4 0.1 select_reduce_fusion.1
  102.5 0.3 convert_reduce_fusion
  102.8 0.1 and_not_fusion
  102.9 0.0 copy-done.3
  102.9 0.1 fusion.1
  103.0 1.3 copy.44
  104.3 0.0 copy-start
  104.3 95.2 %experts_by_links.1 = (f32[128,1536]{1,0:T(8,128)}, f32[128,1536]{1,0:T(8,128)}, f32[8,8,128]{2,1,0:T(8,128)}, f32[2,1536,128]{2,1,0:T(8,128)}, f32[2,1536,128]{...) custom-call(bf16[4,2,2,128,1536]{4,3,2,1,0:T(8,128)(2,1)} %get-tuple, ...), custom_call_target="tpu_custom_call" | custom-call | tf_op jit(solution)/shard_map/experts_by_links/pallas_call | solution.py:538
  199.5 0.8 slice.23
  200.3 0.0 copy-done
  200.3 0.0 copy-start.2
  200.3 0.0 copy-start.1
  200.3 2.9 multiply_reduce_fusion
  203.2 0.0 copy-done.2
  203.2 0.3 fusion.7
  203.5 0.0 copy-done.1
  203.5 1.3 fusion.10
  204.8 0.7 reshape.128.small_in
  205.6 107.7 %back_by_links.1 = (bf16[4,2,80,768]{3,2,1,0:T(8,128)(2,1)}, bf16[4,2,80,768]{3,2,1,0:T(8,128)(2,1)}, bf16[4,2,48,1536]{3,2,1,0:T(8,128)(2,1)}, f32[128,1536]{1,...) custom-call(bf16[128,1536]{1,0:T(8,128)(2,1)} %get-tuple-element.98., ...), custom_call_target="tpu_custom_call" | custom-call | tf_op jit(solution)/shard_map/back_by_links/pallas_call | solution.py:1324
  313.3 10.5 %deliver.1 = (f32[2,1536,128]{2,1,0:T(8,128)}, f32[2,1536,128]{2,1,0:T(8,128)}, f32[256,1536]{1,0:T(8,128)}, f32[128,1536]{1,0:T(8,128)}, bf16[128,1536]{1,0:T(8...) custom-call(f32[128,1536]{1,0:T(8,128)} %get-tuple-element.72.rows_i, ...), custom_call_target="tpu_custom_call" | custom-call | tf_op jit(solution)/shard_map/deliver/pallas_call | solution.py:1511
  (9 shorter events, 0.1 us)
Async XLA Ops:
  0.6 6.5 %copy-start.4 = (bf16[2,1536,128]{2,1,0:T(8,128)(2,1)S(1)}, bf16[2,1536,128]{2,1,0:T(8,128)(2,1)}, u32[]{:S(2)}) copy-start(bf16[2,1536,128]{2,1,0:T(8,128)(2,1)} %param.25) | copy-start | bytes 2359300
  0.7 6.5 %copy-start.5 = (bf16[2,1536,128]{2,1,0:T(8,128)(2,1)S(1)}, bf16[2,1536,128]{2,1,0:T(8,128)(2,1)}, u32[]{:S(2)}) copy-start(bf16[2,1536,128]{2,1,0:T(8,128)(2,1)} %param.24) | copy-start | bytes 2359300
  8.6 90.3 %copy-start.6 = (bf16[16,1536]{1,0:T(8,128)(2,1)S(1)}, bf16[16,1536]{1,0:T(8,128)(2,1)}, u32[]{:S(2)}) copy-start(bf16[16,1536]{1,0:T(8,128)(2,1)} %param.23) | copy-start | bytes 147460
  97.5 5.4 %copy-start.3 = (s32[8,16,512]{2,1,0:T(8,128)S(1)}, s32[8,16,512]{2,1,0:T(8,128)}, u32[]{:S(2)}) copy-start(s32[8,16,512]{2,1,0:T(8,128)} %get-tuple-element.57) | copy-start | bytes 786436
  104.3 96.0 %copy-start = (f32[128,1536]{1,0:T(8,128)S(1)}, f32[128,1536]{1,0:T(8,128)}, u32[]{:S(2)}) copy-start(f32[128,1536]{1,0:T(8,128)} %get-tuple-element.54) | copy-start | bytes 2359300
  200.3 2.9 copy-start.2
  200.3 3.2 copy-start.1

commit v14 on v13

--- a/solution.py
+++ b/solution.py
@@ -490,10 +490,10 @@
     def turn(i, carry):
         during(i, 0, work)
         during(i, 1, core_sum, 1)
+        pl.when(i == blocks)(lambda: small_send(i))
         during(i, 2, y_sum(0), 0)
         during(i, 3, y_sum(1), 0)
         during(i, 0, core_sum, 0)
-        pl.when(i == blocks)(lambda: small_send(i))
         return carry
 
     lax.fori_loop(0, blocks + 2, turn, 0)
@@ -1189,7 +1189,9 @@
             for step in range(folded, depth - 1):
                 out_sum.fold(step)
     first_sum, second_sum = sums
-    small_src[...] = small_in[...]
+    small_src[...] = jnp.zeros_like(small_src)
+    for k in range(width // 128):
+        small_src[:last_row, k, :] = small_in[:, k * 128 : (k + 1) * 128]
     own_gain = gain[...].astype(f32).reshape(1, width)
     for n in range(width // tile):
         cols = slice(n * tile, (n + 1) * tile)
@@ -1313,7 +1315,7 @@
     vmem = pl.BlockSpec(memory_space=pltpu.VMEM)
     anywhere = pl.BlockSpec(memory_space=pltpu.HBM)
     cosine, sine, segment, position = tables
-    blocks = jnp.pad(small, ((0, places - small.shape[0]), (0, 0))).reshape(places, -1, 128)
+    blocks = jax.ShapeDtypeStruct((places, width // 128, 128), f32)
     sizes = [w.shape[0] // ep_size for w in (w_query, w_key, w_value, w_out)]
     total = sum(sizes[:3])
 
@@ -1382,7 +1384,7 @@
         w_query,
         w_key,
         w_value,
-        blocks,
+        small,
         gain,
         inputs,
         middle,

time: 324 us -> 324 us (level)
  no operation moved by 1% of the time
where the time goes in v14:
time: 324 us
  Pallas kernels  302 us (93%)
  other arithmetic  13.8 us (4%)
  matrix products  4.34 us (1%)
    pallas_call x1, Pallas kernels, back_by_links(): pl.pallas_call(functools.partial(back_kernel, ep_size, heads, small.shape...  108 us
    pallas_call x1, Pallas kernels, experts_by_links(): pl.pallas_call(functools.partial(experts_kernel, ep_size, per_owner), out...  95.2 us
    pallas_call x1, Pallas kernels, front_by_links(): pl.pallas_call(functools.partial(front_kernel, ep_size, heads), out_shape...  88.9 us
    pallas_call x1, Pallas kernels, deliver(): pl.pallas_call(functools.partial(deliver_kernel, ep_size, sizes), out_sha...  10.5 us

profile of v14, /device:TPU:0, one launch (start us, length us, event | category | flops | bytes accessed | tf_op | source)
XLA Modules:
  0.0 323.8 jit_solution(7123271848705647685)
XLA Ops:
  0.6 0.0 copy-start.4
  0.7 0.0 copy-start.5
  0.7 0.8 convert_element_type.39
  1.5 0.7 convert_element_type.46
  2.2 1.5 select_reduce_fusion.table
  3.7 1.5 fusion.3.router
  5.1 1.0 multiply_sine_fusion
  6.1 1.0 pad_maximum_fusion.1
  7.1 0.0 copy-done.4
  7.1 0.0 copy-done.5
  7.1 0.1 slice_bitcast_fusion.1
  7.2 1.3 pad_maximum_fusion.enter_near.enter_own
  8.6 0.0 copy-start.6
  8.6 88.9 %front_by_links.1 = (bf16[2,2,128,1536]{3,2,1,0:T(8,128)(2,1)}, bf16[512,384]{1,0:T(8,128)(2,1)}, bf16[512,128]{1,0:T(8,128)(2,1)}, bf16[512,128]{1,0:T(8,128)(2...) custom-call(bf16[128,1536]{1,0:T(8,128)(2,1)} %inputs.3, ...), custom_call_target="tpu_custom_call" | custom-call | tf_op jit(solution)/shard_map/front_by_links/pallas_call | solution.py:956
  97.5 0.0 copy-start.3
  97.5 1.3 multiply_reduce_fusion.2
  98.8 0.0 copy-done.6
  98.8 1.2 fusion.12
  100.0 0.7 select_reduce_fusion.2
  100.8 1.0 fusion
  101.8 0.2 convert_reduce_fusion.1
  102.1 0.1 copy.39
  102.1 0.1 select_reduce_fusion.3
  102.3 0.1 copy.40
  102.4 0.1 select_reduce_fusion.1
  102.5 0.3 convert_reduce_fusion
  102.8 0.1 and_not_fusion
  102.9 0.0 copy-done.3
  102.9 0.1 fusion.1
  103.0 1.3 copy.43
  104.3 0.0 copy-start
  104.3 95.2 %experts_by_links.1 = (f32[128,1536]{1,0:T(8,128)}, f32[128,1536]{1,0:T(8,128)}, f32[8,8,128]{2,1,0:T(8,128)}, f32[2,1536,128]{2,1,0:T(8,128)}, f32[2,1536,128]{...) custom-call(bf16[4,2,2,128,1536]{4,3,2,1,0:T(8,128)(2,1)} %get-tuple, ...), custom_call_target="tpu_custom_call" | custom-call | tf_op jit(solution)/shard_map/experts_by_links/pallas_call | solution.py:538
  199.5 0.8 slice.23
  200.3 0.0 copy-done
  200.3 0.0 copy-start.2
  200.3 0.0 copy-start.1
  200.3 2.9 multiply_reduce_fusion
  203.2 0.0 copy-done.2
  203.2 0.3 fusion.7
  203.5 0.0 copy-done.1
  203.5 1.3 fusion.10
  204.8 0.7 pad_maximum_fusion.3.small_in
  205.5 107.7 %back_by_links.1 = (bf16[4,2,80,768]{3,2,1,0:T(8,128)(2,1)}, bf16[4,2,80,768]{3,2,1,0:T(8,128)(2,1)}, bf16[4,2,48,1536]{3,2,1,0:T(8,128)(2,1)}, f32[128,1536]{1,...) custom-call(bf16[128,1536]{1,0:T(8,128)(2,1)} %get-tuple-element.98., ...), custom_call_target="tpu_custom_call" | custom-call | tf_op jit(solution)/shard_map/back_by_links/pallas_call | solution.py:1326
  313.2 10.5 %deliver.1 = (f32[2,1536,128]{2,1,0:T(8,128)}, f32[2,1536,128]{2,1,0:T(8,128)}, f32[256,1536]{1,0:T(8,128)}, f32[128,1536]{1,0:T(8,128)}, bf16[128,1536]{1,0:T(8...) custom-call(f32[128,1536]{1,0:T(8,128)} %get-tuple-element.72.rows_i, ...), custom_call_target="tpu_custom_call" | custom-call | tf_op jit(solution)/shard_map/deliver/pallas_call | solution.py:1513
  (8 shorter events, 0.1 us)
Async XLA Ops:
  0.6 6.5 %copy-start.4 = (bf16[2,1536,128]{2,1,0:T(8,128)(2,1)S(1)}, bf16[2,1536,128]{2,1,0:T(8,128)(2,1)}, u32[]{:S(2)}) copy-start(bf16[2,1536,128]{2,1,0:T(8,128)(2,1)} %param.25) | copy-start | bytes 2359300
  0.7 6.5 %copy-start.5 = (bf16[2,1536,128]{2,1,0:T(8,128)(2,1)S(1)}, bf16[2,1536,128]{2,1,0:T(8,128)(2,1)}, u32[]{:S(2)}) copy-start(bf16[2,1536,128]{2,1,0:T(8,128)(2,1)} %param.24) | copy-start | bytes 2359300
  8.6 90.3 %copy-start.6 = (bf16[16,1536]{1,0:T(8,128)(2,1)S(1)}, bf16[16,1536]{1,0:T(8,128)(2,1)}, u32[]{:S(2)}) copy-start(bf16[16,1536]{1,0:T(8,128)(2,1)} %param.23) | copy-start | bytes 147460
  97.5 5.4 %copy-start.3 = (s32[8,16,512]{2,1,0:T(8,128)S(1)}, s32[8,16,512]{2,1,0:T(8,128)}, u32[]{:S(2)}) copy-start(s32[8,16,512]{2,1,0:T(8,128)} %get-tuple-element.57) | copy-start | bytes 786436
  104.3 96.0 %copy-start = (f32[128,1536]{1,0:T(8,128)S(1)}, f32[128,1536]{1,0:T(8,128)}, u32[]{:S(2)}) copy-start(f32[128,1536]{1,0:T(8,128)} %get-tuple-element.54) | copy-start | bytes 2359300
  200.3 2.9 copy-start.2
  200.3 3.2 copy-start.1
